TPU v7x, 32 devices: a whole 2x2x4 slice. The times are simulated.
32 devices in a mesh: dp: 4 (over y, x), mp: 8 (over z, core).
Axes of the slice: x: 2, y: 2, z: 4, core: 2. Of those that a mesh axis runs over, the one named last changes fastest.
Arguments:
- fields: float32 [4, 2048, 192], P('dp', 'mp'), may hold values from -6 to 6
- targets: float32 [4, 2, 2048, 192], P('dp', None, 'mp'), may hold values from -6 to 6
- land_mask: int32 [4, 2048, 4], P('dp', 'mp'), may hold values 0 or 1
- lead_index: int32 [4, 2], P('dp'), may hold values from 0 to 6
- var_ids: int32 [48], replicated, may hold values from 0 to 47, each once
- tables: float32 [440, 1024], replicated, may hold values from -4 to 4
- norm_gains: float32 [6, 1024], replicated, may hold values from -0.5 to 1.4, as said below
- tables_first: float32 [440, 1024], replicated, may hold values from -9.536743e-06 to 9.536743e-06
- tables_second: float32 [440, 1024], replicated, may hold values from 9.586172e-14 to 1.5337875e-12
- gains_first: float32 [6, 1024], replicated, may hold values from -3.8146973e-05 to 3.8146973e-05
- gains_second: float32 [6, 1024], replicated, may hold values from 1.5337875e-12 to 2.45406e-11
- w_qkv: float32 [1024, 3072], P(None, 'mp'), may hold values from -0.1875 to 0.1875
- qkv_first: float32 [1024, 3072], P('dp', 'mp'), may hold values from -9.536743e-06 to 9.536743e-06
- qkv_second: float32 [1024, 3072], P('dp', 'mp'), may hold values from 9.586172e-14 to 1.5337875e-12
- w_out: float32 [1024, 1024], P('mp'), may hold values from -0.5 to 0.5
- out_first: float32 [1024, 1024], P('mp', 'dp'), may hold values from -9.536743e-06 to 9.536743e-06
- out_second: float32 [1024, 1024], P('mp', 'dp'), may hold values from 9.586172e-14 to 1.5337875e-12
- w_up: float32 [1024, 4096], P(None, 'mp'), may hold values from -0.1875 to 0.1875
- up_first: float32 [1024, 4096], P('dp', 'mp'), may hold values from -9.536743e-06 to 9.536743e-06
- up_second: float32 [1024, 4096], P('dp', 'mp'), may hold values from 9.586172e-14 to 1.5337875e-12
- w_down: float32 [4096, 1024], P('mp'), may hold values from -0.09375 to 0.09375
- down_first: float32 [4096, 1024], P('mp', 'dp'), may hold values from -9.536743e-06 to 9.536743e-06
- down_second: float32 [4096, 1024], P('mp', 'dp'), may hold values from 9.586172e-14 to 1.5337875e-12
- qkv_average: float32 [1024, 3072], P('dp', 'mp'), may hold values from -0.1875 to 0.1875
Outputs:
- loss: float32 [], replicated
- grad_norm: float32 [], replicated
- tables_new: float32 [440, 1024], replicated
- tables_first_new: float32 [440, 1024], replicated
- tables_second_new: float32 [440, 1024], replicated
- gains_new: float32 [6, 1024], replicated
- gains_first_new: float32 [6, 1024], replicated
- gains_second_new: float32 [6, 1024], replicated
- qkv_new: float32 [1024, 3072], P('dp', 'mp')
- qkv_first_new: float32 [1024, 3072], P('dp', 'mp')
- qkv_second_new: float32 [1024, 3072], P('dp', 'mp')
- out_new: float32 [1024, 1024], P('mp', 'dp')
- out_first_new: float32 [1024, 1024], P('mp', 'dp')
- out_second_new: float32 [1024, 1024], P('mp', 'dp')
- up_new: float32 [1024, 4096], P('dp', 'mp')
- up_first_new: float32 [1024, 4096], P('dp', 'mp')
- up_second_new: float32 [1024, 4096], P('dp', 'mp')
- down_new: float32 [4096, 1024], P('mp', 'dp')
- down_first_new: float32 [4096, 1024], P('mp', 'dp')
- down_second_new: float32 [4096, 1024], P('mp', 'dp')
- qkv_average_new: float32 [1024, 3072], P('dp', 'mp')
Inputs may be any that keep to these rules, and one draw needn't show every extreme that they name: `var_ids`: each value once. `norm_gains`: even rows gains, odd rows biases.
All inputs are finite; a program needn't handle non-finite values. No bound on the sum of `land_mask` on one device may be relied on, other than what follows from the above.
Results may differ from a plain program's by a relative error of at most 0.0054.
The roundings to bfloat16 on the way count: a program that leaves them out, or rounds other values in their place, can miss the bound.
Values may be sent and summed in bfloat16 or wider, within the bound.
A program may use at most 256 MiB of HBM per device.

v0:
```python
from functools import partial
import math

import jax
import jax.numpy as jnp
from jax import lax
from jax.sharding import PartitionSpec as P

D = 1024
HEADS = 16
HEAD_DIM = 64
V = 48
PATCH_ROWS = 32
PATCH_COLS = 64
LEADS = 7
QBLOCK = 512


highest = lax.Precision.HIGHEST
eps_norm = 1e-05
clip_norm = 0.05
beta_first = 0.9
beta_second = 0.999
adam_eps = 1e-08
decay_rate = 0.1
lr_matrix = 0.04
lr_table = 0.1
lr_gain = 0.3
average_keep = 0.9
first_fix = 1.0 - 0.9**10
second_fix = 1.0 - 0.999**10


def layer_norm(values, gain, bias):
    center = values - jnp.mean(values, axis=-1, keepdims=True)
    spread = jnp.mean(center * center, axis=-1, keepdims=True)
    return center * lax.rsqrt(spread + eps_norm) * gain + bias


def lat_weights(pixel_rows):
    row_index = jnp.arange(pixel_rows, dtype=jnp.float32)
    cosine = jnp.cos(((row_index + 0.5) / pixel_rows - 0.5) * math.pi)
    return cosine / jnp.mean(cosine)


def embed_tokens(cells, tables, var_hot, lead_hot):
    count_rows = cells.shape[0]
    patch_tab = tables[: 4 * V].reshape(V, 4, HEADS, HEAD_DIM)
    var_tab = jnp.dot(var_hot, tables[4 * V : 5 * V], precision=highest).reshape(V, HEADS, HEAD_DIM)
    lead_vec = jnp.dot(lead_hot, tables[5 * V : 5 * V + LEADS], precision=highest)
    query = tables[5 * V + LEADS].reshape(HEADS, HEAD_DIM)
    keyed = jnp.einsum("vphc,hc->vph", patch_tab, query, precision=highest)
    biased = jnp.einsum("vhc,hc->vh", var_tab, query, precision=highest)
    pixels = cells.reshape(count_rows, V, 4)
    scores = (jnp.einsum("tvp,vph->tvh", pixels, keyed, precision=highest) + biased) * HEAD_DIM ** (
        -0.5
    )
    shares = jax.nn.softmax(scores, axis=1)
    mixed = (shares[:, :, None, :] * pixels[:, :, :, None]).reshape(count_rows, 4 * V, HEADS)
    merged = jnp.einsum(
        "tkh,khc->thc", mixed, patch_tab.reshape(4 * V, HEADS, HEAD_DIM), precision=highest
    )
    merged = merged + jnp.einsum("tvh,vhc->thc", shares, var_tab, precision=highest)
    return merged.reshape(count_rows, D) + lead_vec


def predict(last_rows, gain, bias, tables):
    normed = layer_norm(last_rows, gain, bias)
    return lax.dot_general(
        normed, tables[5 * V + LEADS + 1 :], (((1,), (1,)), ((), ())), precision=highest
    )


def product_nn(left, right):
    return jnp.dot(left, right, preferred_element_type=jnp.float32)


def product_tn(left, right):
    return lax.dot_general(
        left, right, (((0,), (0,)), ((), ())), preferred_element_type=jnp.float32
    )


def product_nt(left, right):
    return lax.dot_general(
        left, right, (((1,), (1,)), ((), ())), preferred_element_type=jnp.float32
    )


def spread_rows(normed):
    return lax.all_gather(normed, "mp", axis=0, tiled=True)


def fold_rows(partial_sum):
    return lax.psum_scatter(
        partial_sum.astype(jnp.bfloat16), "mp", scatter_dimension=0, tiled=True
    ).astype(jnp.float32)


def spread_grads(grad_rows):
    return lax.all_gather(grad_rows, "mp", axis=0, tiled=True)


def fold_grads(partial_sum):
    return lax.psum_scatter(
        partial_sum.astype(jnp.bfloat16), "mp", scatter_dimension=0, tiled=True
    ).astype(jnp.float32)


def attend(queries, keys, values):
    total, heads, width = queries.shape
    blocks = queries.reshape(total // QBLOCK, QBLOCK, heads, width)

    def one_block(block):
        scores = jnp.einsum(
            "qhc,khc->hqk", block, keys, preferred_element_type=jnp.float32
        ) * width ** (-0.5)
        largest = jnp.max(scores, axis=-1, keepdims=True)
        raised = jnp.exp(scores - largest)
        totals = jnp.sum(raised, axis=-1, keepdims=True)
        probs = (raised / totals).astype(jnp.bfloat16)
        result = jnp.einsum("hqk,khc->qhc", probs, values, preferred_element_type=jnp.float32)
        return (result.astype(jnp.bfloat16), (largest + jnp.log(totals))[..., 0])

    results, logsum = lax.map(one_block, blocks)
    return (results.reshape(total, heads * width), logsum)


def attend_back(grad_out, queries, keys, values, logsum):
    total, heads, width = queries.shape
    scale = width ** (-0.5)
    blocks = queries.reshape(total // QBLOCK, QBLOCK, heads, width)
    grad_blocks = grad_out.reshape(total // QBLOCK, QBLOCK, heads, width)

    def one_block(carry, item):
        key_grad, value_grad = carry
        block, block_grad, block_lse = item
        scores = jnp.einsum("qhc,khc->hqk", block, keys, preferred_element_type=jnp.float32) * scale
        probs = jnp.exp(scores - block_lse[..., None])
        value_grad = value_grad + jnp.einsum(
            "hqk,qhc->khc",
            probs.astype(jnp.bfloat16),
            block_grad,
            preferred_element_type=jnp.float32,
        )
        prob_grad = jnp.einsum(
            "qhc,khc->hqk", block_grad, values, preferred_element_type=jnp.float32
        )
        inner = jnp.sum(probs * prob_grad, axis=-1, keepdims=True)
        score_grad = (probs * (prob_grad - inner) * scale).astype(jnp.bfloat16)
        query_grad = jnp.einsum(
            "hqk,khc->qhc", score_grad, keys, preferred_element_type=jnp.float32
        )
        key_grad = key_grad + jnp.einsum(
            "hqk,qhc->khc", score_grad, block, preferred_element_type=jnp.float32
        )
        return ((key_grad, value_grad), query_grad)

    zeros = jnp.zeros((total, heads, width), jnp.float32)
    (key_grad, value_grad), query_grad = lax.scan(
        one_block, (zeros, zeros), (blocks, grad_blocks, logsum)
    )
    return (query_grad.reshape(total, heads, width), key_grad, value_grad)


def layer_forward(x_first, norm_gains, weights):
    w_qkv, w_out, w_up, w_down = weights
    rows_one = spread_rows(layer_norm(x_first, norm_gains[0], norm_gains[1]).astype(jnp.bfloat16))
    total = rows_one.shape[0]
    packed = product_nn(rows_one, w_qkv).astype(jnp.bfloat16).reshape(total, -1, 3, HEAD_DIM)
    attended, logsum = attend(packed[:, :, 0], packed[:, :, 1], packed[:, :, 2])
    x_mid = x_first + fold_rows(product_nn(attended, w_out))
    normed_two = layer_norm(x_mid, norm_gains[2], norm_gains[3]).astype(jnp.bfloat16)
    rows_two = spread_rows(normed_two)
    hidden = product_nn(rows_two, w_up)
    active = jax.nn.gelu(hidden, approximate=False).astype(jnp.bfloat16)
    branch_out = product_nn(active, w_down)
    x_last = x_mid + fold_rows(branch_out)
    return (x_last, (x_first, x_mid, rows_one, rows_two, packed, attended, logsum, hidden))


def norm_back(inputs, gain, bias, grad):
    _, pull = jax.vjp(layer_norm, inputs, gain, bias)
    return pull(grad)


def layer_backward(grad_last, norm_gains, weights, kept):
    w_qkv, w_out, w_up, w_down = weights
    x_first, x_mid, rows_one, rows_two, packed, attended, logsum, hidden = kept
    total = rows_one.shape[0]
    last_low = grad_last.astype(jnp.bfloat16)
    branch_grad = spread_grads(last_low)
    active = jax.nn.gelu(hidden, approximate=False).astype(jnp.bfloat16)
    down_grad = product_tn(active, branch_grad)
    _, gelu_pull = jax.vjp(partial(jax.nn.gelu, approximate=False), hidden)
    hidden_grad = gelu_pull(product_nt(branch_grad, w_down))[0].astype(jnp.bfloat16)
    up_grad = product_tn(rows_two, hidden_grad)
    unit_part = product_nt(hidden_grad, w_up)
    unit_back = fold_grads(unit_part)
    mid_part, gain_grad_two, bias_grad_two = norm_back(
        x_mid, norm_gains[2], norm_gains[3], unit_back
    )
    grad_mid = grad_last + mid_part
    grad_att = spread_grads(grad_mid.astype(jnp.bfloat16))
    out_grad = product_tn(attended, grad_att)
    attended_grad = product_nt(grad_att, w_out).astype(jnp.bfloat16).reshape(total, -1, HEAD_DIM)
    query_grad, key_grad, value_grad = attend_back(
        attended_grad, packed[:, :, 0], packed[:, :, 1], packed[:, :, 2], logsum
    )
    packed_grad = (
        jnp.stack((query_grad, key_grad, value_grad), axis=2)
        .astype(jnp.bfloat16)
        .reshape(total, -1)
    )
    qkv_grad = product_tn(rows_one, packed_grad)
    first_part, gain_grad_one, bias_grad_one = norm_back(
        x_first, norm_gains[0], norm_gains[1], fold_grads(product_nt(packed_grad, w_qkv))
    )
    gain_rows = jnp.stack((gain_grad_one, bias_grad_one, gain_grad_two, bias_grad_two))
    return (grad_mid + first_part, (qkv_grad, out_grad, up_grad, down_grad), gain_rows)


def adam_step(master, grad, first, second, rate):
    first_new = beta_first * first + (1.0 - beta_first) * grad
    second_new = beta_second * second + (1.0 - beta_second) * grad * grad
    update = first_new / first_fix / (jnp.sqrt(second_new / second_fix) + adam_eps)
    return (master - rate * (update + decay_rate * master), first_new, second_new)


def shards(
    fields,
    targets,
    land_mask,
    lead_index,
    var_ids,
    tables,
    norm_gains,
    tables_first,
    tables_second,
    gains_first,
    gains_second,
    w_qkv,
    qkv_first,
    qkv_second,
    w_out,
    out_first,
    out_second,
    w_up,
    up_first,
    up_second,
    w_down,
    down_first,
    down_second,
    qkv_average,
):
    local_samples, shard_rows, _ = fields.shape
    ocean = 1.0 - land_mask.astype(jnp.float32)
    count = lax.psum(jnp.sum(ocean), ("dp", "mp"))
    denom = 2.0 * V * jnp.maximum(count, 1.0)
    var_hot = (var_ids[:, None] == jnp.arange(V, dtype=jnp.int32)[None, :]).astype(jnp.float32)
    first_row = lax.axis_index("mp") * shard_rows
    patch_row = (first_row + jnp.arange(shard_rows, dtype=jnp.int32)) // PATCH_COLS
    row_hot = (patch_row[:, None] == jnp.arange(PATCH_ROWS, dtype=jnp.int32)[None, :]).astype(
        jnp.float32
    )
    lat_rows = jnp.dot(
        row_hot, lat_weights(2 * PATCH_ROWS).reshape(PATCH_ROWS, 2), precision=highest
    )
    lat_pixels = jnp.broadcast_to(lat_rows[:, :, None], (shard_rows, 2, 2)).reshape(shard_rows, 4)
    weights = tuple((master.astype(jnp.bfloat16) for master in (w_qkv, w_out, w_up, w_down)))
    table_grad = jnp.zeros_like(tables)
    gain_grad = jnp.zeros_like(norm_gains)
    matrix_grads = tuple((jnp.zeros(master.shape, jnp.float32) for master in weights))
    loss_part = jnp.float32(0.0)
    inputs = fields[0]
    weighted = jnp.tile(ocean[0] * lat_pixels, (1, V))
    records = []
    for rollout in range(2):
        lead_hot = (jnp.arange(LEADS, dtype=jnp.int32) == lead_index[0, rollout]).astype(
            jnp.float32
        )
        start_rows, embed_pull = jax.vjp(
            lambda cells, table: embed_tokens(cells, table, var_hot, lead_hot), inputs, tables
        )
        last_rows, kept = layer_forward(start_rows, norm_gains, weights)
        guess, head_pull = jax.vjp(predict, last_rows, norm_gains[4], norm_gains[5], tables)
        miss = guess - targets[0, rollout]
        loss_part = loss_part + jnp.sum(weighted * miss * miss)
        records.append((embed_pull, kept, head_pull, 2.0 * weighted * miss / denom))
        inputs = guess
    carried = jnp.zeros_like(inputs)
    for rollout in (1, 0):
        embed_pull, kept, head_pull, loss_grad = records[rollout]
        row_grad, gain_five, gain_six, head_tables = head_pull(loss_grad + carried)
        row_grad, matrix_part, gain_part = layer_backward(row_grad, norm_gains, weights, kept)
        carried, embed_tables = embed_pull(row_grad)
        table_grad = table_grad + head_tables + embed_tables
        gain_grad = gain_grad + jnp.concatenate(
            (gain_part, jnp.stack((gain_five, gain_six))), axis=0
        )
        matrix_grads = tuple((old + new for old, new in zip(matrix_grads, matrix_part)))
    qkv_grad, out_grad, up_grad, down_grad = matrix_grads
    share_rows = D // lax.axis_size("dp")
    dp_index = lax.axis_index("dp")

    def own_share(full, dim):
        return lax.dynamic_slice_in_dim(full, dp_index * share_rows, share_rows, dim)

    summed = lax.psum((qkv_grad, out_grad, up_grad, down_grad), "dp")
    shares = (
        own_share(summed[0], 0),
        own_share(summed[1], 1),
        own_share(summed[2], 0),
        own_share(summed[3], 1),
    )
    table_sum, gain_sum, loss_sum = lax.psum((table_grad, gain_grad, loss_part), ("dp", "mp"))
    share_square = (
        jnp.sum(shares[0] * shares[0])
        + jnp.sum(shares[1] * shares[1])
        + jnp.sum(shares[2] * shares[2])
        + jnp.sum(shares[3] * shares[3])
    )
    square_sum = lax.psum(share_square, ("dp", "mp"))
    grad_norm = jnp.sqrt(square_sum + jnp.sum(table_sum * table_sum) + jnp.sum(gain_sum * gain_sum))
    factor = jnp.minimum(1.0, clip_norm / (grad_norm + 1e-06))
    tab = adam_step(tables, factor * table_sum, tables_first, tables_second, lr_table)
    gai = adam_step(norm_gains, factor * gain_sum, gains_first, gains_second, lr_gain)
    qkv = adam_step(own_share(w_qkv, 0), factor * shares[0], qkv_first, qkv_second, lr_matrix)
    outp = adam_step(own_share(w_out, 1), factor * shares[1], out_first, out_second, lr_matrix)
    upp = adam_step(own_share(w_up, 0), factor * shares[2], up_first, up_second, lr_matrix)
    down = adam_step(own_share(w_down, 1), factor * shares[3], down_first, down_second, lr_matrix)
    average = average_keep * qkv_average + (1.0 - average_keep) * qkv[0]
    return (
        loss_sum / denom,
        grad_norm,
        tab[0],
        tab[1],
        tab[2],
        gai[0],
        gai[1],
        gai[2],
        qkv[0],
        qkv[1],
        qkv[2],
        outp[0],
        outp[1],
        outp[2],
        upp[0],
        upp[1],
        upp[2],
        down[0],
        down[1],
        down[2],
        average,
    )


def solution(mesh):
    return jax.shard_map(
        shards,
        mesh=mesh,
        in_specs=(
            P("dp", "mp", None),
            P("dp", None, "mp", None),
            P("dp", "mp", None),
            P("dp", None),
            P(),
            P(),
            P(),
            P(),
            P(),
            P(),
            P(),
            P(None, "mp"),
            P("dp", "mp"),
            P("dp", "mp"),
            P("mp", None),
            P("mp", "dp"),
            P("mp", "dp"),
            P(None, "mp"),
            P("dp", "mp"),
            P("dp", "mp"),
            P("mp", None),
            P("mp", "dp"),
            P("mp", "dp"),
            P("dp", "mp"),
        ),
        out_specs=(
            P(),
            P(),
            P(),
            P(),
            P(),
            P(),
            P(),
            P(),
            P("dp", "mp"),
            P("dp", "mp"),
            P("dp", "mp"),
            P("mp", "dp"),
            P("mp", "dp"),
            P("mp", "dp"),
            P("dp", "mp"),
            P("dp", "mp"),
            P("dp", "mp"),
            P("mp", "dp"),
            P("mp", "dp"),
            P("mp", "dp"),
            P("dp", "mp"),
        ),
        check_vma=False,
    )
```

profile of v0, /device:TPU:0, one launch (start us, length us, event | category | flops | bytes accessed | tf_op | source)
XLA Modules:
  0.0 1704.5 jit_solution(3737589082572562041)
XLA Ops:
  40.0 46.9 %all-gather.9.cloned.1.call-done = bf16[2048,1024]{1,0:T(8,128)(2,1)} async-done(((bf16[256,1024]{1,0:T(8,128)(2,1)}), bf16[2048,1024]{1,0:T(8,128)(2,1)}) %all-gather.9.cloned.1.call-update) | async-done | bytes 4194320 | tf_op jit(solution)/shard_map/all_gather | solution.py:91
  94.4 23.7 %while.54 = (s32[]{:T(128)}, bf16[4,512,2,64]{1,3,2,0:T(8,128)(2,1)}, f32[4,2,512]{2,1,0:T(2,128)S(1)}, bf16[4,512,2,64]{1,3,2,0:T(8,128)(2,1)S(1)}, bf16[2048,2...) while((s32[]{:T(128)}, bf16[4,512,2,64]{1,3,2,0:T(8,128)(2,1)}, ...), condition=%wide.region_8.9_spmd, body=%wide.region_5.0_spmd.sunk | while | flops 555809792 | bytes 26509408 | solution.py:125
  123.5 48.8 %reduce-scatter.9.cloned.1.call-done = bf16[256,1024]{1,0:T(8,128)(2,1)} async-done(((bf16[2048,1024]{1,0:T(8,128)(2,1)}), bf16[256,1024]{1,0:T(8,128)(2,1)}) %reduce-scatter.9.cloned.1.call-update) | async-done | bytes 524304 | tf_op jit(solution)/shard_map/reduce_scatter | solution.py:95
  181.7 39.4 %all-gather.11.cloned.1.call-done = bf16[2048,1024]{1,0:T(8,128)(2,1)} async-done(((bf16[256,1024]{1,0:T(8,128)(2,1)}), bf16[2048,1024]{1,0:T(8,128)(2,1)}) %all-gather.11.cloned.1.call-update) | async-done | bytes 4194320 | tf_op jit(solution)/shard_map/all_gather | solution.py:91
  242.5 46.5 %reduce-scatter.11.cloned.1.call-done = bf16[256,1024]{1,0:T(8,128)(2,1)} async-done(((bf16[2048,1024]{1,0:T(8,128)(2,1)}), bf16[256,1024]{1,0:T(8,128)(2,1)}) %reduce-scatter.11.cloned.1.call-update) | async-done | bytes 524304 | tf_op jit(solution)/shard_map/reduce_scatter | solution.py:95
  314.3 45.2 %all-gather.13.cloned.1.call-done = bf16[2048,1024]{1,0:T(8,128)(2,1)} async-done(((bf16[256,1024]{1,0:T(8,128)(2,1)}), bf16[2048,1024]{1,0:T(8,128)(2,1)}) %all-gather.13.cloned.1.call-update) | async-done | bytes 4194320 | tf_op jit(solution)/shard_map/all_gather | solution.py:91
  364.5 21.4 %while.55 = (s32[]{:T(128)}, bf16[4,512,2,64]{1,3,2,0:T(8,128)(2,1)S(1)}, f32[4,2,512]{2,1,0:T(2,128)S(1)}, bf16[4,512,2,64]{1,3,2,0:T(8,128)(2,1)S(1)}, bf16[20...) while((s32[]{:T(128)}, bf16[4,512,2,64]{1,3,2,0:T(8,128)(2,1)S(1)}, ...), condition=%wide.region_23.24_spmd, body=%wide.region_20.23_spmd.sunk | while | flops 555809792 | bytes 26509408 | solution.py:125
  390.1 48.8 %reduce-scatter.13.cloned.1.call-done = bf16[256,1024]{1,0:T(8,128)(2,1)} async-done(((bf16[2048,1024]{1,0:T(8,128)(2,1)}), bf16[256,1024]{1,0:T(8,128)(2,1)}) %reduce-scatter.13.cloned.1.call-update) | async-done | bytes 524304 | tf_op jit(solution)/shard_map/reduce_scatter | solution.py:95
  442.5 45.1 %all-gather.15.cloned.1.call-done = bf16[2048,1024]{1,0:T(8,128)(2,1)} async-done(((bf16[256,1024]{1,0:T(8,128)(2,1)}), bf16[2048,1024]{1,0:T(8,128)(2,1)}) %all-gather.15.cloned.1.call-update) | async-done | bytes 4194320 | tf_op jit(solution)/shard_map/all_gather | solution.py:91
  509.1 40.7 %psum.64 = f32[]{:T(128)} all-reduce(f32[]{:T(128)} %fusion.291), channel_id=1, replica_groups=mesh['dp'=4,'mp'=8] {'dp','mp'}, use_global_device_ids=true, to_apply=%region_33.34 | all-reduce | flops 1 | bytes 8 | tf_op jit(solution)/shard_map/psum | solution.py:258
  565.8 44.9 %all-gather.17.cloned.1.call-done = bf16[2048,1024]{1,0:T(8,128)(2,1)} async-done(((bf16[256,1024]{1,0:T(8,128)(2,1)}), bf16[2048,1024]{1,0:T(8,128)(2,1)}) %all-gather.17.cloned.1.call-update) | async-done | bytes 4194320 | tf_op jit(solution)/shard_map/all_gather | solution.py:101
  625.3 48.8 %reduce-scatter.17.cloned.1.call-done = bf16[256,1024]{1,0:T(8,128)(2,1)} async-done(((bf16[2048,1024]{1,0:T(8,128)(2,1)}), bf16[256,1024]{1,0:T(8,128)(2,1)}) %reduce-scatter.17.cloned.1.call-update) | async-done | bytes 524304 | tf_op jit(solution)/shard_map/reduce_scatter | solution.py:105
  679.8 45.3 %all-gather.19.cloned.1.call-done = bf16[2048,1024]{1,0:T(8,128)(2,1)} async-done(((bf16[256,1024]{1,0:T(8,128)(2,1)}), bf16[2048,1024]{1,0:T(8,128)(2,1)}) %all-gather.19.cloned.1.call-update) | async-done | bytes 4194320 | tf_op jit(solution)/shard_map/all_gather | solution.py:101
  733.3 159.9 %while.56 = (s32[]{:T(128)}, f32[2048,2,64]{0,2,1:T(8,128)}, f32[2048,2,64]{0,2,1:T(8,128)S(1)}, bf16[4,512,2,64]{1,3,2,0:T(8,128)(2,1)}, bf16[4,512,2,64]{1,3,2...) while((s32[]{:T(128)}, f32[2048,2,64]{0,2,1:T(8,128)}, ...), condition=%wide.region_41.42_spmd.clone, body=%wide.region_39.41_spmd.clone.sunk | while | flops 1387272192 | bytes 132411568 | solution.py:160
  742.5 15.8 fusion.510
  903.7 47.6 %reduce-scatter.19.cloned.1.call-done = bf16[256,1024]{1,0:T(8,128)(2,1)} async-done(((bf16[2048,1024]{1,0:T(8,128)(2,1)}), bf16[256,1024]{1,0:T(8,128)(2,1)}) %reduce-scatter.19.cloned.1.call-update) | async-done | bytes 524304 | tf_op jit(solution)/shard_map/reduce_scatter | solution.py:105
  993.3 44.9 %all-gather.21.cloned.1.call-done = bf16[2048,1024]{1,0:T(8,128)(2,1)} async-done(((bf16[256,1024]{1,0:T(8,128)(2,1)}), bf16[2048,1024]{1,0:T(8,128)(2,1)}) %all-gather.21.cloned.1.call-update) | async-done | bytes 4194320 | tf_op jit(solution)/shard_map/all_gather | solution.py:101
  1052.7 48.8 %reduce-scatter.21.cloned.1.call-done = bf16[256,1024]{1,0:T(8,128)(2,1)} async-done(((bf16[2048,1024]{1,0:T(8,128)(2,1)}), bf16[256,1024]{1,0:T(8,128)(2,1)}) %reduce-scatter.21.cloned.1.call-update) | async-done | bytes 524304 | tf_op jit(solution)/shard_map/reduce_scatter | solution.py:105
  1107.3 45.2 %all-gather.23.cloned.1.call-done = bf16[2048,1024]{1,0:T(8,128)(2,1)} async-done(((bf16[256,1024]{1,0:T(8,128)(2,1)}), bf16[2048,1024]{1,0:T(8,128)(2,1)}) %all-gather.23.cloned.1.call-update) | async-done | bytes 4194320 | tf_op jit(solution)/shard_map/all_gather | solution.py:101
  1164.3 166.6 %while.57 = (s32[]{:T(128)}, f32[2048,2,64]{0,2,1:T(8,128)}, f32[2048,2,64]{0,2,1:T(8,128)S(1)}, bf16[4,512,2,64]{1,3,2,0:T(8,128)(2,1)}, bf16[4,512,2,64]{1,3,2...) while((s32[]{:T(128)}, f32[2048,2,64]{0,2,1:T(8,128)}, ...), condition=%wide.region_55.56_spmd.clone, body=%wide.region_53.55_spmd.clone.sunk | while | flops 1387272192 | bytes 136605936 | solution.py:160
  1258.4 15.8 fusion.525
  1462.4 75.1 %all-reduce.17.cloned.1.call-done = (f32[1024,384]{1,0:T(8,128)}, f32[128,1024]{1,0:T(8,128)}, f32[1024,512]{1,0:T(8,128)}, f32[512,1024]{1,0:T(8,128)}) async-done(((f32[1024,384]{1,0:T(8,128)}, f32[128,1024]{1,0:T(8,128)}, f32[1024,512]{1,0:T(8,128)}, f32[512,1024]{1,0:T(8,128)}), (f32[1024,384]{1,0:T(8,128)}, f32[128,1024]{1,0:T(8,128)}, f32[1024,512]{1,0:T(8,128)}, ...) | async-done | bytes 6291472 | tf_op jit(solution)/shard_map/psum | solution.py:309
  1547.1 40.0 %all-reduce.10 = (f32[]{:T(128)}, f32[]{:T(128)}, f32[6,1024]{1,0:T(8,128)S(1)}) all-reduce(f32[]{:T(128)S(6)} %add.516, f32[]{:T(128)S(6)} %add.528, f32[6,1024]{1,0:T(8,128)S(1)} %add.534), channel_id=1, replica_groups=mesh['dp'=4,'mp'=8] {'dp','mp'}, use_global_device_ids=true, to_apply=%region_31.32 | all-reduce | flops 6146 | bytes 49168 | tf_op jit(solution)/shard_map/psum | solution.py:316
  1588.3 88.0 %all-reduce.15.cloned.1.call-done = f32[440,1024]{1,0:T(8,128)} async-done(((f32[440,1024]{1,0:T(8,128)}), f32[440,1024]{1,0:T(8,128)}) %all-reduce.15.cloned.1.call-update) | async-done | bytes 1802256 | tf_op jit(solution)/shard_map/psum | solution.py:316
  (805 shorter events, 754.8 us)
Async XLA Ops:
  7.2 79.7 %all-gather.9.cloned.1.call-start = ((), (), s32[]{:S(2)}) async-start(), calls=%async_computation.8 | async-start | bytes 4718592 | tf_op jit(solution)/shard_map/all_gather | solution.py:91
  14.7 297.5 %copy-start.126 = (f32[1,1024]{1,0:T(1,128)}, f32[1,1024]{1,0:T(1,128)S(1)}, u32[]{:S(2)}) copy-start(f32[1,1024]{1,0:T(1,128)S(1)} %get-tuple-element.512) | copy-start | bytes 12292
  14.7 549.0 %copy-start.124 = (f32[1,1024]{1,0:T(1,128)}, f32[1,1024]{1,0:T(1,128)S(1)}, u32[]{:S(2)}) copy-start(f32[1,1024]{1,0:T(1,128)S(1)} %get-tuple-element.508) | copy-start | bytes 12292
  16.2 291.7 %copy-start.24 = (f32[48,16,64]{2,1,0:T(8,128)}, f32[48,16,64]{2,1,0:T(8,128)S(1)}, u32[]{:S(2)}) copy-start(f32[48,16,64]{2,1,0:T(8,128)S(1)} %reshape.506) | copy-start | bytes 589828
  37.0 135.4 %reduce-scatter.9.cloned.1.call-start = ((), (), s32[]{:S(2)}) async-start(), calls=%async_computation.9 | async-start | bytes 4718592 | tf_op jit(solution)/shard_map/reduce_scatter | solution.py:95
  123.5 97.7 %all-gather.11.cloned.1.call-start = ((), (), s32[]{:S(2)}) async-start(), calls=%async_computation.10 | async-start | bytes 4718592 | tf_op jit(solution)/shard_map/all_gather | solution.py:91
  175.7 113.3 %reduce-scatter.11.cloned.1.call-start = ((), (), s32[]{:S(2)}) async-start(), calls=%async_computation.11 | async-start | bytes 4718592 | tf_op jit(solution)/shard_map/reduce_scatter | solution.py:95
  240.0 119.4 %all-gather.13.cloned.1.call-start = ((), (), s32[]{:S(2)}) async-start(), calls=%async_computation.12 | async-start | bytes 4718592 | tf_op jit(solution)/shard_map/all_gather | solution.py:91
  314.1 124.8 %reduce-scatter.13.cloned.1.call-start = ((), (), s32[]{:S(2)}) async-start(), calls=%async_computation.13 | async-start | bytes 4718592 | tf_op jit(solution)/shard_map/reduce_scatter | solution.py:95
  390.0 97.6 %all-gather.15.cloned.1.call-start = ((), (), s32[]{:S(2)}) async-start(), calls=%async_computation.14 | async-start | bytes 4718592 | tf_op jit(solution)/shard_map/all_gather | solution.py:91
  442.2 115.6 %reduce-scatter.15.cloned.1.call-start = ((), (), s32[]{:S(2)}) async-start(), calls=%async_computation.15 | async-start | bytes 4718592 | tf_op jit(solution)/shard_map/reduce_scatter | solution.py:95
  507.9 102.9 %all-gather.17.cloned.1.call-start = ((), (), s32[]{:S(2)}) async-start(), calls=%async_computation.16 | async-start | bytes 4718592 | tf_op jit(solution)/shard_map/all_gather | solution.py:101
  565.3 108.8 %reduce-scatter.17.cloned.1.call-start = ((), (), s32[]{:S(2)}) async-start(), calls=%async_computation.17 | async-start | bytes 4718592 | tf_op jit(solution)/shard_map/reduce_scatter | solution.py:105
  625.2 99.9 %all-gather.19.cloned.1.call-start = ((), (), s32[]{:S(2)}) async-start(), calls=%async_computation.18 | async-start | bytes 4718592 | tf_op jit(solution)/shard_map/all_gather | solution.py:101
  679.6 271.7 %reduce-scatter.19.cloned.1.call-start = ((), (), s32[]{:S(2)}) async-start(), calls=%async_computation.19 | async-start | bytes 4718592 | tf_op jit(solution)/shard_map/reduce_scatter | solution.py:105
  902.4 135.8 %all-gather.21.cloned.1.call-start = ((), (), s32[]{:S(2)}) async-start(), calls=%async_computation.20 | async-start | bytes 4718592 | tf_op jit(solution)/shard_map/all_gather | solution.py:101
  992.8 108.7 %reduce-scatter.21.cloned.1.call-start = ((), (), s32[]{:S(2)}) async-start(), calls=%async_computation.21 | async-start | bytes 4718592 | tf_op jit(solution)/shard_map/reduce_scatter | solution.py:105
  1052.6 99.9 %all-gather.23.cloned.1.call-start = ((), (), s32[]{:S(2)}) async-start(), calls=%async_computation.22 | async-start | bytes 4718592 | tf_op jit(solution)/shard_map/all_gather | solution.py:101
  1107.1 298.1 %reduce-scatter.23.cloned.1.call-start = ((), (), s32[]{:S(2)}) async-start(), calls=%async_computation.23 | async-start | bytes 4718592 | tf_op jit(solution)/shard_map/reduce_scatter | solution.py:105
  1342.1 195.4 %all-reduce.17.cloned.1.call-start = ((), (), s32[]{:S(2)}) async-start(), calls=%async_computation.25 | async-start | bytes 12582912 | tf_op jit(solution)/shard_map/psum | solution.py:309
  1398.7 277.6 %all-reduce.15.cloned.1.call-start = ((), (), s32[]{:S(2)}) async-start(), calls=%async_computation.24 | async-start | bytes 3604480 | tf_op jit(solution)/shard_map/psum | solution.py:316
  1458.1 222.9 %copy-start.111 = (f32[512,256]{1,0:T(8,128)S(1)}, f32[512,256]{1,0:T(8,128)}, u32[]{:S(2)}) copy-start(f32[512,256]{1,0:T(8,128)} %param.53) | copy-start | bytes 1572868
  1460.9 222.8 %copy-start.113 = (f32[256,512]{1,0:T(8,128)S(1)}, f32[256,512]{1,0:T(8,128)}, u32[]{:S(2)}) copy-start(f32[256,512]{1,0:T(8,128)} %param.50) | copy-start | bytes 1572868
  1460.9 222.8 %copy-start.114 = (f32[256,512]{1,0:T(8,128)S(1)}, f32[256,512]{1,0:T(8,128)}, u32[]{:S(2)}) copy-start(f32[256,512]{1,0:T(8,128)} %param.51) | copy-start | bytes 1572868
  (217 other events, 4179.3 us)
Sparse Core Ops, SparseCore 0:
  37.1 49.8 all-gather.8
  123.6 48.7 reduce-scatter.8
  175.8 45.2 all-gather.10
  240.2 48.7 reduce-scatter.10
  314.2 45.2 all-gather.12
  390.1 48.7 reduce-scatter.12
  442.3 45.2 all-gather.14
  508.0 49.7 reduce-scatter.14
  565.4 45.2 all-gather.16
  625.3 48.7 reduce-scatter.16
  679.8 45.2 all-gather.18
  902.6 48.7 reduce-scatter.18
  992.9 45.2 all-gather.20
  1052.7 48.7 reduce-scatter.20
  1107.2 45.2 all-gather.22
  1342.2 48.7 reduce-scatter.22
  1398.8 138.6 all-reduce.16
  1543.3 132.9 all-reduce.14
where the time goes:
time: 1710 us; the launch traced here: 1700 us
  waiting for transfers between devices  813 us (48%)
  matrix products  550 us (32%)
  other arithmetic  120 us (7%)
  local copies, waits for them, and re-layouts  109 us (6%)
  blocking collectives  80.7 us (5%)
  between operations  27.3 us (2%)
    all_gather x4, waiting for transfers between devices, spread_grads(): return lax.all_gather(grad_rows, 'mp', axis=0, tiled=True)  180 us
    all_gather x4, waiting for transfers between devices, spread_rows(): return lax.all_gather(normed, 'mp', axis=0, tiled=True)  177 us
    reduce_scatter x4, waiting for transfers between devices, fold_rows(): lax.psum_scatter(partial_sum.astype(jnp.bfloat16), 'mp', scatter_dimensio...  147 us
    reduce_scatter x4, waiting for transfers between devices, fold_grads(): lax.psum_scatter(partial_sum.astype(jnp.bfloat16), 'mp', scatter_dimensio...  145 us
    dot_general x8, matrix products, one_block(): jnp.einsum('hqk,khc->qhc', score_grad, keys, preferred_element_type=jnp.f...  127 us
    dot_general x8, matrix products, one_block(): jnp.einsum('hqk,qhc->khc', score_grad, block, preferred_element_type=jnp....  120 us
    psum x1, waiting for transfers between devices, shards(): lax.psum((table_grad, gain_grad, loss_part), ('dp', 'mp'))  88 us
    psum x1, waiting for transfers between devices, shards(): summed = lax.psum((qkv_grad, out_grad, up_grad, down_grad), 'dp')  75.1 us
  transfers between devices with their start and end apart: 18, of which 17 were waited for; matrix products, arithmetic and copies ran while one was open for 8% of the time, Pallas kernels for 0%

commit v1 on v0

v1 whole, which is shorter than its diff:
```python
from functools import partial
import math

import jax
import jax.numpy as jnp
from jax import lax
from jax.experimental import pallas as pl
from jax.experimental.pallas import tpu as pltpu
from jax.sharding import PartitionSpec as P

D = 1024
HEADS = 16
HEAD_DIM = 64
V = 48
PATCH_ROWS = 32
PATCH_COLS = 64
LEADS = 7


highest = lax.Precision.HIGHEST
eps_norm = 1e-05
clip_norm = 0.05
beta_first = 0.9
beta_second = 0.999
adam_eps = 1e-08
decay_rate = 0.1
lr_matrix = 0.04
lr_table = 0.1
lr_gain = 0.3
average_keep = 0.9
first_fix = 1.0 - 0.9**10
second_fix = 1.0 - 0.999**10


def layer_norm(values, gain, bias):
    center = values - jnp.mean(values, axis=-1, keepdims=True)
    spread = jnp.mean(center * center, axis=-1, keepdims=True)
    return center * lax.rsqrt(spread + eps_norm) * gain + bias


def lat_weights(pixel_rows):
    row_index = jnp.arange(pixel_rows, dtype=jnp.float32)
    cosine = jnp.cos(((row_index + 0.5) / pixel_rows - 0.5) * math.pi)
    return cosine / jnp.mean(cosine)


def embed_tokens(cells, tables, var_hot, lead_hot):
    count_rows = cells.shape[0]
    patch_tab = tables[: 4 * V].reshape(V, 4, HEADS, HEAD_DIM)
    var_tab = jnp.dot(var_hot, tables[4 * V : 5 * V], precision=highest).reshape(V, HEADS, HEAD_DIM)
    lead_vec = jnp.dot(lead_hot, tables[5 * V : 5 * V + LEADS], precision=highest)
    query = tables[5 * V + LEADS].reshape(HEADS, HEAD_DIM)
    keyed = jnp.einsum("vphc,hc->vph", patch_tab, query, precision=highest)
    biased = jnp.einsum("vhc,hc->vh", var_tab, query, precision=highest)
    pixels = cells.reshape(count_rows, V, 4)
    scores = (jnp.einsum("tvp,vph->tvh", pixels, keyed, precision=highest) + biased) * HEAD_DIM ** (
        -0.5
    )
    shares = jax.nn.softmax(scores, axis=1)
    mixed = (shares[:, :, None, :] * pixels[:, :, :, None]).reshape(count_rows, 4 * V, HEADS)
    merged = jnp.einsum(
        "tkh,khc->thc", mixed, patch_tab.reshape(4 * V, HEADS, HEAD_DIM), precision=highest
    )
    merged = merged + jnp.einsum("tvh,vhc->thc", shares, var_tab, precision=highest)
    return merged.reshape(count_rows, D) + lead_vec


bf16 = jnp.bfloat16
f32 = jnp.float32
MESH = pl.DeviceIdType.MESH
NT = (((1,), (1,)), ((), ()))
TN = (((0,), (0,)), ((), ()))
VMEM = pl.BlockSpec(memory_space=pltpu.VMEM)
BIG = 56 * 2**20


def is_crossed(sizes):
    return sizes["dp"] == 4 and sizes["mp"] == 8


def mesh_place():
    dp = lax.axis_index("dp")
    mp = lax.axis_index("mp")
    return dp, mp // 2, lax.rem(mp, 2)


def device_of(dp, level, core):
    return {"dp": dp, "mp": level * 2 + core}


def cross_pairs():
    groups = lax.axis_size("dp")
    pairs = []
    for dp in range(groups):
        for level in range(groups):
            for core in range(2):
                source = (dp * groups + level) * 2 + core
                target = (level * groups + dp) * 2 + core
                pairs.append((source, target))
    return pairs


def cross(crossed, value):
    if not crossed:
        return value
    return lax.ppermute(value, ("dp", "mp"), cross_pairs())


def gather_kernel(x_ref, o_ref, send_sem, recv_sem):
    rows = x_ref.shape[0]
    half = rows // 2
    dp, level, core = mesh_place()
    side = dp + 1 - 2 * lax.rem(dp, 2)
    down = lax.rem(dp + 2, 4)
    far = 3 - dp
    to_side = device_of(side, level, core)
    to_down = device_of(down, level, core)
    to_core = device_of(dp, level, 1 - core)

    def rows_of(owner, who, first, size):
        return pl.ds(pl.multiple_of((owner * 2 + who) * rows + first, half), size)

    barrier = pltpu.get_barrier_semaphore()
    for target in (to_side, to_down, to_core):
        pl.semaphore_signal(barrier, inc=1, device_id=target, device_id_type=MESH)
    pl.semaphore_wait(barrier, 3)

    def send(slot, source, where, target):
        copy = pltpu.make_async_remote_copy(
            src_ref=source,
            dst_ref=o_ref.at[where],
            send_sem=send_sem.at[slot],
            recv_sem=recv_sem.at[slot],
            device_id=target,
            device_id_type=MESH,
        )
        copy.start()
        return copy

    first = x_ref.at[pl.ds(0, half)]
    second = x_ref.at[pl.ds(half, half)]
    side_a = send(0, first, rows_of(dp, core, 0, half), to_side)
    down_b = send(1, second, rows_of(dp, core, half, half), to_down)
    side_b = send(2, second, rows_of(dp, core, half, half), to_side)
    down_a = send(3, first, rows_of(dp, core, 0, half), to_down)
    near = send(4, x_ref, rows_of(dp, core, 0, rows), to_core)
    o_ref[rows_of(dp, core, 0, rows)] = x_ref[...]
    side_a.wait_recv()
    place = rows_of(side, core, 0, half)
    far_a = send(5, o_ref.at[place], place, to_down)
    down_b.wait_recv()
    place = rows_of(down, core, half, half)
    far_b = send(6, o_ref.at[place], place, to_side)
    side_b.wait_recv()
    place = rows_of(side, core, 0, rows)
    near_side = send(7, o_ref.at[place], place, to_core)
    down_a.wait_recv()
    place = rows_of(down, core, 0, rows)
    near_down = send(8, o_ref.at[place], place, to_core)
    far_a.wait_recv()
    far_b.wait_recv()
    place = rows_of(far, core, 0, rows)
    near_far = send(9, o_ref.at[place], place, to_core)
    for copy in (near, near_side, near_down, near_far):
        copy.wait_recv()
    for copy in (side_a, down_b, side_b, down_a, near, far_a, far_b, near_side, near_down, near_far):
        copy.wait_send()


def spread_rows(crossed, normed):
    if not crossed:
        return lax.all_gather(normed, "mp", axis=0, tiled=True)
    rows, width = normed.shape
    return pl.pallas_call(
        gather_kernel,
        out_shape=jax.ShapeDtypeStruct((8 * rows, width), normed.dtype),
        in_specs=[VMEM],
        out_specs=VMEM,
        scratch_shapes=[pltpu.SemaphoreType.DMA((10,)), pltpu.SemaphoreType.DMA((10,))],
        compiler_params=pltpu.CompilerParams(
            collective_id=1, has_side_effects=True, vmem_limit_bytes=BIG
        ),
        name="gather_rows",
    )(normed)


def exchange_kernel(to_columns, rows, width, x_ref, o_ref, send_sem, recv_sem):
    dp, level, core = mesh_place()
    me = dp * 2 + core
    barrier = pltpu.get_barrier_semaphore()
    others = []
    for step in (7, 6, 5, 4, 3, 2, 1):
        part = lax.rem(me + step, 8)
        others.append((step, part, device_of(part // 2, level, lax.rem(part, 2))))
    for step, part, target in others:
        pl.semaphore_signal(barrier, inc=1, device_id=target, device_id_type=MESH)
    pl.semaphore_wait(barrier, 7)

    def row_block(ref, part):
        return ref.at[pl.ds(pl.multiple_of(part * rows, rows), rows), :]

    def column_block(ref, part):
        return ref.at[:, pl.ds(pl.multiple_of(part * width, width), width)]

    source_block, target_block = (
        (row_block, column_block) if to_columns else (column_block, row_block)
    )
    copies = []
    for step, part, target in others:
        copy = pltpu.make_async_remote_copy(
            src_ref=source_block(x_ref, part),
            dst_ref=target_block(o_ref, me),
            send_sem=send_sem.at[step],
            recv_sem=recv_sem.at[step],
            device_id=target,
            device_id_type=MESH,
        )
        copy.start()
        copies.append(copy)
    target_block(o_ref, me)[...] = source_block(x_ref, me)[...]
    for copy in copies:
        copy.wait()


def exchange(crossed, value, to_columns, number):
    parts = lax.axis_size("mp")
    if to_columns:
        rows, width = value.shape[0] // parts, value.shape[1]
        shape = (rows, width * parts)
    else:
        rows, width = value.shape[0], value.shape[1] // parts
        shape = (rows * parts, width)
    if not crossed:
        split, joined = (0, 1) if to_columns else (1, 0)
        return lax.all_to_all(value, "mp", split_axis=split, concat_axis=joined, tiled=True)
    return pl.pallas_call(
        partial(exchange_kernel, to_columns, rows, width),
        out_shape=jax.ShapeDtypeStruct(shape, value.dtype),
        in_specs=[VMEM],
        out_specs=VMEM,
        scratch_shapes=[pltpu.SemaphoreType.DMA((8,)), pltpu.SemaphoreType.DMA((8,))],
        compiler_params=pltpu.CompilerParams(
            collective_id=number, has_side_effects=True, vmem_limit_bytes=BIG
        ),
        name="exchange_parts",
    )(value)


def pick_head(value, head, heads):
    if heads == 1:
        return value
    lane = lax.broadcasted_iota(jnp.int32, value.shape, 1) // HEAD_DIM
    return jnp.where(lane == head, value, jnp.zeros_like(value))


def attend_kernel(heads, q_ref, k_ref, v_ref, o_ref, full_ref, lse_ref, vt_ref):
    @pl.when(pl.program_id(0) == 0)
    def _():
        vt_ref[...] = v_ref[...].T

    queries = q_ref[...] * bf16(HEAD_DIM**-0.5)
    keys = k_ref[...]
    outs = []
    for head in range(heads):
        scores = lax.dot_general(
            keys, pick_head(queries, head, heads), NT, preferred_element_type=f32
        )
        largest = jnp.max(scores, axis=0, keepdims=True)
        raised = jnp.exp(scores - largest)
        total = jnp.sum(raised, axis=0, keepdims=True)
        probs = (raised * (1.0 / total)).astype(bf16)
        values = vt_ref[head * HEAD_DIM : (head + 1) * HEAD_DIM, :]
        outs.append(jnp.dot(values, probs, preferred_element_type=f32))
        lse_ref[head : head + 1, :] = largest + jnp.log(total)
    flipped = outs[0] if heads == 1 else jnp.concatenate(outs, axis=0)
    full = flipped.T
    full_ref[...] = full
    o_ref[...] = full.astype(bf16)


def attend(packed):
    total, width = packed.shape[0], packed.shape[1] // 3
    heads = width // HEAD_DIM
    block = min(512, total)
    row_block = pl.BlockSpec((block, width), lambda i: (i, 0))
    return pl.pallas_call(
        partial(attend_kernel, heads),
        grid=(total // block,),
        out_shape=(
            jax.ShapeDtypeStruct((total, width), bf16),
            jax.ShapeDtypeStruct((total, width), f32),
            jax.ShapeDtypeStruct((heads, total), f32),
        ),
        in_specs=[
            row_block,
            pl.BlockSpec((total, width), lambda i: (0, 0)),
            pl.BlockSpec((total, width), lambda i: (0, 0)),
        ],
        out_specs=[row_block, row_block, pl.BlockSpec((heads, block), lambda i: (0, i))],
        scratch_shapes=[pltpu.VMEM((width, total), bf16)],
        compiler_params=pltpu.CompilerParams(vmem_limit_bytes=BIG),
        cost_estimate=pl.CostEstimate(
            flops=16 * total * total * width,
            bytes_accessed=10 * total * width,
            transcendentals=heads * total * total,
        ),
        name="attend",
    )(packed[:, :width], packed[:, width : 2 * width], packed[:, 2 * width :])


def attend_back_kernel(
    heads, q_ref, do_ref, full_ref, lse_ref, k_ref, v_ref, dq_ref, dk_ref, dv_ref, kt_ref, dk_sum, dv_sum
):
    step = pl.program_id(0)
    total = k_ref.shape[0]
    chunk = min(1024, total)

    @pl.when(step == 0)
    def _():
        kt_ref[...] = k_ref[...].T
        dk_sum[...] = jnp.zeros_like(dk_sum)
        dv_sum[...] = jnp.zeros_like(dv_sum)

    scale = HEAD_DIM**-0.5
    queries = q_ref[...]
    grads = do_ref[...]
    products = (grads.astype(f32) * full_ref[...]).T
    query_heads = [pick_head(queries, head, heads) for head in range(heads)]
    grad_heads = [pick_head(grads, head, heads) for head in range(heads)]
    inner = [
        jnp.sum(products[head * HEAD_DIM : (head + 1) * HEAD_DIM], axis=0, keepdims=True) * scale
        for head in range(heads)
    ]
    query_grads = [None] * heads
    for start in range(0, total, chunk):
        rows = slice(start, start + chunk)
        keys = k_ref[rows, :]
        values = v_ref[rows, :]
        value_part = None
        key_part = None
        for head in range(heads):
            scores = lax.dot_general(
                keys, query_heads[head] * bf16(scale), NT, preferred_element_type=f32
            )
            probs = jnp.exp(scores - lse_ref[head : head + 1, :])
            prob_grad = lax.dot_general(
                values, grad_heads[head] * bf16(scale), NT, preferred_element_type=f32
            )
            score_grad = (probs * (prob_grad - inner[head])).astype(bf16)
            one = jnp.dot(probs.astype(bf16), grad_heads[head], preferred_element_type=f32)
            two = jnp.dot(score_grad, query_heads[head], preferred_element_type=f32)
            value_part = one if value_part is None else value_part + one
            key_part = two if key_part is None else key_part + two
            three = jnp.dot(
                kt_ref[head * HEAD_DIM : (head + 1) * HEAD_DIM, rows],
                score_grad,
                preferred_element_type=f32,
            )
            query_grads[head] = three if query_grads[head] is None else query_grads[head] + three
        dv_sum[rows, :] += value_part
        dk_sum[rows, :] += key_part
    flipped = query_grads[0] if heads == 1 else jnp.concatenate(query_grads, axis=0)
    dq_ref[...] = flipped.T.astype(bf16)

    @pl.when(step == pl.num_programs(0) - 1)
    def _():
        dk_ref[...] = dk_sum[...].astype(bf16)
        dv_ref[...] = dv_sum[...].astype(bf16)


def attend_back(grad_out, packed, full, logsum):
    total, width = grad_out.shape
    heads = width // HEAD_DIM
    block = min(256, total)
    row_block = pl.BlockSpec((block, width), lambda i: (i, 0))
    whole = pl.BlockSpec((total, width), lambda i: (0, 0))
    query_grad, key_grad, value_grad = pl.pallas_call(
        partial(attend_back_kernel, heads),
        grid=(total // block,),
        out_shape=(jax.ShapeDtypeStruct((total, width), bf16),) * 3,
        in_specs=[
            row_block,
            row_block,
            row_block,
            pl.BlockSpec((heads, block), lambda i: (0, i)),
            whole,
            whole,
        ],
        out_specs=[row_block, whole, whole],
        scratch_shapes=[
            pltpu.VMEM((width, total), bf16),
            pltpu.VMEM((total, width), f32),
            pltpu.VMEM((total, width), f32),
        ],
        compiler_params=pltpu.CompilerParams(vmem_limit_bytes=BIG),
        cost_estimate=pl.CostEstimate(
            flops=40 * total * total * width,
            bytes_accessed=16 * total * width,
            transcendentals=heads * total * total,
        ),
        name="attend_back",
    )(
        packed[:, :width],
        grad_out,
        full,
        logsum,
        packed[:, width : 2 * width],
        packed[:, 2 * width :],
    )
    return jnp.concatenate((query_grad, key_grad, value_grad), axis=1)


def normed_parts(values):
    center = values - jnp.mean(values, axis=-1, keepdims=True)
    spread = jnp.mean(center * center, axis=-1, keepdims=True)
    inverse = lax.rsqrt(spread + eps_norm)
    return center * inverse, inverse


def norm_grad(unit, inverse, gain, grad):
    scaled = grad * gain
    middle = jnp.mean(scaled, axis=-1, keepdims=True)
    along = jnp.mean(scaled * unit, axis=-1, keepdims=True)
    gain_grad = jnp.sum(grad * unit, axis=0, keepdims=True)
    bias_grad = jnp.sum(grad, axis=0, keepdims=True)
    return inverse * (scaled - middle - unit * along), gain_grad, bias_grad


def gauss_share(values):
    return 0.5 * (1.0 + lax.erf(values * (0.5**0.5)))


def branch_kernel(
    o_ref, x0_ref, gains_ref, out_ref, up_ref, down_ref, head_ref,
    x1_ref, h2_ref, g_ref, act_ref, x2_ref, pred_ref,
):
    step = pl.program_id(0)

    @pl.when(step == 0)
    def _():
        x1_ref[...] = x0_ref[...] + jnp.dot(
            o_ref[...], out_ref[...], preferred_element_type=f32
        )
        unit, _ = normed_parts(x1_ref[...])
        h2_ref[...] = (unit * gains_ref[2:3, :] + gains_ref[3:4, :]).astype(bf16)
        x2_ref[...] = x1_ref[...]

    hidden = jnp.dot(h2_ref[...], up_ref[0], preferred_element_type=f32)
    g_ref[...] = hidden
    active = (hidden * gauss_share(hidden)).astype(bf16)
    act_ref[...] = active
    x2_ref[...] += jnp.dot(active, down_ref[...], preferred_element_type=f32)

    @pl.when(step == pl.num_programs(0) - 1)
    def _():
        unit, _ = normed_parts(x2_ref[...])
        last = unit * gains_ref[4:5, :] + gains_ref[5:6, :]
        pred_ref[...] = lax.dot_general(
            last, head_ref[...], NT, precision=highest, preferred_element_type=f32
        )


def weight_specs(w_out, w_up, w_down):
    _, width, units = w_up.shape
    return (
        pl.BlockSpec(w_out.shape, lambda i: (0, 0)),
        pl.BlockSpec((1, width, units), lambda i: (i, 0, 0)),
        pl.BlockSpec((units, width), lambda i: (i, 0)),
    )


def branch_forward(attended, x_first, norm_gains, gathered, head):
    w_out, w_up, w_down, _ = gathered
    rows, width = x_first.shape
    parts, units = w_up.shape[0], w_up.shape[2]
    fixed = lambda shape: pl.BlockSpec(shape, lambda i: (0, 0))
    by_units = pl.BlockSpec((rows, units), lambda i: (0, i))
    columns = head.shape[0]
    flops = 2 * rows * (width * width + 2 * width * parts * units + 6 * width * columns)
    return pl.pallas_call(
        branch_kernel,
        grid=(parts,),
        out_shape=(
            jax.ShapeDtypeStruct((rows, width), f32),
            jax.ShapeDtypeStruct((rows, width), bf16),
            jax.ShapeDtypeStruct((rows, parts * units), f32),
            jax.ShapeDtypeStruct((rows, parts * units), bf16),
            jax.ShapeDtypeStruct((rows, width), f32),
            jax.ShapeDtypeStruct((rows, columns), f32),
        ),
        in_specs=[
            fixed((rows, width)),
            fixed((rows, width)),
            fixed(norm_gains.shape),
            *weight_specs(w_out, w_up, w_down),
            fixed(head.shape),
        ],
        out_specs=[
            fixed((rows, width)),
            fixed((rows, width)),
            by_units,
            by_units,
            fixed((rows, width)),
            fixed((rows, columns)),
        ],
        compiler_params=pltpu.CompilerParams(vmem_limit_bytes=BIG),
        cost_estimate=pl.CostEstimate(
            flops=flops,
            bytes_accessed=4 * width * parts * units + 6 * rows * parts * units,
            transcendentals=rows * parts * units,
        ),
        name="branch_forward",
    )(attended, x_first, norm_gains, w_out, w_up, w_down, head)


def branch_back_kernel(
    dpred_ref, x2_ref, x1_ref, gains_ref, g_ref, out_ref, up_ref, down_ref, head_ref,
    dx2_ref, dg_ref, dx1_ref, low_ref, do_ref, gain_ref, dhead_ref,
    wide_ref, sum_ref,
):
    step = pl.program_id(0)

    @pl.when(step == 0)
    def _():
        grad = dpred_ref[...]
        unit, inverse = normed_parts(x2_ref[...])
        gain = gains_ref[4:5, :]
        last = unit * gain + gains_ref[5:6, :]
        dhead_ref[...] = lax.dot_general(
            grad, last, TN, precision=highest, preferred_element_type=f32
        )
        row_grad = jnp.dot(grad, head_ref[...], precision=highest, preferred_element_type=f32)
        wide, gain_grad, bias_grad = norm_grad(unit, inverse, gain, row_grad)
        gain_ref[...] = jnp.zeros_like(gain_ref)
        gain_ref[4:5, :] = gain_grad
        gain_ref[5:6, :] = bias_grad
        wide_ref[...] = wide
        dx2_ref[...] = wide.astype(bf16)
        sum_ref[...] = jnp.zeros_like(sum_ref)

    active_grad = lax.dot_general(dx2_ref[...], down_ref[...], NT, preferred_element_type=f32)
    hidden = g_ref[...]
    slope = gauss_share(hidden) + hidden * (
        jnp.exp(-0.5 * hidden * hidden) * (2.0 * math.pi) ** -0.5
    )
    hidden_grad = (active_grad * slope).astype(bf16)
    dg_ref[...] = hidden_grad
    sum_ref[...] += lax.dot_general(hidden_grad, up_ref[0], NT, preferred_element_type=f32)

    @pl.when(step == pl.num_programs(0) - 1)
    def _():
        unit, inverse = normed_parts(x1_ref[...])
        middle, gain_grad, bias_grad = norm_grad(unit, inverse, gains_ref[2:3, :], sum_ref[...])
        gain_ref[2:3, :] = gain_grad
        gain_ref[3:4, :] = bias_grad
        middle = wide_ref[...] + middle
        dx1_ref[...] = middle
        low_ref[...] = middle.astype(bf16)
        total = lax.dot_general(low_ref[...], out_ref[...], NT, preferred_element_type=f32)
        do_ref[...] = total.astype(bf16)


def branch_backward(pred_grad, x_last, x_mid, norm_gains, hidden, gathered, head):
    w_out, w_up, w_down, _ = gathered
    rows, width = x_last.shape
    parts, units = w_up.shape[0], w_up.shape[2]
    fixed = lambda shape: pl.BlockSpec(shape, lambda i: (0, 0))
    by_units = pl.BlockSpec((rows, units), lambda i: (0, i))
    columns = head.shape[0]
    wide = (rows, width)
    flops = 2 * rows * (width * width + 2 * width * parts * units + 12 * width * columns)
    return pl.pallas_call(
        branch_back_kernel,
        grid=(parts,),
        out_shape=(
            jax.ShapeDtypeStruct(wide, bf16),
            jax.ShapeDtypeStruct((rows, parts * units), bf16),
            jax.ShapeDtypeStruct(wide, f32),
            jax.ShapeDtypeStruct(wide, bf16),
            jax.ShapeDtypeStruct(wide, bf16),
            jax.ShapeDtypeStruct((6, width), f32),
            jax.ShapeDtypeStruct((columns, width), f32),
        ),
        in_specs=[
            fixed((rows, columns)),
            fixed(wide),
            fixed(wide),
            fixed(norm_gains.shape),
            by_units,
            *weight_specs(w_out, w_up, w_down),
            fixed(head.shape),
        ],
        out_specs=[
            fixed(wide),
            by_units,
            fixed(wide),
            fixed(wide),
            fixed(wide),
            fixed((6, width)),
            fixed((columns, width)),
        ],
        scratch_shapes=[pltpu.VMEM(wide, f32), pltpu.VMEM(wide, f32)],
        compiler_params=pltpu.CompilerParams(vmem_limit_bytes=BIG),
        cost_estimate=pl.CostEstimate(
            flops=flops,
            bytes_accessed=4 * width * parts * units + 6 * rows * parts * units,
            transcendentals=2 * rows * parts * units,
        ),
        name="branch_backward",
    )(pred_grad, x_last, x_mid, norm_gains, hidden, w_out, w_up, w_down, head)


def wide_piece(piece):
    half = piece.shape[0] // 2
    return jnp.concatenate((piece[:half], piece[half:]), axis=1)


def tall_piece(piece):
    half = piece.shape[1] // 2
    return jnp.concatenate((piece[:, :half], piece[:, half:]), axis=0)


def both_steps(left_a, right_a, left_b, right_b):
    product = lax.dot_general(left_a[...], right_a[...], TN, preferred_element_type=f32)
    return product + lax.dot_general(left_b[...], right_b[...], TN, preferred_element_type=f32)


def down_pieces(refs):
    product = both_steps(*refs)
    share = product.shape[1] // 4
    return [wide_piece(product[:, i * share : (i + 1) * share]) for i in range(4)]


def up_out_pieces(refs):
    up = both_steps(*refs[:4])
    share = up.shape[0] // 4
    out = both_steps(*refs[4:])
    size = out.shape[1] // 4
    return [
        jnp.concatenate(
            (up[i * share : (i + 1) * share], wide_piece(out[:, i * size : (i + 1) * size])), axis=0
        )
        for i in range(4)
    ]


def outer_other_kernel(make, count, where_ref, *refs):
    o_ref = refs[count]
    for split, piece in enumerate(make(refs[:count])):
        o_ref[0, split] = piece.astype(bf16)


def outer_own_kernel(make, count, where_ref, *refs):
    other_ref, send_ref, keep_ref, held_ref = refs[count:]
    for split, piece in enumerate(make(refs[:count])):
        held_ref[split] = (piece + other_ref[0, split].astype(f32)).astype(bf16)
    x, y = where_ref[1], where_ref[2]
    early = pl.program_id(0) < 2
    for which in range(2):
        send_ref[0, which] = held_ref[jnp.where(early, which * 2 + 1 - x, (1 - y) * 2 + which)]
        keep_ref[0, which] = held_ref[jnp.where(early, which * 2 + x, y * 2 + which)]


def outer_half(operands, make, height, where, other):
    specs = []
    for value, blocked in operands:
        rows, size = value.shape
        if blocked:
            specs.append(pl.BlockSpec((rows, size // 8), lambda i, w: (0, i * 2 + w[0])))
        else:
            specs.append(pl.BlockSpec((rows, size), lambda i, w: (0, 0)))
    values = [value for value, _ in operands]
    count = len(values)
    whole = pl.BlockSpec((1, 4, height, 512), lambda i, w: (i, 0, 0, 0))
    half = pl.BlockSpec((1, 2, height, 512), lambda i, w: (i, 0, 0, 0))
    rows = values[0].shape[0]
    cost = pl.CostEstimate(
        flops=2 * 2 * rows * 16 * height * 512, bytes_accessed=3 * 16 * height * 512, transcendentals=0
    )
    params = pltpu.CompilerParams(vmem_limit_bytes=BIG)
    if other is None:
        return pl.pallas_call(
            partial(outer_other_kernel, make, count),
            out_shape=jax.ShapeDtypeStruct((4, 4, height, 512), bf16),
            grid_spec=pltpu.PrefetchScalarGridSpec(
                num_scalar_prefetch=1, grid=(4,), in_specs=specs, out_specs=whole
            ),
            compiler_params=params,
            cost_estimate=cost,
            name="outer_other",
        )(where, *values)
    return pl.pallas_call(
        partial(outer_own_kernel, make, count),
        out_shape=(jax.ShapeDtypeStruct((4, 2, height, 512), bf16),) * 2,
        grid_spec=pltpu.PrefetchScalarGridSpec(
            num_scalar_prefetch=1,
            grid=(4,),
            in_specs=specs + [whole],
            out_specs=[half, half],
            scratch_shapes=[pltpu.VMEM((4, height, 512), bf16)],
        ),
        compiler_params=params,
        cost_estimate=cost,
        name="outer_own",
    )(where, *values, other)


def device_pairs(move):
    pairs = []
    for dp in range(4):
        for level in range(4):
            for core in range(2):
                to_dp, to_level, to_core = move(dp, level, core)
                pairs.append(((dp * 4 + level) * 2 + core, (to_dp * 4 + to_level) * 2 + to_core))
    return pairs


def shift(value, move):
    return lax.ppermute(value, ("dp", "mp"), device_pairs(move))


def to_core(dp, level, core):
    return dp, level, 1 - core


def to_side(dp, level, core):
    return dp ^ 1, level, core


def to_down(dp, level, core):
    return dp ^ 2, level, core


def choose(value, index, axis=0):
    return lax.dynamic_index_in_dim(value, index, axis, keepdims=False)


def sum_levels(pieces, level):
    total = choose(pieces, level).astype(f32)
    for step in range(1, 4):
        piece = choose(pieces, lax.rem(level + step, 4)).astype(bf16)
        moved = shift(piece, lambda dp, z, core: (dp, (z + step) % 4, core))
        total = total + moved.astype(f32)
    return total


def tie(*values):
    return lax.optimization_barrier(values)


def first_sums(send, keep):
    first = keep[:2].astype(f32) + shift(send[:2], to_side).astype(f32)
    second = keep[2:].astype(f32) + shift(send[2:], to_down).astype(f32)
    return first.astype(bf16), second.astype(bf16)


def second_sums(first, second, x, y):
    first_moved = shift(choose(first, 1 - y, 1), to_down)
    second_moved = shift(choose(second, 1 - x, 1), to_side)
    first = choose(first, y, 1).astype(f32) + first_moved.astype(f32)
    second = choose(second, x, 1).astype(f32) + second_moved.astype(f32)
    return jnp.concatenate((first, second))


def outer_plain(lefts, rights, by_rows):
    dp, mp = lax.axis_size("dp"), lax.axis_size("mp")
    grads = sum(
        lax.dot_general(left, right, TN, preferred_element_type=f32)
        for left, right in zip(lefts, rights)
    ).astype(bf16)
    rows, width = grads.shape
    if by_rows:
        grads = grads.reshape(dp, rows // dp, mp, width // mp).transpose(0, 2, 1, 3)
    else:
        grads = grads.reshape(mp, rows // mp, dp, width // dp).transpose(2, 0, 1, 3)
    grads = grads.reshape((dp * mp,) + grads.shape[2:])
    return lax.psum_scatter(grads, ("dp", "mp"), scatter_dimension=0, tiled=False).astype(f32)


def exchange_sum_kernel(
    x_ref, t_ref, o_ref, s_ref, work_ref, pair_ref, quad_ref, eight_ref, deep_ref, tile_ref,
    send_sem, recv_sem,
):
    dp, level, core = mesh_place()
    x, y = lax.rem(dp, 2), dp // 2
    side = device_of(dp + 1 - 2 * x, level, core)
    down = device_of(lax.rem(dp + 2, 4), level, core)
    near = device_of(dp, level, 1 - core)
    deep = [device_of(dp, lax.rem(level + step, 4), core) for step in (1, 2, 3)]
    barrier = pltpu.get_barrier_semaphore()
    for target in (side, down, near, *deep):
        pl.semaphore_signal(barrier, inc=1, device_id=target, device_id_type=MESH)
    pl.semaphore_wait(barrier, 6)
    started = []

    def send(source, target_ref, target):
        slot = len(started)
        copy = pltpu.make_async_remote_copy(
            src_ref=source,
            dst_ref=target_ref,
            send_sem=send_sem.at[slot],
            recv_sem=recv_sem.at[slot],
            device_id=target,
            device_id_type=MESH,
        )
        copy.start()
        started.append(copy)
        return copy

    half = x_ref.shape[0] // 2
    quarter, eighth, part, unit = half // 2, half // 4, half // 8, half // 16

    def rows(start, size):
        return pl.ds(pl.multiple_of(start, unit), size)

    copy = send(x_ref.at[rows((1 - core) * half, half)], pair_ref, near)
    copy.wait_recv()
    work_ref[...] = x_ref[rows(core * half, half)] + pair_ref[...]
    one = send(work_ref.at[rows((1 - x) * eighth, eighth)], quad_ref.at[0], side)
    two = send(work_ref.at[rows(quarter + (1 - y) * eighth, eighth)], quad_ref.at[1], down)
    base_a = x * eighth
    base_b = quarter + y * eighth
    wide_a, wide_b = core * half + base_a, core * half + base_b
    one.wait_recv()
    work_ref[rows(base_a, eighth)] += quad_ref[0]
    one = send(work_ref.at[rows(base_a + (1 - y) * part, part)], eight_ref.at[0], down)
    two.wait_recv()
    work_ref[rows(base_b, eighth)] += quad_ref[1]
    two = send(work_ref.at[rows(base_b + (1 - x) * part, part)], eight_ref.at[1], side)
    base_a = base_a + y * part
    base_b = base_b + x * part
    one.wait_recv()
    work_ref[rows(base_a, part)] += eight_ref[0]
    two.wait_recv()
    work_ref[rows(base_b, part)] += eight_ref[1]

    def level_start(which):
        late = which // 2
        return (1 - late) * base_a + late * base_b + lax.rem(which, 2) * unit

    copies = []
    for step in (1, 2, 3):
        source = work_ref.at[rows(level_start(lax.rem(level + step, 4)), unit)]
        copies.append(send(source, deep_ref.at[step - 1], deep[step - 1]))
    for copy in copies:
        copy.wait_recv()
    total = work_ref[rows(level_start(level), unit)] + deep_ref[0] + deep_ref[1] + deep_ref[2]
    mine = rows(core * half + level_start(level), unit)
    base_a = core * half + base_a
    base_b = core * half + base_b
    o_ref[mine] = total
    row = lax.broadcasted_iota(jnp.int32, t_ref.shape, 0)
    tile_ref[0] = t_ref[...] + jnp.where(row == 0, jnp.sum(total * total), 0.0)
    copies = []
    for step in (1, 2, 3):
        copies.append(send(o_ref.at[mine], o_ref.at[mine], deep[step - 1]))
        copies.append(send(tile_ref.at[0], tile_ref.at[step], deep[step - 1]))
    for copy in copies:
        copy.wait_recv()
    one = send(o_ref.at[rows(base_a, part)], o_ref.at[rows(base_a, part)], down)
    two = send(o_ref.at[rows(base_b, part)], o_ref.at[rows(base_b, part)], side)
    tile_ref[4] = tile_ref[0] + tile_ref[1] + tile_ref[2] + tile_ref[3]
    three = send(tile_ref.at[4], tile_ref.at[5], side)
    one.wait_recv()
    one = send(o_ref.at[rows(wide_a, eighth)], o_ref.at[rows(wide_a, eighth)], side)
    two.wait_recv()
    two = send(o_ref.at[rows(wide_b, eighth)], o_ref.at[rows(wide_b, eighth)], down)
    three.wait_recv()
    tile_ref[6] = tile_ref[4] + tile_ref[5]
    three = send(tile_ref.at[6], tile_ref.at[7], down)
    one.wait_recv()
    two.wait_recv()
    one = send(o_ref.at[rows(core * half, half)], o_ref.at[rows(core * half, half)], near)
    three.wait_recv()
    tile_ref[8] = tile_ref[6] + tile_ref[7]
    three = send(tile_ref.at[8], tile_ref.at[9], near)
    one.wait_recv()
    three.wait_recv()
    s_ref[...] = tile_ref[8] + tile_ref[9]
    for copy in started:
        copy.wait_send()


def exchange_sum(value, tile):
    rows, width = value.shape
    return pl.pallas_call(
        exchange_sum_kernel,
        out_shape=(jax.ShapeDtypeStruct(value.shape, f32), jax.ShapeDtypeStruct(tile.shape, f32)),
        in_specs=[VMEM, VMEM],
        out_specs=[VMEM, VMEM],
        scratch_shapes=[
            pltpu.VMEM((rows // 2, width), f32),
            pltpu.VMEM((rows // 2, width), f32),
            pltpu.VMEM((2, rows // 8, width), f32),
            pltpu.VMEM((2, rows // 16, width), f32),
            pltpu.VMEM((3, rows // 32, width), f32),
            pltpu.VMEM((10,) + tile.shape, f32),
            pltpu.SemaphoreType.DMA((24,)),
            pltpu.SemaphoreType.DMA((24,)),
        ],
        compiler_params=pltpu.CompilerParams(
            collective_id=5, has_side_effects=True, vmem_limit_bytes=BIG
        ),
        name="exchange_sum",
    )(value, tile)


def tile_sum_kernel(t_ref, s_ref, tile_ref, send_sem, recv_sem):
    dp, level, core = mesh_place()
    x = lax.rem(dp, 2)
    side = device_of(dp + 1 - 2 * x, level, core)
    down = device_of(lax.rem(dp + 2, 4), level, core)
    near = device_of(dp, level, 1 - core)
    deep = [device_of(dp, lax.rem(level + step, 4), core) for step in (1, 2, 3)]
    barrier = pltpu.get_barrier_semaphore()
    for target in (side, down, near, *deep):
        pl.semaphore_signal(barrier, inc=1, device_id=target, device_id_type=MESH)
    pl.semaphore_wait(barrier, 6)

    def send(slot, source, target_ref, target):
        copy = pltpu.make_async_remote_copy(
            src_ref=source,
            dst_ref=target_ref,
            send_sem=send_sem.at[slot],
            recv_sem=recv_sem.at[slot],
            device_id=target,
            device_id_type=MESH,
        )
        copy.start()
        return copy

    copies = [send(step, t_ref, tile_ref.at[step], deep[step]) for step in range(3)]
    for copy in copies:
        copy.wait()
    tile_ref[3] = t_ref[...] + tile_ref[0] + tile_ref[1] + tile_ref[2]
    send(3, tile_ref.at[3], tile_ref.at[4], side).wait()
    tile_ref[5] = tile_ref[3] + tile_ref[4]
    send(4, tile_ref.at[5], tile_ref.at[6], down).wait()
    tile_ref[7] = tile_ref[5] + tile_ref[6]
    send(5, tile_ref.at[7], tile_ref.at[8], near).wait()
    s_ref[...] = tile_ref[7] + tile_ref[8]


def sum_everywhere(crossed, value):
    if not crossed:
        return lax.psum(value, ("dp", "mp"))
    tile = jnp.broadcast_to(value, (8, 128))
    total = pl.pallas_call(
        tile_sum_kernel,
        out_shape=jax.ShapeDtypeStruct(tile.shape, f32),
        in_specs=[VMEM],
        out_specs=VMEM,
        scratch_shapes=[
            pltpu.VMEM((9,) + tile.shape, f32),
            pltpu.SemaphoreType.DMA((6,)),
            pltpu.SemaphoreType.DMA((6,)),
        ],
        compiler_params=pltpu.CompilerParams(collective_id=6, has_side_effects=True),
        name="tile_sum",
    )(tile)
    return total[0, 0]


def entry_back_kernel(grad_ref, qkv_ref, x0_ref, mid_ref, gains_ref, o_ref, gain_ref, sum_ref):
    sum_ref[...] = jnp.dot(grad_ref[...], qkv_ref[...], preferred_element_type=f32)
    unit, inverse = normed_parts(x0_ref[...])
    part, gain_grad, bias_grad = norm_grad(unit, inverse, gains_ref[0:1, :], sum_ref[...])
    o_ref[...] = mid_ref[...] + part
    gain_ref[0:1, :] = gain_grad
    gain_ref[1:2, :] = bias_grad


def entry_backward(token_grad, qkv_t, x_first, mid_grad, norm_gains):
    rows, width = x_first.shape
    return pl.pallas_call(
        entry_back_kernel,
        out_shape=(jax.ShapeDtypeStruct((rows, width), f32), jax.ShapeDtypeStruct((2, width), f32)),
        scratch_shapes=[pltpu.VMEM((rows, width), f32)],
        compiler_params=pltpu.CompilerParams(vmem_limit_bytes=BIG),
        name="entry_backward",
    )(token_grad, qkv_t, x_first, mid_grad, norm_gains)


def adam_step(master, grad, first, second, rate):
    first_new = beta_first * first + (1.0 - beta_first) * grad
    second_new = beta_second * second + (1.0 - beta_second) * grad * grad
    update = first_new / first_fix / (jnp.sqrt(second_new / second_fix) + adam_eps)
    return (master - rate * (update + decay_rate * master), first_new, second_new)


def by_kind(shard):
    rows = shard.shape[0]
    return shard.reshape(rows, -1, 3, HEAD_DIM).transpose(0, 2, 1, 3).reshape(rows, -1)


def by_head(shard):
    rows = shard.shape[0]
    return shard.reshape(rows, 3, -1, HEAD_DIM).transpose(0, 2, 1, 3).reshape(rows, -1)


def gather_weights_kernel(count, *refs):
    shards, outs = refs[:count], refs[count : 2 * count]
    send_sem, recv_sem, own_sem = refs[2 * count :]
    dp, level, core = mesh_place()
    x = lax.rem(dp, 2)
    columns = {"here": dp, "side": dp + 1 - 2 * x, "down": lax.rem(dp + 2, 4), "far": 3 - dp}
    side = device_of(columns["side"], level, core)
    down = device_of(columns["down"], level, core)
    near = device_of(dp, level, 1 - core)
    deep = [device_of(dp, lax.rem(level + step, 4), core) for step in (1, 2, 3)]
    barrier = pltpu.get_barrier_semaphore()
    for target in (side, down, near, *deep):
        pl.semaphore_signal(barrier, inc=1, device_id=target, device_id_type=MESH)
    pl.semaphore_wait(barrier, 6)
    started = []

    def send(source, target_ref, target):
        slot = len(started)
        copy = pltpu.make_async_remote_copy(
            src_ref=source,
            dst_ref=target_ref,
            send_sem=send_sem.at[slot],
            recv_sem=recv_sem.at[slot],
            device_id=target,
            device_id_type=MESH,
        )
        copy.start()
        started.append(copy)
        return copy

    def place(out, source, column, half=None):
        rows = out.shape[1] // 4
        start, size = columns[column] * rows, rows
        if half is not None:
            start, size = start + half * (rows // 2), rows // 2
        return out.at[source * 2 + core, pl.ds(pl.multiple_of(start, rows // 2), size), :]

    def pass_on(out, source, column, target, half=None):
        where = place(out, source, column, half)
        return send(where, where, target)

    chunks = []
    for index in range(count):
        rows = outs[index].shape[1] // 4
        own = shards[index].at[pl.ds(pl.multiple_of(dp * rows, rows), rows), :]
        for step in (1, 2, 3):
            copy = send(own, place(outs[index], level, "here"), deep[step - 1])
            chunks.append((outs[index], lax.rem(level + 4 - step, 4), copy))
    ends = []
    locals_ = []
    for index in range(count):
        ends.append(send(shards[index], outs[index].at[level * 2 + core], near))
        copy = pltpu.make_async_copy(
            shards[index], outs[index].at[level * 2 + core], own_sem.at[index]
        )
        copy.start()
        locals_.append(copy)
    plane, hops = {}, {}
    total = len(chunks)
    for step in range(total + 2):
        if step < total:
            out, source, copy = chunks[step]
            copy.wait_recv()
            plane[step] = (
                pass_on(out, source, "here", side),
                pass_on(out, source, "here", down),
            )
            ends.append(pass_on(out, source, "here", near))
        if 0 <= step - 1 < total:
            out, source, _ = chunks[step - 1]
            from_side, from_down = plane[step - 1]
            from_side.wait_recv()
            one = pass_on(out, source, "side", down, 0)
            from_down.wait_recv()
            two = pass_on(out, source, "down", side, 1)
            hops[step - 1] = (one, two)
            ends.append(pass_on(out, source, "side", near))
            ends.append(pass_on(out, source, "down", near))
        if 0 <= step - 2 < total:
            out, source, _ = chunks[step - 2]
            for copy in hops[step - 2]:
                copy.wait_recv()
            ends.append(pass_on(out, source, "far", near))
    for copy in ends:
        copy.wait_recv()
    for copy in started:
        copy.wait_send()
    for copy in locals_:
        copy.wait()


def gather_weights(crossed, shards):
    if not crossed:
        dp, mp = lax.axis_size("dp"), lax.axis_size("mp")
        return [lax.all_gather(shard, "mp") for shard in shards]
    count = len(shards)
    copies = count * 3 * 9 + count
    anywhere = pl.BlockSpec(memory_space=pl.ANY)
    return pl.pallas_call(
        partial(gather_weights_kernel, count),
        out_shape=[jax.ShapeDtypeStruct((8,) + shard.shape, bf16) for shard in shards],
        in_specs=[anywhere] * count,
        out_specs=[anywhere] * count,
        scratch_shapes=[
            pltpu.SemaphoreType.DMA((copies,)),
            pltpu.SemaphoreType.DMA((copies,)),
            pltpu.SemaphoreType.DMA((count,)),
        ],
        compiler_params=pltpu.CompilerParams(
            collective_id=7, has_side_effects=True, vmem_limit_bytes=BIG
        ),
        name="gather_weights",
    )(*shards)


def own_qkv_share(crossed, grad):
    dp = lax.axis_size("dp")
    rows = grad.shape[0] // dp
    if not crossed:
        return lax.psum_scatter(grad, "dp", scatter_dimension=0, tiled=True)
    _, level, _ = mesh_place()
    return cross(crossed, sum_levels(grad.reshape((dp, rows) + grad.shape[1:]), level))


def shards(
    crossed,
    fields,
    targets,
    land_mask,
    lead_index,
    var_ids,
    tables,
    norm_gains,
    tables_first,
    tables_second,
    gains_first,
    gains_second,
    w_qkv,
    qkv_first,
    qkv_second,
    w_out,
    out_first,
    out_second,
    w_up,
    up_first,
    up_second,
    w_down,
    down_first,
    down_second,
    qkv_average,
):
    local_samples, shard_rows, _ = fields.shape
    dp_size, parts = lax.axis_size("dp"), lax.axis_size("mp")
    dp_index = lax.axis_index("dp")
    place, level, core = mesh_place()
    part = place * 2 + core if crossed else lax.axis_index("mp")
    share_rows = D // dp_size

    def own_share(full, dim):
        return lax.dynamic_slice_in_dim(full, dp_index * share_rows, share_rows, dim)

    masters = (own_share(w_qkv, 0), own_share(w_out, 1), own_share(w_up, 0), own_share(w_down, 1))
    inputs = cross(crossed, fields[0])
    leads = cross(crossed, lead_index[0])
    qkv_local = cross(crossed, by_kind(w_qkv.astype(bf16)))
    low = lambda master: master.astype(bf16)
    w_outs, w_ups, w_downs = gather_weights(crossed, (low(w_out), low(w_up), low(w_down)))
    qkv_rows = 3 * D // (parts * dp_size)
    qkv_piece = lax.dynamic_slice_in_dim(by_kind(low(w_qkv)).T, dp_index * qkv_rows, qkv_rows, 0)
    w_outs, qkv_piece = tie(w_outs, qkv_piece)
    qkv_t = lax.all_gather(qkv_piece, ("mp", "dp"), axis=0, tiled=True)
    gathered = (w_outs.reshape(D, D), w_ups, w_downs.reshape(-1, D), qkv_t)
    answers = cross(crossed, targets[0])
    ocean = 1.0 - cross(crossed, land_mask[0]).astype(f32)
    count = sum_everywhere(crossed, jnp.sum(ocean))
    denom = 2.0 * V * jnp.maximum(count, 1.0)
    var_hot = (var_ids[:, None] == jnp.arange(V, dtype=jnp.int32)[None, :]).astype(f32)
    first_row = part * shard_rows
    patch_row = (first_row + jnp.arange(shard_rows, dtype=jnp.int32)) // PATCH_COLS
    row_hot = (patch_row[:, None] == jnp.arange(PATCH_ROWS, dtype=jnp.int32)[None, :]).astype(f32)
    lat_rows = jnp.dot(
        row_hot, lat_weights(2 * PATCH_ROWS).reshape(PATCH_ROWS, 2), precision=highest
    )
    lat_pixels = jnp.broadcast_to(lat_rows[:, :, None], (shard_rows, 2, 2)).reshape(shard_rows, 4)
    weighted = jnp.tile(ocean * lat_pixels, (1, V))
    head = tables[5 * V + LEADS + 1 :]
    loss_part = f32(0.0)
    records = []
    for rollout in range(2):
        lead_hot = (jnp.arange(LEADS, dtype=jnp.int32) == leads[rollout]).astype(f32)
        x_first, embed_pull = jax.vjp(
            lambda cells, table: embed_tokens(cells, table, var_hot, lead_hot), inputs, tables
        )
        normed = layer_norm(x_first, norm_gains[0], norm_gains[1]).astype(bf16)
        rows_one = spread_rows(crossed, normed)
        packed = jnp.dot(rows_one, qkv_local, preferred_element_type=f32).astype(bf16)
        own_out, full, logsum = attend(packed)
        attended = exchange(crossed, own_out, True, 2)
        x_mid, rows_two, hidden, active, x_last, guess = branch_forward(
            attended, x_first, norm_gains, gathered, head
        )
        miss = guess - answers[rollout]
        loss_part = loss_part + jnp.sum(weighted * miss * miss)
        records.append(
            (embed_pull, x_first, rows_one, packed, full, logsum, attended, x_mid, rows_two,
             hidden, active, x_last, 2.0 * weighted * miss / denom)
        )
        inputs = guess
    carried = jnp.zeros_like(inputs)
    table_grad = jnp.zeros((5 * V + LEADS + 1, D), f32)
    head_total = jnp.zeros_like(head)
    gain_grad = jnp.zeros_like(norm_gains)
    qkv_grad = jnp.zeros((D, qkv_local.shape[1]), f32)
    kept = []

    def sources(index, other, blocked):
        listed = []
        for step in kept:
            listed += [(step[index], blocked), (step[other], not blocked)]
        return listed

    for rollout in (1, 0):
        (embed_pull, x_first, rows_one, packed, full, logsum, attended, x_mid, rows_two,
         hidden, active, x_last, loss_grad) = records[rollout]
        last_low, hidden_grad, mid_grad, mid_low, out_grad, gain_part, head_grad = branch_backward(
            loss_grad + carried, x_last, x_mid, norm_gains, hidden, gathered, head
        )
        kept.append((attended, rows_two, active, mid_low, hidden_grad, last_low))
        last_turn = crossed and rollout == 0
        if last_turn:
            listed = (
                (sources(2, 5, True), down_pieces, 256),
                (sources(1, 4, False) + sources(0, 3, True), up_out_pieces, 320),
            )
            x, y = lax.rem(place, 2), place // 2
            where = lambda which: jnp.stack((which, x, y)).astype(jnp.int32)
            others = [outer_half(*group, where(1 - core), None) for group in listed]
            out_grad, *others = tie(out_grad, *others)
            others = [shift(other, to_core) for other in others]
        own_grad = exchange(crossed, out_grad, False, 3)
        if last_turn:
            halves = []
            for group, other in zip(listed, others):
                halves += outer_half(*group, where(core), other)
            own_grad, *halves = tie(own_grad, *halves)
            sums = [first_sums(*halves[:2]), first_sums(*halves[2:])]
        packed_grad = attend_back(own_grad, packed, full, logsum)
        if last_turn:
            packed_grad, *sums[0] = tie(packed_grad, *sums[0])
            down_pieces_sum = second_sums(*sums[0], x, y)
        token_grad = exchange(crossed, packed_grad, True, 4)
        if last_turn:
            token_grad, *sums[1] = tie(token_grad, *sums[1])
            up_out_sum = second_sums(*sums[1], x, y)
        qkv_grad = qkv_grad + lax.dot_general(
            rows_one, packed_grad, TN, preferred_element_type=f32
        )
        row_grad, gain_one = entry_backward(token_grad, gathered[3], x_first, mid_grad, norm_gains)
        gain_part = gain_part + jnp.pad(gain_one, ((0, 4), (0, 0)))
        carried, embed_tables = embed_pull(row_grad)
        table_grad = table_grad + embed_tables[: 5 * V + LEADS + 1]
        head_total = head_total + head_grad
        gain_grad = gain_grad + gain_part

    def pair(index):
        return (kept[0][index], kept[1][index])

    if crossed:
        down_share = tall_piece(sum_levels(down_pieces_sum, level))
        up_out = sum_levels(up_out_sum, level)
        up_share = up_out[:256]
        out_share = tall_piece(up_out[256:])
    else:
        down_share = outer_plain(pair(2), pair(5), False)
        up_share = outer_plain(pair(1), pair(4), True)
        out_share = outer_plain(pair(0), pair(3), False)
    shares = (by_head(own_qkv_share(crossed, qkv_grad)), out_share, up_share, down_share)
    share_square = sum(jnp.sum(share * share) for share in shares)
    head_sum = lax.psum(jnp.concatenate((head_total, gain_grad[2:])), ("dp", "mp"))
    last_rows = jnp.concatenate((table_grad, gain_grad[:2]))
    if crossed:
        last_rows = jnp.pad(last_rows, ((0, -last_rows.shape[0] % 256), (0, 0)))
        row = jnp.arange(8, dtype=jnp.int32)[:, None]
        tile = jnp.where(row == 0, share_square, jnp.where(row == 1, loss_part, 0.0))
        last_sum, tile_sum = exchange_sum(last_rows, jnp.broadcast_to(tile, (8, 128)))
        square_sum, loss_sum = tile_sum[0, 0], tile_sum[1, 0]
    else:
        last_sum, loss_sum, square_sum = lax.psum(
            (last_rows, loss_part, share_square), ("dp", "mp")
        )
        square_sum = square_sum + jnp.sum(last_sum * last_sum)
    square_sum = square_sum + jnp.sum(head_sum * head_sum)
    embed_rows = 5 * V + LEADS + 1
    table_sum = jnp.concatenate((last_sum[:embed_rows], head_sum[: 4 * V]))
    gain_sum = jnp.concatenate((last_sum[embed_rows : embed_rows + 2], head_sum[4 * V :]))
    grad_norm = jnp.sqrt(square_sum)
    factor = jnp.minimum(1.0, clip_norm / (grad_norm + 1e-06))
    tab = adam_step(tables, factor * table_sum, tables_first, tables_second, lr_table)
    gai = adam_step(norm_gains, factor * gain_sum, gains_first, gains_second, lr_gain)
    qkv = adam_step(masters[0], factor * shares[0], qkv_first, qkv_second, lr_matrix)
    outp = adam_step(masters[1], factor * shares[1], out_first, out_second, lr_matrix)
    upp = adam_step(masters[2], factor * shares[2], up_first, up_second, lr_matrix)
    down = adam_step(masters[3], factor * shares[3], down_first, down_second, lr_matrix)
    average = average_keep * qkv_average + (1.0 - average_keep) * qkv[0]
    return (
        loss_sum / denom,
        grad_norm,
        tab[0],
        tab[1],
        tab[2],
        gai[0],
        gai[1],
        gai[2],
        qkv[0],
        qkv[1],
        qkv[2],
        outp[0],
        outp[1],
        outp[2],
        upp[0],
        upp[1],
        upp[2],
        down[0],
        down[1],
        down[2],
        average,
    )


def solution(mesh):
    return jax.shard_map(
        partial(shards, is_crossed(mesh.shape)),
        mesh=mesh,
        in_specs=(
            P("dp", "mp", None),
            P("dp", None, "mp", None),
            P("dp", "mp", None),
            P("dp", None),
            P(),
            P(),
            P(),
            P(),
            P(),
            P(),
            P(),
            P(None, "mp"),
            P("dp", "mp"),
            P("dp", "mp"),
            P("mp", None),
            P("mp", "dp"),
            P("mp", "dp"),
            P(None, "mp"),
            P("dp", "mp"),
            P("dp", "mp"),
            P("mp", None),
            P("mp", "dp"),
            P("mp", "dp"),
            P("dp", "mp"),
        ),
        out_specs=(
            P(),
            P(),
            P(),
            P(),
            P(),
            P(),
            P(),
            P(),
            P("dp", "mp"),
            P("dp", "mp"),
            P("dp", "mp"),
            P("mp", "dp"),
            P("mp", "dp"),
            P("mp", "dp"),
            P("dp", "mp"),
            P("dp", "mp"),
            P("dp", "mp"),
            P("mp", "dp"),
            P("mp", "dp"),
            P("mp", "dp"),
            P("dp", "mp"),
        ),
        check_vma=False,
    )
```

time: 1710 us -> 1080 us (0.63)
  waiting for transfers between devices: 813 us -> 122 us
  Pallas kernels: 0 us -> 572 us
  matrix products: 550 us -> 88.1 us
  blocking collectives: 80.7 us -> 0 us
  starting transfers between devices: 4.14 us -> 50.5 us
  other arithmetic: 120 us -> 87.9 us
    pallas_call x0 -> x25, Pallas kernels: none -> 572 us  [the longest x1 160 us: gather_weights(): pl.pallas_call(partial(gather_weights_kernel, count), out_shape=[jax.Shap...]
    dot_general x86 -> x4, matrix products: 486 us -> 18.3 us  [the longest x2 9.52 us: shards(): jnp.dot(rows_one, qkv_local, preferred_element_type=f32).astype(bf16)]
    all_gather x8 -> x1, waiting for transfers between devices: 357 us -> 0.01 us  [shards(): qkv_t = lax.all_gather(qkv_piece, ('mp', 'dp'), axis=0, tiled=True)]
    reduce_scatter x8 -> x0, waiting for transfers between devices: 293 us -> none  [the longest x4 147 us: fold_rows(): lax.psum_scatter(partial_sum.astype(jnp.bfloat16), 'mp', scatter_dimensio...]
    psum x2 -> x1, waiting for transfers between devices: 163 us -> 81.4 us  [shards(): lax.psum(jnp.concatenate((head_total, gain_grad[2:])), ('dp', 'mp'))]
    psum x2 -> x0, blocking collectives: 80.7 us -> none  [the longest x1 40.7 us: shards(): count = lax.psum(jnp.sum(ocean), ('dp', 'mp'))]
    ppermute x0 -> x25, starting transfers between devices: none -> 50.4 us  [the longest x19 26.6 us: shift(): return lax.ppermute(value, ('dp', 'mp'), device_pairs(move))]
    ppermute x0 -> x25, waiting for transfers between devices: none -> 40.9 us  [the longest x19 40.9 us: shift(): return lax.ppermute(value, ('dp', 'mp'), device_pairs(move))]
  transfers between devices with their start and end apart: 18 -> 27, of which waited for: 17 -> 6; matrix products, arithmetic and copies ran while one was open for 8% -> 21% of each run, Pallas kernels for 0% -> 45%
where the time goes in v1:
time: 1080 us; the launch traced here: 1070 us
  Pallas kernels  572 us (53%)
  local copies, waits for them, and re-layouts  122 us (11%)
  waiting for transfers between devices  122 us (11%)
  matrix products  88.1 us (8%)
  other arithmetic  87.9 us (8%)
  starting transfers between devices  50.5 us (5%)
  between operations  25.7 us (2%)
    pallas_call x1, Pallas kernels, gather_weights(): pl.pallas_call(partial(gather_weights_kernel, count), out_shape=[jax.Shap...  160 us
    pallas_call x6, Pallas kernels, exchange(): pl.pallas_call(partial(exchange_kernel, to_columns, rows, width), out_sha...  93.5 us
    psum x1, waiting for transfers between devices, shards(): lax.psum(jnp.concatenate((head_total, gain_grad[2:])), ('dp', 'mp'))  81.4 us
    pallas_call x2, Pallas kernels, attend_back(): pl.pallas_call(partial(attend_back_kernel, heads), grid=(total // block,)...  51.1 us
    pallas_call x2, Pallas kernels, spread_rows(): pl.pallas_call(gather_kernel, out_shape=jax.ShapeDtypeStruct((8 * rows, w...  48.8 us
    pallas_call x2, Pallas kernels, branch_forward(): pl.pallas_call(branch_kernel, grid=(parts,), out_shape=(jax.ShapeDtypeStr...  46.6 us
    ppermute x19, waiting for transfers between devices, shift(): return lax.ppermute(value, ('dp', 'mp'), device_pairs(move))  40.9 us
    pallas_call x2, Pallas kernels, branch_backward(): pl.pallas_call(branch_back_kernel, grid=(parts,), out_shape=(jax.ShapeDty...  39.6 us
  transfers between devices with their start and end apart: 27, of which 6 were waited for; matrix products, arithmetic and copies ran while one was open for 21% of the time, Pallas kernels for 45%

profile of v1, /device:TPU:0, one launch (start us, length us, event | category | flops | bytes accessed | tf_op | source)
XLA Modules:
  0.0 1069.0 jit_solution(3053321408856944199)
XLA Ops:
  36.9 160.0 %gather_weights.1 = (bf16[8,128,1024]{2,1,0:T(8,128)(2,1)}, bf16[8,1024,512]{2,1,0:T(8,128)(2,1)}, bf16[8,512,1024]{2,1,0:T(8,128)(2,1)}) custom-call(bf16[128,1024]{1,0:T(8,128)(2,1)} %convert_element_type.193.refs_0_, bf16[1024,512]{1,0:T(8,128)(2,1)} %convert_element_type.194.refs_1_, bf16[512,1024]{1,0:T(8,128)(2,1)} %convert_element_type.195.refs_2_), custom_call_target="tpu_custom_call" | custom-call | tf_op jit(solution)/shard_map/gather_weights/pallas_call | solution.py:1099
  217.2 17.2 %tile_sum.1 = f32[8,128]{1,0:T(8,128)} custom-call(f32[8,128]{1,0:T(8,128)} %broadcast_in_dim.24.t_ref), custom_call_target="tpu_custom_call" | custom-call | tf_op jit(solution)/shard_map/tile_sum/pallas_call | solution.py:948
  258.5 24.6 %gather_rows.2 = bf16[2048,1024]{1,0:T(8,128)(2,1)} custom-call(bf16[256,1024]{1,0:T(8,128)(2,1)} %get-tuple-element.241.x_ref), custom_call_target="tpu_custom_call" | custom-call | tf_op jit(solution)/shard_map/gather_rows/pallas_call | solution.py:174
  289.2 16.2 %attend.2 = (bf16[2048,128]{1,0:T(8,128)(2,1)}, f32[2048,128]{1,0:T(8,128)}, f32[2,2048]{1,0:T(2,128)}) custom-call(bf16[2048,128]{1,0:T(8,128)(2,1)} %get-tuple-element.261.q_ref, bf16[2048,128]{1,0:T(8,128)(2,1)} %get-tuple-element.260.k_ref, bf16[2048,128]{1,0:T(8,128)(2,1)} %get-tuple-element.259.v_ref), custom_call_target="tpu_custom_call" | custom-call | flops 8589934592 | bytes 2621440 | tf_op jit(solution)/shard_map/attend/pallas_call | solution.py:286
  305.4 11.5 %exchange_parts.6.o_ref.refs_6_ = bf16[256,1024]{1,0:T(8,128)(2,1)} custom-call(bf16[2048,128]{1,0:T(8,128)(2,1)} %get-tuple-element.88.x_ref), custom_call_target="tpu_custom_call" | custom-call | tf_op jit(solution)/shard_map/exchange_parts/pallas_call | solution.py:236
  317.0 29.0 %branch_forward.2 = (f32[256,1024]{1,0:T(8,128)}, bf16[256,1024]{1,0:T(8,128)(2,1)}, f32[256,4096]{1,0:T(8,128)}, bf16[256,4096]{1,0:T(8,128)(2,1)}, f32[256,1024]{1,0:T(8,128)}, /*index=5*/f32[256,192]{1,0:T(8,128)}) custom-call(bf16[256,1024]{1,0:T(8,128)(2,1)} %exchange_parts.6.o_ref.refs_6_, f32[256,1024]{1,0:T(8,128)} %get-tuple-element.242.x0_ref, ...), custom_call_target="tpu_custom_call" | custom-call | flops 5435817984 | bytes 23068672 | tf_op jit(solution)/shard_map/branch_forward/pallas_call | solution.py:480
  370.9 24.2 %gather_rows.3 = bf16[2048,1024]{1,0:T(8,128)(2,1)} custom-call(bf16[256,1024]{1,0:T(8,128)(2,1)} %get-tuple-element.239.x_ref), custom_call_target="tpu_custom_call" | custom-call | tf_op jit(solution)/shard_map/gather_rows/pallas_call | solution.py:174
  401.1 16.2 %attend.3 = (bf16[2048,128]{1,0:T(8,128)(2,1)}, f32[2048,128]{1,0:T(8,128)}, f32[2,2048]{1,0:T(2,128)}) custom-call(bf16[2048,128]{1,0:T(8,128)(2,1)} %get-tuple-element.258.q_ref, bf16[2048,128]{1,0:T(8,128)(2,1)} %get-tuple-element.257.k_ref, bf16[2048,128]{1,0:T(8,128)(2,1)} %get-tuple-element.256.v_ref), custom_call_target="tpu_custom_call" | custom-call | flops 8589934592 | bytes 2621440 | tf_op jit(solution)/shard_map/attend/pallas_call | solution.py:286
  417.4 11.5 %exchange_parts.7.o_ref.refs_4_ = bf16[256,1024]{1,0:T(8,128)(2,1)} custom-call(bf16[2048,128]{1,0:T(8,128)(2,1)} %get-tuple-element.94.x_ref), custom_call_target="tpu_custom_call" | custom-call | tf_op jit(solution)/shard_map/exchange_parts/pallas_call | solution.py:236
  428.9 17.6 %branch_forward.3 = (f32[256,1024]{1,0:T(8,128)}, bf16[256,1024]{1,0:T(8,128)(2,1)}, f32[256,4096]{1,0:T(8,128)}, bf16[256,4096]{1,0:T(8,128)(2,1)}, f32[256,1024]{1,0:T(8,128)}, /*index=5*/f32[256,192]{1,0:T(8,128)}) custom-call(bf16[256,1024]{1,0:T(8,128)(2,1)} %exchange_parts.7.o_ref.refs_4_, f32[256,1024]{1,0:T(8,128)} %get-tuple-element.240.x0_ref, ...), custom_call_target="tpu_custom_call" | custom-call | flops 5435817984 | bytes 23068672 | tf_op jit(solution)/shard_map/branch_forward/pallas_call | solution.py:480
  448.3 19.8 %branch_backward.2 = (bf16[256,1024]{1,0:T(8,128)(2,1)}, bf16[256,4096]{1,0:T(8,128)(2,1)}, f32[256,1024]{1,0:T(8,128)}, bf16[256,1024]{1,0:T(8,128)(2,1)}, bf16...) custom-call(f32[256,192]{1,0:T(8,128)} %multiply_divide_fusion.dpred_ref, ...), custom_call_target="tpu_custom_call" | custom-call | flops 6039797760 | bytes 23068672 | tf_op jit(solution)/shard_map/branch_backward/pallas_call | solution.py:572
  468.1 11.5 %exchange_parts.8.do_ref = bf16[2048,128]{1,0:T(8,128)(2,1)} custom-call(bf16[256,1024]{1,0:T(8,128)(2,1)} %get-tuple-element.99.x_ref), custom_call_target="tpu_custom_call" | custom-call | tf_op jit(solution)/shard_map/exchange_parts/pallas_call | solution.py:236
  479.6 25.8 %attend_back.2 = (bf16[2048,128]{1,0:T(8,128)(2,1)}, bf16[2048,128]{1,0:T(8,128)(2,1)}, bf16[2048,128]{1,0:T(8,128)(2,1)}) custom-call(bf16[2048,128]{1,0:T(8,128)(2,1)} %get-tuple-element.258.q_ref, bf16[2048,128]{1,0:T(8,128)(2,1)} %exchange_parts.8.do_ref, f32[2048,128]{1,0:T(8,128)} %get-tuple-element.100.full_ref, ...), custom_call_target="tpu_custom_call" | custom-call | flops 21474836480 | bytes 4194304 | tf_op jit(solution)/shard_map/attend_back/pallas_call | solution.py:377
  509.1 23.5 %exchange_parts.9.grad_ref = bf16[256,3072]{1,0:T(8,128)(2,1)} custom-call(bf16[2048,384]{1,0:T(8,128)(2,1)} %copy-done.41), custom_call_target="tpu_custom_call" | custom-call | tf_op jit(solution)/shard_map/exchange_parts/pallas_call | solution.py:236
  574.7 19.8 %branch_backward.3 = (bf16[256,1024]{1,0:T(8,128)(2,1)}, bf16[256,4096]{1,0:T(8,128)(2,1)}, f32[256,1024]{1,0:T(8,128)}, bf16[256,1024]{1,0:T(8,128)(2,1)}, bf16...) custom-call(f32[256,192]{1,0:T(8,128)} %get-tuple-element.262.dpred_ref, ...), custom_call_target="tpu_custom_call" | custom-call | flops 6039797760 | bytes 23068672 | tf_op jit(solution)/shard_map/branch_backward/pallas_call | solution.py:572
  601.2 8.0 outer_other.3
  626.3 11.5 %exchange_parts.10.do_ref = bf16[2048,128]{1,0:T(8,128)(2,1)} custom-call(bf16[256,1024]{1,0:T(8,128)(2,1)} %get-tuple-element.122.x_ref), custom_call_target="tpu_custom_call" | custom-call | tf_op jit(solution)/shard_map/exchange_parts/pallas_call | solution.py:236
  677.0 9.1 outer_own.3
  696.8 25.4 %attend_back.3 = (bf16[2048,128]{1,0:T(8,128)(2,1)}, bf16[2048,128]{1,0:T(8,128)(2,1)}, bf16[2048,128]{1,0:T(8,128)(2,1)}) custom-call(bf16[2048,128]{1,0:T(8,128)(2,1)} %get-tuple-element.261.q_ref, bf16[2048,128]{1,0:T(8,128)(2,1)} %exchange_parts.10.do_ref, f32[2048,128]{1,0:T(8,128)} %get-tuple-element.130.full_ref, ...), custom_call_target="tpu_custom_call" | custom-call | flops 21474836480 | bytes 4194304 | tf_op jit(solution)/shard_map/attend_back/pallas_call | solution.py:377
  723.9 19.3 %collective-permute-done.8 = bf16[2,2,256,512]{3,2,1,0:T(8,128)(2,1)S(1)} collective-permute-done((bf16[2,2,256,512]{3,2,1,0:T(8,128)(2,1)S(1)}, bf16[2,2,256,512]{3,2,1,0:T(8,128)(2,1)S(1)}, u32[]{:S(2)}, u32[]{:S(2)}) %collective-permute-start.8) | collective-permute-done | bytes 1048608 | tf_op jit(solution)/shard_map/ppermute | solution.py:719
  748.7 24.0 %exchange_parts.11.grad_ref = bf16[256,3072]{1,0:T(8,128)(2,1)} custom-call(bf16[2048,384]{1,0:T(8,128)(2,1)} %copy-done.26), custom_call_target="tpu_custom_call" | custom-call | tf_op jit(solution)/shard_map/exchange_parts/pallas_call | solution.py:236
  878.5 81.4 %all-reduce.13.cloned.1.call-done = f32[196,1024]{1,0:T(8,128)} async-done(((f32[196,1024]{1,0:T(8,128)}), f32[196,1024]{1,0:T(8,128)}) %all-reduce.13.cloned.1.call-update) | async-done | bytes 802832 | tf_op jit(solution)/shard_map/psum | solution.py:1279
  977.4 13.5 %collective-permute-done.18 = bf16[320,512]{1,0:T(8,128)(2,1)S(1)} collective-permute-done((bf16[320,512]{1,0:T(8,128)(2,1)S(1)}, bf16[320,512]{1,0:T(8,128)(2,1)S(1)}, u32[]{:S(2)}, u32[]{:S(2)}) %collective-permute-start.18) | collective-permute-done | bytes 327712 | tf_op jit(solution)/shard_map/ppermute | solution.py:719
  995.8 37.5 %exchange_sum.1 = (f32[256,1024]{1,0:T(8,128)}, f32[8,128]{1,0:T(8,128)}) custom-call(f32[256,1024]{1,0:T(8,128)} %select_maximum_fusion.x_ref, f32[8,128]{1,0:T(8,128)} %broadcast_in_dim.64.t_ref), custom_call_target="tpu_custom_call" | custom-call | tf_op jit(solution)/shard_map/exchange_sum/pallas_call | solution.py:886
  (485 shorter events, 385.2 us)
Async XLA Ops:
  7.2 526.0 %all-gather.2.cloned.1.call-start = ((), (), s32[]{:S(2)}) async-start(), calls=%async_computation | async-start | bytes 6488064 | tf_op jit(solution)/shard_map/all_gather | solution.py:1171
  7.2 230.0 %collective-permute-start = (f32[256,192]{0,1:T(8,128)}, f32[256,192]{0,1:T(8,128)}, u32[]{:S(2)}, u32[]{:S(2)}) collective-permute-start(f32[256,192]{0,1:T(8,128)} %bitcast.402), channel_id=1, source_target_pairs={{0,0},{1,1},{2,8},{3,9},{4,16},{5,17},{6,24},{7,25},{8,2},{9,3},{1... | collective-permute-start | bytes 589832 | tf_op jit(solution)/shard_map/ppermute | solution.py:106
  10.2 200.0 %collective-permute-start.1 = (s32[2]{0:T(128)}, s32[2]{0:T(128)S(1)}, u32[]{:S(2)}, u32[]{:S(2)}) collective-permute-start(s32[2]{0:T(128)} %bitcast.403), channel_id=1, source_target_pairs={{0,0},{1,1},{2,8},{3,9},{4,16},{5,17},{6,24},{7,25},{8,2},{9,3},{1... | collective-permute-start | bytes 32 | tf_op jit(solution)/shard_map/ppermute | solution.py:106
  14.8 268.3 %collective-permute-start.2 = (bf16[1024,384]{0,1:T(8,128)(2,1)}, bf16[1024,384]{0,1:T(8,128)(2,1)}, u32[]{:S(2)}, u32[]{:S(2)}) collective-permute-start(bf16[1024,384]{0,1:T(8,128)(2,1)} %bitcast.24), channel_id=1, source_target_pairs={{0,0},{1,1},{2,8},{3,9},{4,16},{5,17},{6,24},{7,25},{8,2},{9,3},{1... | collective-permute-start | bytes 2359304 | tf_op jit(solution)/shard_map/ppermute | solution.py:106
  22.3 192.4 %collective-permute-start.3 = (s32[256,4]{0,1:T(4,128)}, s32[256,4]{0,1:T(4,128)}, u32[]{:S(2)}, u32[]{:S(2)}) collective-permute-start(s32[256,4]{0,1:T(4,128)} %bitcast.35), channel_id=1, source_target_pairs={{0,0},{1,1},{2,8},{3,9},{4,16},{5,17},{6,24},{7,25},{8,2},{9,3},{1... | collective-permute-start | bytes 12296 | tf_op jit(solution)/shard_map/ppermute | solution.py:106
  25.2 421.3 %collective-permute-start.4 = (f32[2,256,192]{2,1,0:T(8,128)}, f32[2,256,192]{2,1,0:T(8,128)}, u32[]{:S(2)}, u32[]{:S(2)}) collective-permute-start(f32[2,256,192]{2,1,0:T(8,128)} %bitcast.36), channel_id=1, source_target_pairs={{0,0},{1,1},{2,8},{3,9},{4,16},{5,17},{6,24},{7,25},{8,2},{9,3},{1... | collective-permute-start | bytes 1179656 | tf_op jit(solution)/shard_map/ppermute | solution.py:106
  197.0 762.9 %all-reduce.13.cloned.1.call-start = ((), (), s32[]{:S(2)}) async-start(), calls=%async_computation.1 | async-start | bytes 1638400 | tf_op jit(solution)/shard_map/psum | solution.py:1279
  609.2 67.7 %collective-permute-start.6 = (bf16[4,4,320,512]{3,2,1,0:T(8,128)(2,1)}, bf16[4,4,320,512]{3,2,1,0:T(8,128)(2,1)}, u32[]{:S(2)}, u32[]{:S(2)}) collective-permute-start(bf16[4,4,320,512]{3,2,1,0:T(8,128)(2,1)} %outer_other.3), channel_id=1, source_target_pairs={{0,1},{1,0},{2,3},{3,2},{4,5},{5,4},{6,7},{7,6},{8,9},{9,8},{10,11... | collective-permute-start | bytes 15728648 | tf_op jit(solution)/shard_map/ppermute | solution.py:719
  609.3 59.9 %collective-permute-start.5 = (bf16[4,4,256,512]{3,2,1,0:T(8,128)(2,1)}, bf16[4,4,256,512]{3,2,1,0:T(8,128)(2,1)}, u32[]{:S(2)}, u32[]{:S(2)}) collective-permute-start(bf16[4,4,256,512]{3,2,1,0:T(8,128)(2,1)} %outer_other.2), channel_id=1, source_target_pairs={{0,1},{1,0},{2,3},{3,2},{4,5},{5,4},{6,7},{7,6},{8,9},{9,8},{10,11... | collective-permute-start | bytes 12582920 | tf_op jit(solution)/shard_map/ppermute | solution.py:719
  690.5 107.5 %collective-permute-start.10 = (bf16[2,2,320,512]{3,2,1,0:T(8,128)(2,1)}, bf16[2,2,320,512]{3,2,1,0:T(8,128)(2,1)}, u32[]{:S(2)}, u32[]{:S(2)}) collective-permute-start(bf16[2,2,320,512]{3,2,1,0:T(8,128)(2,1)} %slice.164), channel_id=1, source_target_pairs={{0,16},{1,17},{2,18},{3,19},{4,20},{5,21},{6,22},{7,23},{8,24},{9,... | collective-permute-start | bytes 3932168 | tf_op jit(solution)/shard_map/ppermute | solution.py:719
  692.5 108.4 %collective-permute-start.9 = (bf16[2,2,320,512]{3,2,0,1:T(8,128)(2,1)}, bf16[2,2,320,512]{3,2,0,1:T(8,128)(2,1)}, u32[]{:S(2)}, u32[]{:S(2)}) collective-permute-start(bf16[2,2,320,512]{3,2,0,1:T(8,128)(2,1)} %slice.190), channel_id=1, source_target_pairs={{0,8},{1,9},{2,10},{3,11},{4,12},{5,13},{6,14},{7,15},{8,0},{9,1},... | collective-permute-start | bytes 3932168 | tf_op jit(solution)/shard_map/ppermute | solution.py:719
  693.0 50.2 %collective-permute-start.8 = (bf16[2,2,256,512]{3,2,1,0:T(8,128)(2,1)S(1)}, bf16[2,2,256,512]{3,2,1,0:T(8,128)(2,1)S(1)}, u32[]{:S(2)}, u32[]{:S(2)}) collective-permute-start(bf16[2,2,256,512]{3,2,1,0:T(8,128)(2,1)S(1)} %slice.160), channel_id=1, source_target_pairs={{0,16},{1,17},{2,18},{3,19},{4,20},{5,21},{6,22},{7,23},{8,24},{9,... | collective-permute-start | bytes 3145736 | tf_op jit(solution)/shard_map/ppermute | solution.py:719
  695.4 49.4 %collective-permute-start.7 = (bf16[2,2,256,512]{3,2,0,1:T(8,128)(2,1)}, bf16[2,2,256,512]{3,2,0,1:T(8,128)(2,1)S(1)}, u32[]{:S(2)}, u32[]{:S(2)}) collective-permute-start(bf16[2,2,256,512]{3,2,0,1:T(8,128)(2,1)} %slice.188), channel_id=1, source_target_pairs={{0,8},{1,9},{2,10},{3,11},{4,12},{5,13},{6,14},{7,15},{8,0},{9,1},... | collective-permute-start | bytes 3145736 | tf_op jit(solution)/shard_map/ppermute | solution.py:719
  777.9 12.7 %collective-permute-start.12 = (bf16[256,384]{0,1:T(8,128)(2,1)}, bf16[256,384]{0,1:T(8,128)(2,1)}, u32[]{:S(2)}, u32[]{:S(2)}) collective-permute-start(bf16[256,384]{0,1:T(8,128)(2,1)} %bitcast.386), channel_id=1, source_target_pairs={{0,4},{1,5},{2,6},{3,7},{4,0},{5,1},{6,2},{7,3},{8,12},{9,13},{10,... | collective-permute-start | bytes 589832 | tf_op jit(solution)/shard_map/ppermute | solution.py:719
  787.9 81.7 %collective-permute-start.21 = (bf16[2,256,512]{2,1,0:T(8,128)(2,1)}, bf16[2,256,512]{2,1,0:T(8,128)(2,1)}, u32[]{:S(2)}, u32[]{:S(2)}) collective-permute-start(bf16[2,256,512]{2,1,0:T(8,128)(2,1)} %dynamic-slice_bitcast_fusion.2), channel_id=1, source_target_pairs={{0,8},{1,9},{2,10},{3,11},{4,12},{5,13},{6,14},{7,15},{8,0},{9,1},... | collective-permute-start | bytes 1572872 | tf_op jit(solution)/shard_map/ppermute | solution.py:719
  790.6 80.2 %collective-permute-start.20 = (bf16[2,256,512]{2,1,0:T(8,128)(2,1)}, bf16[2,256,512]{2,1,0:T(8,128)(2,1)}, u32[]{:S(2)}, u32[]{:S(2)}) collective-permute-start(bf16[2,256,512]{2,1,0:T(8,128)(2,1)} %dynamic-slice_bitcast_fusion.3), channel_id=1, source_target_pairs={{0,16},{1,17},{2,18},{3,19},{4,20},{5,21},{6,22},{7,23},{8,24},{9,... | collective-permute-start | bytes 1572872 | tf_op jit(solution)/shard_map/ppermute | solution.py:719
  793.4 81.6 %collective-permute-start.14 = (f32[256,384]{0,1:T(8,128)}, f32[256,384]{0,1:T(8,128)}, u32[]{:S(2)}, u32[]{:S(2)}) collective-permute-start(f32[256,384]{0,1:T(8,128)} %fusion.84), channel_id=1, source_target_pairs={{0,0},{1,1},{2,8},{3,9},{4,16},{5,17},{6,24},{7,25},{8,2},{9,3},{1... | collective-permute-start | bytes 1179656 | tf_op jit(solution)/shard_map/ppermute | solution.py:106
  822.9 139.1 %collective-permute-start.16 = (bf16[2,320,512]{2,1,0:T(8,128)(2,1)}, bf16[2,320,512]{2,1,0:T(8,128)(2,1)}, u32[]{:S(2)}, u32[]{:S(2)}) collective-permute-start(bf16[2,320,512]{2,1,0:T(8,128)(2,1)} %dynamic-slice_bitcast_fusion), channel_id=1, source_target_pairs={{0,8},{1,9},{2,10},{3,11},{4,12},{5,13},{6,14},{7,15},{8,0},{9,1},... | collective-permute-start | bytes 1966088 | tf_op jit(solution)/shard_map/ppermute | solution.py:719
  826.9 136.3 %collective-permute-start.15 = (bf16[2,320,512]{2,1,0:T(8,128)(2,1)}, bf16[2,320,512]{2,1,0:T(8,128)(2,1)}, u32[]{:S(2)}, u32[]{:S(2)}) collective-permute-start(bf16[2,320,512]{2,1,0:T(8,128)(2,1)} %dynamic-slice_bitcast_fusion.1), channel_id=1, source_target_pairs={{0,16},{1,17},{2,18},{3,19},{4,20},{5,21},{6,22},{7,23},{8,24},{9,... | collective-permute-start | bytes 1966088 | tf_op jit(solution)/shard_map/ppermute | solution.py:719
  873.0 96.1 %collective-permute-start.22 = (bf16[256,512]{1,0:T(8,128)(2,1)}, bf16[256,512]{1,0:T(8,128)(2,1)}, u32[]{:S(2)}, u32[]{:S(2)}) collective-permute-start(bf16[256,512]{1,0:T(8,128)(2,1)} %get-tuple-element.246), channel_id=1, source_target_pairs={{0,2},{1,3},{2,4},{3,5},{4,6},{5,7},{6,0},{7,1},{8,10},{9,11},{10,... | collective-permute-start | bytes 786440 | tf_op jit(solution)/shard_map/ppermute | solution.py:719
  873.2 97.4 %collective-permute-start.23 = (bf16[256,512]{1,0:T(8,128)(2,1)}, bf16[256,512]{1,0:T(8,128)(2,1)}, u32[]{:S(2)}, u32[]{:S(2)}) collective-permute-start(bf16[256,512]{1,0:T(8,128)(2,1)} %get-tuple-element.247), channel_id=1, source_target_pairs={{0,4},{1,5},{2,6},{3,7},{4,0},{5,1},{6,2},{7,3},{8,12},{9,13},{10,... | collective-permute-start | bytes 786440 | tf_op jit(solution)/shard_map/ppermute | solution.py:719
  875.0 95.6 %collective-permute-start.24 = (bf16[256,512]{1,0:T(8,128)(2,1)}, bf16[256,512]{1,0:T(8,128)(2,1)}, u32[]{:S(2)}, u32[]{:S(2)}) collective-permute-start(bf16[256,512]{1,0:T(8,128)(2,1)} %get-tuple-element.248), channel_id=1, source_target_pairs={{0,6},{1,7},{2,0},{3,1},{4,2},{5,3},{6,4},{7,5},{8,14},{9,15},{10,... | collective-permute-start | bytes 786440 | tf_op jit(solution)/shard_map/ppermute | solution.py:719
  967.7 23.2 %collective-permute-start.18 = (bf16[320,512]{1,0:T(8,128)(2,1)S(1)}, bf16[320,512]{1,0:T(8,128)(2,1)S(1)}, u32[]{:S(2)}, u32[]{:S(2)}) collective-permute-start(bf16[320,512]{1,0:T(8,128)(2,1)S(1)} %get-tuple-element.244), channel_id=1, source_target_pairs={{0,4},{1,5},{2,6},{3,7},{4,0},{5,1},{6,2},{7,3},{8,12},{9,13},{10,... | collective-permute-start | bytes 983048 | tf_op jit(solution)/shard_map/ppermute | solution.py:719
  969.1 21.8 %collective-permute-start.19 = (bf16[320,512]{1,0:T(8,128)(2,1)S(1)}, bf16[320,512]{1,0:T(8,128)(2,1)S(1)}, u32[]{:S(2)}, u32[]{:S(2)}) collective-permute-start(bf16[320,512]{1,0:T(8,128)(2,1)S(1)} %get-tuple-element.245), channel_id=1, source_target_pairs={{0,6},{1,7},{2,0},{3,1},{4,2},{5,3},{6,4},{7,5},{8,14},{9,15},{10,... | collective-permute-start | bytes 983048 | tf_op jit(solution)/shard_map/ppermute | solution.py:719
  (117 other events, 1100.9 us)
Sparse Core Ops, SparseCore 0:
  197.1 73.9 all-gather.1
  820.9 138.9 all-reduce.12

commit v2 on v1

--- a/solution.py
+++ b/solution.py
@@ -42,27 +42,6 @@
     row_index = jnp.arange(pixel_rows, dtype=jnp.float32)
     cosine = jnp.cos(((row_index + 0.5) / pixel_rows - 0.5) * math.pi)
     return cosine / jnp.mean(cosine)
-
-
-def embed_tokens(cells, tables, var_hot, lead_hot):
-    count_rows = cells.shape[0]
-    patch_tab = tables[: 4 * V].reshape(V, 4, HEADS, HEAD_DIM)
-    var_tab = jnp.dot(var_hot, tables[4 * V : 5 * V], precision=highest).reshape(V, HEADS, HEAD_DIM)
-    lead_vec = jnp.dot(lead_hot, tables[5 * V : 5 * V + LEADS], precision=highest)
-    query = tables[5 * V + LEADS].reshape(HEADS, HEAD_DIM)
-    keyed = jnp.einsum("vphc,hc->vph", patch_tab, query, precision=highest)
-    biased = jnp.einsum("vhc,hc->vh", var_tab, query, precision=highest)
-    pixels = cells.reshape(count_rows, V, 4)
-    scores = (jnp.einsum("tvp,vph->tvh", pixels, keyed, precision=highest) + biased) * HEAD_DIM ** (
-        -0.5
-    )
-    shares = jax.nn.softmax(scores, axis=1)
-    mixed = (shares[:, :, None, :] * pixels[:, :, :, None]).reshape(count_rows, 4 * V, HEADS)
-    merged = jnp.einsum(
-        "tkh,khc->thc", mixed, patch_tab.reshape(4 * V, HEADS, HEAD_DIM), precision=highest
-    )
-    merged = merged + jnp.einsum("tvh,vhc->thc", shares, var_tab, precision=highest)
-    return merged.reshape(count_rows, D) + lead_vec
 
 
 bf16 = jnp.bfloat16
@@ -961,24 +940,278 @@
     return total[0, 0]
 
 
-def entry_back_kernel(grad_ref, qkv_ref, x0_ref, mid_ref, gains_ref, o_ref, gain_ref, sum_ref):
-    sum_ref[...] = jnp.dot(grad_ref[...], qkv_ref[...], preferred_element_type=f32)
-    unit, inverse = normed_parts(x0_ref[...])
-    part, gain_grad, bias_grad = norm_grad(unit, inverse, gains_ref[0:1, :], sum_ref[...])
-    o_ref[...] = mid_ref[...] + part
-    gain_ref[0:1, :] = gain_grad
-    gain_ref[1:2, :] = bias_grad
-
-
-def entry_backward(token_grad, qkv_t, x_first, mid_grad, norm_gains):
+def split_low(values):
+    high = values.astype(bf16)
+    return high, (values - high.astype(f32)).astype(bf16)
+
+
+def three_products(left, right, dims=(((1,), (0,)), ((), ()))):
+    def product(one, two):
+        return lax.dot_general(one, two, dims, preferred_element_type=f32)
+
+    return product(left[0], right[0]) + (product(left[1], right[0]) + product(left[0], right[1]))
+
+
+def exact_product(left, right, dims=(((1,), (0,)), ((), ()))):
+    return lax.dot_general(left, right, dims, precision=highest, preferred_element_type=f32)
+
+
+def head_marks(width):
+    head = lax.broadcasted_iota(jnp.int32, (HEADS, width), 0)
+    column = lax.broadcasted_iota(jnp.int32, (HEADS, width), 1)
+    return jnp.where(column // HEAD_DIM == head, 1.0, 0.0).astype(f32)
+
+
+def quarter_marks(padded):
+    row = lax.broadcasted_iota(jnp.int32, (padded, V), 0)
+    column = lax.broadcasted_iota(jnp.int32, (padded, V), 1)
+    return jnp.where(row // 4 == column, 0.25, 0.0).astype(f32)
+
+
+def tables_kernel(tables_ref, hot_ref, patch_ref, var_ref, keyed_ref, bias_ref):
+    padded, width = patch_ref.shape
+    query = tables_ref[5 * V + LEADS : 5 * V + LEADS + 1, :]
+    patch_ref[...] = jnp.zeros_like(patch_ref)
+    patch_ref[: 4 * V, :] = tables_ref[: 4 * V, :]
+    chosen = exact_product(hot_ref[...], tables_ref[4 * V : 5 * V, :])
+    var_ref[...] = exact_product(quarter_marks(padded), chosen)
+    marks = head_marks(width)
+    scale = HEAD_DIM**-0.5
+    keyed_ref[...] = exact_product(marks, patch_ref[...] * query, NT) * scale
+    bias = exact_product(marks, var_ref[...] * query, NT) * (4.0 * scale)
+    column = lax.broadcasted_iota(jnp.int32, bias.shape, 1)
+    bias_ref[...] = jnp.where(column < 4 * V, bias, -1e30)
+
+
+def prepare_tables(tables, var_hot):
+    padded = 256
+    return pl.pallas_call(
+        tables_kernel,
+        out_shape=(
+            jax.ShapeDtypeStruct((padded, D), f32),
+            jax.ShapeDtypeStruct((padded, D), f32),
+            jax.ShapeDtypeStruct((HEADS, padded), f32),
+            jax.ShapeDtypeStruct((HEADS, padded), f32),
+        ),
+        compiler_params=pltpu.CompilerParams(vmem_limit_bytes=BIG),
+        name="prepare_tables",
+    )(tables, var_hot)
+
+
+def four_sum(values):
+    size = values.shape[1]
+    lane = lax.broadcasted_iota(jnp.int32, values.shape, 1)
+    values = values + jnp.where(
+        lane % 2 == 0, pltpu.roll(values, size - 1, 1), pltpu.roll(values, 1, 1)
+    )
+    return values + jnp.where(
+        lane % 4 < 2, pltpu.roll(values, size - 2, 1), pltpu.roll(values, 2, 1)
+    )
+
+
+def cell_shares(cells, keyed, bias):
+    scores = four_sum(cells * keyed) + bias
+    raised = jnp.exp(scores - jnp.max(scores, axis=1, keepdims=True))
+    total = jnp.sum(raised, axis=1, keepdims=True) * 0.25
+    return raised * (1.0 / total)
+
+
+def embed_pair(pair, cells, keyed_ref, bias_ref, patch_ref, var_ref, x0_ref):
+    patch = split_low(patch_ref[...])
+    variable = split_low(var_ref[...])
+    outs = []
+    for which in range(2):
+        row = pl.ds(pair * 2 + which, 1)
+        shares = cell_shares(cells, keyed_ref[row, :], bias_ref[row, :])
+        outs.append(
+            three_products(split_low(shares * cells), patch)
+            + three_products(split_low(shares), variable)
+        )
+    lane = lax.broadcasted_iota(jnp.int32, outs[0].shape, 1)
+    columns = pl.ds(pl.multiple_of(pair * 2 * HEAD_DIM, 2 * HEAD_DIM), 2 * HEAD_DIM)
+    x0_ref[:, columns] = jnp.where(lane < HEAD_DIM, outs[0], outs[1])
+
+
+def embed_kernel(
+    u_ref, keyed_ref, bias_ref, patch_ref, var_ref, lead_ref, gains_ref, x0_ref, h1_ref
+):
+    pair = pl.program_id(0)
+    embed_pair(pair, u_ref[...], keyed_ref, bias_ref, patch_ref, var_ref, x0_ref)
+
+    @pl.when(pair == pl.num_programs(0) - 1)
+    def _():
+        x0_ref[...] += lead_ref[...]
+        unit, _ = normed_parts(x0_ref[...])
+        h1_ref[...] = (unit * gains_ref[0:1, :] + gains_ref[1:2, :]).astype(bf16)
+
+
+def embed_forward(cells, prepared, lead_row, norm_gains):
+    patch, variable, keyed, bias = prepared
+    rows, padded = cells.shape
+    fixed = lambda shape: pl.BlockSpec(shape, lambda i: (0, 0))
+    by_pair = pl.BlockSpec((padded, 2 * HEAD_DIM), lambda i: (0, i))
+    return pl.pallas_call(
+        embed_kernel,
+        grid=(HEADS // 2,),
+        out_shape=(
+            jax.ShapeDtypeStruct((rows, D), f32),
+            jax.ShapeDtypeStruct((rows, D), bf16),
+        ),
+        in_specs=[
+            fixed((rows, padded)),
+            fixed(keyed.shape),
+            fixed(bias.shape),
+            by_pair,
+            by_pair,
+            fixed((1, D)),
+            fixed(norm_gains.shape),
+        ],
+        out_specs=[fixed((rows, D)), fixed((rows, D))],
+        compiler_params=pltpu.CompilerParams(vmem_limit_bytes=BIG),
+        cost_estimate=pl.CostEstimate(
+            flops=24 * rows * padded * D, bytes_accessed=14 * rows * D, transcendentals=16 * rows * padded
+        ),
+        name="embed_forward",
+    )(cells, keyed, bias, patch, variable, lead_row, norm_gains)
+
+
+def entry_back_kernel(
+    grad_ref, qkv_ref, x0_ref, mid_ref, gains_ref, u_ref, keyed_ref, bias_ref, patch_ref, var_ref,
+    du_ref, gain_ref, lead_ref, dpatch_ref, dvar_ref, dkeyed_ref, dbias_ref,
+    dx_ref, flip_ref,
+):
+    pair = pl.program_id(0)
+
+    @pl.when(pair == 0)
+    def _():
+        row_grad = jnp.dot(grad_ref[...], qkv_ref[...], preferred_element_type=f32)
+        unit, inverse = normed_parts(x0_ref[...])
+        part, gain_grad, bias_grad = norm_grad(unit, inverse, gains_ref[0:1, :], row_grad)
+        total = mid_ref[...] + part
+        dx_ref[...] = total
+        flip_ref[...] = total.T
+        lead_ref[...] = jnp.sum(total, axis=0, keepdims=True)
+        gain_ref[0:1, :] = gain_grad
+        gain_ref[1:2, :] = bias_grad
+        du_ref[...] = jnp.zeros_like(du_ref)
+
+    cells = u_ref[...]
+    size = 2 * HEAD_DIM
+    columns = pl.ds(pl.multiple_of(pair * size, size), size)
+    grads = dx_ref[:, columns]
+    lane = lax.broadcasted_iota(jnp.int32, grads.shape, 1)
+    patch = split_low(patch_ref[...])
+    variable = split_low(var_ref[...])
+    cells_grad = None
+    for which in range(2):
+        row = pl.ds(pair * 2 + which, 1)
+        keyed = keyed_ref[row, :]
+        shares = cell_shares(cells, keyed, bias_ref[row, :])
+        one = split_low(jnp.where(lane // HEAD_DIM == which, grads, 0.0))
+        mixed_grad = three_products(one, patch, NT)
+        share_grad = mixed_grad * cells + three_products(one, variable, NT)
+        weighted = shares * share_grad
+        inner = jnp.sum(weighted, axis=1, keepdims=True)
+        score_grad = four_sum(weighted) - shares * inner
+        piece = mixed_grad * shares + score_grad * keyed
+        cells_grad = piece if cells_grad is None else cells_grad + piece
+        scale = HEAD_DIM**-0.5
+        dkeyed_ref[row, :] = jnp.sum(score_grad * cells, axis=0, keepdims=True) * scale
+        dbias_ref[row, :] = jnp.sum(score_grad, axis=0, keepdims=True) * scale
+        rows = pl.ds(pl.multiple_of(pair * size + which * HEAD_DIM, HEAD_DIM), HEAD_DIM)
+        flipped = split_low(flip_ref[rows, :])
+        mine = slice(which * HEAD_DIM, (which + 1) * HEAD_DIM)
+        dpatch_ref[mine, :] = three_products(flipped, split_low(shares * cells))
+        dvar_ref[mine, :] = three_products(flipped, split_low(shares))
+    du_ref[...] += cells_grad
+
+
+def entry_backward(token_grad, qkv_t, x_first, mid_grad, norm_gains, cells, prepared):
+    patch, variable, keyed, bias = prepared
     rows, width = x_first.shape
+    padded = cells.shape[1]
+    fixed = lambda shape: pl.BlockSpec(shape, lambda i: (0, 0))
+    by_pair = pl.BlockSpec((padded, 2 * HEAD_DIM), lambda i: (0, i))
+    flipped = pl.BlockSpec((2 * HEAD_DIM, padded), lambda i: (i, 0))
     return pl.pallas_call(
         entry_back_kernel,
-        out_shape=(jax.ShapeDtypeStruct((rows, width), f32), jax.ShapeDtypeStruct((2, width), f32)),
-        scratch_shapes=[pltpu.VMEM((rows, width), f32)],
+        grid=(HEADS // 2,),
+        out_shape=(
+            jax.ShapeDtypeStruct((rows, padded), f32),
+            jax.ShapeDtypeStruct((2, width), f32),
+            jax.ShapeDtypeStruct((1, width), f32),
+            jax.ShapeDtypeStruct((width, padded), f32),
+            jax.ShapeDtypeStruct((width, padded), f32),
+            jax.ShapeDtypeStruct(keyed.shape, f32),
+            jax.ShapeDtypeStruct(bias.shape, f32),
+        ),
+        in_specs=[
+            fixed(token_grad.shape),
+            fixed(qkv_t.shape),
+            fixed((rows, width)),
+            fixed((rows, width)),
+            fixed(norm_gains.shape),
+            fixed(cells.shape),
+            fixed(keyed.shape),
+            fixed(bias.shape),
+            by_pair,
+            by_pair,
+        ],
+        out_specs=[
+            fixed((rows, padded)),
+            fixed((2, width)),
+            fixed((1, width)),
+            flipped,
+            flipped,
+            fixed(keyed.shape),
+            fixed(bias.shape),
+        ],
+        scratch_shapes=[pltpu.VMEM((rows, width), f32), pltpu.VMEM((width, rows), f32)],
         compiler_params=pltpu.CompilerParams(vmem_limit_bytes=BIG),
+        cost_estimate=pl.CostEstimate(
+            flops=60 * rows * padded * D, bytes_accessed=40 * rows * D, transcendentals=16 * rows * padded
+        ),
         name="entry_backward",
-    )(token_grad, qkv_t, x_first, mid_grad, norm_gains)
+    )(token_grad, qkv_t, x_first, mid_grad, norm_gains, cells, keyed, bias, patch, variable)
+
+
+def table_grads_kernel(
+    pa_ref, pb_ref, va_ref, vb_ref, ka_ref, kb_ref, ba_ref, bb_ref,
+    patch_ref, var_ref, query_ref, hot_ref, lead_hot_ref, lead_ref, gain_ref, head_ref, high_ref, o_ref,
+):
+    padded, width = patch_ref.shape
+    marks = head_marks(width)
+    query = query_ref[...]
+    keyed_grad = exact_product(ka_ref[...] + kb_ref[...], marks, TN)
+    bias_grad = exact_product(ba_ref[...] + bb_ref[...], marks, TN)
+    o_ref[...] = jnp.zeros_like(o_ref)
+    patch_grad = (pa_ref[...] + pb_ref[...]).T + keyed_grad * query
+    o_ref[: 4 * V, :] = patch_grad[: 4 * V, :]
+    var_grad = (va_ref[...] + vb_ref[...]).T + bias_grad * query
+    var_rows = exact_product(quarter_marks(padded), var_grad, TN)
+    o_ref[4 * V : 5 * V, :] = exact_product(hot_ref[...], var_rows, TN)
+    lead_rows = exact_product(lead_hot_ref[...], lead_ref[...], TN)
+    o_ref[5 * V : 5 * V + LEADS, :] = lead_rows[:LEADS, :]
+    query_grad = jnp.sum(
+        keyed_grad * patch_ref[...] + bias_grad * var_ref[...], axis=0, keepdims=True
+    )
+    o_ref[5 * V + LEADS : 5 * V + LEADS + 1, :] = query_grad
+    o_ref[5 * V + LEADS + 1 : 5 * V + LEADS + 3, :] = gain_ref[...]
+    o_ref[padded : padded + 4 * V, :] = head_ref[...]
+    o_ref[padded + 4 * V : padded + 4 * V + 4, :] = high_ref[...]
+
+
+def table_grads(first, second, prepared, query, var_hot, lead_hots, leads, gain_rows, head, high):
+    patch, variable, _, _ = prepared
+    operands = []
+    for one, two in zip(first, second):
+        operands += [one, two]
+    return pl.pallas_call(
+        table_grads_kernel,
+        out_shape=jax.ShapeDtypeStruct((2 * patch.shape[0], D), f32),
+        compiler_params=pltpu.CompilerParams(vmem_limit_bytes=BIG),
+        name="table_grads",
+    )(*operands, patch, variable, query, var_hot, lead_hots, leads, gain_rows, head, high)
 
 
 def adam_step(master, grad, first, second, rate):
@@ -998,25 +1231,28 @@
     return shard.reshape(rows, 3, -1, HEAD_DIM).transpose(0, 2, 1, 3).reshape(rows, -1)
 
 
-def gather_weights_kernel(count, *refs):
-    shards, outs = refs[:count], refs[count : 2 * count]
-    send_sem, recv_sem, own_sem = refs[2 * count :]
+def start_kernel(halves, *refs):
+    count = len(halves)
+    packed_ref, qkv_ref, targets_ref, keyed_ref, bias_ref, patch_ref, var_ref, lead_ref, gains_ref = refs[:9]
+    shards = refs[9 : 9 + count]
+    x0_ref, h1_ref, cells_ref, qkv_out, targets_out = refs[9 + count : 14 + count]
+    outs = refs[14 + count : 14 + 2 * count]
+    held_ref, send_sem, recv_sem, own_sem = refs[14 + 2 * count :]
+    step = pl.program_id(0)
     dp, level, core = mesh_place()
     x = lax.rem(dp, 2)
     columns = {"here": dp, "side": dp + 1 - 2 * x, "down": lax.rem(dp + 2, 4), "far": 3 - dp}
     side = device_of(columns["side"], level, core)
     down = device_of(columns["down"], level, core)
     near = device_of(dp, level, 1 - core)
-    deep = [device_of(dp, lax.rem(level + step, 4), core) for step in (1, 2, 3)]
-    barrier = pltpu.get_barrier_semaphore()
-    for target in (side, down, near, *deep):
-        pl.semaphore_signal(barrier, inc=1, device_id=target, device_id_type=MESH)
-    pl.semaphore_wait(barrier, 6)
-    started = []
-
-    def send(source, target_ref, target):
-        slot = len(started)
-        copy = pltpu.make_async_remote_copy(
+    across = device_of(level, dp, core)
+    deep = [device_of(dp, lax.rem(level + move, 4), core) for move in (1, 2, 3)]
+    slots = [0]
+
+    def remote(source, target_ref, target):
+        slot = slots[0]
+        slots[0] += 1
+        return pltpu.make_async_remote_copy(
             src_ref=source,
             dst_ref=target_ref,
             send_sem=send_sem.at[slot],
@@ -1024,93 +1260,197 @@
             device_id=target,
             device_id_type=MESH,
         )
-        copy.start()
-        started.append(copy)
-        return copy
-
-    def place(out, source, column, half=None):
+
+    def place(out, source, column, half, pieces):
         rows = out.shape[1] // 4
-        start, size = columns[column] * rows, rows
-        if half is not None:
-            start, size = start + half * (rows // 2), rows // 2
-        return out.at[source * 2 + core, pl.ds(pl.multiple_of(start, rows // 2), size), :]
-
-    def pass_on(out, source, column, target, half=None):
-        where = place(out, source, column, half)
-        return send(where, where, target)
-
+        size = rows // pieces
+        start = pl.multiple_of(columns[column] * rows + half * size, size)
+        return out.at[source * 2 + core, pl.ds(start, size), :]
+
+    def pass_on(out, source, column, target, cut):
+        where = place(out, source, column, *cut)
+        return remote(where, where, target)
+
+    moves = [(packed_ref, held_ref), (qkv_ref, qkv_out), (targets_ref, targets_out)]
+    crossing = [remote(source, target_ref, across) for source, target_ref in moves]
+    staying = [
+        pltpu.make_async_copy(source, target_ref, own_sem.at[count + index])
+        for index, (source, target_ref) in enumerate(moves)
+    ]
+    mine = [outs[index].at[level * 2 + core] for index in range(count)]
+    given = [remote(shards[index], mine[index], near) for index in range(count)]
+    kept = [
+        pltpu.make_async_copy(shards[index], mine[index], own_sem.at[index]) for index in range(count)
+    ]
     chunks = []
     for index in range(count):
-        rows = outs[index].shape[1] // 4
-        own = shards[index].at[pl.ds(pl.multiple_of(dp * rows, rows), rows), :]
-        for step in (1, 2, 3):
-            copy = send(own, place(outs[index], level, "here"), deep[step - 1])
-            chunks.append((outs[index], lax.rem(level + 4 - step, 4), copy))
-    ends = []
-    locals_ = []
-    for index in range(count):
-        ends.append(send(shards[index], outs[index].at[level * 2 + core], near))
-        copy = pltpu.make_async_copy(
-            shards[index], outs[index].at[level * 2 + core], own_sem.at[index]
-        )
-        copy.start()
-        locals_.append(copy)
-    plane, hops = {}, {}
+        out, pieces = outs[index], halves[index]
+        for half in range(pieces):
+            full = out.shape[1] // 4
+            size = full // pieces
+            own = shards[index].at[pl.ds(pl.multiple_of(dp * full + half * size, size), size), :]
+            cut = (half, pieces)
+            for move in (1, 2, 3):
+                source = lax.rem(level + 4 - move, 4)
+                chunks.append(
+                    {
+                        "level": remote(own, place(out, level, "here", *cut), deep[move - 1]),
+                        "side": pass_on(out, source, "here", side, cut),
+                        "down": pass_on(out, source, "here", down, cut),
+                        "hop_down": pass_on(out, source, "side", down, (2 * half, 2 * pieces)),
+                        "hop_side": pass_on(out, source, "down", side, (2 * half + 1, 2 * pieces)),
+                        "here_near": pass_on(out, source, "here", near, cut),
+                        "side_near": pass_on(out, source, "side", near, cut),
+                        "down_near": pass_on(out, source, "down", near, cut),
+                        "far_near": pass_on(out, source, "far", near, cut),
+                    }
+                )
     total = len(chunks)
-    for step in range(total + 2):
-        if step < total:
-            out, source, copy = chunks[step]
-            copy.wait_recv()
-            plane[step] = (
-                pass_on(out, source, "here", side),
-                pass_on(out, source, "here", down),
-            )
-            ends.append(pass_on(out, source, "here", near))
-        if 0 <= step - 1 < total:
-            out, source, _ = chunks[step - 1]
-            from_side, from_down = plane[step - 1]
-            from_side.wait_recv()
-            one = pass_on(out, source, "side", down, 0)
-            from_down.wait_recv()
-            two = pass_on(out, source, "down", side, 1)
-            hops[step - 1] = (one, two)
-            ends.append(pass_on(out, source, "side", near))
-            ends.append(pass_on(out, source, "down", near))
-        if 0 <= step - 2 < total:
-            out, source, _ = chunks[step - 2]
-            for copy in hops[step - 2]:
-                copy.wait_recv()
-            ends.append(pass_on(out, source, "far", near))
-    for copy in ends:
-        copy.wait_recv()
-    for copy in started:
-        copy.wait_send()
-    for copy in locals_:
-        copy.wait()
-
-
-def gather_weights(crossed, shards):
-    if not crossed:
-        dp, mp = lax.axis_size("dp"), lax.axis_size("mp")
-        return [lax.all_gather(shard, "mp") for shard in shards]
+    groups = total // 3
+
+    def start_group(number):
+        for chunk in chunks[3 * number : 3 * number + 3]:
+            chunk["level"].start()
+
+    @pl.when(step == 0)
+    def _():
+        barrier = pltpu.get_barrier_semaphore()
+        for target in (side, down, near, *deep):
+            pl.semaphore_signal(barrier, inc=1, device_id=target, device_id_type=MESH)
+
+        @pl.when(dp != level)
+        def _():
+            pl.semaphore_signal(barrier, inc=1, device_id=across, device_id_type=MESH)
+            pl.semaphore_wait(barrier, 7)
+            for copy in crossing[:2]:
+                copy.start()
+
+        @pl.when(dp == level)
+        def _():
+            pl.semaphore_wait(barrier, 6)
+            for copy in staying:
+                copy.start()
+
+        start_group(0)
+        start_group(1)
+        for copy in (*given, *kept):
+            copy.start()
+
+    for number in range(total + 2):
+
+        @pl.when(step == number)
+        def _(number=number):
+            if number < total:
+                chunk = chunks[number]
+                chunk["level"].wait_recv()
+                chunk["side"].start()
+                chunk["down"].start()
+                chunk["here_near"].start()
+                if number % 3 == 2 and number // 3 + 2 < groups:
+                    start_group(number // 3 + 2)
+            if 0 <= number - 1 < total:
+                chunk = chunks[number - 1]
+                chunk["side"].wait_recv()
+                chunk["hop_down"].start()
+                chunk["down"].wait_recv()
+                chunk["hop_side"].start()
+                chunk["side_near"].start()
+                chunk["down_near"].start()
+            if 0 <= number - 2 < total:
+                chunk = chunks[number - 2]
+                chunk["hop_down"].wait_recv()
+                chunk["hop_side"].wait_recv()
+                chunk["far_near"].start()
+
+    @pl.when(step == 1)
+    def _():
+        @pl.when(dp != level)
+        def _():
+            crossing[2].start()
+            crossing[0].wait_recv()
+
+        @pl.when(dp == level)
+        def _():
+            staying[0].wait()
+
+        cells_ref[...] = held_ref[...]
+
+    @pl.when((step >= 1) & (step <= HEADS // 2))
+    def _():
+        embed_pair(step - 1, held_ref[...], keyed_ref, bias_ref, patch_ref, var_ref, x0_ref)
+
+    @pl.when(step == HEADS // 2 + 1)
+    def _():
+        lead = held_ref[0:1, 4 * V + 4 : 4 * V + 5]
+        row = lax.broadcasted_iota(jnp.int32, (1, 8), 1).astype(f32)
+        lead_hot = jnp.where(row == lead, 1.0, 0.0).astype(f32)
+        x0_ref[...] += exact_product(lead_hot, lead_ref[...])
+        unit, _ = normed_parts(x0_ref[...])
+        h1_ref[...] = (unit * gains_ref[0:1, :] + gains_ref[1:2, :]).astype(bf16)
+
+    @pl.when(step == total + 1)
+    def _():
+        for copy in given:
+            copy.wait()
+        for copy in kept:
+            copy.wait()
+        for chunk in chunks:
+            for name in ("here_near", "side_near", "down_near", "far_near"):
+                chunk[name].wait_recv()
+            for copy in chunk.values():
+                copy.wait_send()
+
+        @pl.when(dp != level)
+        def _():
+            crossing[1].wait_recv()
+            crossing[2].wait_recv()
+            for copy in crossing:
+                copy.wait_send()
+
+        @pl.when(dp == level)
+        def _():
+            for copy in staying[1:]:
+                copy.wait()
+
+
+def start_program(packed, qkv, targets, prepared, lead_table, norm_gains, shards, halves):
+    patch, variable, keyed, bias = prepared
     count = len(shards)
-    copies = count * 3 * 9 + count
+    copies = sum(halves) * 27 + count + 3
+    rows, padded = packed.shape
     anywhere = pl.BlockSpec(memory_space=pl.ANY)
+    fixed = lambda shape: pl.BlockSpec(shape, lambda i: (0, 0))
+    by_pair = pl.BlockSpec(
+        (padded, 2 * HEAD_DIM), lambda i: (0, jnp.clip(i - 1, 0, HEADS // 2 - 1))
+    )
     return pl.pallas_call(
-        partial(gather_weights_kernel, count),
-        out_shape=[jax.ShapeDtypeStruct((8,) + shard.shape, bf16) for shard in shards],
-        in_specs=[anywhere] * count,
-        out_specs=[anywhere] * count,
+        partial(start_kernel, halves),
+        grid=(sum(halves) * 3 + 2,),
+        out_shape=[
+            jax.ShapeDtypeStruct((rows, D), f32),
+            jax.ShapeDtypeStruct((rows, D), bf16),
+            jax.ShapeDtypeStruct(packed.shape, f32),
+            jax.ShapeDtypeStruct(qkv.shape, bf16),
+            jax.ShapeDtypeStruct(targets.shape, f32),
+        ]
+        + [jax.ShapeDtypeStruct((8,) + shard.shape, bf16) for shard in shards],
+        in_specs=[anywhere] * 3
+        + [fixed(keyed.shape), fixed(bias.shape), by_pair, by_pair]
+        + [fixed(lead_table.shape), fixed(norm_gains.shape)]
+        + [anywhere] * count,
+        out_specs=[fixed((rows, D)), fixed((rows, D)), fixed(packed.shape)]
+        + [anywhere] * (count + 2),
         scratch_shapes=[
+            pltpu.VMEM(packed.shape, f32),
             pltpu.SemaphoreType.DMA((copies,)),
             pltpu.SemaphoreType.DMA((copies,)),
-            pltpu.SemaphoreType.DMA((count,)),
+            pltpu.SemaphoreType.DMA((count + 3,)),
         ],
         compiler_params=pltpu.CompilerParams(
             collective_id=7, has_side_effects=True, vmem_limit_bytes=BIG
         ),
-        name="gather_weights",
-    )(*shards)
+        name="start_program",
+    )(packed, qkv, targets, keyed, bias, patch, variable, lead_table, norm_gains, *shards)
 
 
 def own_qkv_share(crossed, grad):
@@ -1160,21 +1500,35 @@
         return lax.dynamic_slice_in_dim(full, dp_index * share_rows, share_rows, dim)
 
     masters = (own_share(w_qkv, 0), own_share(w_out, 1), own_share(w_up, 0), own_share(w_down, 1))
-    inputs = cross(crossed, fields[0])
-    leads = cross(crossed, lead_index[0])
-    qkv_local = cross(crossed, by_kind(w_qkv.astype(bf16)))
+    var_hot = (var_ids[:, None] == jnp.arange(V, dtype=jnp.int32)[None, :]).astype(f32)
+    prepared = prepare_tables(tables, var_hot)
     low = lambda master: master.astype(bf16)
-    w_outs, w_ups, w_downs = gather_weights(crossed, (low(w_out), low(w_up), low(w_down)))
-    qkv_rows = 3 * D // (parts * dp_size)
-    qkv_piece = lax.dynamic_slice_in_dim(by_kind(low(w_qkv)).T, dp_index * qkv_rows, qkv_rows, 0)
-    w_outs, qkv_piece = tie(w_outs, qkv_piece)
-    qkv_t = lax.all_gather(qkv_piece, ("mp", "dp"), axis=0, tiled=True)
-    gathered = (w_outs.reshape(D, D), w_ups, w_downs.reshape(-1, D), qkv_t)
-    answers = cross(crossed, targets[0])
-    ocean = 1.0 - cross(crossed, land_mask[0]).astype(f32)
+    qkv_low = by_kind(low(w_qkv))
+    packed = jnp.concatenate(
+        (
+            fields[0],
+            land_mask[0].astype(f32),
+            jnp.broadcast_to(lead_index.astype(f32), (shard_rows, 2)),
+            jnp.zeros((shard_rows, 64 - 6), f32),
+        ),
+        axis=1,
+    )
+    if crossed:
+        x_first, normed, packed, qkv_local, answers, w_outs, w_ups, w_downs, qkv_t = start_program(
+            packed, qkv_low, targets[0], prepared, tables[5 * V : 5 * V + 8], norm_gains,
+            (low(w_out), low(w_up), low(w_down), qkv_low.T), (1, 2, 2, 1),
+        )
+    else:
+        qkv_local, answers = qkv_low, targets[0]
+        w_outs, w_ups, w_downs, qkv_t = [
+            lax.all_gather(shard, "mp")
+            for shard in (low(w_out), low(w_up), low(w_down), qkv_low.T)
+        ]
+    gathered = (w_outs.reshape(D, D), w_ups, w_downs.reshape(-1, D), qkv_t.reshape(3 * D, D))
+    leads = packed[0, 4 * V + 4 : 4 * V + 6].astype(jnp.int32)
+    ocean = 1.0 - packed[:, 4 * V : 4 * V + 4]
     count = sum_everywhere(crossed, jnp.sum(ocean))
     denom = 2.0 * V * jnp.maximum(count, 1.0)
-    var_hot = (var_ids[:, None] == jnp.arange(V, dtype=jnp.int32)[None, :]).astype(f32)
     first_row = part * shard_rows
     patch_row = (first_row + jnp.arange(shard_rows, dtype=jnp.int32)) // PATCH_COLS
     row_hot = (patch_row[:, None] == jnp.arange(PATCH_ROWS, dtype=jnp.int32)[None, :]).astype(f32)
@@ -1187,11 +1541,12 @@
     loss_part = f32(0.0)
     records = []
     for rollout in range(2):
-        lead_hot = (jnp.arange(LEADS, dtype=jnp.int32) == leads[rollout]).astype(f32)
-        x_first, embed_pull = jax.vjp(
-            lambda cells, table: embed_tokens(cells, table, var_hot, lead_hot), inputs, tables
-        )
-        normed = layer_norm(x_first, norm_gains[0], norm_gains[1]).astype(bf16)
+        cells = packed
+        if rollout == 1:
+            cells = jnp.pad(guess, ((0, 0), (0, 64)))
+        if rollout == 1 or not crossed:
+            lead_row = lax.dynamic_slice_in_dim(tables, 5 * V + leads[rollout], 1, 0)
+            x_first, normed = embed_forward(cells, prepared, lead_row, norm_gains)
         rows_one = spread_rows(crossed, normed)
         packed = jnp.dot(rows_one, qkv_local, preferred_element_type=f32).astype(bf16)
         own_out, full, logsum = attend(packed)
@@ -1202,14 +1557,14 @@
         miss = guess - answers[rollout]
         loss_part = loss_part + jnp.sum(weighted * miss * miss)
         records.append(
-            (embed_pull, x_first, rows_one, packed, full, logsum, attended, x_mid, rows_two,
+            (cells, x_first, rows_one, packed, full, logsum, attended, x_mid, rows_two,
              hidden, active, x_last, 2.0 * weighted * miss / denom)
         )
-        inputs = guess
-    carried = jnp.zeros_like(inputs)
-    table_grad = jnp.zeros((5 * V + LEADS + 1, D), f32)
+    carried = jnp.zeros_like(guess)
     head_total = jnp.zeros_like(head)
-    gain_grad = jnp.zeros_like(norm_gains)
+    gain_high = jnp.zeros((4, D), f32)
+    gain_low = jnp.zeros((2, D), f32)
+    table_parts, lead_sums = [], []
     qkv_grad = jnp.zeros((D, qkv_local.shape[1]), f32)
     kept = []
 
@@ -1220,11 +1575,13 @@
         return listed
 
     for rollout in (1, 0):
-        (embed_pull, x_first, rows_one, packed, full, logsum, attended, x_mid, rows_two,
+        (cells, x_first, rows_one, packed, full, logsum, attended, x_mid, rows_two,
          hidden, active, x_last, loss_grad) = records[rollout]
         last_low, hidden_grad, mid_grad, mid_low, out_grad, gain_part, head_grad = branch_backward(
             loss_grad + carried, x_last, x_mid, norm_gains, hidden, gathered, head
         )
+        head_total = head_total + head_grad
+        gain_high = gain_high + gain_part[2:]
         kept.append((attended, rows_two, active, mid_low, hidden_grad, last_low))
         last_turn = crossed and rollout == 0
         if last_turn:
@@ -1255,12 +1612,13 @@
         qkv_grad = qkv_grad + lax.dot_general(
             rows_one, packed_grad, TN, preferred_element_type=f32
         )
-        row_grad, gain_one = entry_backward(token_grad, gathered[3], x_first, mid_grad, norm_gains)
-        gain_part = gain_part + jnp.pad(gain_one, ((0, 4), (0, 0)))
-        carried, embed_tables = embed_pull(row_grad)
-        table_grad = table_grad + embed_tables[: 5 * V + LEADS + 1]
-        head_total = head_total + head_grad
-        gain_grad = gain_grad + gain_part
+        cells_grad, gain_one, lead_sum, *table_part = entry_backward(
+            token_grad, gathered[3], x_first, mid_grad, norm_gains, cells, prepared
+        )
+        carried = cells_grad[:, : 4 * V]
+        gain_low = gain_low + gain_one
+        table_parts.append(table_part)
+        lead_sums.append(lead_sum)
 
     def pair(index):
         return (kept[0][index], kept[1][index])
@@ -1276,10 +1634,14 @@
         out_share = outer_plain(pair(0), pair(3), False)
     shares = (by_head(own_qkv_share(crossed, qkv_grad)), out_share, up_share, down_share)
     share_square = sum(jnp.sum(share * share) for share in shares)
-    head_sum = lax.psum(jnp.concatenate((head_total, gain_grad[2:])), ("dp", "mp"))
-    last_rows = jnp.concatenate((table_grad, gain_grad[:2]))
+    lead_hots = (leads[:, None] == jnp.arange(8, dtype=jnp.int32)[None, :]).astype(f32)
+    lead_hots = jnp.pad(lead_hots, ((0, 6), (0, 0)))
+    lead_rows = jnp.pad(jnp.concatenate((lead_sums[1], lead_sums[0])), ((0, 6), (0, 0)))
+    query = tables[5 * V + LEADS : 5 * V + LEADS + 1]
+    last_rows = table_grads(
+        *table_parts, prepared, query, var_hot, lead_hots, lead_rows, gain_low, head_total, gain_high
+    )
     if crossed:
-        last_rows = jnp.pad(last_rows, ((0, -last_rows.shape[0] % 256), (0, 0)))
         row = jnp.arange(8, dtype=jnp.int32)[:, None]
         tile = jnp.where(row == 0, share_square, jnp.where(row == 1, loss_part, 0.0))
         last_sum, tile_sum = exchange_sum(last_rows, jnp.broadcast_to(tile, (8, 128)))
@@ -1289,10 +1651,10 @@
             (last_rows, loss_part, share_square), ("dp", "mp")
         )
         square_sum = square_sum + jnp.sum(last_sum * last_sum)
-    square_sum = square_sum + jnp.sum(head_sum * head_sum)
+    head_sum = last_sum[256:]
     embed_rows = 5 * V + LEADS + 1
     table_sum = jnp.concatenate((last_sum[:embed_rows], head_sum[: 4 * V]))
-    gain_sum = jnp.concatenate((last_sum[embed_rows : embed_rows + 2], head_sum[4 * V :]))
+    gain_sum = jnp.concatenate((last_sum[embed_rows : embed_rows + 2], head_sum[4 * V : 4 * V + 4]))
     grad_norm = jnp.sqrt(square_sum)
     factor = jnp.minimum(1.0, clip_norm / (grad_norm + 1e-06))
     tab = adam_step(tables, factor * table_sum, tables_first, tables_second, lr_table)

time: 1080 us -> 907 us (0.84)
  Pallas kernels: 572 us -> 694 us
  waiting for transfers between devices: 122 us -> 37.1 us
  matrix products: 88.1 us -> 17.3 us
  local copies, waits for them, and re-layouts: 122 us -> 54.1 us
  other arithmetic: 87.9 us -> 52.3 us
  starting transfers between devices: 50.5 us -> 28.5 us
  between operations: 25.7 us -> 12.2 us
    pallas_call x3 -> x6, Pallas kernels: 174 us -> 285 us  [the longest x1 207 us: start_program(): pl.pallas_call(partial(start_kernel, halves), grid=(sum(halves) * 3 + 2,)...]
    psum x1 -> x0, waiting for transfers between devices: 81.4 us -> none  [shards(): lax.psum(jnp.concatenate((head_total, gain_grad[2:])), ('dp', 'mp'))]
    dot_general x27 -> x0, matrix products: 69.7 us -> none  [the longest x6 30.3 us: embed_tokens(): jnp.einsum('tkh,khc->thc', mixed, patch_tab.reshape(4 * V, HEADS, HEAD_DI...]
    reshape x16 -> x1, local copies, waits for them, and re-layouts: 24.2 us -> 1.17 us  [by_kind(): shard.reshape(rows, -1, 3, HEAD_DIM).transpose(0, 2, 1, 3).reshape(rows, -1)]
    ppermute x6 -> x1, starting transfers between devices: 23.8 us -> 1.64 us  [cross(): return lax.ppermute(value, ('dp', 'mp'), cross_pairs())]
    reduce_sum x13 -> x0, other arithmetic: 19.2 us -> none  [the longest x2 8.19 us: embed_tokens(): shares[:, :, None, :] * pixels[:, :, :, None]]
    pallas_call x1, Pallas kernels: 37.5 us -> 50.8 us  [exchange_sum(): pl.pallas_call(exchange_sum_kernel, out_shape=(jax.ShapeDtypeStruct(value...]
    pallas_call x2, Pallas kernels: 46.6 us -> 35 us  [branch_forward(): pl.pallas_call(branch_kernel, grid=(parts,), out_shape=(jax.ShapeDtypeStr...]
  transfers between devices with their start and end apart: 27 -> 20, of which waited for: 6 -> 5; matrix products, arithmetic and copies ran while one was open for 21% -> 5% of each run, Pallas kernels for 45% -> 12%
where the time goes in v2:
time: 907 us; the launch traced here: 896 us
  Pallas kernels  694 us (77%)
  local copies, waits for them, and re-layouts  54.1 us (6%)
  other arithmetic  52.3 us (6%)
  waiting for transfers between devices  37.1 us (4%)
  starting transfers between devices  28.5 us (3%)
  matrix products  17.3 us (2%)
  between operations  12.2 us (1%)
    pallas_call x1, Pallas kernels, start_program(): pl.pallas_call(partial(start_kernel, halves), grid=(sum(halves) * 3 + 2,)...  207 us
    pallas_call x6, Pallas kernels, exchange(): pl.pallas_call(partial(exchange_kernel, to_columns, rows, width), out_sha...  103 us
    pallas_call x2, Pallas kernels, attend_back(): pl.pallas_call(partial(attend_back_kernel, heads), grid=(total // block,)...  51.4 us
    pallas_call x1, Pallas kernels, exchange_sum(): pl.pallas_call(exchange_sum_kernel, out_shape=(jax.ShapeDtypeStruct(value...  50.8 us
    pallas_call x2, Pallas kernels, entry_backward(): pl.pallas_call(entry_back_kernel, grid=(HEADS // 2,), out_shape=(jax.Shap...  50 us
    pallas_call x2, Pallas kernels, spread_rows(): pl.pallas_call(gather_kernel, out_shape=jax.ShapeDtypeStruct((8 * rows, w...  48.5 us
    pallas_call x2, Pallas kernels, branch_backward(): pl.pallas_call(branch_back_kernel, grid=(parts,), out_shape=(jax.ShapeDty...  39.7 us
    ppermute x19, waiting for transfers between devices, shift(): return lax.ppermute(value, ('dp', 'mp'), device_pairs(move))  37.1 us
  transfers between devices with their start and end apart: 20, of which 5 were waited for; matrix products, arithmetic and copies ran while one was open for 5% of the time, Pallas kernels for 12%

profile of v2, /device:TPU:0, one launch (start us, length us, event | category | flops | bytes accessed | tf_op | source)
XLA Modules:
  0.0 895.7 jit_solution(7285392264511739033)
XLA Ops:
  21.0 207.4 %start_program.1 = (f32[256,1024]{1,0:T(8,128)}, bf16[256,1024]{1,0:T(8,128)(2,1)}, f32[256,256]{1,0:T(8,128)}, bf16[1024,384]{1,0:T(8,128)(2,1)}, f32[2,256,192...) custom-call(f32[256,256]{1,0:T(8,128)} %maximum_maximum_fusion.refs_, ...), custom_call_target="tpu_custom_call" | custom-call | tf_op jit(solution)/shard_map/start_program/pallas_call | solution.py:1426
  228.4 24.7 %gather_rows.2 = bf16[2048,1024]{1,0:T(8,128)(2,1)} custom-call(bf16[256,1024]{1,0:T(8,128)(2,1)} %get-tuple-element.111.x_ref), custom_call_target="tpu_custom_call" | custom-call | tf_op jit(solution)/shard_map/gather_rows/pallas_call | solution.py:153
  259.0 16.4 %attend.2 = (bf16[2048,128]{1,0:T(8,128)(2,1)}, f32[2048,128]{1,0:T(8,128)}, f32[2,2048]{1,0:T(2,128)}) custom-call(bf16[2048,128]{1,0:T(8,128)(2,1)} %get-tuple-element.272.q_ref, bf16[2048,128]{1,0:T(8,128)(2,1)} %get-tuple-element.271.k_ref, bf16[2048,128]{1,0:T(8,128)(2,1)} %get-tuple-element.270.v_ref), custom_call_target="tpu_custom_call" | custom-call | flops 8589934592 | bytes 2621440 | tf_op jit(solution)/shard_map/attend/pallas_call | solution.py:265
  275.4 11.5 %exchange_parts.6.o_ref.refs_6_ = bf16[256,1024]{1,0:T(8,128)(2,1)} custom-call(bf16[2048,128]{1,0:T(8,128)(2,1)} %get-tuple-element.113.x_ref), custom_call_target="tpu_custom_call" | custom-call | tf_op jit(solution)/shard_map/exchange_parts/pallas_call | solution.py:215
  287.0 17.5 %branch_forward.2 = (f32[256,1024]{1,0:T(8,128)}, bf16[256,1024]{1,0:T(8,128)(2,1)}, f32[256,4096]{1,0:T(8,128)}, bf16[256,4096]{1,0:T(8,128)(2,1)}, f32[256,1024]{1,0:T(8,128)}, /*index=5*/f32[256,192]{1,0:T(8,128)}) custom-call(bf16[256,1024]{1,0:T(8,128)(2,1)} %exchange_parts.6.o_ref.refs_6_, f32[256,1024]{1,0:T(8,128)} %get-tuple-element.114.x0_ref, ...), custom_call_target="tpu_custom_call" | custom-call | flops 5435817984 | bytes 23068672 | tf_op jit(solution)/shard_map/branch_forward/pallas_call | solution.py:459
  308.7 15.7 %embed_forward.1 = (f32[256,1024]{1,0:T(8,128)}, bf16[256,1024]{1,0:T(8,128)(2,1)}) custom-call(f32[256,256]{1,0:T(8,128)} %pad.14.u_ref, f32[16,256]{1,0:T(8,128)} %get-tuple-element.107.refs_3_.keyed_ref, f32[16,256]{1,0:T(8,128)} %get-tuple-element.108.refs_4_.bias_ref, f32[256,1024]{1,0:T(8,128)} %get-tuple-element.109.refs_5_.patch_ref, ...), custom_call_target="tpu_custom_call" | custom-call | flops 1610612736 | bytes 3670016 | tf_op jit(solution)/shard_map/embed_forward/pallas_call | solution.py:1053
  324.4 23.8 %gather_rows.3 = bf16[2048,1024]{1,0:T(8,128)(2,1)} custom-call(bf16[256,1024]{1,0:T(8,128)(2,1)} %get-tuple-element.120.x_ref), custom_call_target="tpu_custom_call" | custom-call | tf_op jit(solution)/shard_map/gather_rows/pallas_call | solution.py:153
  353.9 16.4 %attend.3 = (bf16[2048,128]{1,0:T(8,128)(2,1)}, f32[2048,128]{1,0:T(8,128)}, f32[2,2048]{1,0:T(2,128)}) custom-call(bf16[2048,128]{1,0:T(8,128)(2,1)} %get-tuple-element.269.q_ref, bf16[2048,128]{1,0:T(8,128)(2,1)} %get-tuple-element.268.k_ref, bf16[2048,128]{1,0:T(8,128)(2,1)} %get-tuple-element.267.v_ref), custom_call_target="tpu_custom_call" | custom-call | flops 8589934592 | bytes 2621440 | tf_op jit(solution)/shard_map/attend/pallas_call | solution.py:265
  370.3 11.5 %exchange_parts.7.o_ref.refs_4_ = bf16[256,1024]{1,0:T(8,128)(2,1)} custom-call(bf16[2048,128]{1,0:T(8,128)(2,1)} %get-tuple-element.121.x_ref), custom_call_target="tpu_custom_call" | custom-call | tf_op jit(solution)/shard_map/exchange_parts/pallas_call | solution.py:215
  384.9 16.5 %tile_sum.1 = f32[8,128]{1,0:T(8,128)} custom-call(f32[8,128]{1,0:T(8,128)} %broadcast_in_dim.47.t_ref), custom_call_target="tpu_custom_call" | custom-call | tf_op jit(solution)/shard_map/tile_sum/pallas_call | solution.py:927
  403.0 17.5 %branch_forward.3 = (f32[256,1024]{1,0:T(8,128)}, bf16[256,1024]{1,0:T(8,128)(2,1)}, f32[256,4096]{1,0:T(8,128)}, bf16[256,4096]{1,0:T(8,128)(2,1)}, f32[256,1024]{1,0:T(8,128)}, /*index=5*/f32[256,192]{1,0:T(8,128)}) custom-call(bf16[256,1024]{1,0:T(8,128)(2,1)} %exchange_parts.7.o_ref.refs_4_, f32[256,1024]{1,0:T(8,128)} %get-tuple-element.122.x0_ref, ...), custom_call_target="tpu_custom_call" | custom-call | flops 5435817984 | bytes 23068672 | tf_op jit(solution)/shard_map/branch_forward/pallas_call | solution.py:459
  422.8 19.8 %branch_backward.2 = (bf16[256,1024]{1,0:T(8,128)(2,1)}, bf16[256,4096]{1,0:T(8,128)(2,1)}, f32[256,1024]{1,0:T(8,128)}, bf16[256,1024]{1,0:T(8,128)(2,1)}, bf16...) custom-call(f32[256,192]{1,0:T(8,128)} %multiply_divide_fusion.dpred_ref, ...), custom_call_target="tpu_custom_call" | custom-call | flops 6039797760 | bytes 23068672 | tf_op jit(solution)/shard_map/branch_backward/pallas_call | solution.py:551
  442.6 11.5 %exchange_parts.8.do_ref = bf16[2048,128]{1,0:T(8,128)(2,1)} custom-call(bf16[256,1024]{1,0:T(8,128)(2,1)} %get-tuple-element.128.x_ref), custom_call_target="tpu_custom_call" | custom-call | tf_op jit(solution)/shard_map/exchange_parts/pallas_call | solution.py:215
  454.2 25.8 %attend_back.2 = (bf16[2048,128]{1,0:T(8,128)(2,1)}, bf16[2048,128]{1,0:T(8,128)(2,1)}, bf16[2048,128]{1,0:T(8,128)(2,1)}) custom-call(bf16[2048,128]{1,0:T(8,128)(2,1)} %get-tuple-element.269.q_ref, bf16[2048,128]{1,0:T(8,128)(2,1)} %exchange_parts.8.do_ref, f32[2048,128]{1,0:T(8,128)} %get-tuple-element.129.full_ref, ...), custom_call_target="tpu_custom_call" | custom-call | flops 21474836480 | bytes 4194304 | tf_op jit(solution)/shard_map/attend_back/pallas_call | solution.py:356
  483.6 23.5 %exchange_parts.9.grad_ref = bf16[256,3072]{1,0:T(8,128)(2,1)} custom-call(bf16[2048,384]{1,0:T(8,128)(2,1)} %copy-done.10), custom_call_target="tpu_custom_call" | custom-call | tf_op jit(solution)/shard_map/exchange_parts/pallas_call | solution.py:215
  507.2 24.9 %entry_backward.2 = (f32[256,256]{1,0:T(8,128)}, f32[2,1024]{1,0:T(2,128)}, f32[1,1024]{1,0:T(1,128)}, f32[1024,256]{1,0:T(8,128)}, f32[1024,256]{1,0:T(8,128)}, /*index=5*/f32[16,256]{1,0:T(8,128)}, f32[16,256]{1,0:T(8,128)}) custom-call(bf16[256,3072]{1,0:T(8,128)(2,1)} %exchange_parts.9.grad_ref, bf16[3072,1024]{1,0:T(8,128)(2,1)} %bitcast.142, ...), custom_call_target="tpu_custom_call" | custom-call | flops 4026531840 | bytes 10485760 | tf_op jit(solution)/shard_map/entry_backward/pallas_call | solution.py:1136
  535.1 19.9 %branch_backward.3 = (bf16[256,1024]{1,0:T(8,128)(2,1)}, bf16[256,4096]{1,0:T(8,128)(2,1)}, f32[256,1024]{1,0:T(8,128)}, bf16[256,1024]{1,0:T(8,128)(2,1)}, bf16...) custom-call(f32[256,192]{1,0:T(8,128)} %get-tuple-element.273.dpred_ref, ...), custom_call_target="tpu_custom_call" | custom-call | flops 6039797760 | bytes 23068672 | tf_op jit(solution)/shard_map/branch_backward/pallas_call | solution.py:551
  570.3 11.5 %exchange_parts.10.do_ref = bf16[2048,128]{1,0:T(8,128)(2,1)} custom-call(bf16[256,1024]{1,0:T(8,128)(2,1)} %get-tuple-element.152.x_ref), custom_call_target="tpu_custom_call" | custom-call | tf_op jit(solution)/shard_map/exchange_parts/pallas_call | solution.py:215
  622.3 25.6 %attend_back.3 = (bf16[2048,128]{1,0:T(8,128)(2,1)}, bf16[2048,128]{1,0:T(8,128)(2,1)}, bf16[2048,128]{1,0:T(8,128)(2,1)}) custom-call(bf16[2048,128]{1,0:T(8,128)(2,1)} %get-tuple-element.272.q_ref, bf16[2048,128]{1,0:T(8,128)(2,1)} %exchange_parts.10.do_ref, f32[2048,128]{1,0:T(8,128)} %get-tuple-element.160.full_ref, ...), custom_call_target="tpu_custom_call" | custom-call | flops 21474836480 | bytes 4194304 | tf_op jit(solution)/shard_map/attend_back/pallas_call | solution.py:356
  655.8 33.0 %exchange_parts.11.grad_ref = bf16[256,3072]{1,0:T(8,128)(2,1)} custom-call(bf16[2048,384]{1,0:T(8,128)(2,1)} %copy-done.3), custom_call_target="tpu_custom_call" | custom-call | tf_op jit(solution)/shard_map/exchange_parts/pallas_call | solution.py:215
  723.9 25.1 %entry_backward.3 = (f32[256,256]{1,0:T(8,128)}, f32[2,1024]{1,0:T(2,128)}, f32[1,1024]{1,0:T(1,128)}, f32[1024,256]{1,0:T(8,128)}, f32[1024,256]{1,0:T(8,128)}, /*index=5*/f32[16,256]{1,0:T(8,128)}, f32[16,256]{1,0:T(8,128)}) custom-call(bf16[256,3072]{1,0:T(8,128)(2,1)} %exchange_parts.11.grad_ref, bf16[3072,1024]{1,0:T(8,128)(2,1)} %bitcast.143, ...), custom_call_target="tpu_custom_call" | custom-call | flops 4026531840 | bytes 10485760 | tf_op jit(solution)/shard_map/entry_backward/pallas_call | solution.py:1136
  774.4 14.7 %collective-permute-done.18 = bf16[256,512]{1,0:T(8,128)(2,1)S(1)} collective-permute-done((bf16[256,512]{1,0:T(8,128)(2,1)S(1)}, bf16[256,512]{1,0:T(8,128)(2,1)S(1)}, u32[]{:S(2)}, u32[]{:S(2)}) %collective-permute-start.18) | collective-permute-done | bytes 262176 | tf_op jit(solution)/shard_map/ppermute | solution.py:698
  790.9 15.2 %collective-permute-done.13 = bf16[320,512]{1,0:T(8,128)(2,1)S(1)} collective-permute-done((bf16[320,512]{1,0:T(8,128)(2,1)S(1)}, bf16[320,512]{1,0:T(8,128)(2,1)S(1)}, u32[]{:S(2)}, u32[]{:S(2)}) %collective-permute-start.13) | collective-permute-done | bytes 327712 | tf_op jit(solution)/shard_map/ppermute | solution.py:698
  811.1 50.8 %exchange_sum.1 = (f32[512,1024]{1,0:T(8,128)}, f32[8,128]{1,0:T(8,128)}) custom-call(f32[512,1024]{1,0:T(8,128)} %table_grads.1.x_ref, f32[8,128]{1,0:T(8,128)} %broadcast_in_dim.51.t_ref), custom_call_target="tpu_custom_call" | custom-call | tf_op jit(solution)/shard_map/exchange_sum/pallas_call | solution.py:865
  (265 shorter events, 203.2 us)
Async XLA Ops:
  569.8 34.7 %collective-permute-start.1 = (bf16[4,4,320,512]{3,2,1,0:T(8,128)(2,1)}, bf16[4,4,320,512]{3,2,1,0:T(8,128)(2,1)}, u32[]{:S(2)}, u32[]{:S(2)}) collective-permute-start(bf16[4,4,320,512]{3,2,1,0:T(8,128)(2,1)} %outer_other.3), channel_id=1, source_target_pairs={{0,1},{1,0},{2,3},{3,2},{4,5},{5,4},{6,7},{7,6},{8,9},{9,8},{10,11... | collective-permute-start | bytes 15728648 | tf_op jit(solution)/shard_map/ppermute | solution.py:698
  569.8 27.0 %collective-permute-start = (bf16[4,4,256,512]{3,2,1,0:T(8,128)(2,1)}, bf16[4,4,256,512]{3,2,1,0:T(8,128)(2,1)}, u32[]{:S(2)}, u32[]{:S(2)}) collective-permute-start(bf16[4,4,256,512]{3,2,1,0:T(8,128)(2,1)} %outer_other.2), channel_id=1, source_target_pairs={{0,1},{1,0},{2,3},{3,2},{4,5},{5,4},{6,7},{7,6},{8,9},{9,8},{10,11... | collective-permute-start | bytes 12582920 | tf_op jit(solution)/shard_map/ppermute | solution.py:698
  616.9 32.7 %collective-permute-start.3 = (bf16[2,2,256,512]{3,2,1,0:T(8,128)(2,1)S(1)}, bf16[2,2,256,512]{3,2,1,0:T(8,128)(2,1)S(1)}, u32[]{:S(2)}, u32[]{:S(2)}) collective-permute-start(bf16[2,2,256,512]{3,2,1,0:T(8,128)(2,1)S(1)} %slice.142), channel_id=1, source_target_pairs={{0,16},{1,17},{2,18},{3,19},{4,20},{5,21},{6,22},{7,23},{8,24},{9,... | collective-permute-start | bytes 3145736 | tf_op jit(solution)/shard_map/ppermute | solution.py:698
  618.3 33.0 %collective-permute-start.2 = (bf16[2,2,256,512]{3,2,0,1:T(8,128)(2,1)S(1)}, bf16[2,2,256,512]{3,2,0,1:T(8,128)(2,1)S(1)}, u32[]{:S(2)}, u32[]{:S(2)}) collective-permute-start(bf16[2,2,256,512]{3,2,0,1:T(8,128)(2,1)S(1)} %slice.168), channel_id=1, source_target_pairs={{0,8},{1,9},{2,10},{3,11},{4,12},{5,13},{6,14},{7,15},{8,0},{9,1},... | collective-permute-start | bytes 3145736 | tf_op jit(solution)/shard_map/ppermute | solution.py:698
  618.9 91.1 %collective-permute-start.5 = (bf16[2,2,320,512]{3,2,1,0:T(8,128)(2,1)}, bf16[2,2,320,512]{3,2,1,0:T(8,128)(2,1)}, u32[]{:S(2)}, u32[]{:S(2)}) collective-permute-start(bf16[2,2,320,512]{3,2,1,0:T(8,128)(2,1)} %slice.146), channel_id=1, source_target_pairs={{0,16},{1,17},{2,18},{3,19},{4,20},{5,21},{6,22},{7,23},{8,24},{9,... | collective-permute-start | bytes 3932168 | tf_op jit(solution)/shard_map/ppermute | solution.py:698
  620.9 90.9 %collective-permute-start.4 = (bf16[2,2,320,512]{3,2,0,1:T(8,128)(2,1)}, bf16[2,2,320,512]{3,2,0,1:T(8,128)(2,1)}, u32[]{:S(2)}, u32[]{:S(2)}) collective-permute-start(bf16[2,2,320,512]{3,2,0,1:T(8,128)(2,1)} %slice.170), channel_id=1, source_target_pairs={{0,8},{1,9},{2,10},{3,11},{4,12},{5,13},{6,14},{7,15},{8,0},{9,1},... | collective-permute-start | bytes 3932168 | tf_op jit(solution)/shard_map/ppermute | solution.py:698
  655.8 33.1 %copy-start.30 = (f32[1024,384]{1,0:T(8,128)}, f32[1024,384]{1,0:T(8,128)S(1)}, u32[]{:S(2)}) copy-start(f32[1024,384]{1,0:T(8,128)S(1)} %convolution_add_fusion) | copy-start | bytes 4718596
  689.8 10.5 %collective-permute-start.6 = (bf16[256,384]{0,1:T(8,128)(2,1)}, bf16[256,384]{0,1:T(8,128)(2,1)}, u32[]{:S(2)}, u32[]{:S(2)}) collective-permute-start(bf16[256,384]{0,1:T(8,128)(2,1)} %bitcast.141), channel_id=1, source_target_pairs={{0,2},{1,3},{2,4},{3,5},{4,6},{5,7},{6,0},{7,1},{8,10},{9,11},{10,... | collective-permute-start | bytes 589832 | tf_op jit(solution)/shard_map/ppermute | solution.py:698
  691.2 14.0 %collective-permute-start.7 = (bf16[256,384]{0,1:T(8,128)(2,1)}, bf16[256,384]{0,1:T(8,128)(2,1)}, u32[]{:S(2)}, u32[]{:S(2)}) collective-permute-start(bf16[256,384]{0,1:T(8,128)(2,1)} %bitcast.112), channel_id=1, source_target_pairs={{0,4},{1,5},{2,6},{3,7},{4,0},{5,1},{6,2},{7,3},{8,12},{9,13},{10,... | collective-permute-start | bytes 589832 | tf_op jit(solution)/shard_map/ppermute | solution.py:698
  693.8 12.6 %collective-permute-start.8 = (bf16[256,384]{0,1:T(8,128)(2,1)S(1)}, bf16[256,384]{0,1:T(8,128)(2,1)}, u32[]{:S(2)}, u32[]{:S(2)}) collective-permute-start(bf16[256,384]{0,1:T(8,128)(2,1)S(1)} %bitcast.140), channel_id=1, source_target_pairs={{0,6},{1,7},{2,0},{3,1},{4,2},{5,3},{6,4},{7,5},{8,14},{9,15},{10,... | collective-permute-start | bytes 589832 | tf_op jit(solution)/shard_map/ppermute | solution.py:698
  700.3 58.5 %collective-permute-start.16 = (bf16[2,256,512]{2,1,0:T(8,128)(2,1)S(1)}, bf16[2,256,512]{2,1,0:T(8,128)(2,1)}, u32[]{:S(2)}, u32[]{:S(2)}) collective-permute-start(bf16[2,256,512]{2,1,0:T(8,128)(2,1)S(1)} %dynamic-slice_bitcast_fusion.2), channel_id=1, source_target_pairs={{0,8},{1,9},{2,10},{3,11},{4,12},{5,13},{6,14},{7,15},{8,0},{9,1},... | collective-permute-start | bytes 1572872 | tf_op jit(solution)/shard_map/ppermute | solution.py:698
  705.2 54.9 %collective-permute-start.15 = (bf16[2,256,512]{2,1,0:T(8,128)(2,1)}, bf16[2,256,512]{2,1,0:T(8,128)(2,1)}, u32[]{:S(2)}, u32[]{:S(2)}) collective-permute-start(bf16[2,256,512]{2,1,0:T(8,128)(2,1)} %dynamic-slice_bitcast_fusion.3), channel_id=1, source_target_pairs={{0,16},{1,17},{2,18},{3,19},{4,20},{5,21},{6,22},{7,23},{8,24},{9,... | collective-permute-start | bytes 1572872 | tf_op jit(solution)/shard_map/ppermute | solution.py:698
  708.4 53.3 %collective-permute-start.9 = (f32[256,384]{0,1:T(8,128)}, f32[256,384]{0,1:T(8,128)S(1)}, u32[]{:S(2)}, u32[]{:S(2)}) collective-permute-start(f32[256,384]{0,1:T(8,128)} %fusion.28), channel_id=1, source_target_pairs={{0,0},{1,1},{2,8},{3,9},{4,16},{5,17},{6,24},{7,25},{8,2},{9,3},{1... | collective-permute-start | bytes 1179656 | tf_op jit(solution)/shard_map/ppermute | solution.py:85
  714.3 51.9 %collective-permute-start.11 = (bf16[2,320,512]{2,1,0:T(8,128)(2,1)}, bf16[2,320,512]{2,1,0:T(8,128)(2,1)}, u32[]{:S(2)}, u32[]{:S(2)}) collective-permute-start(bf16[2,320,512]{2,1,0:T(8,128)(2,1)} %dynamic-slice_bitcast_fusion), channel_id=1, source_target_pairs={{0,8},{1,9},{2,10},{3,11},{4,12},{5,13},{6,14},{7,15},{8,0},{9,1},... | collective-permute-start | bytes 1966088 | tf_op jit(solution)/shard_map/ppermute | solution.py:698
  720.4 47.1 %collective-permute-start.10 = (bf16[2,320,512]{2,1,0:T(8,128)(2,1)}, bf16[2,320,512]{2,1,0:T(8,128)(2,1)}, u32[]{:S(2)}, u32[]{:S(2)}) collective-permute-start(bf16[2,320,512]{2,1,0:T(8,128)(2,1)} %dynamic-slice_bitcast_fusion.1), channel_id=1, source_target_pairs={{0,16},{1,17},{2,18},{3,19},{4,20},{5,21},{6,22},{7,23},{8,24},{9,... | collective-permute-start | bytes 1966088 | tf_op jit(solution)/shard_map/ppermute | solution.py:698
  723.8 25.1 %copy-start.48 = (f32[2,1024]{1,0:T(2,128)S(1)}, f32[2,1024]{1,0:T(2,128)}, u32[]{:S(2)}) copy-start(f32[2,1024]{1,0:T(2,128)} %get-tuple-element.181) | copy-start | bytes 24580
  723.8 26.4 %copy-start.50 = (f32[1,1024]{1,0:T(1,128)S(1)}, f32[1,1024]{1,0:T(1,128)}, u32[]{:S(2)}) copy-start(f32[1,1024]{1,0:T(1,128)} %get-tuple-element.180) | copy-start | bytes 12292
  761.5 11.2 %collective-permute-start.17 = (bf16[256,512]{1,0:T(8,128)(2,1)S(1)}, bf16[256,512]{1,0:T(8,128)(2,1)S(1)}, u32[]{:S(2)}, u32[]{:S(2)}) collective-permute-start(bf16[256,512]{1,0:T(8,128)(2,1)S(1)} %get-tuple-element.259), channel_id=1, source_target_pairs={{0,2},{1,3},{2,4},{3,5},{4,6},{5,7},{6,0},{7,1},{8,10},{9,11},{10,... | collective-permute-start | bytes 786440 | tf_op jit(solution)/shard_map/ppermute | solution.py:698
  761.6 27.5 %collective-permute-start.18 = (bf16[256,512]{1,0:T(8,128)(2,1)S(1)}, bf16[256,512]{1,0:T(8,128)(2,1)S(1)}, u32[]{:S(2)}, u32[]{:S(2)}) collective-permute-start(bf16[256,512]{1,0:T(8,128)(2,1)S(1)} %get-tuple-element.260), channel_id=1, source_target_pairs={{0,4},{1,5},{2,6},{3,7},{4,0},{5,1},{6,2},{7,3},{8,12},{9,13},{10,... | collective-permute-start | bytes 786440 | tf_op jit(solution)/shard_map/ppermute | solution.py:698
  761.7 27.4 %collective-permute-start.19 = (bf16[256,512]{1,0:T(8,128)(2,1)S(1)}, bf16[256,512]{1,0:T(8,128)(2,1)S(1)}, u32[]{:S(2)}, u32[]{:S(2)}) collective-permute-start(bf16[256,512]{1,0:T(8,128)(2,1)S(1)} %get-tuple-element.261), channel_id=1, source_target_pairs={{0,6},{1,7},{2,0},{3,1},{4,2},{5,3},{6,4},{7,5},{8,14},{9,15},{10,... | collective-permute-start | bytes 786440 | tf_op jit(solution)/shard_map/ppermute | solution.py:698
  769.1 21.8 %collective-permute-start.12 = (bf16[320,512]{1,0:T(8,128)(2,1)S(1)}, bf16[320,512]{1,0:T(8,128)(2,1)S(1)}, u32[]{:S(2)}, u32[]{:S(2)}) collective-permute-start(bf16[320,512]{1,0:T(8,128)(2,1)S(1)} %get-tuple-element.256), channel_id=1, source_target_pairs={{0,2},{1,3},{2,4},{3,5},{4,6},{5,7},{6,0},{7,1},{8,10},{9,11},{10,... | collective-permute-start | bytes 983048 | tf_op jit(solution)/shard_map/ppermute | solution.py:698
  769.7 36.4 %collective-permute-start.13 = (bf16[320,512]{1,0:T(8,128)(2,1)S(1)}, bf16[320,512]{1,0:T(8,128)(2,1)S(1)}, u32[]{:S(2)}, u32[]{:S(2)}) collective-permute-start(bf16[320,512]{1,0:T(8,128)(2,1)S(1)} %get-tuple-element.257), channel_id=1, source_target_pairs={{0,4},{1,5},{2,6},{3,7},{4,0},{5,1},{6,2},{7,3},{8,12},{9,13},{10,... | collective-permute-start | bytes 983048 | tf_op jit(solution)/shard_map/ppermute | solution.py:698
  772.7 33.5 %collective-permute-start.14 = (bf16[320,512]{1,0:T(8,128)(2,1)S(1)}, bf16[320,512]{1,0:T(8,128)(2,1)S(1)}, u32[]{:S(2)}, u32[]{:S(2)}) collective-permute-start(bf16[320,512]{1,0:T(8,128)(2,1)S(1)} %get-tuple-element.258), channel_id=1, source_target_pairs={{0,6},{1,7},{2,0},{3,1},{4,2},{5,3},{6,4},{7,5},{8,14},{9,15},{10,... | collective-permute-start | bytes 983048 | tf_op jit(solution)/shard_map/ppermute | solution.py:698
  806.4 56.2 %copy-start.31 = (f32[64,256]{1,0:T(8,128)}, f32[64,256]{1,0:T(8,128)S(1)}, u32[]{:S(2)}) copy-start(f32[64,256]{1,0:T(8,128)S(1)} %get-tuple-element.275) | copy-start | bytes 196612
  (50 other events, 402.3 us)

commit v3 on v2

--- a/solution.py
+++ b/solution.py
@@ -232,14 +232,10 @@
     return jnp.where(lane == head, value, jnp.zeros_like(value))
 
 
-def attend_kernel(heads, q_ref, k_ref, v_ref, o_ref, full_ref, lse_ref, vt_ref):
-    @pl.when(pl.program_id(0) == 0)
-    def _():
-        vt_ref[...] = v_ref[...].T
-
-    queries = q_ref[...] * bf16(HEAD_DIM**-0.5)
+def attend_rows(heads, queries, k_ref, vt_ref):
+    queries = queries * bf16(HEAD_DIM**-0.5)
     keys = k_ref[...]
-    outs = []
+    outs, sums = [], []
     for head in range(heads):
         scores = lax.dot_general(
             keys, pick_head(queries, head, heads), NT, preferred_element_type=f32
@@ -250,9 +246,19 @@
         probs = (raised * (1.0 / total)).astype(bf16)
         values = vt_ref[head * HEAD_DIM : (head + 1) * HEAD_DIM, :]
         outs.append(jnp.dot(values, probs, preferred_element_type=f32))
-        lse_ref[head : head + 1, :] = largest + jnp.log(total)
+        sums.append(largest + jnp.log(total))
     flipped = outs[0] if heads == 1 else jnp.concatenate(outs, axis=0)
-    full = flipped.T
+    return flipped.T, sums
+
+
+def attend_kernel(heads, q_ref, k_ref, v_ref, o_ref, full_ref, lse_ref, vt_ref):
+    @pl.when(pl.program_id(0) == 0)
+    def _():
+        vt_ref[...] = v_ref[...].T
+
+    full, sums = attend_rows(heads, q_ref[...], k_ref, vt_ref)
+    for head in range(heads):
+        lse_ref[head : head + 1, :] = sums[head]
     full_ref[...] = full
     o_ref[...] = full.astype(bf16)
 
@@ -1231,13 +1237,18 @@
     return shard.reshape(rows, 3, -1, HEAD_DIM).transpose(0, 2, 1, 3).reshape(rows, -1)
 
 
+lag_one, lag_two, ahead = 2, 4, 3
+embed_at, gather_at, project_at, attend_at = 3, 11, 14, 18
+
+
 def start_kernel(halves, *refs):
     count = len(halves)
-    packed_ref, qkv_ref, targets_ref, keyed_ref, bias_ref, patch_ref, var_ref, lead_ref, gains_ref = refs[:9]
-    shards = refs[9 : 9 + count]
-    x0_ref, h1_ref, cells_ref, qkv_out, targets_out = refs[9 + count : 14 + count]
+    packed_ref, keyed_ref, bias_ref, patch_ref, var_ref, lead_ref, gains_ref = refs[:7]
+    shards = refs[7 : 7 + count]
+    x0_ref, cells_ref, qkv_ref, o_ref, full_ref, lse_ref, rows_out = refs[7 + count : 14 + count]
     outs = refs[14 + count : 14 + 2 * count]
-    held_ref, send_sem, recv_sem, own_sem = refs[14 + 2 * count :]
+    (held_ref, h1_ref, rows_ref, weight_ref, vt_ref, send_sem, recv_sem,
+     level_send, level_recv, own_sem) = refs[14 + 2 * count :]
     step = pl.program_id(0)
     dp, level, core = mesh_place()
     x = lax.rem(dp, 2)
@@ -1246,7 +1257,10 @@
     down = device_of(columns["down"], level, core)
     near = device_of(dp, level, 1 - core)
     across = device_of(level, dp, core)
-    deep = [device_of(dp, lax.rem(level + move, 4), core) for move in (1, 2, 3)]
+    middle = lax.rem(level, 3) != 0
+    late = level // 2
+    sources = (level + 1 - 2 * lax.rem(level, 2), 2 - late, 3 * (1 - late))
+    onward = (3 - level, lax.rem(3 * level + 1, 4), lax.rem(3 * level + 1, 4))
     slots = [0]
 
     def remote(source, target_ref, target):
@@ -1271,30 +1285,44 @@
         where = place(out, source, column, *cut)
         return remote(where, where, target)
 
-    moves = [(packed_ref, held_ref), (qkv_ref, qkv_out), (targets_ref, targets_out)]
-    crossing = [remote(source, target_ref, across) for source, target_ref in moves]
-    staying = [
-        pltpu.make_async_copy(source, target_ref, own_sem.at[count + index])
-        for index, (source, target_ref) in enumerate(moves)
-    ]
+    crossing = remote(packed_ref, held_ref, across)
+    staying = pltpu.make_async_copy(packed_ref, held_ref, own_sem.at[count])
     mine = [outs[index].at[level * 2 + core] for index in range(count)]
     given = [remote(shards[index], mine[index], near) for index in range(count)]
     kept = [
         pltpu.make_async_copy(shards[index], mine[index], own_sem.at[index]) for index in range(count)
     ]
-    chunks = []
+    chunks, openings = [], []
     for index in range(count):
         out, pieces = outs[index], halves[index]
         for half in range(pieces):
+            group = len(openings)
             full = out.shape[1] // 4
             size = full // pieces
             own = shards[index].at[pl.ds(pl.multiple_of(dp * full + half * size, size), size), :]
             cut = (half, pieces)
-            for move in (1, 2, 3):
-                source = lax.rem(level + 4 - move, 4)
+
+            def along(source_ref, source, target_level, slot):
+                return pltpu.make_async_remote_copy(
+                    src_ref=source_ref,
+                    dst_ref=place(out, source, "here", *cut),
+                    send_sem=level_send.at[group * 5 + slot],
+                    recv_sem=level_recv.at[group * 4 + source],
+                    device_id=device_of(dp, target_level, core),
+                    device_id_type=MESH,
+                )
+
+            openings.append(
+                (
+                    along(own, level, lax.rem(level + 1, 4), 0),
+                    along(own, level, lax.rem(level + 3, 4), 1),
+                )
+            )
+            for turn in range(3):
+                source = sources[turn]
                 chunks.append(
                     {
-                        "level": remote(own, place(out, level, "here", *cut), deep[move - 1]),
+                        "level": along(place(out, source, "here", *cut), source, onward[turn], 2 + turn),
                         "side": pass_on(out, source, "here", side, cut),
                         "down": pass_on(out, source, "here", down, cut),
                         "hop_down": pass_on(out, source, "side", down, (2 * half, 2 * pieces)),
@@ -1305,16 +1333,52 @@
                         "far_near": pass_on(out, source, "far", near, cut),
                     }
                 )
+    groups = len(openings)
+    order = []
+    for number in range(groups + 2):
+        for turn in range(3):
+            if 0 <= number - turn < groups:
+                order.append((number - turn, turn))
+    chunks = [chunks[3 * group + turn] for group, turn in order]
     total = len(chunks)
-    groups = total // 3
 
     def start_group(number):
-        for chunk in chunks[3 * number : 3 * number + 3]:
-            chunk["level"].start()
+        @pl.when(level < 3)
+        def _():
+            openings[number][0].start()
+
+        @pl.when(level > 0)
+        def _():
+            openings[number][1].start()
+
+    rows = h1_ref.shape[0]
+    cut = rows // 2
+
+    def rows_of(owner, who, first, size):
+        return rows_ref.at[pl.ds(pl.multiple_of((owner * 2 + who) * rows + first, cut), size)]
+
+    def relay(place_ref, target):
+        return remote(place_ref, place_ref, target)
+
+    first_half, second_half = h1_ref.at[pl.ds(0, cut)], h1_ref.at[pl.ds(cut, cut)]
+    beside, below, far = columns["side"], columns["down"], columns["far"]
+    side_a = remote(first_half, rows_of(dp, core, 0, cut), side)
+    down_b = remote(second_half, rows_of(dp, core, cut, cut), down)
+    side_b = remote(second_half, rows_of(dp, core, cut, cut), side)
+    down_a = remote(first_half, rows_of(dp, core, 0, cut), down)
+    near_own = remote(h1_ref, rows_of(dp, core, 0, rows), near)
+    far_a = relay(rows_of(beside, core, 0, cut), down)
+    far_b = relay(rows_of(below, core, cut, cut), side)
+    near_side = relay(rows_of(beside, core, 0, rows), near)
+    near_down = relay(rows_of(below, core, 0, rows), near)
+    near_far = relay(rows_of(far, core, 0, rows), near)
+    weight = pltpu.make_async_copy(outs[0].at[dp * 2 + core], weight_ref, own_sem.at[count + 1])
+    save = pltpu.make_async_copy(rows_ref, rows_out, own_sem.at[count + 2])
 
     @pl.when(step == 0)
     def _():
         barrier = pltpu.get_barrier_semaphore()
+        deep = [device_of(dp, lax.rem(level + move, 4), core) for move in (1, 2, 3)]
         for target in (side, down, near, *deep):
             pl.semaphore_signal(barrier, inc=1, device_id=target, device_id_type=MESH)
 
@@ -1322,64 +1386,67 @@
         def _():
             pl.semaphore_signal(barrier, inc=1, device_id=across, device_id_type=MESH)
             pl.semaphore_wait(barrier, 7)
-            for copy in crossing[:2]:
-                copy.start()
+            crossing.start()
 
         @pl.when(dp == level)
         def _():
             pl.semaphore_wait(barrier, 6)
-            for copy in staying:
-                copy.start()
-
-        start_group(0)
-        start_group(1)
+            staying.start()
+
+        for number in range(ahead):
+            start_group(number)
         for copy in (*given, *kept):
             copy.start()
 
-    for number in range(total + 2):
+    for number in range(total + lag_two):
 
         @pl.when(step == number)
         def _(number=number):
             if number < total:
                 chunk = chunks[number]
                 chunk["level"].wait_recv()
+
+                @pl.when(middle)
+                def _():
+                    chunk["level"].start()
+
                 chunk["side"].start()
                 chunk["down"].start()
                 chunk["here_near"].start()
-                if number % 3 == 2 and number // 3 + 2 < groups:
-                    start_group(number // 3 + 2)
-            if 0 <= number - 1 < total:
-                chunk = chunks[number - 1]
+                group, turn = order[number]
+                if turn == 0 and group + ahead < groups:
+                    start_group(group + ahead)
+            if 0 <= number - lag_one < total:
+                chunk = chunks[number - lag_one]
                 chunk["side"].wait_recv()
                 chunk["hop_down"].start()
                 chunk["down"].wait_recv()
                 chunk["hop_side"].start()
                 chunk["side_near"].start()
                 chunk["down_near"].start()
-            if 0 <= number - 2 < total:
-                chunk = chunks[number - 2]
+            if 0 <= number - lag_two < total:
+                chunk = chunks[number - lag_two]
                 chunk["hop_down"].wait_recv()
                 chunk["hop_side"].wait_recv()
                 chunk["far_near"].start()
 
-    @pl.when(step == 1)
+    @pl.when(step == embed_at)
     def _():
         @pl.when(dp != level)
         def _():
-            crossing[2].start()
-            crossing[0].wait_recv()
+            crossing.wait_recv()
 
         @pl.when(dp == level)
         def _():
-            staying[0].wait()
+            staying.wait()
 
         cells_ref[...] = held_ref[...]
 
-    @pl.when((step >= 1) & (step <= HEADS // 2))
+    @pl.when((step >= embed_at) & (step < embed_at + HEADS // 2))
     def _():
-        embed_pair(step - 1, held_ref[...], keyed_ref, bias_ref, patch_ref, var_ref, x0_ref)
-
-    @pl.when(step == HEADS // 2 + 1)
+        embed_pair(step - embed_at, held_ref[...], keyed_ref, bias_ref, patch_ref, var_ref, x0_ref)
+
+    @pl.when(step == gather_at)
     def _():
         lead = held_ref[0:1, 4 * V + 4 : 4 * V + 5]
         row = lax.broadcasted_iota(jnp.int32, (1, 8), 1).astype(f32)
@@ -1387,70 +1454,150 @@
         x0_ref[...] += exact_product(lead_hot, lead_ref[...])
         unit, _ = normed_parts(x0_ref[...])
         h1_ref[...] = (unit * gains_ref[0:1, :] + gains_ref[1:2, :]).astype(bf16)
-
-    @pl.when(step == total + 1)
+        for copy in (side_a, down_b, side_b, down_a, near_own):
+            copy.start()
+        rows_of(dp, core, 0, rows)[...] = h1_ref[...]
+        kept[0].wait()
+        weight.start()
+
+    @pl.when(step == gather_at + 1)
+    def _():
+        side_a.wait_recv()
+        far_a.start()
+        down_b.wait_recv()
+        far_b.start()
+        side_b.wait_recv()
+        near_side.start()
+        down_a.wait_recv()
+        near_down.start()
+
+    @pl.when(step == gather_at + 2)
+    def _():
+        far_a.wait_recv()
+        far_b.wait_recv()
+        near_far.start()
+        for copy in (near_own, near_side, near_down):
+            copy.wait_recv()
+
+    block = rows_ref.shape[0] // 4
+
+    @pl.when(step == project_at)
+    def _():
+        near_far.wait_recv()
+        save.start()
+        weight.wait()
+
+    @pl.when((step >= project_at) & (step < project_at + 4))
+    def _():
+        where = pl.ds(pl.multiple_of((step - project_at) * block, block), block)
+        qkv_ref[where, :] = lax.dot_general(
+            rows_ref[where, :], weight_ref[...], NT, preferred_element_type=f32
+        ).astype(bf16)
+
+    width = o_ref.shape[1]
+    heads = width // HEAD_DIM
+
+    @pl.when(step == attend_at)
+    def _():
+        vt_ref[...] = qkv_ref[:, 2 * width :].T
+
+    @pl.when((step >= attend_at) & (step < attend_at + 4))
+    def _():
+        where = pl.ds(pl.multiple_of((step - attend_at) * block, block), block)
+        full, sums = attend_rows(
+            heads, qkv_ref[where, :width], qkv_ref.at[:, width : 2 * width], vt_ref
+        )
+        for head in range(heads):
+            lse_ref[head : head + 1, where] = sums[head]
+        full_ref[where, :] = full
+        o_ref[where, :] = full.astype(bf16)
+
+    @pl.when(step == total + lag_two - 1)
     def _():
         for copy in given:
             copy.wait()
-        for copy in kept:
+        for copy in kept[1:]:
             copy.wait()
+        for number in range(groups):
+
+            @pl.when(level < 3)
+            def _(number=number):
+                openings[number][0].wait_send()
+
+            @pl.when(level > 0)
+            def _(number=number):
+                openings[number][1].wait_send()
+
         for chunk in chunks:
             for name in ("here_near", "side_near", "down_near", "far_near"):
                 chunk[name].wait_recv()
-            for copy in chunk.values():
-                copy.wait_send()
+            for name, copy in chunk.items():
+                if name != "level":
+                    copy.wait_send()
+
+            @pl.when(middle)
+            def _(chunk=chunk):
+                chunk["level"].wait_send()
+
+        for copy in (side_a, down_b, side_b, down_a, near_own, far_a, far_b, near_side, near_down, near_far):
+            copy.wait_send()
+        save.wait()
 
         @pl.when(dp != level)
         def _():
-            crossing[1].wait_recv()
-            crossing[2].wait_recv()
-            for copy in crossing:
-                copy.wait_send()
-
-        @pl.when(dp == level)
-        def _():
-            for copy in staying[1:]:
-                copy.wait()
-
-
-def start_program(packed, qkv, targets, prepared, lead_table, norm_gains, shards, halves):
+            crossing.wait_send()
+
+
+def start_program(packed, prepared, lead_table, norm_gains, shards, halves):
     patch, variable, keyed, bias = prepared
     count = len(shards)
-    copies = sum(halves) * 27 + count + 3
+    groups = sum(halves)
+    copies = groups * 24 + count + 11
     rows, padded = packed.shape
+    total = 8 * rows
+    width = shards[0].shape[0] // 3
+    heads = width // HEAD_DIM
     anywhere = pl.BlockSpec(memory_space=pl.ANY)
     fixed = lambda shape: pl.BlockSpec(shape, lambda i: (0, 0))
     by_pair = pl.BlockSpec(
-        (padded, 2 * HEAD_DIM), lambda i: (0, jnp.clip(i - 1, 0, HEADS // 2 - 1))
+        (padded, 2 * HEAD_DIM), lambda i: (0, jnp.clip(i - embed_at, 0, HEADS // 2 - 1))
     )
+    shapes = [
+        ((rows, D), f32),
+        (packed.shape, f32),
+        ((total, 3 * width), bf16),
+        ((total, width), bf16),
+        ((total, width), f32),
+        ((heads, total), f32),
+    ]
     return pl.pallas_call(
         partial(start_kernel, halves),
-        grid=(sum(halves) * 3 + 2,),
-        out_shape=[
-            jax.ShapeDtypeStruct((rows, D), f32),
-            jax.ShapeDtypeStruct((rows, D), bf16),
-            jax.ShapeDtypeStruct(packed.shape, f32),
-            jax.ShapeDtypeStruct(qkv.shape, bf16),
-            jax.ShapeDtypeStruct(targets.shape, f32),
-        ]
+        grid=(groups * 3 + lag_two,),
+        out_shape=[jax.ShapeDtypeStruct(shape, kind) for shape, kind in shapes]
+        + [jax.ShapeDtypeStruct((total, D), bf16)]
         + [jax.ShapeDtypeStruct((8,) + shard.shape, bf16) for shard in shards],
-        in_specs=[anywhere] * 3
+        in_specs=[anywhere]
         + [fixed(keyed.shape), fixed(bias.shape), by_pair, by_pair]
         + [fixed(lead_table.shape), fixed(norm_gains.shape)]
-        + [anywhere] * count,
-        out_specs=[fixed((rows, D)), fixed((rows, D)), fixed(packed.shape)]
-        + [anywhere] * (count + 2),
+        + [fixed(shard.shape) for shard in shards],
+        out_specs=[fixed(shape) for shape, _ in shapes] + [anywhere] * (count + 1),
         scratch_shapes=[
             pltpu.VMEM(packed.shape, f32),
+            pltpu.VMEM((rows, D), bf16),
+            pltpu.VMEM((total, D), bf16),
+            pltpu.VMEM(shards[0].shape, bf16),
+            pltpu.VMEM((width, total), bf16),
             pltpu.SemaphoreType.DMA((copies,)),
             pltpu.SemaphoreType.DMA((copies,)),
+            pltpu.SemaphoreType.DMA((groups * 5,)),
+            pltpu.SemaphoreType.DMA((groups * 4,)),
             pltpu.SemaphoreType.DMA((count + 3,)),
         ],
         compiler_params=pltpu.CompilerParams(
             collective_id=7, has_side_effects=True, vmem_limit_bytes=BIG
         ),
         name="start_program",
-    )(packed, qkv, targets, keyed, bias, patch, variable, lead_table, norm_gains, *shards)
+    )(packed, keyed, bias, patch, variable, lead_table, norm_gains, *shards)
 
 
 def own_qkv_share(crossed, grad):
@@ -1514,19 +1661,25 @@
         axis=1,
     )
     if crossed:
-        x_first, normed, packed, qkv_local, answers, w_outs, w_ups, w_downs, qkv_t = start_program(
-            packed, qkv_low, targets[0], prepared, tables[5 * V : 5 * V + 8], norm_gains,
-            (low(w_out), low(w_up), low(w_down), qkv_low.T), (1, 2, 2, 1),
+        (
+            x_first, cells, packed, own_out, full, logsum, rows_one, qkv_t, w_outs, w_ups, w_downs
+        ) = start_program(
+            packed, prepared, tables[5 * V : 5 * V + 8], norm_gains,
+            (qkv_low.T, low(w_out), low(w_up), low(w_down)), (1, 1, 2, 2),
         )
+        later_targets, own_out = tie(targets[0], own_out)
+        answers = cross(crossed, later_targets)
     else:
-        qkv_local, answers = qkv_low, targets[0]
+        cells = packed
+        answers = targets[0]
         w_outs, w_ups, w_downs, qkv_t = [
             lax.all_gather(shard, "mp")
             for shard in (low(w_out), low(w_up), low(w_down), qkv_low.T)
         ]
     gathered = (w_outs.reshape(D, D), w_ups, w_downs.reshape(-1, D), qkv_t.reshape(3 * D, D))
-    leads = packed[0, 4 * V + 4 : 4 * V + 6].astype(jnp.int32)
-    ocean = 1.0 - packed[:, 4 * V : 4 * V + 4]
+    qkv_local = choose(qkv_t, part)
+    leads = cells[0, 4 * V + 4 : 4 * V + 6].astype(jnp.int32)
+    ocean = 1.0 - cells[:, 4 * V : 4 * V + 4]
     count = sum_everywhere(crossed, jnp.sum(ocean))
     denom = 2.0 * V * jnp.maximum(count, 1.0)
     first_row = part * shard_rows
@@ -1541,15 +1694,16 @@
     loss_part = f32(0.0)
     records = []
     for rollout in range(2):
-        cells = packed
         if rollout == 1:
             cells = jnp.pad(guess, ((0, 0), (0, 64)))
         if rollout == 1 or not crossed:
             lead_row = lax.dynamic_slice_in_dim(tables, 5 * V + leads[rollout], 1, 0)
             x_first, normed = embed_forward(cells, prepared, lead_row, norm_gains)
-        rows_one = spread_rows(crossed, normed)
-        packed = jnp.dot(rows_one, qkv_local, preferred_element_type=f32).astype(bf16)
-        own_out, full, logsum = attend(packed)
+            rows_one = spread_rows(crossed, normed)
+            packed = lax.dot_general(
+                rows_one, qkv_local, NT, preferred_element_type=f32
+            ).astype(bf16)
+            own_out, full, logsum = attend(packed)
         attended = exchange(crossed, own_out, True, 2)
         x_mid, rows_two, hidden, active, x_last, guess = branch_forward(
             attended, x_first, norm_gains, gathered, head
@@ -1565,7 +1719,7 @@
     gain_high = jnp.zeros((4, D), f32)
     gain_low = jnp.zeros((2, D), f32)
     table_parts, lead_sums = [], []
-    qkv_grad = jnp.zeros((D, qkv_local.shape[1]), f32)
+    qkv_grad = jnp.zeros((D, qkv_local.shape[0]), f32)
     kept = []
 
     def sources(index, other, blocked):

time: 907 us -> 804 us (0.89)
  Pallas kernels: 694 us -> 599 us
    pallas_call x1, Pallas kernels: 207 us -> 144 us  [start_program(): pl.pallas_call(partial(start_kernel, halves), grid=(groups * 3 + lag_two,...]
    pallas_call x2 -> x1, Pallas kernels: 48.5 us -> 25.5 us  [spread_rows(): pl.pallas_call(gather_kernel, out_shape=jax.ShapeDtypeStruct((8 * rows, w...]
    pallas_call x2 -> x1, Pallas kernels: 32.8 us -> 16.2 us  [attend(): pl.pallas_call(partial(attend_kernel, heads), grid=(total // block,), out...]
    pallas_call x6, Pallas kernels: 103 us -> 114 us  [exchange(): pl.pallas_call(partial(exchange_kernel, to_columns, rows, width), out_sha...]
    unnamed x124 -> x120, local copies, waits for them, and re-layouts: 23.6 us -> 25.9 us
  transfers between devices with their start and end apart: 20 -> 21, of which waited for: 5 -> 5; matrix products, arithmetic and copies ran while one was open for 5% -> 8% of each run, Pallas kernels for 12% -> 31%
where the time goes in v3:
time: 804 us; the launch traced here: 798 us
  Pallas kernels  599 us (75%)
  local copies, waits for them, and re-layouts  54.9 us (7%)
  other arithmetic  52.7 us (7%)
  waiting for transfers between devices  37.4 us (5%)
  starting transfers between devices  28.6 us (4%)
  matrix products  13.1 us (2%)
  between operations  12.1 us (2%)
    pallas_call x1, Pallas kernels, start_program(): pl.pallas_call(partial(start_kernel, halves), grid=(groups * 3 + lag_two,...  144 us
    pallas_call x6, Pallas kernels, exchange(): pl.pallas_call(partial(exchange_kernel, to_columns, rows, width), out_sha...  114 us
    pallas_call x2, Pallas kernels, attend_back(): pl.pallas_call(partial(attend_back_kernel, heads), grid=(total // block,)...  51 us
    pallas_call x2, Pallas kernels, entry_backward(): pl.pallas_call(entry_back_kernel, grid=(HEADS // 2,), out_shape=(jax.Shap...  50.3 us
    pallas_call x1, Pallas kernels, exchange_sum(): pl.pallas_call(exchange_sum_kernel, out_shape=(jax.ShapeDtypeStruct(value...  50.1 us
    pallas_call x2, Pallas kernels, branch_backward(): pl.pallas_call(branch_back_kernel, grid=(parts,), out_shape=(jax.ShapeDty...  39.5 us
    ppermute x19, waiting for transfers between devices, shift(): return lax.ppermute(value, ('dp', 'mp'), device_pairs(move))  37.4 us
    pallas_call x2, Pallas kernels, branch_forward(): pl.pallas_call(branch_kernel, grid=(parts,), out_shape=(jax.ShapeDtypeStr...  34.9 us
  transfers between devices with their start and end apart: 21, of which 5 were waited for; matrix products, arithmetic and copies ran while one was open for 8% of the time, Pallas kernels for 31%

profile of v3, /device:TPU:0, one launch (start us, length us, event | category | flops | bytes accessed | tf_op | source)
XLA Modules:
  0.0 798.0 jit_solution(8113649972108301712)
XLA Ops:
  16.7 144.5 %start_program.1 = (f32[256,1024]{1,0:T(8,128)}, f32[256,256]{1,0:T(8,128)}, bf16[2048,384]{1,0:T(8,128)(2,1)}, bf16[2048,128]{1,0:T(8,128)(2,1)}, f32[2048,128]...) custom-call(f32[256,256]{1,0:T(8,128)} %maximum_maximum_fusion.refs_, ...), custom_call_target="tpu_custom_call" | custom-call | tf_op jit(solution)/shard_map/start_program/pallas_call | solution.py:1573
  163.7 22.7 %exchange_parts.6.o_ref.refs_6_ = bf16[256,1024]{1,0:T(8,128)(2,1)} custom-call(bf16[2048,128]{1,0:T(8,128)(2,1)} %get-tuple-element.113.x_ref), custom_call_target="tpu_custom_call" | custom-call | tf_op jit(solution)/shard_map/exchange_parts/pallas_call | solution.py:215
  186.4 17.4 %branch_forward.2 = (f32[256,1024]{1,0:T(8,128)}, bf16[256,1024]{1,0:T(8,128)(2,1)}, f32[256,4096]{1,0:T(8,128)}, bf16[256,4096]{1,0:T(8,128)(2,1)}, f32[256,1024]{1,0:T(8,128)}, /*index=5*/f32[256,192]{1,0:T(8,128)}) custom-call(bf16[256,1024]{1,0:T(8,128)(2,1)} %exchange_parts.6.o_ref.refs_6_, f32[256,1024]{1,0:T(8,128)} %get-tuple-element.114.x0_ref, ...), custom_call_target="tpu_custom_call" | custom-call | flops 5435817984 | bytes 23068672 | tf_op jit(solution)/shard_map/branch_forward/pallas_call | solution.py:465
  208.7 15.7 %embed_forward.1 = (f32[256,1024]{1,0:T(8,128)}, bf16[256,1024]{1,0:T(8,128)(2,1)}) custom-call(f32[256,256]{1,0:T(8,128)} %pad.14.u_ref, f32[16,256]{1,0:T(8,128)} %get-tuple-element.108.refs_1_.keyed_ref, f32[16,256]{1,0:T(8,128)} %get-tuple-element.109.refs_2_.bias_ref, f32[256,1024]{1,0:T(8,128)} %get-tuple-element.110.refs_3_.patch_ref, ...), custom_call_target="tpu_custom_call" | custom-call | flops 1610612736 | bytes 3670016 | tf_op jit(solution)/shard_map/embed_forward/pallas_call | solution.py:1059
  224.3 25.5 %gather_rows.1 = bf16[2048,1024]{1,0:T(8,128)(2,1)} custom-call(bf16[256,1024]{1,0:T(8,128)(2,1)} %get-tuple-element.120.x_ref), custom_call_target="tpu_custom_call" | custom-call | tf_op jit(solution)/shard_map/gather_rows/pallas_call | solution.py:153
  255.8 16.2 %attend.1 = (bf16[2048,128]{1,0:T(8,128)(2,1)}, f32[2048,128]{1,0:T(8,128)}, f32[2,2048]{1,0:T(2,128)}) custom-call(bf16[2048,128]{1,0:T(8,128)(2,1)} %get-tuple-element.274.q_ref, bf16[2048,128]{1,0:T(8,128)(2,1)} %get-tuple-element.273.k_ref, bf16[2048,128]{1,0:T(8,128)(2,1)} %get-tuple-element.272.v_ref), custom_call_target="tpu_custom_call" | custom-call | flops 8589934592 | bytes 2621440 | tf_op jit(solution)/shard_map/attend/pallas_call | solution.py:271
  272.1 11.5 %exchange_parts.7.o_ref.refs_4_ = bf16[256,1024]{1,0:T(8,128)(2,1)} custom-call(bf16[2048,128]{1,0:T(8,128)(2,1)} %get-tuple-element.122.x_ref), custom_call_target="tpu_custom_call" | custom-call | tf_op jit(solution)/shard_map/exchange_parts/pallas_call | solution.py:215
  287.6 13.8 %tile_sum.1 = f32[8,128]{1,0:T(8,128)} custom-call(f32[8,128]{1,0:T(8,128)} %broadcast_in_dim.47.t_ref), custom_call_target="tpu_custom_call" | custom-call | tf_op jit(solution)/shard_map/tile_sum/pallas_call | solution.py:933
  304.2 17.6 %branch_forward.3 = (f32[256,1024]{1,0:T(8,128)}, bf16[256,1024]{1,0:T(8,128)(2,1)}, f32[256,4096]{1,0:T(8,128)}, bf16[256,4096]{1,0:T(8,128)(2,1)}, f32[256,1024]{1,0:T(8,128)}, /*index=5*/f32[256,192]{1,0:T(8,128)}) custom-call(bf16[256,1024]{1,0:T(8,128)(2,1)} %exchange_parts.7.o_ref.refs_4_, f32[256,1024]{1,0:T(8,128)} %get-tuple-element.123.x0_ref, ...), custom_call_target="tpu_custom_call" | custom-call | flops 5435817984 | bytes 23068672 | tf_op jit(solution)/shard_map/branch_forward/pallas_call | solution.py:465
  323.6 19.8 %branch_backward.2 = (bf16[256,1024]{1,0:T(8,128)(2,1)}, bf16[256,4096]{1,0:T(8,128)(2,1)}, f32[256,1024]{1,0:T(8,128)}, bf16[256,1024]{1,0:T(8,128)(2,1)}, bf16...) custom-call(f32[256,192]{1,0:T(8,128)} %multiply_divide_fusion.dpred_ref, ...), custom_call_target="tpu_custom_call" | custom-call | flops 6039797760 | bytes 23068672 | tf_op jit(solution)/shard_map/branch_backward/pallas_call | solution.py:557
  343.4 11.5 %exchange_parts.8.do_ref = bf16[2048,128]{1,0:T(8,128)(2,1)} custom-call(bf16[256,1024]{1,0:T(8,128)(2,1)} %get-tuple-element.129.x_ref), custom_call_target="tpu_custom_call" | custom-call | tf_op jit(solution)/shard_map/exchange_parts/pallas_call | solution.py:215
  355.0 25.4 %attend_back.2 = (bf16[2048,128]{1,0:T(8,128)(2,1)}, bf16[2048,128]{1,0:T(8,128)(2,1)}, bf16[2048,128]{1,0:T(8,128)(2,1)}) custom-call(bf16[2048,128]{1,0:T(8,128)(2,1)} %get-tuple-element.274.q_ref, bf16[2048,128]{1,0:T(8,128)(2,1)} %exchange_parts.8.do_ref, f32[2048,128]{1,0:T(8,128)} %get-tuple-element.130.full_ref, ...), custom_call_target="tpu_custom_call" | custom-call | flops 21474836480 | bytes 4194304 | tf_op jit(solution)/shard_map/attend_back/pallas_call | solution.py:362
  384.1 23.5 %exchange_parts.9.grad_ref = bf16[256,3072]{1,0:T(8,128)(2,1)} custom-call(bf16[2048,384]{1,0:T(8,128)(2,1)} %copy-done.9), custom_call_target="tpu_custom_call" | custom-call | tf_op jit(solution)/shard_map/exchange_parts/pallas_call | solution.py:215
  407.6 25.2 %entry_backward.2 = (f32[256,256]{1,0:T(8,128)}, f32[2,1024]{1,0:T(2,128)}, f32[1,1024]{1,0:T(1,128)}, f32[1024,256]{1,0:T(8,128)}, f32[1024,256]{1,0:T(8,128)}, /*index=5*/f32[16,256]{1,0:T(8,128)}, f32[16,256]{1,0:T(8,128)}) custom-call(bf16[256,3072]{1,0:T(8,128)(2,1)} %exchange_parts.9.grad_ref, bf16[3072,1024]{1,0:T(8,128)(2,1)} %bitcast.145, ...), custom_call_target="tpu_custom_call" | custom-call | flops 4026531840 | bytes 10485760 | tf_op jit(solution)/shard_map/entry_backward/pallas_call | solution.py:1142
  435.3 19.8 %branch_backward.3 = (bf16[256,1024]{1,0:T(8,128)(2,1)}, bf16[256,4096]{1,0:T(8,128)(2,1)}, f32[256,1024]{1,0:T(8,128)}, bf16[256,1024]{1,0:T(8,128)(2,1)}, bf16...) custom-call(f32[256,192]{1,0:T(8,128)} %get-tuple-element.275.dpred_ref, ...), custom_call_target="tpu_custom_call" | custom-call | flops 6039797760 | bytes 23068672 | tf_op jit(solution)/shard_map/branch_backward/pallas_call | solution.py:557
  461.8 8.0 %outer_other.3 = bf16[4,4,320,512]{3,2,1,0:T(8,128)(2,1)} custom-call(s32[3]{0:T(128)} %add_add_fusion.where_ref, bf16[256,1024]{1,0:T(8,128)(2,1)} %get-tuple-element.147.refs_0_, bf16[256,4096]{1,0:T(8,128)(2,1)} %get-tuple-element.148.refs_1_, bf16[256,1024]{1,0:T(8,128)(2,1)} %get-tuple-element.149.refs_2_, ...), custom_call_target="tpu_custom_call" | custom-call | flops 2684354560 | bytes 7864320 | tf_op jit(solution)/shard_map/outer_other/pallas_call | solution.py:667
  478.7 11.6 %exchange_parts.10.do_ref = bf16[2048,128]{1,0:T(8,128)(2,1)} custom-call(bf16[256,1024]{1,0:T(8,128)(2,1)} %get-tuple-element.153.x_ref), custom_call_target="tpu_custom_call" | custom-call | tf_op jit(solution)/shard_map/exchange_parts/pallas_call | solution.py:215
  507.9 9.3 %outer_own.3 = (bf16[4,2,320,512]{3,2,1,0:T(8,128)(2,1)}, bf16[4,2,320,512]{3,2,1,0:T(8,128)(2,1)}) custom-call(s32[3]{0:T(128)} %add_add_fusion.1.where_ref, bf16[256,1024]{1,0:T(8,128)(2,1)} %get-tuple-element.147.refs_0_, bf16[256,4096]{1,0:T(8,128)(2,1)} %get-tuple-element.148.refs_1_, bf16[256,1024]{1,0:T(8,128)(2,1)} %get-tuple-element.149.refs_2_, ...), custom_call_target="tpu_custom_call" | custom-call | flops 2684354560 | bytes 7864320 | tf_op jit(solution)/shard_map/outer_own/pallas_call | solution.py:677
  525.8 25.5 %attend_back.3 = (bf16[2048,128]{1,0:T(8,128)(2,1)}, bf16[2048,128]{1,0:T(8,128)(2,1)}, bf16[2048,128]{1,0:T(8,128)(2,1)}) custom-call(bf16[2048,128]{1,0:T(8,128)(2,1)} %get-tuple-element.271.q_ref, bf16[2048,128]{1,0:T(8,128)(2,1)} %exchange_parts.10.do_ref, f32[2048,128]{1,0:T(8,128)} %get-tuple-element.161.full_ref, ...), custom_call_target="tpu_custom_call" | custom-call | flops 21474836480 | bytes 4194304 | tf_op jit(solution)/shard_map/attend_back/pallas_call | solution.py:362
  559.3 33.0 %exchange_parts.11.grad_ref = bf16[256,3072]{1,0:T(8,128)(2,1)} custom-call(bf16[2048,384]{1,0:T(8,128)(2,1)} %copy-done.2), custom_call_target="tpu_custom_call" | custom-call | tf_op jit(solution)/shard_map/exchange_parts/pallas_call | solution.py:215
  626.7 25.1 %entry_backward.3 = (f32[256,256]{1,0:T(8,128)}, f32[2,1024]{1,0:T(2,128)}, f32[1,1024]{1,0:T(1,128)}, f32[1024,256]{1,0:T(8,128)}, f32[1024,256]{1,0:T(8,128)}, /*index=5*/f32[16,256]{1,0:T(8,128)}, f32[16,256]{1,0:T(8,128)}) custom-call(bf16[256,3072]{1,0:T(8,128)(2,1)} %exchange_parts.11.grad_ref, bf16[3072,1024]{1,0:T(8,128)(2,1)} %bitcast.146, ...), custom_call_target="tpu_custom_call" | custom-call | flops 4026531840 | bytes 10485760 | tf_op jit(solution)/shard_map/entry_backward/pallas_call | solution.py:1142
  677.2 15.3 %collective-permute-done.19 = bf16[256,512]{1,0:T(8,128)(2,1)S(1)} collective-permute-done((bf16[256,512]{1,0:T(8,128)(2,1)S(1)}, bf16[256,512]{1,0:T(8,128)(2,1)S(1)}, u32[]{:S(2)}, u32[]{:S(2)}) %collective-permute-start.19) | collective-permute-done | bytes 262176 | tf_op jit(solution)/shard_map/ppermute | solution.py:704
  693.8 15.5 %collective-permute-done.14 = bf16[320,512]{1,0:T(8,128)(2,1)S(1)} collective-permute-done((bf16[320,512]{1,0:T(8,128)(2,1)S(1)}, bf16[320,512]{1,0:T(8,128)(2,1)S(1)}, u32[]{:S(2)}, u32[]{:S(2)}) %collective-permute-start.14) | collective-permute-done | bytes 327712 | tf_op jit(solution)/shard_map/ppermute | solution.py:704
  714.2 50.1 %exchange_sum.1 = (f32[512,1024]{1,0:T(8,128)}, f32[8,128]{1,0:T(8,128)}) custom-call(f32[512,1024]{1,0:T(8,128)} %table_grads.1.x_ref, f32[8,128]{1,0:T(8,128)} %broadcast_in_dim.51.t_ref), custom_call_target="tpu_custom_call" | custom-call | tf_op jit(solution)/shard_map/exchange_sum/pallas_call | solution.py:871
  (259 shorter events, 182.5 us)
Async XLA Ops:
  16.7 145.2 %copy-start = (f32[440,1024]{1,0:T(8,128)S(1)}, f32[440,1024]{1,0:T(8,128)}, u32[]{:S(2)}) copy-start(f32[440,1024]{1,0:T(8,128)} %tables_ref.1) | copy-start | bytes 5406724
  161.2 160.5 %collective-permute-start = (f32[2,256,192]{2,1,0:T(8,128)S(1)}, f32[2,256,192]{2,1,0:T(8,128)S(1)}, u32[]{:S(2)}, u32[]{:S(2)}) collective-permute-start(f32[2,256,192]{2,1,0:T(8,128)S(1)} %bitcast.142), channel_id=1, source_target_pairs={{0,0},{1,1},{2,8},{3,9},{4,16},{5,17},{6,24},{7,25},{8,2},{9,3},{1... | collective-permute-start | bytes 1179656 | tf_op jit(solution)/shard_map/ppermute | solution.py:85
  469.9 38.0 %collective-permute-start.2 = (bf16[4,4,320,512]{3,2,1,0:T(8,128)(2,1)}, bf16[4,4,320,512]{3,2,1,0:T(8,128)(2,1)}, u32[]{:S(2)}, u32[]{:S(2)}) collective-permute-start(bf16[4,4,320,512]{3,2,1,0:T(8,128)(2,1)} %outer_other.3), channel_id=1, source_target_pairs={{0,1},{1,0},{2,3},{3,2},{4,5},{5,4},{6,7},{7,6},{8,9},{9,8},{10,11... | collective-permute-start | bytes 15728648 | tf_op jit(solution)/shard_map/ppermute | solution.py:704
  469.9 30.3 %collective-permute-start.1 = (bf16[4,4,256,512]{3,2,1,0:T(8,128)(2,1)}, bf16[4,4,256,512]{3,2,1,0:T(8,128)(2,1)}, u32[]{:S(2)}, u32[]{:S(2)}) collective-permute-start(bf16[4,4,256,512]{3,2,1,0:T(8,128)(2,1)} %outer_other.2), channel_id=1, source_target_pairs={{0,1},{1,0},{2,3},{3,2},{4,5},{5,4},{6,7},{7,6},{8,9},{9,8},{10,11... | collective-permute-start | bytes 12582920 | tf_op jit(solution)/shard_map/ppermute | solution.py:704
  520.4 32.7 %collective-permute-start.4 = (bf16[2,2,256,512]{3,2,1,0:T(8,128)(2,1)S(1)}, bf16[2,2,256,512]{3,2,1,0:T(8,128)(2,1)S(1)}, u32[]{:S(2)}, u32[]{:S(2)}) collective-permute-start(bf16[2,2,256,512]{3,2,1,0:T(8,128)(2,1)S(1)} %slice.139), channel_id=1, source_target_pairs={{0,16},{1,17},{2,18},{3,19},{4,20},{5,21},{6,22},{7,23},{8,24},{9,... | collective-permute-start | bytes 3145736 | tf_op jit(solution)/shard_map/ppermute | solution.py:704
  521.1 33.6 %collective-permute-start.3 = (bf16[2,2,256,512]{3,2,0,1:T(8,128)(2,1)S(1)}, bf16[2,2,256,512]{3,2,0,1:T(8,128)(2,1)S(1)}, u32[]{:S(2)}, u32[]{:S(2)}) collective-permute-start(bf16[2,2,256,512]{3,2,0,1:T(8,128)(2,1)S(1)} %slice.164), channel_id=1, source_target_pairs={{0,8},{1,9},{2,10},{3,11},{4,12},{5,13},{6,14},{7,15},{8,0},{9,1},... | collective-permute-start | bytes 3145736 | tf_op jit(solution)/shard_map/ppermute | solution.py:704
  521.8 91.1 %collective-permute-start.6 = (bf16[2,2,320,512]{3,2,1,0:T(8,128)(2,1)}, bf16[2,2,320,512]{3,2,1,0:T(8,128)(2,1)}, u32[]{:S(2)}, u32[]{:S(2)}) collective-permute-start(bf16[2,2,320,512]{3,2,1,0:T(8,128)(2,1)} %slice.143), channel_id=1, source_target_pairs={{0,16},{1,17},{2,18},{3,19},{4,20},{5,21},{6,22},{7,23},{8,24},{9,... | collective-permute-start | bytes 3932168 | tf_op jit(solution)/shard_map/ppermute | solution.py:704
  524.3 90.3 %collective-permute-start.5 = (bf16[2,2,320,512]{3,2,0,1:T(8,128)(2,1)}, bf16[2,2,320,512]{3,2,0,1:T(8,128)(2,1)}, u32[]{:S(2)}, u32[]{:S(2)}) collective-permute-start(bf16[2,2,320,512]{3,2,0,1:T(8,128)(2,1)} %slice.166), channel_id=1, source_target_pairs={{0,8},{1,9},{2,10},{3,11},{4,12},{5,13},{6,14},{7,15},{8,0},{9,1},... | collective-permute-start | bytes 3932168 | tf_op jit(solution)/shard_map/ppermute | solution.py:704
  559.3 33.1 %copy-start.31 = (f32[1024,384]{1,0:T(8,128)}, f32[1024,384]{1,0:T(8,128)S(1)}, u32[]{:S(2)}) copy-start(f32[1024,384]{1,0:T(8,128)S(1)} %convolution_add_fusion) | copy-start | bytes 4718596
  593.2 10.5 %collective-permute-start.7 = (bf16[256,384]{0,1:T(8,128)(2,1)}, bf16[256,384]{0,1:T(8,128)(2,1)}, u32[]{:S(2)}, u32[]{:S(2)}) collective-permute-start(bf16[256,384]{0,1:T(8,128)(2,1)} %bitcast.144), channel_id=1, source_target_pairs={{0,2},{1,3},{2,4},{3,5},{4,6},{5,7},{6,0},{7,1},{8,10},{9,11},{10,... | collective-permute-start | bytes 589832 | tf_op jit(solution)/shard_map/ppermute | solution.py:704
  594.7 14.0 %collective-permute-start.8 = (bf16[256,384]{0,1:T(8,128)(2,1)}, bf16[256,384]{0,1:T(8,128)(2,1)}, u32[]{:S(2)}, u32[]{:S(2)}) collective-permute-start(bf16[256,384]{0,1:T(8,128)(2,1)} %bitcast.119), channel_id=1, source_target_pairs={{0,4},{1,5},{2,6},{3,7},{4,0},{5,1},{6,2},{7,3},{8,12},{9,13},{10,... | collective-permute-start | bytes 589832 | tf_op jit(solution)/shard_map/ppermute | solution.py:704
  597.3 12.0 %collective-permute-start.9 = (bf16[256,384]{0,1:T(8,128)(2,1)S(1)}, bf16[256,384]{0,1:T(8,128)(2,1)}, u32[]{:S(2)}, u32[]{:S(2)}) collective-permute-start(bf16[256,384]{0,1:T(8,128)(2,1)S(1)} %bitcast.143), channel_id=1, source_target_pairs={{0,6},{1,7},{2,0},{3,1},{4,2},{5,3},{6,4},{7,5},{8,14},{9,15},{10,... | collective-permute-start | bytes 589832 | tf_op jit(solution)/shard_map/ppermute | solution.py:704
  603.8 57.9 %collective-permute-start.17 = (bf16[2,256,512]{2,1,0:T(8,128)(2,1)S(1)}, bf16[2,256,512]{2,1,0:T(8,128)(2,1)}, u32[]{:S(2)}, u32[]{:S(2)}) collective-permute-start(bf16[2,256,512]{2,1,0:T(8,128)(2,1)S(1)} %dynamic-slice_bitcast_fusion.2), channel_id=1, source_target_pairs={{0,8},{1,9},{2,10},{3,11},{4,12},{5,13},{6,14},{7,15},{8,0},{9,1},... | collective-permute-start | bytes 1572872 | tf_op jit(solution)/shard_map/ppermute | solution.py:704
  608.7 54.2 %collective-permute-start.16 = (bf16[2,256,512]{2,1,0:T(8,128)(2,1)}, bf16[2,256,512]{2,1,0:T(8,128)(2,1)}, u32[]{:S(2)}, u32[]{:S(2)}) collective-permute-start(bf16[2,256,512]{2,1,0:T(8,128)(2,1)} %dynamic-slice_bitcast_fusion.3), channel_id=1, source_target_pairs={{0,16},{1,17},{2,18},{3,19},{4,20},{5,21},{6,22},{7,23},{8,24},{9,... | collective-permute-start | bytes 1572872 | tf_op jit(solution)/shard_map/ppermute | solution.py:704
  611.2 53.8 %collective-permute-start.10 = (f32[256,384]{0,1:T(8,128)}, f32[256,384]{0,1:T(8,128)S(1)}, u32[]{:S(2)}, u32[]{:S(2)}) collective-permute-start(f32[256,384]{0,1:T(8,128)} %fusion.30), channel_id=1, source_target_pairs={{0,0},{1,1},{2,8},{3,9},{4,16},{5,17},{6,24},{7,25},{8,2},{9,3},{1... | collective-permute-start | bytes 1179656 | tf_op jit(solution)/shard_map/ppermute | solution.py:85
  617.2 51.9 %collective-permute-start.12 = (bf16[2,320,512]{2,1,0:T(8,128)(2,1)}, bf16[2,320,512]{2,1,0:T(8,128)(2,1)}, u32[]{:S(2)}, u32[]{:S(2)}) collective-permute-start(bf16[2,320,512]{2,1,0:T(8,128)(2,1)} %dynamic-slice_bitcast_fusion), channel_id=1, source_target_pairs={{0,8},{1,9},{2,10},{3,11},{4,12},{5,13},{6,14},{7,15},{8,0},{9,1},... | collective-permute-start | bytes 1966088 | tf_op jit(solution)/shard_map/ppermute | solution.py:704
  623.9 46.5 %collective-permute-start.11 = (bf16[2,320,512]{2,1,0:T(8,128)(2,1)}, bf16[2,320,512]{2,1,0:T(8,128)(2,1)}, u32[]{:S(2)}, u32[]{:S(2)}) collective-permute-start(bf16[2,320,512]{2,1,0:T(8,128)(2,1)} %dynamic-slice_bitcast_fusion.1), channel_id=1, source_target_pairs={{0,16},{1,17},{2,18},{3,19},{4,20},{5,21},{6,22},{7,23},{8,24},{9,... | collective-permute-start | bytes 1966088 | tf_op jit(solution)/shard_map/ppermute | solution.py:704
  664.4 11.2 %collective-permute-start.18 = (bf16[256,512]{1,0:T(8,128)(2,1)S(1)}, bf16[256,512]{1,0:T(8,128)(2,1)S(1)}, u32[]{:S(2)}, u32[]{:S(2)}) collective-permute-start(bf16[256,512]{1,0:T(8,128)(2,1)S(1)} %get-tuple-element.261), channel_id=1, source_target_pairs={{0,2},{1,3},{2,4},{3,5},{4,6},{5,7},{6,0},{7,1},{8,10},{9,11},{10,... | collective-permute-start | bytes 786440 | tf_op jit(solution)/shard_map/ppermute | solution.py:704
  664.5 28.0 %collective-permute-start.19 = (bf16[256,512]{1,0:T(8,128)(2,1)S(1)}, bf16[256,512]{1,0:T(8,128)(2,1)S(1)}, u32[]{:S(2)}, u32[]{:S(2)}) collective-permute-start(bf16[256,512]{1,0:T(8,128)(2,1)S(1)} %get-tuple-element.262), channel_id=1, source_target_pairs={{0,4},{1,5},{2,6},{3,7},{4,0},{5,1},{6,2},{7,3},{8,12},{9,13},{10,... | collective-permute-start | bytes 786440 | tf_op jit(solution)/shard_map/ppermute | solution.py:704
  665.0 27.4 %collective-permute-start.20 = (bf16[256,512]{1,0:T(8,128)(2,1)S(1)}, bf16[256,512]{1,0:T(8,128)(2,1)S(1)}, u32[]{:S(2)}, u32[]{:S(2)}) collective-permute-start(bf16[256,512]{1,0:T(8,128)(2,1)S(1)} %get-tuple-element.263), channel_id=1, source_target_pairs={{0,6},{1,7},{2,0},{3,1},{4,2},{5,3},{6,4},{7,5},{8,14},{9,15},{10,... | collective-permute-start | bytes 786440 | tf_op jit(solution)/shard_map/ppermute | solution.py:704
  672.0 21.8 %collective-permute-start.13 = (bf16[320,512]{1,0:T(8,128)(2,1)S(1)}, bf16[320,512]{1,0:T(8,128)(2,1)S(1)}, u32[]{:S(2)}, u32[]{:S(2)}) collective-permute-start(bf16[320,512]{1,0:T(8,128)(2,1)S(1)} %get-tuple-element.258), channel_id=1, source_target_pairs={{0,2},{1,3},{2,4},{3,5},{4,6},{5,7},{6,0},{7,1},{8,10},{9,11},{10,... | collective-permute-start | bytes 983048 | tf_op jit(solution)/shard_map/ppermute | solution.py:704
  672.6 36.7 %collective-permute-start.14 = (bf16[320,512]{1,0:T(8,128)(2,1)S(1)}, bf16[320,512]{1,0:T(8,128)(2,1)S(1)}, u32[]{:S(2)}, u32[]{:S(2)}) collective-permute-start(bf16[320,512]{1,0:T(8,128)(2,1)S(1)} %get-tuple-element.259), channel_id=1, source_target_pairs={{0,4},{1,5},{2,6},{3,7},{4,0},{5,1},{6,2},{7,3},{8,12},{9,13},{10,... | collective-permute-start | bytes 983048 | tf_op jit(solution)/shard_map/ppermute | solution.py:704
  675.6 33.7 %collective-permute-start.15 = (bf16[320,512]{1,0:T(8,128)(2,1)S(1)}, bf16[320,512]{1,0:T(8,128)(2,1)S(1)}, u32[]{:S(2)}, u32[]{:S(2)}) collective-permute-start(bf16[320,512]{1,0:T(8,128)(2,1)S(1)} %get-tuple-element.260), channel_id=1, source_target_pairs={{0,6},{1,7},{2,0},{3,1},{4,2},{5,3},{6,4},{7,5},{8,14},{9,15},{10,... | collective-permute-start | bytes 983048 | tf_op jit(solution)/shard_map/ppermute | solution.py:704
  709.6 55.5 %copy-start.32 = (f32[64,256]{1,0:T(8,128)}, f32[64,256]{1,0:T(8,128)S(1)}, u32[]{:S(2)}) copy-start(f32[64,256]{1,0:T(8,128)S(1)} %get-tuple-element.277) | copy-start | bytes 196612
  (49 other events, 410.4 us)

commit v4 on v3

--- a/solution.py
+++ b/solution.py
@@ -763,7 +763,7 @@
 
 
 def exchange_sum_kernel(
-    x_ref, t_ref, o_ref, s_ref, work_ref, pair_ref, quad_ref, eight_ref, deep_ref, tile_ref,
+    x_ref, loss_ref, qkv_ref, up_out_ref, down_ref, o_ref, s_ref, work_ref, pair_ref, quad_ref, eight_ref, deep_ref, tile_ref,
     send_sem, recv_sem,
 ):
     dp, level, core = mesh_place()
@@ -834,8 +834,11 @@
     base_a = core * half + base_a
     base_b = core * half + base_b
     o_ref[mine] = total
-    row = lax.broadcasted_iota(jnp.int32, t_ref.shape, 0)
-    tile_ref[0] = t_ref[...] + jnp.where(row == 0, jnp.sum(total * total), 0.0)
+    row = lax.broadcasted_iota(jnp.int32, s_ref.shape, 0)
+    squares = jnp.sum(total * total)
+    for ref in (qkv_ref, up_out_ref, down_ref):
+        squares += jnp.sum(ref[...] * ref[...])
+    tile_ref[0] = jnp.where(row == 0, squares, jnp.where(row == 1, loss_ref[...], 0.0))
     copies = []
     for step in (1, 2, 3):
         copies.append(send(o_ref.at[mine], o_ref.at[mine], deep[step - 1]))
@@ -866,12 +869,13 @@
         copy.wait_send()
 
 
-def exchange_sum(value, tile):
+def exchange_sum(value, loss, *shares):
     rows, width = value.shape
+    tile = jax.ShapeDtypeStruct((8, 128), f32)
     return pl.pallas_call(
         exchange_sum_kernel,
-        out_shape=(jax.ShapeDtypeStruct(value.shape, f32), jax.ShapeDtypeStruct(tile.shape, f32)),
-        in_specs=[VMEM, VMEM],
+        out_shape=(jax.ShapeDtypeStruct(value.shape, f32), tile),
+        in_specs=[VMEM] * 5,
         out_specs=[VMEM, VMEM],
         scratch_shapes=[
             pltpu.VMEM((rows // 2, width), f32),
@@ -887,63 +891,7 @@
             collective_id=5, has_side_effects=True, vmem_limit_bytes=BIG
         ),
         name="exchange_sum",
-    )(value, tile)
-
-
-def tile_sum_kernel(t_ref, s_ref, tile_ref, send_sem, recv_sem):
-    dp, level, core = mesh_place()
-    x = lax.rem(dp, 2)
-    side = device_of(dp + 1 - 2 * x, level, core)
-    down = device_of(lax.rem(dp + 2, 4), level, core)
-    near = device_of(dp, level, 1 - core)
-    deep = [device_of(dp, lax.rem(level + step, 4), core) for step in (1, 2, 3)]
-    barrier = pltpu.get_barrier_semaphore()
-    for target in (side, down, near, *deep):
-        pl.semaphore_signal(barrier, inc=1, device_id=target, device_id_type=MESH)
-    pl.semaphore_wait(barrier, 6)
-
-    def send(slot, source, target_ref, target):
-        copy = pltpu.make_async_remote_copy(
-            src_ref=source,
-            dst_ref=target_ref,
-            send_sem=send_sem.at[slot],
-            recv_sem=recv_sem.at[slot],
-            device_id=target,
-            device_id_type=MESH,
-        )
-        copy.start()
-        return copy
-
-    copies = [send(step, t_ref, tile_ref.at[step], deep[step]) for step in range(3)]
-    for copy in copies:
-        copy.wait()
-    tile_ref[3] = t_ref[...] + tile_ref[0] + tile_ref[1] + tile_ref[2]
-    send(3, tile_ref.at[3], tile_ref.at[4], side).wait()
-    tile_ref[5] = tile_ref[3] + tile_ref[4]
-    send(4, tile_ref.at[5], tile_ref.at[6], down).wait()
-    tile_ref[7] = tile_ref[5] + tile_ref[6]
-    send(5, tile_ref.at[7], tile_ref.at[8], near).wait()
-    s_ref[...] = tile_ref[7] + tile_ref[8]
-
-
-def sum_everywhere(crossed, value):
-    if not crossed:
-        return lax.psum(value, ("dp", "mp"))
-    tile = jnp.broadcast_to(value, (8, 128))
-    total = pl.pallas_call(
-        tile_sum_kernel,
-        out_shape=jax.ShapeDtypeStruct(tile.shape, f32),
-        in_specs=[VMEM],
-        out_specs=VMEM,
-        scratch_shapes=[
-            pltpu.VMEM((9,) + tile.shape, f32),
-            pltpu.SemaphoreType.DMA((6,)),
-            pltpu.SemaphoreType.DMA((6,)),
-        ],
-        compiler_params=pltpu.CompilerParams(collective_id=6, has_side_effects=True),
-        name="tile_sum",
-    )(tile)
-    return total[0, 0]
+    )(value, loss.reshape(1, 1), *shares)
 
 
 def split_low(values):
@@ -1227,6 +1175,74 @@
     return (master - rate * (update + decay_rate * master), first_new, second_new)
 
 
+def update_kernel(packed, *refs):
+    where_ref, sums_ref, tile_ref, count_ref = refs[:4]
+    shares = list(refs[4 : 4 + (3 if packed else 4)])
+    rest = refs[4 + len(shares) :]
+    states, average_ref, outs = rest[:18], rest[18], rest[19:]
+    norm = jnp.sqrt(tile_ref[0:1, 0:1])
+    factor = jnp.minimum(1.0, clip_norm / (norm + 1e-06))
+    outs[1][...] = norm
+    outs[0][...] = tile_ref[1:2, 0:1] / (2.0 * V * jnp.maximum(count_ref[...], 1.0))
+    embed_rows = 5 * V + LEADS + 1
+    padded = 256
+
+    def apply(index, grad, rate, rows=slice(None)):
+        master, first, second = (ref[rows, :] for ref in states[3 * index : 3 * index + 3])
+        new = adam_step(master, factor * grad, first, second, rate)
+        for ref, value in zip(outs[2 + 3 * index : 5 + 3 * index], new):
+            ref[rows, :] = value
+        return new[0]
+
+    apply(0, sums_ref[:embed_rows, :], lr_table, slice(0, embed_rows))
+    apply(0, sums_ref[padded : padded + 4 * V, :], lr_table, slice(embed_rows, embed_rows + 4 * V))
+    apply(1, sums_ref[embed_rows : embed_rows + 2, :], lr_gain, slice(0, 2))
+    apply(1, sums_ref[padded + 4 * V : padded + 4 * V + 4, :], lr_gain, slice(2, 6))
+    if packed:
+        up_out = shares[1]
+        grads = (
+            shares[0][...], tall_piece(up_out[256:, :]), up_out[:256, :], tall_piece(shares[2][...])
+        )
+    else:
+        grads = [share[...] for share in shares]
+    qkv_new = apply(2, grads[0], lr_matrix)
+    for index in range(1, 4):
+        apply(2 + index, grads[index], lr_matrix)
+    outs[20][...] = average_keep * average_ref[...] + (1.0 - average_keep) * qkv_new
+
+
+def update_all(packed, where, sums, tile, count, shares, states, average):
+    operands = [sums, tile, count.reshape(1, 1), *shares]
+    fixed = lambda shape: pl.BlockSpec(shape, lambda i, w: (0, 0))
+    in_specs = [fixed(value.shape) for value in operands]
+    out_shapes = [(1, 1), (1, 1)]
+    for master, first, second in states:
+        if master.shape == first.shape:
+            in_specs.append(fixed(master.shape))
+        elif master.shape[0] == first.shape[0]:
+            in_specs.append(pl.BlockSpec(first.shape, lambda i, w: (0, w[0])))
+        else:
+            in_specs.append(pl.BlockSpec(first.shape, lambda i, w: (w[0], 0)))
+        in_specs += [fixed(first.shape)] * 2
+        operands += [master, first, second]
+        out_shapes += [first.shape] * 3
+    operands.append(average)
+    in_specs.append(fixed(average.shape))
+    out_shapes.append(average.shape)
+    return pl.pallas_call(
+        partial(update_kernel, packed),
+        grid_spec=pltpu.PrefetchScalarGridSpec(
+            num_scalar_prefetch=1,
+            grid=(1,),
+            in_specs=in_specs,
+            out_specs=[fixed(shape) for shape in out_shapes],
+        ),
+        out_shape=[jax.ShapeDtypeStruct(shape, f32) for shape in out_shapes],
+        compiler_params=pltpu.CompilerParams(vmem_limit_bytes=60 * 2**20),
+        name="update_all",
+    )(where, *operands)
+
+
 def by_kind(shard):
     rows = shard.shape[0]
     return shard.reshape(rows, -1, 3, HEAD_DIM).transpose(0, 2, 1, 3).reshape(rows, -1)
@@ -1245,10 +1261,10 @@
     count = len(halves)
     packed_ref, keyed_ref, bias_ref, patch_ref, var_ref, lead_ref, gains_ref = refs[:7]
     shards = refs[7 : 7 + count]
-    x0_ref, cells_ref, qkv_ref, o_ref, full_ref, lse_ref, rows_out = refs[7 + count : 14 + count]
-    outs = refs[14 + count : 14 + 2 * count]
-    (held_ref, h1_ref, rows_ref, weight_ref, vt_ref, send_sem, recv_sem,
-     level_send, level_recv, own_sem) = refs[14 + 2 * count :]
+    x0_ref, cells_ref, qkv_ref, o_ref, full_ref, lse_ref, count_ref, rows_out = refs[7 + count : 15 + count]
+    outs = refs[15 + count : 15 + 2 * count]
+    (held_ref, h1_ref, rows_ref, weight_ref, vt_ref, tile_ref, send_sem, recv_sem,
+     level_send, level_recv, own_sem) = refs[15 + 2 * count :]
     step = pl.program_id(0)
     dp, level, core = mesh_place()
     x = lax.rem(dp, 2)
@@ -1372,13 +1388,19 @@
     near_side = relay(rows_of(beside, core, 0, rows), near)
     near_down = relay(rows_of(below, core, 0, rows), near)
     near_far = relay(rows_of(far, core, 0, rows), near)
+    tiles = [
+        remote(tile_ref.at[0], tile_ref.at[1], side),
+        remote(tile_ref.at[2], tile_ref.at[3], down),
+        remote(tile_ref.at[4], tile_ref.at[5], near),
+    ]
+    deep = [device_of(dp, lax.rem(level + move, 4), core) for move in (1, 2, 3)]
+    level_tiles = [remote(tile_ref.at[6], tile_ref.at[7 + move], deep[move]) for move in range(3)]
     weight = pltpu.make_async_copy(outs[0].at[dp * 2 + core], weight_ref, own_sem.at[count + 1])
     save = pltpu.make_async_copy(rows_ref, rows_out, own_sem.at[count + 2])
 
     @pl.when(step == 0)
     def _():
         barrier = pltpu.get_barrier_semaphore()
-        deep = [device_of(dp, lax.rem(level + move, 4), core) for move in (1, 2, 3)]
         for target in (side, down, near, *deep):
             pl.semaphore_signal(barrier, inc=1, device_id=target, device_id_type=MESH)
 
@@ -1441,6 +1463,25 @@
             staying.wait()
 
         cells_ref[...] = held_ref[...]
+        lane = lax.broadcasted_iota(jnp.int32, held_ref.shape, 1)
+        ocean = jnp.where((lane >= 4 * V) & (lane < 4 * V + 4), 1.0 - held_ref[...], 0.0)
+        tile_ref[0] = jnp.broadcast_to(jnp.sum(ocean), tile_ref.shape[1:])
+        tiles[0].start()
+
+    for turn in range(3):
+
+        @pl.when(step == embed_at + 2 + turn)
+        def _(turn=turn):
+            tiles[turn].wait_recv()
+            tile_ref[2 * turn + 2] = tile_ref[2 * turn] + tile_ref[2 * turn + 1]
+            for copy in (tiles[1:2], tiles[2:3], level_tiles)[turn]:
+                copy.start()
+
+    @pl.when(step == embed_at + 6)
+    def _():
+        for copy in level_tiles:
+            copy.wait_recv()
+        count_ref[...] = tile_ref[6] + tile_ref[7] + tile_ref[8] + tile_ref[9]
 
     @pl.when((step >= embed_at) & (step < embed_at + HEADS // 2))
     def _():
@@ -1541,6 +1582,8 @@
 
         for copy in (side_a, down_b, side_b, down_a, near_own, far_a, far_b, near_side, near_down, near_far):
             copy.wait_send()
+        for copy in (*tiles, *level_tiles):
+            copy.wait_send()
         save.wait()
 
         @pl.when(dp != level)
@@ -1552,7 +1595,7 @@
     patch, variable, keyed, bias = prepared
     count = len(shards)
     groups = sum(halves)
-    copies = groups * 24 + count + 11
+    copies = groups * 24 + count + 17
     rows, padded = packed.shape
     total = 8 * rows
     width = shards[0].shape[0] // 3
@@ -1569,6 +1612,7 @@
         ((total, width), bf16),
         ((total, width), f32),
         ((heads, total), f32),
+        ((8, 128), f32),
     ]
     return pl.pallas_call(
         partial(start_kernel, halves),
@@ -1587,6 +1631,7 @@
             pltpu.VMEM((total, D), bf16),
             pltpu.VMEM(shards[0].shape, bf16),
             pltpu.VMEM((width, total), bf16),
+            pltpu.VMEM((10, 8, 128), f32),
             pltpu.SemaphoreType.DMA((copies,)),
             pltpu.SemaphoreType.DMA((copies,)),
             pltpu.SemaphoreType.DMA((groups * 5,)),
@@ -1646,7 +1691,6 @@
     def own_share(full, dim):
         return lax.dynamic_slice_in_dim(full, dp_index * share_rows, share_rows, dim)
 
-    masters = (own_share(w_qkv, 0), own_share(w_out, 1), own_share(w_up, 0), own_share(w_down, 1))
     var_hot = (var_ids[:, None] == jnp.arange(V, dtype=jnp.int32)[None, :]).astype(f32)
     prepared = prepare_tables(tables, var_hot)
     low = lambda master: master.astype(bf16)
@@ -1662,16 +1706,17 @@
     )
     if crossed:
         (
-            x_first, cells, packed, own_out, full, logsum, rows_one, qkv_t, w_outs, w_ups, w_downs
+            x_first, cells, packed, own_out, full, logsum, count, rows_one,
+            qkv_t, w_outs, w_ups, w_downs
         ) = start_program(
             packed, prepared, tables[5 * V : 5 * V + 8], norm_gains,
             (qkv_low.T, low(w_out), low(w_up), low(w_down)), (1, 1, 2, 2),
         )
-        later_targets, own_out = tie(targets[0], own_out)
-        answers = cross(crossed, later_targets)
+        count = count[0, 0]
     else:
         cells = packed
         answers = targets[0]
+        count = lax.psum(jnp.sum(1.0 - cells[:, 4 * V : 4 * V + 4]), ("dp", "mp"))
         w_outs, w_ups, w_downs, qkv_t = [
             lax.all_gather(shard, "mp")
             for shard in (low(w_out), low(w_up), low(w_down), qkv_low.T)
@@ -1680,7 +1725,6 @@
     qkv_local = choose(qkv_t, part)
     leads = cells[0, 4 * V + 4 : 4 * V + 6].astype(jnp.int32)
     ocean = 1.0 - cells[:, 4 * V : 4 * V + 4]
-    count = sum_everywhere(crossed, jnp.sum(ocean))
     denom = 2.0 * V * jnp.maximum(count, 1.0)
     first_row = part * shard_rows
     patch_row = (first_row + jnp.arange(shard_rows, dtype=jnp.int32)) // PATCH_COLS
@@ -1705,6 +1749,9 @@
             ).astype(bf16)
             own_out, full, logsum = attend(packed)
         attended = exchange(crossed, own_out, True, 2)
+        if crossed and rollout == 0:
+            later_targets, attended = tie(targets[0], attended)
+            answers = cross(crossed, later_targets)
         x_mid, rows_two, hidden, active, x_last, guess = branch_forward(
             attended, x_first, norm_gains, gathered, head
         )
@@ -1777,17 +1824,6 @@
     def pair(index):
         return (kept[0][index], kept[1][index])
 
-    if crossed:
-        down_share = tall_piece(sum_levels(down_pieces_sum, level))
-        up_out = sum_levels(up_out_sum, level)
-        up_share = up_out[:256]
-        out_share = tall_piece(up_out[256:])
-    else:
-        down_share = outer_plain(pair(2), pair(5), False)
-        up_share = outer_plain(pair(1), pair(4), True)
-        out_share = outer_plain(pair(0), pair(3), False)
-    shares = (by_head(own_qkv_share(crossed, qkv_grad)), out_share, up_share, down_share)
-    share_square = sum(jnp.sum(share * share) for share in shares)
     lead_hots = (leads[:, None] == jnp.arange(8, dtype=jnp.int32)[None, :]).astype(f32)
     lead_hots = jnp.pad(lead_hots, ((0, 6), (0, 0)))
     lead_rows = jnp.pad(jnp.concatenate((lead_sums[1], lead_sums[0])), ((0, 6), (0, 0)))
@@ -1795,52 +1831,36 @@
     last_rows = table_grads(
         *table_parts, prepared, query, var_hot, lead_hots, lead_rows, gain_low, head_total, gain_high
     )
+    qkv_share = by_head(own_qkv_share(crossed, qkv_grad))
+    where = dp_index.astype(jnp.int32).reshape(1)
     if crossed:
+        shares = (qkv_share, sum_levels(up_out_sum, level), sum_levels(down_pieces_sum, level))
+        last_sum, tile = exchange_sum(last_rows, loss_part, *shares)
+        masters = (w_qkv, w_out, w_up, w_down)
+    else:
+        shares = (
+            qkv_share,
+            outer_plain(pair(0), pair(3), False),
+            outer_plain(pair(1), pair(4), True),
+            outer_plain(pair(2), pair(5), False),
+        )
+        squares = sum(jnp.sum(share * share) for share in shares)
+        last_sum, loss_sum, squares = lax.psum((last_rows, loss_part, squares), ("dp", "mp"))
+        squares = squares + jnp.sum(last_sum * last_sum)
         row = jnp.arange(8, dtype=jnp.int32)[:, None]
-        tile = jnp.where(row == 0, share_square, jnp.where(row == 1, loss_part, 0.0))
-        last_sum, tile_sum = exchange_sum(last_rows, jnp.broadcast_to(tile, (8, 128)))
-        square_sum, loss_sum = tile_sum[0, 0], tile_sum[1, 0]
-    else:
-        last_sum, loss_sum, square_sum = lax.psum(
-            (last_rows, loss_part, share_square), ("dp", "mp")
-        )
-        square_sum = square_sum + jnp.sum(last_sum * last_sum)
-    head_sum = last_sum[256:]
-    embed_rows = 5 * V + LEADS + 1
-    table_sum = jnp.concatenate((last_sum[:embed_rows], head_sum[: 4 * V]))
-    gain_sum = jnp.concatenate((last_sum[embed_rows : embed_rows + 2], head_sum[4 * V : 4 * V + 4]))
-    grad_norm = jnp.sqrt(square_sum)
-    factor = jnp.minimum(1.0, clip_norm / (grad_norm + 1e-06))
-    tab = adam_step(tables, factor * table_sum, tables_first, tables_second, lr_table)
-    gai = adam_step(norm_gains, factor * gain_sum, gains_first, gains_second, lr_gain)
-    qkv = adam_step(masters[0], factor * shares[0], qkv_first, qkv_second, lr_matrix)
-    outp = adam_step(masters[1], factor * shares[1], out_first, out_second, lr_matrix)
-    upp = adam_step(masters[2], factor * shares[2], up_first, up_second, lr_matrix)
-    down = adam_step(masters[3], factor * shares[3], down_first, down_second, lr_matrix)
-    average = average_keep * qkv_average + (1.0 - average_keep) * qkv[0]
-    return (
-        loss_sum / denom,
-        grad_norm,
-        tab[0],
-        tab[1],
-        tab[2],
-        gai[0],
-        gai[1],
-        gai[2],
-        qkv[0],
-        qkv[1],
-        qkv[2],
-        outp[0],
-        outp[1],
-        outp[2],
-        upp[0],
-        upp[1],
-        upp[2],
-        down[0],
-        down[1],
-        down[2],
-        average,
+        tile = jnp.where(row == 0, squares, jnp.where(row == 1, loss_sum, 0.0))
+        tile = jnp.broadcast_to(tile, (8, 128))
+        masters = (own_share(w_qkv, 0), own_share(w_out, 1), own_share(w_up, 0), own_share(w_down, 1))
+    states = (
+        (tables, tables_first, tables_second),
+        (norm_gains, gains_first, gains_second),
+        (masters[0], qkv_first, qkv_second),
+        (masters[1], out_first, out_second),
+        (masters[2], up_first, up_second),
+        (masters[3], down_first, down_second),
     )
+    results = update_all(crossed, where, last_sum, tile, count, shares, states, qkv_average)
+    return (results[0][0, 0], results[1][0, 0], *results[2:])
 
 
 def solution(mesh):

time: 804 us -> 745 us (0.927)
  local copies, waits for them, and re-layouts: 54.9 us -> 26 us
  other arithmetic: 52.7 us -> 33.4 us
    unnamed x120 -> x69, local copies, waits for them, and re-layouts: 25.9 us -> 8.34 us
    sub x5 -> x0, other arithmetic: 11.4 us -> none  [adam_step(): master - rate * (update + decay_rate * master)]
  transfers between devices with their start and end apart: 21 -> 21, of which waited for: 5 -> 5; matrix products, arithmetic and copies ran while one was open for 8% -> 7% of each run, Pallas kernels for 31% -> 30%
where the time goes in v4:
time: 745 us; the launch traced here: 740 us
  Pallas kernels  601 us (81%)
  other arithmetic  33.4 us (4%)
  waiting for transfers between devices  32.8 us (4%)
  starting transfers between devices  26.9 us (4%)
  local copies, waits for them, and re-layouts  26 us (3%)
  matrix products  15.2 us (2%)
    pallas_call x1, Pallas kernels, start_program(): pl.pallas_call(partial(start_kernel, halves), grid=(groups * 3 + lag_two,...  150 us
    pallas_call x6, Pallas kernels, exchange(): pl.pallas_call(partial(exchange_kernel, to_columns, rows, width), out_sha...  107 us
    pallas_call x1, Pallas kernels, exchange_sum(): pl.pallas_call(exchange_sum_kernel, out_shape=(jax.ShapeDtypeStruct(value...  52.3 us
    pallas_call x2, Pallas kernels, attend_back(): pl.pallas_call(partial(attend_back_kernel, heads), grid=(total // block,)...  50.8 us
    pallas_call x2, Pallas kernels, entry_backward(): pl.pallas_call(entry_back_kernel, grid=(HEADS // 2,), out_shape=(jax.Shap...  50.2 us
    pallas_call x2, Pallas kernels, branch_backward(): pl.pallas_call(branch_back_kernel, grid=(parts,), out_shape=(jax.ShapeDty...  39.6 us
    pallas_call x2, Pallas kernels, branch_forward(): pl.pallas_call(branch_kernel, grid=(parts,), out_shape=(jax.ShapeDtypeStr...  35 us
    ppermute x19, waiting for transfers between devices, shift(): return lax.ppermute(value, ('dp', 'mp'), device_pairs(move))  32.8 us
  transfers between devices with their start and end apart: 21, of which 5 were waited for; matrix products, arithmetic and copies ran while one was open for 7% of the time, Pallas kernels for 30%

profile of v4, /device:TPU:0, one launch (start us, length us, event | category | flops | bytes accessed | tf_op | source)
XLA Modules:
  0.0 740.2 jit_solution(857892753115565941)
XLA Ops:
  16.2 150.2 %start_program.1 = (f32[256,1024]{1,0:T(8,128)}, f32[256,256]{1,0:T(8,128)}, bf16[2048,384]{1,0:T(8,128)(2,1)}, bf16[2048,128]{1,0:T(8,128)(2,1)}, f32[2048,128]...) custom-call(f32[256,256]{1,0:T(8,128)} %maximum_maximum_fusion.refs_, ...), custom_call_target="tpu_custom_call" | custom-call | tf_op jit(solution)/shard_map/start_program/pallas_call | solution.py:1617
  166.4 11.5 %exchange_parts.6.o_ref.refs_6_ = bf16[256,1024]{1,0:T(8,128)(2,1)} custom-call(bf16[2048,128]{1,0:T(8,128)(2,1)} %get-tuple-element.134.x_ref), custom_call_target="tpu_custom_call" | custom-call | tf_op jit(solution)/shard_map/exchange_parts/pallas_call | solution.py:215
  181.7 17.4 %branch_forward.2 = (f32[256,1024]{1,0:T(8,128)}, bf16[256,1024]{1,0:T(8,128)(2,1)}, f32[256,4096]{1,0:T(8,128)}, bf16[256,4096]{1,0:T(8,128)(2,1)}, f32[256,1024]{1,0:T(8,128)}, /*index=5*/f32[256,192]{1,0:T(8,128)}) custom-call(bf16[256,1024]{1,0:T(8,128)(2,1)} %exchange_parts.6.o_ref.refs_6_, f32[256,1024]{1,0:T(8,128)} %get-tuple-element.136.x0_ref, ...), custom_call_target="tpu_custom_call" | custom-call | flops 5435817984 | bytes 23068672 | tf_op jit(solution)/shard_map/branch_forward/pallas_call | solution.py:465
  204.2 15.7 %embed_forward.1 = (f32[256,1024]{1,0:T(8,128)}, bf16[256,1024]{1,0:T(8,128)(2,1)}) custom-call(f32[256,256]{1,0:T(8,128)} %pad.14.u_ref, f32[16,256]{1,0:T(8,128)} %get-tuple-element.130.refs_1_.keyed_ref, f32[16,256]{1,0:T(8,128)} %get-tuple-element.131.refs_2_.bias_ref, f32[256,1024]{1,0:T(8,128)} %get-tuple-element.132.refs_3_.patch_ref, ...), custom_call_target="tpu_custom_call" | custom-call | flops 1610612736 | bytes 3670016 | tf_op jit(solution)/shard_map/embed_forward/pallas_call | solution.py:1007
  219.8 28.0 %gather_rows.1 = bf16[2048,1024]{1,0:T(8,128)(2,1)} custom-call(bf16[256,1024]{1,0:T(8,128)(2,1)} %get-tuple-element.142.x_ref), custom_call_target="tpu_custom_call" | custom-call | tf_op jit(solution)/shard_map/gather_rows/pallas_call | solution.py:153
  253.8 16.2 %attend.1 = (bf16[2048,128]{1,0:T(8,128)(2,1)}, f32[2048,128]{1,0:T(8,128)}, f32[2,2048]{1,0:T(2,128)}) custom-call(bf16[2048,128]{1,0:T(8,128)(2,1)} %get-tuple-element.265.q_ref, bf16[2048,128]{1,0:T(8,128)(2,1)} %get-tuple-element.264.k_ref, bf16[2048,128]{1,0:T(8,128)(2,1)} %get-tuple-element.263.v_ref), custom_call_target="tpu_custom_call" | custom-call | flops 8589934592 | bytes 2621440 | tf_op jit(solution)/shard_map/attend/pallas_call | solution.py:271
  270.1 11.9 %exchange_parts.7.o_ref.refs_4_ = bf16[256,1024]{1,0:T(8,128)(2,1)} custom-call(bf16[2048,128]{1,0:T(8,128)(2,1)} %get-tuple-element.144.x_ref), custom_call_target="tpu_custom_call" | custom-call | tf_op jit(solution)/shard_map/exchange_parts/pallas_call | solution.py:215
  285.9 17.6 %branch_forward.3 = (f32[256,1024]{1,0:T(8,128)}, bf16[256,1024]{1,0:T(8,128)(2,1)}, f32[256,4096]{1,0:T(8,128)}, bf16[256,4096]{1,0:T(8,128)(2,1)}, f32[256,1024]{1,0:T(8,128)}, /*index=5*/f32[256,192]{1,0:T(8,128)}) custom-call(bf16[256,1024]{1,0:T(8,128)(2,1)} %exchange_parts.7.o_ref.refs_4_, f32[256,1024]{1,0:T(8,128)} %get-tuple-element.145.x0_ref, ...), custom_call_target="tpu_custom_call" | custom-call | flops 5435817984 | bytes 23068672 | tf_op jit(solution)/shard_map/branch_forward/pallas_call | solution.py:465
  305.2 19.8 %branch_backward.2 = (bf16[256,1024]{1,0:T(8,128)(2,1)}, bf16[256,4096]{1,0:T(8,128)(2,1)}, f32[256,1024]{1,0:T(8,128)}, bf16[256,1024]{1,0:T(8,128)(2,1)}, bf16...) custom-call(f32[256,192]{1,0:T(8,128)} %multiply_divide_fusion.dpred_ref, ...), custom_call_target="tpu_custom_call" | custom-call | flops 6039797760 | bytes 23068672 | tf_op jit(solution)/shard_map/branch_backward/pallas_call | solution.py:557
  325.0 11.5 %exchange_parts.8.do_ref = bf16[2048,128]{1,0:T(8,128)(2,1)} custom-call(bf16[256,1024]{1,0:T(8,128)(2,1)} %get-tuple-element.152.x_ref), custom_call_target="tpu_custom_call" | custom-call | tf_op jit(solution)/shard_map/exchange_parts/pallas_call | solution.py:215
  336.5 25.4 %attend_back.2 = (bf16[2048,128]{1,0:T(8,128)(2,1)}, bf16[2048,128]{1,0:T(8,128)(2,1)}, bf16[2048,128]{1,0:T(8,128)(2,1)}) custom-call(bf16[2048,128]{1,0:T(8,128)(2,1)} %get-tuple-element.265.q_ref, bf16[2048,128]{1,0:T(8,128)(2,1)} %exchange_parts.8.do_ref, f32[2048,128]{1,0:T(8,128)} %get-tuple-element.153.full_ref, ...), custom_call_target="tpu_custom_call" | custom-call | flops 21474836480 | bytes 4194304 | tf_op jit(solution)/shard_map/attend_back/pallas_call | solution.py:362
  365.6 23.4 %exchange_parts.9.grad_ref = bf16[256,3072]{1,0:T(8,128)(2,1)} custom-call(bf16[2048,384]{1,0:T(8,128)(2,1)} %copy-done.5), custom_call_target="tpu_custom_call" | custom-call | tf_op jit(solution)/shard_map/exchange_parts/pallas_call | solution.py:215
  389.1 25.2 %entry_backward.2 = (f32[256,256]{1,0:T(8,128)}, f32[2,1024]{1,0:T(2,128)}, f32[1,1024]{1,0:T(1,128)}, f32[1024,256]{1,0:T(8,128)}, f32[1024,256]{1,0:T(8,128)}, /*index=5*/f32[16,256]{1,0:T(8,128)}, f32[16,256]{1,0:T(8,128)}) custom-call(bf16[256,3072]{1,0:T(8,128)(2,1)} %exchange_parts.9.grad_ref, bf16[3072,1024]{1,0:T(8,128)(2,1)} %bitcast.143, ...), custom_call_target="tpu_custom_call" | custom-call | flops 4026531840 | bytes 10485760 | tf_op jit(solution)/shard_map/entry_backward/pallas_call | solution.py:1090
  416.7 19.8 %branch_backward.3 = (bf16[256,1024]{1,0:T(8,128)(2,1)}, bf16[256,4096]{1,0:T(8,128)(2,1)}, f32[256,1024]{1,0:T(8,128)}, bf16[256,1024]{1,0:T(8,128)(2,1)}, bf16...) custom-call(f32[256,192]{1,0:T(8,128)} %get-tuple-element.266.dpred_ref, ...), custom_call_target="tpu_custom_call" | custom-call | flops 6039797760 | bytes 23068672 | tf_op jit(solution)/shard_map/branch_backward/pallas_call | solution.py:557
  443.2 8.1 %outer_other.3 = bf16[4,4,320,512]{3,2,1,0:T(8,128)(2,1)} custom-call(s32[3]{0:T(128)} %add_add_fusion.where_ref, bf16[256,1024]{1,0:T(8,128)(2,1)} %get-tuple-element.170.refs_0_, bf16[256,4096]{1,0:T(8,128)(2,1)} %get-tuple-element.171.refs_1_, bf16[256,1024]{1,0:T(8,128)(2,1)} %get-tuple-element.172.refs_2_, ...), custom_call_target="tpu_custom_call" | custom-call | flops 2684354560 | bytes 7864320 | tf_op jit(solution)/shard_map/outer_other/pallas_call | solution.py:667
  454.4 11.6 %exchange_parts.10.do_ref = bf16[2048,128]{1,0:T(8,128)(2,1)} custom-call(bf16[256,1024]{1,0:T(8,128)(2,1)} %get-tuple-element.176.x_ref), custom_call_target="tpu_custom_call" | custom-call | tf_op jit(solution)/shard_map/exchange_parts/pallas_call | solution.py:215
  482.3 9.2 %outer_own.3 = (bf16[4,2,320,512]{3,2,1,0:T(8,128)(2,1)}, bf16[4,2,320,512]{3,2,1,0:T(8,128)(2,1)}) custom-call(s32[3]{0:T(128)} %add_add_fusion.1.where_ref, bf16[256,1024]{1,0:T(8,128)(2,1)} %get-tuple-element.170.refs_0_, bf16[256,4096]{1,0:T(8,128)(2,1)} %get-tuple-element.171.refs_1_, bf16[256,1024]{1,0:T(8,128)(2,1)} %get-tuple-element.172.refs_2_, ...), custom_call_target="tpu_custom_call" | custom-call | flops 2684354560 | bytes 7864320 | tf_op jit(solution)/shard_map/outer_own/pallas_call | solution.py:677
  497.6 25.4 %attend_back.3 = (bf16[2048,128]{1,0:T(8,128)(2,1)}, bf16[2048,128]{1,0:T(8,128)(2,1)}, bf16[2048,128]{1,0:T(8,128)(2,1)}) custom-call(bf16[2048,128]{1,0:T(8,128)(2,1)} %get-tuple-element.262.q_ref, bf16[2048,128]{1,0:T(8,128)(2,1)} %exchange_parts.10.do_ref, f32[2048,128]{1,0:T(8,128)} %get-tuple-element.184.full_ref, ...), custom_call_target="tpu_custom_call" | custom-call | flops 21474836480 | bytes 4194304 | tf_op jit(solution)/shard_map/attend_back/pallas_call | solution.py:362
  526.5 36.7 %exchange_parts.11.grad_ref = bf16[256,3072]{1,0:T(8,128)(2,1)} custom-call(bf16[2048,384]{1,0:T(8,128)(2,1)} %pad_maximum_fusion.x_ref), custom_call_target="tpu_custom_call" | custom-call | tf_op jit(solution)/shard_map/exchange_parts/pallas_call | solution.py:215
  598.7 25.0 %entry_backward.3 = (f32[256,256]{1,0:T(8,128)}, f32[2,1024]{1,0:T(2,128)}, f32[1,1024]{1,0:T(1,128)}, f32[1024,256]{1,0:T(8,128)}, f32[1024,256]{1,0:T(8,128)}, /*index=5*/f32[16,256]{1,0:T(8,128)}, f32[16,256]{1,0:T(8,128)}) custom-call(bf16[256,3072]{1,0:T(8,128)(2,1)} %exchange_parts.11.grad_ref, bf16[3072,1024]{1,0:T(8,128)(2,1)} %bitcast.144, ...), custom_call_target="tpu_custom_call" | custom-call | flops 4026531840 | bytes 10485760 | tf_op jit(solution)/shard_map/entry_backward/pallas_call | solution.py:1090
  648.8 8.2 %collective-permute-done.19 = bf16[256,512]{1,0:T(8,128)(2,1)} collective-permute-done((bf16[256,512]{1,0:T(8,128)(2,1)}, bf16[256,512]{1,0:T(8,128)(2,1)}, u32[]{:S(2)}, u32[]{:S(2)}) %collective-permute-start.19) | collective-permute-done | bytes 262176 | tf_op jit(solution)/shard_map/ppermute | solution.py:704
  659.4 14.0 %collective-permute-done.14 = bf16[320,512]{1,0:T(8,128)(2,1)} collective-permute-done((bf16[320,512]{1,0:T(8,128)(2,1)}, bf16[320,512]{1,0:T(8,128)(2,1)}, u32[]{:S(2)}, u32[]{:S(2)}) %collective-permute-start.14) | collective-permute-done | bytes 327712 | tf_op jit(solution)/shard_map/ppermute | solution.py:704
  675.5 52.3 %exchange_sum.1 = (f32[512,1024]{1,0:T(8,128)}, f32[8,128]{1,0:T(8,128)}) custom-call(f32[512,1024]{1,0:T(8,128)} %table_grads.1.x_ref, f32[1,1]{1,0:T(1,128)} %bitcast.23.loss_ref, f32[256,384]{1,0:T(8,128)} %copy.107.qkv_ref.refs_4_, f32[320,512]{1,0:T(8,128)} %fusion.8.up_out_ref.refs_5_, f32[256,512]{1,0:T(8,128)} %fusion.19.down_ref.refs_6_), custom_call_target="tpu_custom_call" | custom-call | tf_op jit(solution)/shard_map/exchange_sum/pallas_call | solution.py:875
  727.8 12.2 %update_all.1 = (f32[1,1]{1,0:T(1,128)}, f32[1,1]{1,0:T(1,128)}, f32[440,1024]{1,0:T(8,128)}, f32[440,1024]{1,0:T(8,128)}, f32[440,1024]{1,0:T(8,128)}, /*index=...) custom-call(s32[1]{0:T(128)} %bitcast.refs_0_, ...), custom_call_target="tpu_custom_call" | custom-call | tf_op jit(solution)/shard_map/update_all/pallas_call | solution.py:1232
  (181 shorter events, 138.6 us)
Async XLA Ops:
  16.2 161.7 %copy-start.19 = (f32[1,2,256,192]{2,3,1,0:T(8,128)S(1)}, f32[1,2,256,192]{2,3,1,0:T(8,128)}, u32[]{:S(2)}) copy-start(f32[1,2,256,192]{2,3,1,0:T(8,128)} %param.25) | copy-start | bytes 1179652
  178.1 125.4 %collective-permute-start = (f32[2,256,192]{2,1,0:T(8,128)S(1)}, f32[2,256,192]{2,1,0:T(8,128)S(1)}, u32[]{:S(2)}, u32[]{:S(2)}) collective-permute-start(f32[2,256,192]{2,1,0:T(8,128)S(1)} %bitcast.138), channel_id=1, source_target_pairs={{0,0},{1,1},{2,8},{3,9},{4,16},{5,17},{6,24},{7,25},{8,2},{9,3},{1... | collective-permute-start | bytes 1179656 | tf_op jit(solution)/shard_map/ppermute | solution.py:85
  451.3 31.0 %collective-permute-start.2 = (bf16[4,4,320,512]{3,2,1,0:T(8,128)(2,1)}, bf16[4,4,320,512]{3,2,1,0:T(8,128)(2,1)}, u32[]{:S(2)}, u32[]{:S(2)}) collective-permute-start(bf16[4,4,320,512]{3,2,1,0:T(8,128)(2,1)} %outer_other.3), channel_id=1, source_target_pairs={{0,1},{1,0},{2,3},{3,2},{4,5},{5,4},{6,7},{7,6},{8,9},{9,8},{10,11... | collective-permute-start | bytes 15728648 | tf_op jit(solution)/shard_map/ppermute | solution.py:704
  451.4 23.2 %collective-permute-start.1 = (bf16[4,4,256,512]{3,2,1,0:T(8,128)(2,1)}, bf16[4,4,256,512]{3,2,1,0:T(8,128)(2,1)}, u32[]{:S(2)}, u32[]{:S(2)}) collective-permute-start(bf16[4,4,256,512]{3,2,1,0:T(8,128)(2,1)} %outer_other.2), channel_id=1, source_target_pairs={{0,1},{1,0},{2,3},{3,2},{4,5},{5,4},{6,7},{7,6},{8,9},{9,8},{10,11... | collective-permute-start | bytes 12582920 | tf_op jit(solution)/shard_map/ppermute | solution.py:704
  491.7 34.1 %collective-permute-start.3 = (bf16[2,2,256,512]{3,2,0,1:T(8,128)(2,1)S(1)}, bf16[2,2,256,512]{3,2,0,1:T(8,128)(2,1)S(1)}, u32[]{:S(2)}, u32[]{:S(2)}) collective-permute-start(bf16[2,2,256,512]{3,2,0,1:T(8,128)(2,1)S(1)} %get-tuple-element.254), channel_id=1, source_target_pairs={{0,8},{1,9},{2,10},{3,11},{4,12},{5,13},{6,14},{7,15},{8,0},{9,1},... | collective-permute-start | bytes 3145736 | tf_op jit(solution)/shard_map/ppermute | solution.py:704
  492.4 33.5 %collective-permute-start.4 = (bf16[2,2,256,512]{3,2,0,1:T(8,128)(2,1)S(1)}, bf16[2,2,256,512]{3,2,0,1:T(8,128)(2,1)S(1)}, u32[]{:S(2)}, u32[]{:S(2)}) collective-permute-start(bf16[2,2,256,512]{3,2,0,1:T(8,128)(2,1)S(1)} %get-tuple-element.253), channel_id=1, source_target_pairs={{0,16},{1,17},{2,18},{3,19},{4,20},{5,21},{6,22},{7,23},{8,24},{9,... | collective-permute-start | bytes 3145736 | tf_op jit(solution)/shard_map/ppermute | solution.py:704
  495.6 93.1 %collective-permute-start.5 = (bf16[2,2,320,512]{3,2,0,1:T(8,128)(2,1)}, bf16[2,2,320,512]{3,2,0,1:T(8,128)(2,1)}, u32[]{:S(2)}, u32[]{:S(2)}) collective-permute-start(bf16[2,2,320,512]{3,2,0,1:T(8,128)(2,1)} %get-tuple-element.247), channel_id=1, source_target_pairs={{0,8},{1,9},{2,10},{3,11},{4,12},{5,13},{6,14},{7,15},{8,0},{9,1},... | collective-permute-start | bytes 3932168 | tf_op jit(solution)/shard_map/ppermute | solution.py:704
  497.0 91.7 %collective-permute-start.6 = (bf16[2,2,320,512]{3,2,0,1:T(8,128)(2,1)}, bf16[2,2,320,512]{3,2,0,1:T(8,128)(2,1)}, u32[]{:S(2)}, u32[]{:S(2)}) collective-permute-start(bf16[2,2,320,512]{3,2,0,1:T(8,128)(2,1)} %get-tuple-element.246), channel_id=1, source_target_pairs={{0,16},{1,17},{2,18},{3,19},{4,20},{5,21},{6,22},{7,23},{8,24},{9,... | collective-permute-start | bytes 3932168 | tf_op jit(solution)/shard_map/ppermute | solution.py:704
  526.5 36.8 %copy-start.4 = (bf16[2048,384]{1,0:T(8,128)(2,1)S(1)}, bf16[2048,384]{1,0:T(8,128)(2,1)}, u32[]{:S(2)}) copy-start(bf16[2048,384]{1,0:T(8,128)(2,1)} %pad_maximum_fusion.x_ref) | copy-start | bytes 4718596
  526.5 36.8 %copy-start.29 = (f32[1024,384]{1,0:T(8,128)S(1)}, f32[1024,384]{1,0:T(8,128)}, u32[]{:S(2)}) copy-start(f32[1024,384]{1,0:T(8,128)} %fusion.65) | copy-start | bytes 4718596
  569.2 10.1 %collective-permute-start.7 = (bf16[256,384]{0,1:T(8,128)(2,1)S(1)}, bf16[256,384]{0,1:T(8,128)(2,1)}, u32[]{:S(2)}, u32[]{:S(2)}) collective-permute-start(bf16[256,384]{0,1:T(8,128)(2,1)S(1)} %bitcast.142), channel_id=1, source_target_pairs={{0,2},{1,3},{2,4},{3,5},{4,6},{5,7},{6,0},{7,1},{8,10},{9,11},{10,... | collective-permute-start | bytes 589832 | tf_op jit(solution)/shard_map/ppermute | solution.py:704
  569.7 14.8 %collective-permute-start.8 = (bf16[256,384]{0,1:T(8,128)(2,1)S(1)}, bf16[256,384]{0,1:T(8,128)(2,1)}, u32[]{:S(2)}, u32[]{:S(2)}) collective-permute-start(bf16[256,384]{0,1:T(8,128)(2,1)S(1)} %bitcast.141), channel_id=1, source_target_pairs={{0,4},{1,5},{2,6},{3,7},{4,0},{5,1},{6,2},{7,3},{8,12},{9,13},{10,... | collective-permute-start | bytes 589832 | tf_op jit(solution)/shard_map/ppermute | solution.py:704
  570.8 14.3 %collective-permute-start.9 = (bf16[256,384]{0,1:T(8,128)(2,1)S(1)}, bf16[256,384]{0,1:T(8,128)(2,1)}, u32[]{:S(2)}, u32[]{:S(2)}) collective-permute-start(bf16[256,384]{0,1:T(8,128)(2,1)S(1)} %bitcast.140), channel_id=1, source_target_pairs={{0,6},{1,7},{2,0},{3,1},{4,2},{5,3},{6,4},{7,5},{8,14},{9,15},{10,... | collective-permute-start | bytes 589832 | tf_op jit(solution)/shard_map/ppermute | solution.py:704
  579.3 45.7 %collective-permute-start.17 = (bf16[2,256,512]{2,1,0:T(8,128)(2,1)}, bf16[2,256,512]{2,1,0:T(8,128)(2,1)S(1)}, u32[]{:S(2)}, u32[]{:S(2)}) collective-permute-start(bf16[2,256,512]{2,1,0:T(8,128)(2,1)} %dynamic-slice_bitcast_fusion.2), channel_id=1, source_target_pairs={{0,8},{1,9},{2,10},{3,11},{4,12},{5,13},{6,14},{7,15},{8,0},{9,1},... | collective-permute-start | bytes 1572872 | tf_op jit(solution)/shard_map/ppermute | solution.py:704
  584.5 40.7 %collective-permute-start.16 = (bf16[2,256,512]{2,1,0:T(8,128)(2,1)S(1)}, bf16[2,256,512]{2,1,0:T(8,128)(2,1)}, u32[]{:S(2)}, u32[]{:S(2)}) collective-permute-start(bf16[2,256,512]{2,1,0:T(8,128)(2,1)S(1)} %dynamic-slice_bitcast_fusion.3), channel_id=1, source_target_pairs={{0,16},{1,17},{2,18},{3,19},{4,20},{5,21},{6,22},{7,23},{8,24},{9,... | collective-permute-start | bytes 1572872 | tf_op jit(solution)/shard_map/ppermute | solution.py:704
  587.1 47.9 %collective-permute-start.10 = (f32[256,384]{0,1:T(8,128)}, f32[256,384]{0,1:T(8,128)S(1)}, u32[]{:S(2)}, u32[]{:S(2)}) collective-permute-start(f32[256,384]{0,1:T(8,128)} %fusion.25), channel_id=1, source_target_pairs={{0,0},{1,1},{2,8},{3,9},{4,16},{5,17},{6,24},{7,25},{8,2},{9,3},{1... | collective-permute-start | bytes 1179656 | tf_op jit(solution)/shard_map/ppermute | solution.py:85
  591.3 38.0 %collective-permute-start.12 = (bf16[2,320,512]{2,1,0:T(8,128)(2,1)S(1)}, bf16[2,320,512]{2,1,0:T(8,128)(2,1)}, u32[]{:S(2)}, u32[]{:S(2)}) collective-permute-start(bf16[2,320,512]{2,1,0:T(8,128)(2,1)S(1)} %dynamic-slice_bitcast_fusion), channel_id=1, source_target_pairs={{0,8},{1,9},{2,10},{3,11},{4,12},{5,13},{6,14},{7,15},{8,0},{9,1},... | collective-permute-start | bytes 1966088 | tf_op jit(solution)/shard_map/ppermute | solution.py:704
  596.5 36.5 %collective-permute-start.11 = (bf16[2,320,512]{2,1,0:T(8,128)(2,1)S(1)}, bf16[2,320,512]{2,1,0:T(8,128)(2,1)S(1)}, u32[]{:S(2)}, u32[]{:S(2)}) collective-permute-start(bf16[2,320,512]{2,1,0:T(8,128)(2,1)S(1)} %dynamic-slice_bitcast_fusion.1), channel_id=1, source_target_pairs={{0,16},{1,17},{2,18},{3,19},{4,20},{5,21},{6,22},{7,23},{8,24},{9,... | collective-permute-start | bytes 1966088 | tf_op jit(solution)/shard_map/ppermute | solution.py:704
  627.9 11.2 %collective-permute-start.18 = (bf16[256,512]{1,0:T(8,128)(2,1)S(1)}, bf16[256,512]{1,0:T(8,128)(2,1)}, u32[]{:S(2)}, u32[]{:S(2)}) collective-permute-start(bf16[256,512]{1,0:T(8,128)(2,1)S(1)} %get-tuple-element.248), channel_id=1, source_target_pairs={{0,2},{1,3},{2,4},{3,5},{4,6},{5,7},{6,0},{7,1},{8,10},{9,11},{10,... | collective-permute-start | bytes 786440 | tf_op jit(solution)/shard_map/ppermute | solution.py:704
  628.7 28.4 %collective-permute-start.19 = (bf16[256,512]{1,0:T(8,128)(2,1)}, bf16[256,512]{1,0:T(8,128)(2,1)}, u32[]{:S(2)}, u32[]{:S(2)}) collective-permute-start(bf16[256,512]{1,0:T(8,128)(2,1)} %get-tuple-element.249), channel_id=1, source_target_pairs={{0,4},{1,5},{2,6},{3,7},{4,0},{5,1},{6,2},{7,3},{8,12},{9,13},{10,... | collective-permute-start | bytes 786440 | tf_op jit(solution)/shard_map/ppermute | solution.py:704
  629.3 27.8 %collective-permute-start.20 = (bf16[256,512]{1,0:T(8,128)(2,1)}, bf16[256,512]{1,0:T(8,128)(2,1)}, u32[]{:S(2)}, u32[]{:S(2)}) collective-permute-start(bf16[256,512]{1,0:T(8,128)(2,1)} %get-tuple-element.250), channel_id=1, source_target_pairs={{0,6},{1,7},{2,0},{3,1},{4,2},{5,3},{6,4},{7,5},{8,14},{9,15},{10,... | collective-permute-start | bytes 786440 | tf_op jit(solution)/shard_map/ppermute | solution.py:704
  634.4 25.0 %collective-permute-start.13 = (bf16[320,512]{1,0:T(8,128)(2,1)}, bf16[320,512]{1,0:T(8,128)(2,1)S(1)}, u32[]{:S(2)}, u32[]{:S(2)}) collective-permute-start(bf16[320,512]{1,0:T(8,128)(2,1)} %get-tuple-element.241), channel_id=1, source_target_pairs={{0,2},{1,3},{2,4},{3,5},{4,6},{5,7},{6,0},{7,1},{8,10},{9,11},{10,... | collective-permute-start | bytes 983048 | tf_op jit(solution)/shard_map/ppermute | solution.py:704
  634.9 38.4 %collective-permute-start.14 = (bf16[320,512]{1,0:T(8,128)(2,1)}, bf16[320,512]{1,0:T(8,128)(2,1)}, u32[]{:S(2)}, u32[]{:S(2)}) collective-permute-start(bf16[320,512]{1,0:T(8,128)(2,1)} %get-tuple-element.242), channel_id=1, source_target_pairs={{0,4},{1,5},{2,6},{3,7},{4,0},{5,1},{6,2},{7,3},{8,12},{9,13},{10,... | collective-permute-start | bytes 983048 | tf_op jit(solution)/shard_map/ppermute | solution.py:704
  639.1 34.2 %collective-permute-start.15 = (bf16[320,512]{1,0:T(8,128)(2,1)}, bf16[320,512]{1,0:T(8,128)(2,1)}, u32[]{:S(2)}, u32[]{:S(2)}) collective-permute-start(bf16[320,512]{1,0:T(8,128)(2,1)} %get-tuple-element.243), channel_id=1, source_target_pairs={{0,6},{1,7},{2,0},{3,1},{4,2},{5,3},{6,4},{7,5},{8,14},{9,15},{10,... | collective-permute-start | bytes 983048 | tf_op jit(solution)/shard_map/ppermute | solution.py:704
  (27 other events, 240.8 us)

commit v5 on v4

--- a/solution.py
+++ b/solution.py
@@ -293,23 +293,12 @@
     )(packed[:, :width], packed[:, width : 2 * width], packed[:, 2 * width :])
 
 
-def attend_back_kernel(
-    heads, q_ref, do_ref, full_ref, lse_ref, k_ref, v_ref, dq_ref, dk_ref, dv_ref, kt_ref, dk_sum, dv_sum
+def attend_back_rows(
+    heads, chunk, queries, grads, full, sums, k_ref, v_ref, kt_ref, dk_sum, dv_sum
 ):
-    step = pl.program_id(0)
     total = k_ref.shape[0]
-    chunk = min(1024, total)
-
-    @pl.when(step == 0)
-    def _():
-        kt_ref[...] = k_ref[...].T
-        dk_sum[...] = jnp.zeros_like(dk_sum)
-        dv_sum[...] = jnp.zeros_like(dv_sum)
-
     scale = HEAD_DIM**-0.5
-    queries = q_ref[...]
-    grads = do_ref[...]
-    products = (grads.astype(f32) * full_ref[...]).T
+    products = (grads.astype(f32) * full).T
     query_heads = [pick_head(queries, head, heads) for head in range(heads)]
     grad_heads = [pick_head(grads, head, heads) for head in range(heads)]
     inner = [
@@ -327,7 +316,7 @@
             scores = lax.dot_general(
                 keys, query_heads[head] * bf16(scale), NT, preferred_element_type=f32
             )
-            probs = jnp.exp(scores - lse_ref[head : head + 1, :])
+            probs = jnp.exp(scores - sums[head])
             prob_grad = lax.dot_general(
                 values, grad_heads[head] * bf16(scale), NT, preferred_element_type=f32
             )
@@ -345,7 +334,25 @@
         dv_sum[rows, :] += value_part
         dk_sum[rows, :] += key_part
     flipped = query_grads[0] if heads == 1 else jnp.concatenate(query_grads, axis=0)
-    dq_ref[...] = flipped.T.astype(bf16)
+    return flipped.T.astype(bf16)
+
+
+def attend_back_kernel(
+    heads, q_ref, do_ref, full_ref, lse_ref, k_ref, v_ref, dq_ref, dk_ref, dv_ref, kt_ref, dk_sum, dv_sum
+):
+    step = pl.program_id(0)
+
+    @pl.when(step == 0)
+    def _():
+        kt_ref[...] = k_ref[...].T
+        dk_sum[...] = jnp.zeros_like(dk_sum)
+        dv_sum[...] = jnp.zeros_like(dv_sum)
+
+    sums = [lse_ref[head : head + 1, :] for head in range(heads)]
+    dq_ref[...] = attend_back_rows(
+        heads, min(1024, k_ref.shape[0]), q_ref[...], do_ref[...], full_ref[...], sums,
+        k_ref, v_ref, kt_ref, dk_sum, dv_sum,
+    )
 
     @pl.when(step == pl.num_programs(0) - 1)
     def _():
@@ -433,7 +440,7 @@
     hidden = jnp.dot(h2_ref[...], up_ref[0], preferred_element_type=f32)
     g_ref[...] = hidden
     active = (hidden * gauss_share(hidden)).astype(bf16)
-    act_ref[...] = active
+    act_ref[0, 0] = active
     x2_ref[...] += jnp.dot(active, down_ref[...], preferred_element_type=f32)
 
     @pl.when(step == pl.num_programs(0) - 1)
@@ -460,6 +467,7 @@
     parts, units = w_up.shape[0], w_up.shape[2]
     fixed = lambda shape: pl.BlockSpec(shape, lambda i: (0, 0))
     by_units = pl.BlockSpec((rows, units), lambda i: (0, i))
+    by_core = pl.BlockSpec((1, 1, rows, units), lambda i: (i % 2, i // 2, 0, 0))
     columns = head.shape[0]
     flops = 2 * rows * (width * width + 2 * width * parts * units + 6 * width * columns)
     return pl.pallas_call(
@@ -469,7 +477,7 @@
             jax.ShapeDtypeStruct((rows, width), f32),
             jax.ShapeDtypeStruct((rows, width), bf16),
             jax.ShapeDtypeStruct((rows, parts * units), f32),
-            jax.ShapeDtypeStruct((rows, parts * units), bf16),
+            jax.ShapeDtypeStruct((2, parts // 2, rows, units), bf16),
             jax.ShapeDtypeStruct((rows, width), f32),
             jax.ShapeDtypeStruct((rows, columns), f32),
         ),
@@ -484,7 +492,7 @@
             fixed((rows, width)),
             fixed((rows, width)),
             by_units,
-            by_units,
+            by_core,
             fixed((rows, width)),
             fixed((rows, columns)),
         ],
@@ -529,7 +537,7 @@
         jnp.exp(-0.5 * hidden * hidden) * (2.0 * math.pi) ** -0.5
     )
     hidden_grad = (active_grad * slope).astype(bf16)
-    dg_ref[...] = hidden_grad
+    dg_ref[0, 0] = hidden_grad
     sum_ref[...] += lax.dot_general(hidden_grad, up_ref[0], NT, preferred_element_type=f32)
 
     @pl.when(step == pl.num_programs(0) - 1)
@@ -551,6 +559,7 @@
     parts, units = w_up.shape[0], w_up.shape[2]
     fixed = lambda shape: pl.BlockSpec(shape, lambda i: (0, 0))
     by_units = pl.BlockSpec((rows, units), lambda i: (0, i))
+    by_core = pl.BlockSpec((1, 1, rows, units), lambda i: (i % 2, i // 2, 0, 0))
     columns = head.shape[0]
     wide = (rows, width)
     flops = 2 * rows * (width * width + 2 * width * parts * units + 12 * width * columns)
@@ -559,7 +568,7 @@
         grid=(parts,),
         out_shape=(
             jax.ShapeDtypeStruct(wide, bf16),
-            jax.ShapeDtypeStruct((rows, parts * units), bf16),
+            jax.ShapeDtypeStruct((2, parts // 2, rows, units), bf16),
             jax.ShapeDtypeStruct(wide, f32),
             jax.ShapeDtypeStruct(wide, bf16),
             jax.ShapeDtypeStruct(wide, bf16),
@@ -577,7 +586,7 @@
         ],
         out_specs=[
             fixed(wide),
-            by_units,
+            by_core,
             fixed(wide),
             fixed(wide),
             fixed(wide),
@@ -595,156 +604,469 @@
     )(pred_grad, x_last, x_mid, norm_gains, hidden, w_out, w_up, w_down, head)
 
 
-def wide_piece(piece):
-    half = piece.shape[0] // 2
-    return jnp.concatenate((piece[:half], piece[half:]), axis=1)
-
-
-def tall_piece(piece):
-    half = piece.shape[1] // 2
-    return jnp.concatenate((piece[:, :half], piece[:, half:]), axis=0)
-
-
-def both_steps(left_a, right_a, left_b, right_b):
-    product = lax.dot_general(left_a[...], right_a[...], TN, preferred_element_type=f32)
-    return product + lax.dot_general(left_b[...], right_b[...], TN, preferred_element_type=f32)
-
-
-def down_pieces(refs):
-    product = both_steps(*refs)
-    share = product.shape[1] // 4
-    return [wide_piece(product[:, i * share : (i + 1) * share]) for i in range(4)]
-
-
-def up_out_pieces(refs):
-    up = both_steps(*refs[:4])
-    share = up.shape[0] // 4
-    out = both_steps(*refs[4:])
-    size = out.shape[1] // 4
-    return [
-        jnp.concatenate(
-            (up[i * share : (i + 1) * share], wide_piece(out[:, i * size : (i + 1) * size])), axis=0
-        )
-        for i in range(4)
+def plane_parts(me):
+    return [(move, lax.rem(me + move, 8)) for move in (7, 6, 5, 4, 3, 2, 1)]
+
+
+def swap_kernel(*refs):
+    value_ref, act_ref, dg_ref, o_ref, dx2_ref, h2_ref, dx1_ref = refs[:7]
+    rows_ref, act_out, dg_out, o_out, dx2_out, h2_out, dx1_out = refs[7:14]
+    send_sem, recv_sem, own_sem = refs[14:]
+    dp, level, core = mesh_place()
+    me = dp * 2 + core
+    rows, width = value_ref.shape[0], value_ref.shape[1] // 8
+    near = device_of(dp, level, 1 - core)
+    barrier = pltpu.get_barrier_semaphore()
+    others = [
+        (part, device_of(part // 2, level, lax.rem(part, 2))) for _, part in plane_parts(me)
     ]
-
-
-def outer_other_kernel(make, count, where_ref, *refs):
-    o_ref = refs[count]
-    for split, piece in enumerate(make(refs[:count])):
-        o_ref[0, split] = piece.astype(bf16)
-
-
-def outer_own_kernel(make, count, where_ref, *refs):
-    other_ref, send_ref, keep_ref, held_ref = refs[count:]
-    for split, piece in enumerate(make(refs[:count])):
-        held_ref[split] = (piece + other_ref[0, split].astype(f32)).astype(bf16)
-    x, y = where_ref[1], where_ref[2]
-    early = pl.program_id(0) < 2
-    for which in range(2):
-        send_ref[0, which] = held_ref[jnp.where(early, which * 2 + 1 - x, (1 - y) * 2 + which)]
-        keep_ref[0, which] = held_ref[jnp.where(early, which * 2 + x, y * 2 + which)]
-
-
-def outer_half(operands, make, height, where, other):
-    specs = []
-    for value, blocked in operands:
-        rows, size = value.shape
-        if blocked:
-            specs.append(pl.BlockSpec((rows, size // 8), lambda i, w: (0, i * 2 + w[0])))
-        else:
-            specs.append(pl.BlockSpec((rows, size), lambda i, w: (0, 0)))
-    values = [value for value, _ in operands]
-    count = len(values)
-    whole = pl.BlockSpec((1, 4, height, 512), lambda i, w: (i, 0, 0, 0))
-    half = pl.BlockSpec((1, 2, height, 512), lambda i, w: (i, 0, 0, 0))
-    rows = values[0].shape[0]
-    cost = pl.CostEstimate(
-        flops=2 * 2 * rows * 16 * height * 512, bytes_accessed=3 * 16 * height * 512, transcendentals=0
+    for _, target in others:
+        pl.semaphore_signal(barrier, inc=1, device_id=target, device_id_type=MESH)
+    pl.semaphore_wait(barrier, 7)
+    started = []
+
+    def send(source, target_ref, target):
+        slot = len(started)
+        copy = pltpu.make_async_remote_copy(
+            src_ref=source,
+            dst_ref=target_ref,
+            send_sem=send_sem.at[slot],
+            recv_sem=recv_sem.at[slot],
+            device_id=target,
+            device_id_type=MESH,
+        )
+        copy.start()
+        started.append(copy)
+
+    def row_block(part):
+        return rows_ref.at[pl.ds(pl.multiple_of(part * rows, rows), rows), :]
+
+    def column_block(ref, part):
+        return ref.at[:, pl.ds(pl.multiple_of(part * width, width), width)]
+
+    for part, target in others:
+        send(column_block(value_ref, part), row_block(me), target)
+    locals_ = []
+
+    def keep(source, target_ref):
+        copy = pltpu.make_async_copy(source, target_ref, own_sem.at[len(locals_)])
+        copy.start()
+        locals_.append(copy)
+
+    for source, out in ((act_ref, act_out), (dg_ref, dg_out)):
+        send(source.at[1 - core], out.at[1], near)
+        keep(source.at[core], out.at[0])
+    for index in range(4):
+        send(column_block(o_ref, index * 2 + 1 - core), o_out.at[1, index], near)
+        keep(column_block(o_ref, index * 2 + core), o_out.at[0, index])
+    for source, out in ((dx2_ref, dx2_out), (h2_ref, h2_out), (dx1_ref, dx1_out)):
+        send(source, out, near)
+    row_block(me)[...] = column_block(value_ref, me)[...]
+    for copy in started:
+        copy.wait()
+    for copy in locals_:
+        copy.wait()
+
+
+def exchange_swap(value, act, dg, attended, dx2, h2, dx1):
+    rows, width = value.shape
+    anywhere = pl.BlockSpec(memory_space=pl.ANY)
+    outs = [
+        (8 * rows, width // 8), act.shape, dg.shape, (2, 4, rows, width // 8),
+        dx2.shape, h2.shape, dx1.shape,
+    ]
+    return pl.pallas_call(
+        swap_kernel,
+        out_shape=[jax.ShapeDtypeStruct(shape, bf16) for shape in outs],
+        in_specs=[VMEM] * 7,
+        out_specs=[VMEM] + [anywhere] * 6,
+        scratch_shapes=[
+            pltpu.SemaphoreType.DMA((16,)),
+            pltpu.SemaphoreType.DMA((16,)),
+            pltpu.SemaphoreType.DMA((6,)),
+        ],
+        compiler_params=pltpu.CompilerParams(
+            collective_id=3, has_side_effects=True, vmem_limit_bytes=BIG
+        ),
+        name="exchange_swap",
+    )(value, act, dg, attended, dx2, h2, dx1)
+
+
+wait_one, wait_two, pieces_at = 2, 4, 9
+turns = 14
+
+
+def finish_kernel(*refs):
+    steps = (refs[0:9], refs[9:18])
+    qkv_ref, do_ref, full_ref, lse_ref, rows_ref, prev_ref = refs[18:24]
+    token_out, share_ref, down_ref, up_out_ref = refs[24:28]
+    (dqkv_ref, kt_ref, dk_sum, dv_sum, held_ref, send_a, keep_a, one_a, two_a, own_a, deep_a,
+     send_b, keep_b, one_b, two_b, own_b, deep_b, piece_send, piece_recv, piece_own, landing_ref,
+     one_send, one_recv, two_send, two_recv, deep_send, deep_recv, part_send, part_recv,
+     piece_send_sem, piece_recv_sem, cross_sem, own_sem) = refs[28:]
+    groups = (
+        (send_a, keep_a, one_a, two_a, own_a, deep_a, down_ref),
+        (send_b, keep_b, one_b, two_b, own_b, deep_b, up_out_ref),
     )
-    params = pltpu.CompilerParams(vmem_limit_bytes=BIG)
-    if other is None:
-        return pl.pallas_call(
-            partial(outer_other_kernel, make, count),
-            out_shape=jax.ShapeDtypeStruct((4, 4, height, 512), bf16),
-            grid_spec=pltpu.PrefetchScalarGridSpec(
-                num_scalar_prefetch=1, grid=(4,), in_specs=specs, out_specs=whole
-            ),
-            compiler_params=params,
-            cost_estimate=cost,
-            name="outer_other",
-        )(where, *values)
+    turn = pl.program_id(0)
+    dp, level, core = mesh_place()
+    me = dp * 2 + core
+    x, y = lax.rem(dp, 2), dp // 2
+    side, down = dp + 1 - 2 * x, lax.rem(dp + 2, 4)
+    across = device_of(level, dp, core)
+    width = do_ref.shape[1]
+    heads = width // HEAD_DIM
+    rows = do_ref.shape[0] // 8
+    others = [
+        (move, part, device_of(part // 2, level, lax.rem(part, 2))) for move, part in plane_parts(me)
+    ]
+
+    def remote(source, target_ref, send_sem, recv_sem, target):
+        return pltpu.make_async_remote_copy(
+            src_ref=source,
+            dst_ref=target_ref,
+            send_sem=send_sem,
+            recv_sem=recv_sem,
+            device_id=target,
+            device_id_type=MESH,
+        )
+
+    def place_of(index):
+        depth = lax.rem(index, 2) * 2 + index // 2
+        early = 1 - depth // 2
+        return depth, early
+
+    def first_copy(group, index):
+        send_ref, _, one_ref = groups[group][:3]
+        depth, early = place_of(index)
+        slot = index * 2 + group
+        target = device_of(early * side + (1 - early) * down, level, core)
+        return remote(
+            send_ref.at[depth], one_ref.at[depth], one_send.at[slot], one_recv.at[slot], target
+        )
+
+    def second_copy(group, index):
+        _, keep_ref, _, two_ref = groups[group][:4]
+        depth, early = place_of(index)
+        slot = index * 2 + group
+        which = early * (1 - y) + (1 - early) * (1 - x)
+        target = device_of(early * down + (1 - early) * side, level, core)
+        return remote(
+            keep_ref.at[depth, which], two_ref.at[depth], two_send.at[slot], two_recv.at[slot], target
+        )
+
+    def deep_copy(group, index):
+        _, keep_ref, _, _, _, deep_ref = groups[group][:6]
+        depth, early = place_of(index)
+        slot = index * 2 + group
+        which = early * y + (1 - early) * x
+        place = lax.rem(level + 7 - depth, 4)
+        return remote(
+            keep_ref.at[depth, which],
+            deep_ref.at[place],
+            deep_send.at[slot],
+            deep_recv.at[group * 4 + place],
+            device_of(dp, depth, core),
+        )
+
+    def part_copy(move, part, target):
+        return remote(
+            dqkv_ref.at[pl.ds(pl.multiple_of(part * rows, rows), rows), :],
+            token_out.at[:, pl.ds(pl.multiple_of(me * 3 * width, 3 * width), 3 * width)],
+            part_send.at[move],
+            part_recv.at[move],
+            target,
+        )
+
+    def piece_copy(index):
+        place = lax.rem(level + 7 - index, 4)
+        return remote(
+            piece_send.at[index],
+            piece_recv.at[place],
+            piece_send_sem.at[index],
+            piece_recv_sem.at[place],
+            device_of(dp, index, core),
+        )
+
+    own_part = pltpu.make_async_copy(
+        dqkv_ref.at[pl.ds(pl.multiple_of(me * rows, rows), rows), :],
+        token_out.at[:, pl.ds(pl.multiple_of(me * 3 * width, 3 * width), 3 * width)],
+        own_sem,
+    )
+    crossing = remote(piece_own, landing_ref, cross_sem.at[0], cross_sem.at[1], across)
+
+    @pl.when(turn == 0)
+    def _():
+        barrier = pltpu.get_barrier_semaphore()
+        deep = [device_of(dp, lax.rem(level + move, 4), core) for move in (1, 2, 3)]
+        for target in [target for _, _, target in others] + deep:
+            pl.semaphore_signal(barrier, inc=1, device_id=target, device_id_type=MESH)
+
+        @pl.when(dp != level)
+        def _():
+            pl.semaphore_signal(barrier, inc=1, device_id=across, device_id_type=MESH)
+            pl.semaphore_wait(barrier, 11)
+
+        @pl.when(dp == level)
+        def _():
+            pl.semaphore_wait(barrier, 10)
+
+        kt_ref[...] = qkv_ref[:, width : 2 * width].T
+        dk_sum[...] = jnp.zeros_like(dk_sum)
+        dv_sum[...] = jnp.zeros_like(dv_sum)
+
+    def summed(lefts, rights):
+        total = None
+        for left, right in zip(lefts, rights):
+            part = lax.dot_general(left, right, TN, preferred_element_type=f32)
+            total = part if total is None else total + part
+        return total
+
+    for group in range(2):
+        send_ref, keep_ref, one_ref, two_ref, own_ref, deep_ref, _ = groups[group]
+        height = keep_ref.shape[2]
+
+        @pl.when((lax.rem(turn + group, 2) == 0) & (turn < 8))
+        def _(group=group, send_ref=send_ref, keep_ref=keep_ref, height=height):
+            index = turn // 2
+            depth, early = place_of(index)
+            lefts, rights, smalls, wides = [], [], [], []
+            for act, dg, o, dx2, dx2_near, h2, h2_near, dx1, dx1_near in steps:
+                for source in range(2):
+                    if group == 0:
+                        lefts.append(act[source, 0])
+                        rights.append((dx2, dx2_near)[source][...])
+                    else:
+                        lefts.append(dg[source, 0])
+                        rights.append((h2, h2_near)[source][...])
+                        smalls.append(o[source, 0])
+                        wides.append((dx1, dx1_near)[source][...])
+            size = rights[0].shape[1] // 4
+            tops = summed(lefts, rights)
+            for split in range(4):
+                held_ref[split, : tops.shape[0], :] = tops[:, split * size : (split + 1) * size].astype(bf16)
+            if group == 1:
+                ends = summed(smalls, wides)
+                for split in range(4):
+                    held_ref[split, tops.shape[0] : height, :] = ends[
+                        :, split * size : (split + 1) * size
+                    ].astype(bf16)
+            for which in range(2):
+                moved = early * (which * 2 + 1 - x) + (1 - early) * ((1 - y) * 2 + which)
+                stays = early * (which * 2 + x) + (1 - early) * (y * 2 + which)
+                send_ref[depth, which] = held_ref[moved, :height, :]
+                keep_ref[depth, which] = held_ref[stays, :height, :]
+            first_copy(group, index).start()
+
+        after = turn - wait_one
+
+        @pl.when((lax.rem(after + 8 + group, 2) == 0) & (after >= 0) & (after < 8))
+        def _(group=group, keep_ref=keep_ref, one_ref=one_ref):
+            index = after // 2
+            depth, _ = place_of(index)
+            first_copy(group, index).wait_recv()
+            for which in range(2):
+                keep_ref[depth, which] = (
+                    keep_ref[depth, which].astype(f32) + one_ref[depth, which].astype(f32)
+                ).astype(bf16)
+            second_copy(group, index).start()
+
+        later = turn - wait_two
+
+        @pl.when((lax.rem(later + 8 + group, 2) == 0) & (later >= 0) & (later < 8))
+        def _(group=group, keep_ref=keep_ref, two_ref=two_ref, own_ref=own_ref):
+            index = later // 2
+            depth, early = place_of(index)
+            second_copy(group, index).wait_recv()
+            which = early * y + (1 - early) * x
+            total = keep_ref[depth, which].astype(f32) + two_ref[depth].astype(f32)
+
+            @pl.when(depth == level)
+            def _():
+                own_ref[...] = total
+
+            @pl.when(depth != level)
+            def _():
+                keep_ref[depth, which] = total.astype(bf16)
+                deep_copy(group, index).start()
+
+    @pl.when(turn < 8)
+    def _():
+        where = pl.ds(pl.multiple_of(turn * rows, rows), rows)
+        sums = [lse_ref[head : head + 1, where] for head in range(heads)]
+        dqkv_ref[where, :width] = attend_back_rows(
+            heads, 512, qkv_ref[where, :width], do_ref[where, :], full_ref[where, :], sums,
+            qkv_ref.at[:, width : 2 * width], qkv_ref.at[:, 2 * width :], kt_ref, dk_sum, dv_sum,
+        )
+
+    @pl.when(turn == 8)
+    def _():
+        dqkv_ref[:, width : 2 * width] = dk_sum[...].astype(bf16)
+        dqkv_ref[:, 2 * width :] = dv_sum[...].astype(bf16)
+        for other in others:
+            part_copy(*other).start()
+        own_part.start()
+
+    for index in range(4):
+
+        @pl.when(turn == pieces_at + index)
+        def _(index=index):
+            piece = prev_ref[...] + lax.dot_general(
+                rows_ref[...], dqkv_ref[...], TN, preferred_element_type=f32
+            )
+
+            @pl.when(level == index)
+            def _():
+                piece_own[...] = piece
+
+            @pl.when(level != index)
+            def _():
+                piece_send[index] = piece.astype(bf16)
+                piece_copy(index).start()
+
+    @pl.when(turn == turns - 1)
+    def _():
+        for place in range(3):
+            remote(
+                piece_send.at[0], piece_recv.at[place], piece_send_sem.at[0],
+                piece_recv_sem.at[place], across,
+            ).wait_recv()
+        piece_own[...] += (
+            piece_recv[0].astype(f32) + piece_recv[1].astype(f32) + piece_recv[2].astype(f32)
+        )
+
+        @pl.when(dp != level)
+        def _():
+            crossing.start()
+
+        for group in range(2):
+            _, keep_ref, _, _, own_ref, deep_ref, result_ref = groups[group]
+            for place in range(3):
+                remote(
+                    keep_ref.at[0, 0], deep_ref.at[place], deep_send.at[0],
+                    deep_recv.at[group * 4 + place], across,
+                ).wait_recv()
+            result_ref[...] = own_ref[...] + (
+                deep_ref[0].astype(f32) + deep_ref[1].astype(f32) + deep_ref[2].astype(f32)
+            )
+        for other in others:
+            part_copy(*other).wait()
+        own_part.wait()
+        for index in range(4):
+            depth = (index % 2) * 2 + index // 2
+            for group in range(2):
+                first_copy(group, index).wait_send()
+                second_copy(group, index).wait_send()
+
+                @pl.when(depth != level)
+                def _(group=group, index=index):
+                    deep_copy(group, index).wait_send()
+
+            @pl.when(level != index)
+            def _(index=index):
+                piece_copy(index).wait_send()
+
+        @pl.when(dp != level)
+        def _():
+            crossing.wait()
+            share_ref[...] = landing_ref[...]
+
+        @pl.when(dp == level)
+        def _():
+            share_ref[...] = piece_own[...]
+
+
+def finish_program(kept, packed, own_grad, full, logsum, rows_one, earlier):
+    rows, width = own_grad.shape[0] // 8, own_grad.shape[1]
+    once = lambda shape: pl.BlockSpec(
+        shape, lambda i: (0,) * len(shape), pipeline_mode=pl.Buffered(1)
+    )
+
+    def chunk(shape):
+        def where(i):
+            index = jnp.minimum(i // 2, 3)
+            return 0, lax.rem(index, 2) * 2 + index // 2, 0, 0
+
+        return pl.BlockSpec((2, 1) + shape, where)
+
+    in_specs, operands = [], []
+    for act, dg, o, dx2, dx2_near, h2, h2_near, dx1, dx1_near in kept:
+        operands += [act, dg, o, dx2, dx2_near, h2, h2_near, dx1, dx1_near]
+        in_specs += [chunk(act.shape[2:]), chunk(dg.shape[2:]), chunk(o.shape[2:])]
+        in_specs += [once(dx2.shape)] * 6
+    piece = lambda i: jnp.clip(i - pieces_at, 0, 3)
+    in_specs += [
+        once(packed.shape),
+        once(own_grad.shape),
+        once(full.shape),
+        once(logsum.shape),
+        pl.BlockSpec((8 * rows, D // 4), lambda i: (0, piece(i))),
+        pl.BlockSpec((D // 4, 3 * width), lambda i: (piece(i), 0)),
+    ]
+    operands += [packed, own_grad, full, logsum, rows_one, earlier]
+    fixed = lambda shape: pl.BlockSpec(shape, lambda i: (0, 0))
+    units = kept[0][0].shape[3]
+    heights = (units, units + width)
+    share = D // 4
+    scratch = [
+        pltpu.VMEM((8 * rows, 3 * width), bf16),
+        pltpu.VMEM((width, 8 * rows), bf16),
+        pltpu.VMEM((8 * rows, width), f32),
+        pltpu.VMEM((8 * rows, width), f32),
+        pltpu.VMEM((4, heights[1], share), bf16),
+    ]
+    for height in heights:
+        scratch += [
+            pltpu.VMEM((4, 2, height, share), bf16),
+            pltpu.VMEM((4, 2, height, share), bf16),
+            pltpu.VMEM((4, 2, height, share), bf16),
+            pltpu.VMEM((4, height, share), bf16),
+            pltpu.VMEM((height, share), f32),
+            pltpu.VMEM((3, height, share), bf16),
+        ]
+    scratch += [
+        pltpu.VMEM((4, share, 3 * width), bf16),
+        pltpu.VMEM((3, share, 3 * width), bf16),
+        pltpu.VMEM((share, 3 * width), f32),
+        pltpu.VMEM((share, 3 * width), f32),
+    ]
+    scratch += [pltpu.SemaphoreType.DMA((8,))] * 8
+    scratch += [
+        pltpu.SemaphoreType.DMA((4,)),
+        pltpu.SemaphoreType.DMA((4,)),
+        pltpu.SemaphoreType.DMA((2,)),
+        pltpu.SemaphoreType.DMA,
+    ]
     return pl.pallas_call(
-        partial(outer_own_kernel, make, count),
-        out_shape=(jax.ShapeDtypeStruct((4, 2, height, 512), bf16),) * 2,
-        grid_spec=pltpu.PrefetchScalarGridSpec(
-            num_scalar_prefetch=1,
-            grid=(4,),
-            in_specs=specs + [whole],
-            out_specs=[half, half],
-            scratch_shapes=[pltpu.VMEM((4, height, 512), bf16)],
+        finish_kernel,
+        grid=(turns,),
+        out_shape=[
+            jax.ShapeDtypeStruct((rows, 24 * width), bf16),
+            jax.ShapeDtypeStruct((share, 3 * width), f32),
+            jax.ShapeDtypeStruct((heights[0], share), f32),
+            jax.ShapeDtypeStruct((heights[1], share), f32),
+        ],
+        in_specs=in_specs,
+        out_specs=[
+            pl.BlockSpec(memory_space=pl.ANY),
+            fixed((share, 3 * width)),
+            fixed((heights[0], share)),
+            fixed((heights[1], share)),
+        ],
+        scratch_shapes=scratch,
+        compiler_params=pltpu.CompilerParams(
+            collective_id=4, has_side_effects=True, vmem_limit_bytes=60 * 2**20
         ),
-        compiler_params=params,
-        cost_estimate=cost,
-        name="outer_own",
-    )(where, *values, other)
-
-
-def device_pairs(move):
-    pairs = []
-    for dp in range(4):
-        for level in range(4):
-            for core in range(2):
-                to_dp, to_level, to_core = move(dp, level, core)
-                pairs.append(((dp * 4 + level) * 2 + core, (to_dp * 4 + to_level) * 2 + to_core))
-    return pairs
-
-
-def shift(value, move):
-    return lax.ppermute(value, ("dp", "mp"), device_pairs(move))
-
-
-def to_core(dp, level, core):
-    return dp, level, 1 - core
-
-
-def to_side(dp, level, core):
-    return dp ^ 1, level, core
-
-
-def to_down(dp, level, core):
-    return dp ^ 2, level, core
+        name="finish_program",
+    )(*operands)
+
+
+def tie(*values):
+    return lax.optimization_barrier(values)
 
 
 def choose(value, index, axis=0):
     return lax.dynamic_index_in_dim(value, index, axis, keepdims=False)
-
-
-def sum_levels(pieces, level):
-    total = choose(pieces, level).astype(f32)
-    for step in range(1, 4):
-        piece = choose(pieces, lax.rem(level + step, 4)).astype(bf16)
-        moved = shift(piece, lambda dp, z, core: (dp, (z + step) % 4, core))
-        total = total + moved.astype(f32)
-    return total
-
-
-def tie(*values):
-    return lax.optimization_barrier(values)
-
-
-def first_sums(send, keep):
-    first = keep[:2].astype(f32) + shift(send[:2], to_side).astype(f32)
-    second = keep[2:].astype(f32) + shift(send[2:], to_down).astype(f32)
-    return first.astype(bf16), second.astype(bf16)
-
-
-def second_sums(first, second, x, y):
-    first_moved = shift(choose(first, 1 - y, 1), to_down)
-    second_moved = shift(choose(second, 1 - x, 1), to_side)
-    first = choose(first, y, 1).astype(f32) + first_moved.astype(f32)
-    second = choose(second, x, 1).astype(f32) + second_moved.astype(f32)
-    return jnp.concatenate((first, second))
 
 
 def outer_plain(lefts, rights, by_rows):
@@ -1199,9 +1521,9 @@
     apply(1, sums_ref[embed_rows : embed_rows + 2, :], lr_gain, slice(0, 2))
     apply(1, sums_ref[padded + 4 * V : padded + 4 * V + 4, :], lr_gain, slice(2, 6))
     if packed:
-        up_out = shares[1]
+        units = shares[2].shape[0]
         grads = (
-            shares[0][...], tall_piece(up_out[256:, :]), up_out[:256, :], tall_piece(shares[2][...])
+            shares[0][...], shares[1][units:, :], shares[1][:units, :].T, shares[2][...]
         )
     else:
         grads = [share[...] for share in shares]
@@ -1645,15 +1967,6 @@
     )(packed, keyed, bias, patch, variable, lead_table, norm_gains, *shards)
 
 
-def own_qkv_share(crossed, grad):
-    dp = lax.axis_size("dp")
-    rows = grad.shape[0] // dp
-    if not crossed:
-        return lax.psum_scatter(grad, "dp", scatter_dimension=0, tiled=True)
-    _, level, _ = mesh_place()
-    return cross(crossed, sum_levels(grad.reshape((dp, rows) + grad.shape[1:]), level))
-
-
 def shards(
     crossed,
     fields,
@@ -1769,12 +2082,6 @@
     qkv_grad = jnp.zeros((D, qkv_local.shape[0]), f32)
     kept = []
 
-    def sources(index, other, blocked):
-        listed = []
-        for step in kept:
-            listed += [(step[index], blocked), (step[other], not blocked)]
-        return listed
-
     for rollout in (1, 0):
         (cells, x_first, rows_one, packed, full, logsum, attended, x_mid, rows_two,
          hidden, active, x_last, loss_grad) = records[rollout]
@@ -1783,36 +2090,29 @@
         )
         head_total = head_total + head_grad
         gain_high = gain_high + gain_part[2:]
-        kept.append((attended, rows_two, active, mid_low, hidden_grad, last_low))
-        last_turn = crossed and rollout == 0
-        if last_turn:
-            listed = (
-                (sources(2, 5, True), down_pieces, 256),
-                (sources(1, 4, False) + sources(0, 3, True), up_out_pieces, 320),
+        if crossed:
+            (
+                own_grad, act_both, dg_both, o_both, dx2_near, h2_near, dx1_near
+            ) = exchange_swap(
+                out_grad, active, hidden_grad, attended, last_low, rows_two, mid_low
             )
-            x, y = lax.rem(place, 2), place // 2
-            where = lambda which: jnp.stack((which, x, y)).astype(jnp.int32)
-            others = [outer_half(*group, where(1 - core), None) for group in listed]
-            out_grad, *others = tie(out_grad, *others)
-            others = [shift(other, to_core) for other in others]
-        own_grad = exchange(crossed, out_grad, False, 3)
-        if last_turn:
-            halves = []
-            for group, other in zip(listed, others):
-                halves += outer_half(*group, where(core), other)
-            own_grad, *halves = tie(own_grad, *halves)
-            sums = [first_sums(*halves[:2]), first_sums(*halves[2:])]
-        packed_grad = attend_back(own_grad, packed, full, logsum)
-        if last_turn:
-            packed_grad, *sums[0] = tie(packed_grad, *sums[0])
-            down_pieces_sum = second_sums(*sums[0], x, y)
-        token_grad = exchange(crossed, packed_grad, True, 4)
-        if last_turn:
-            token_grad, *sums[1] = tie(token_grad, *sums[1])
-            up_out_sum = second_sums(*sums[1], x, y)
-        qkv_grad = qkv_grad + lax.dot_general(
-            rows_one, packed_grad, TN, preferred_element_type=f32
-        )
+            kept.append(
+                (act_both, dg_both, o_both, last_low, dx2_near, rows_two, h2_near, mid_low, dx1_near)
+            )
+        else:
+            flat = lambda value: value.transpose(2, 1, 0, 3).reshape(shard_rows, -1)
+            kept.append((attended, rows_two, flat(active), mid_low, flat(hidden_grad), last_low))
+            own_grad = exchange(crossed, out_grad, False, 3)
+        if crossed and rollout == 0:
+            token_grad, qkv_share, down_sum, up_out_sum = finish_program(
+                kept, packed, own_grad, full, logsum, rows_one, qkv_grad
+            )
+        else:
+            packed_grad = attend_back(own_grad, packed, full, logsum)
+            token_grad = exchange(crossed, packed_grad, True, 4 + 4)
+            qkv_grad = qkv_grad + lax.dot_general(
+                rows_one, packed_grad, TN, preferred_element_type=f32
+            )
         cells_grad, gain_one, lead_sum, *table_part = entry_backward(
             token_grad, gathered[3], x_first, mid_grad, norm_gains, cells, prepared
         )
@@ -1831,10 +2131,12 @@
     last_rows = table_grads(
         *table_parts, prepared, query, var_hot, lead_hots, lead_rows, gain_low, head_total, gain_high
     )
-    qkv_share = by_head(own_qkv_share(crossed, qkv_grad))
+    if not crossed:
+        qkv_share = lax.psum_scatter(qkv_grad, "dp", scatter_dimension=0, tiled=True)
+    qkv_share = by_head(qkv_share)
     where = dp_index.astype(jnp.int32).reshape(1)
     if crossed:
-        shares = (qkv_share, sum_levels(up_out_sum, level), sum_levels(down_pieces_sum, level))
+        shares = (qkv_share, up_out_sum, down_sum)
         last_sum, tile = exchange_sum(last_rows, loss_part, *shares)
         masters = (w_qkv, w_out, w_up, w_down)
     else:

time: 745 us -> 744 us (level)
  Pallas kernels: 601 us -> 689 us
  waiting for transfers between devices: 32.8 us -> 0.01 us
  starting transfers between devices: 26.9 us -> 0.69 us
  other arithmetic: 33.4 us -> 15.2 us
    pallas_call x4 -> x3, Pallas kernels: 31.8 us -> 172 us  [the longest x1 144 us: finish_program(): pl.pallas_call(finish_kernel, grid=(turns,), out_shape=[jax.ShapeDtypeStr...]
    pallas_call x6 -> x3, Pallas kernels: 107 us -> 47.4 us  [exchange(): pl.pallas_call(partial(exchange_kernel, to_columns, rows, width), out_sha...]
    pallas_call x1, Pallas kernels: 52.3 us -> 85.8 us  [exchange_sum(): pl.pallas_call(exchange_sum_kernel, out_shape=(jax.ShapeDtypeStruct(value...]
    ppermute x19 -> x0, waiting for transfers between devices: 32.8 us -> none  [shift(): return lax.ppermute(value, ('dp', 'mp'), device_pairs(move))]
    pallas_call x2 -> x1, Pallas kernels: 50.8 us -> 25.5 us  [attend_back(): pl.pallas_call(partial(attend_back_kernel, heads), grid=(total // block,)...]
    ppermute x19 -> x0, starting transfers between devices: 24.5 us -> none  [shift(): return lax.ppermute(value, ('dp', 'mp'), device_pairs(move))]
    add x7 -> x0, other arithmetic: 9.57 us -> none  [the longest x3 6.37 us: sum_levels(): total = total + moved.astype(f32)]
  transfers between devices with their start and end apart: 21 -> 1, of which waited for: 5 -> 0; matrix products, arithmetic and copies ran while one was open for 7% -> 2% of each run, Pallas kernels for 30% -> 14%
where the time goes in v5:
time: 744 us; the launch traced here: 740 us
  Pallas kernels  689 us (93%)
  local copies, waits for them, and re-layouts  19.5 us (3%)
  other arithmetic  15.2 us (2%)
  matrix products  9.87 us (1%)
    pallas_call x1, Pallas kernels, start_program(): pl.pallas_call(partial(start_kernel, halves), grid=(groups * 3 + lag_two,...  150 us
    pallas_call x1, Pallas kernels, finish_program(): pl.pallas_call(finish_kernel, grid=(turns,), out_shape=[jax.ShapeDtypeStr...  144 us
    pallas_call x1, Pallas kernels, exchange_sum(): pl.pallas_call(exchange_sum_kernel, out_shape=(jax.ShapeDtypeStruct(value...  85.8 us
    pallas_call x2, Pallas kernels, entry_backward(): pl.pallas_call(entry_back_kernel, grid=(HEADS // 2,), out_shape=(jax.Shap...  49.9 us
    pallas_call x3, Pallas kernels, exchange(): pl.pallas_call(partial(exchange_kernel, to_columns, rows, width), out_sha...  47.4 us
    pallas_call x2, Pallas kernels, branch_backward(): pl.pallas_call(branch_back_kernel, grid=(parts,), out_shape=(jax.ShapeDty...  39.6 us
    pallas_call x2, Pallas kernels, branch_forward(): pl.pallas_call(branch_kernel, grid=(parts,), out_shape=(jax.ShapeDtypeStr...  35.3 us
    pallas_call x1, Pallas kernels, spread_rows(): pl.pallas_call(gather_kernel, out_shape=jax.ShapeDtypeStruct((8 * rows, w...  27.8 us
  transfers between devices with their start and end apart: 1, of which 0 were waited for; matrix products, arithmetic and copies ran while one was open for 2% of the time, Pallas kernels for 14%

profile of v5, /device:TPU:0, one launch (start us, length us, event | category | flops | bytes accessed | tf_op | source)
XLA Modules:
  0.0 739.6 jit_solution(13793756120989253518)
XLA Ops:
  3.4 4.9 prepare_tables.1
  15.4 149.8 %start_program.1 = (f32[256,1024]{1,0:T(8,128)}, f32[256,256]{1,0:T(8,128)}, bf16[2048,384]{1,0:T(8,128)(2,1)}, bf16[2048,128]{1,0:T(8,128)(2,1)}, f32[2048,128]...) custom-call(f32[256,256]{1,0:T(8,128)} %maximum_maximum_fusion.refs_, ...), custom_call_target="tpu_custom_call" | custom-call | tf_op jit(solution)/shard_map/start_program/pallas_call | solution.py:1939
  165.2 11.5 %exchange_parts.3.o_ref.refs_3_ = bf16[256,1024]{1,0:T(8,128)(2,1)} custom-call(bf16[2048,128]{1,0:T(8,128)(2,1)} %get-tuple-element.131.x_ref), custom_call_target="tpu_custom_call" | custom-call | tf_op jit(solution)/shard_map/exchange_parts/pallas_call | solution.py:215
  180.6 17.4 %branch_forward.2 = (f32[256,1024]{1,0:T(8,128)}, bf16[256,1024]{1,0:T(8,128)(2,1)}, f32[256,4096]{1,0:T(8,128)}, bf16[2,4,256,512]{3,2,1,0:T(8,128)(2,1)}, f32[256,1024]{1,0:T(8,128)}, /*index=5*/f32[256,192]{1,0:T(8,128)}) custom-call(bf16[256,1024]{1,0:T(8,128)(2,1)} %exchange_parts.3.o_ref.refs_3_, f32[256,1024]{1,0:T(8,128)} %get-tuple-element.133.x0_ref, ...), custom_call_target="tpu_custom_call" | custom-call | flops 5435817984 | bytes 23068672 | tf_op jit(solution)/shard_map/branch_forward/pallas_call | solution.py:473
  203.1 15.7 %embed_forward.1 = (f32[256,1024]{1,0:T(8,128)}, bf16[256,1024]{1,0:T(8,128)(2,1)}) custom-call(f32[256,256]{1,0:T(8,128)} %pad.14.u_ref, f32[16,256]{1,0:T(8,128)} %get-tuple-element.127.refs_1_.keyed_ref, f32[16,256]{1,0:T(8,128)} %get-tuple-element.128.refs_2_.bias_ref, f32[256,1024]{1,0:T(8,128)} %get-tuple-element.129.refs_3_.patch_ref, ...), custom_call_target="tpu_custom_call" | custom-call | flops 1610612736 | bytes 3670016 | tf_op jit(solution)/shard_map/embed_forward/pallas_call | solution.py:1329
  218.8 27.8 %gather_rows.1 = bf16[2048,1024]{1,0:T(8,128)(2,1)} custom-call(bf16[256,1024]{1,0:T(8,128)(2,1)} %get-tuple-element.139.x_ref), custom_call_target="tpu_custom_call" | custom-call | tf_op jit(solution)/shard_map/gather_rows/pallas_call | solution.py:153
  246.6 4.8 convolution_convert_fusion
  252.6 16.2 %attend.1 = (bf16[2048,128]{1,0:T(8,128)(2,1)}, f32[2048,128]{1,0:T(8,128)}, f32[2,2048]{1,0:T(2,128)}) custom-call(bf16[2048,128]{1,0:T(8,128)(2,1)} %get-tuple-element.239.q_ref, bf16[2048,128]{1,0:T(8,128)(2,1)} %get-tuple-element.238.k_ref, bf16[2048,128]{1,0:T(8,128)(2,1)} %get-tuple-element.237.v_ref), custom_call_target="tpu_custom_call" | custom-call | flops 8589934592 | bytes 2621440 | tf_op jit(solution)/shard_map/attend/pallas_call | solution.py:271
  268.8 11.9 %exchange_parts.4.o_ref.refs_3_ = bf16[256,1024]{1,0:T(8,128)(2,1)} custom-call(bf16[2048,128]{1,0:T(8,128)(2,1)} %get-tuple-element.141.x_ref), custom_call_target="tpu_custom_call" | custom-call | tf_op jit(solution)/shard_map/exchange_parts/pallas_call | solution.py:215
  284.7 17.9 %branch_forward.3 = (f32[256,1024]{1,0:T(8,128)}, bf16[256,1024]{1,0:T(8,128)(2,1)}, f32[256,4096]{1,0:T(8,128)}, bf16[2,4,256,512]{3,2,1,0:T(8,128)(2,1)}, f32[256,1024]{1,0:T(8,128)}, /*index=5*/f32[256,192]{1,0:T(8,128)}) custom-call(bf16[256,1024]{1,0:T(8,128)(2,1)} %exchange_parts.4.o_ref.refs_3_, f32[256,1024]{1,0:T(8,128)} %get-tuple-element.142.x0_ref, ...), custom_call_target="tpu_custom_call" | custom-call | flops 5435817984 | bytes 23068672 | tf_op jit(solution)/shard_map/branch_forward/pallas_call | solution.py:473
  304.3 19.8 %branch_backward.2 = (bf16[256,1024]{1,0:T(8,128)(2,1)}, bf16[2,4,256,512]{3,2,1,0:T(8,128)(2,1)}, f32[256,1024]{1,0:T(8,128)}, bf16[256,1024]{1,0:T(8,128)(2,1)...) custom-call(f32[256,192]{1,0:T(8,128)} %multiply_divide_fusion.dpred_ref, ...), custom_call_target="tpu_custom_call" | custom-call | flops 6039797760 | bytes 23068672 | tf_op jit(solution)/shard_map/branch_backward/pallas_call | solution.py:566
  324.2 13.7 %exchange_swap.2 = (bf16[2048,128]{1,0:T(8,128)(2,1)}, bf16[2,4,256,512]{3,2,1,0:T(8,128)(2,1)}, bf16[2,4,256,512]{3,2,1,0:T(8,128)(2,1)}, bf16[2,4,256,128]{3,2...) custom-call(bf16[256,1024]{1,0:T(8,128)(2,1)} %get-tuple-element.149.refs_0_, ...), custom_call_target="tpu_custom_call" | custom-call | tf_op jit(solution)/shard_map/exchange_swap/pallas_call | solution.py:678
  337.9 25.5 %attend_back.1 = (bf16[2048,128]{1,0:T(8,128)(2,1)}, bf16[2048,128]{1,0:T(8,128)(2,1)}, bf16[2048,128]{1,0:T(8,128)(2,1)}) custom-call(bf16[2048,128]{1,0:T(8,128)(2,1)} %get-tuple-element.239.q_ref, bf16[2048,128]{1,0:T(8,128)(2,1)} %get-tuple-element.155.do_ref, f32[2048,128]{1,0:T(8,128)} %get-tuple-element.156.full_ref, ...), custom_call_target="tpu_custom_call" | custom-call | flops 21474836480 | bytes 4194304 | tf_op jit(solution)/shard_map/attend_back/pallas_call | solution.py:369
  367.1 23.9 %exchange_parts.5.grad_ref = bf16[256,3072]{1,0:T(8,128)(2,1)} custom-call(bf16[2048,384]{1,0:T(8,128)(2,1)} %copy-done.3), custom_call_target="tpu_custom_call" | custom-call | tf_op jit(solution)/shard_map/exchange_parts/pallas_call | solution.py:215
  391.1 4.9 fusion.32.refs_23_
  396.0 24.9 %entry_backward.2 = (f32[256,256]{1,0:T(8,128)}, f32[2,1024]{1,0:T(2,128)}, f32[1,1024]{1,0:T(1,128)}, f32[1024,256]{1,0:T(8,128)}, f32[1024,256]{1,0:T(8,128)}, /*index=5*/f32[16,256]{1,0:T(8,128)}, f32[16,256]{1,0:T(8,128)}) custom-call(bf16[256,3072]{1,0:T(8,128)(2,1)} %exchange_parts.5.grad_ref, bf16[3072,1024]{1,0:T(8,128)(2,1)} %bitcast.68, ...), custom_call_target="tpu_custom_call" | custom-call | flops 4026531840 | bytes 10485760 | tf_op jit(solution)/shard_map/entry_backward/pallas_call | solution.py:1412
  420.9 2.4 fusion.3
  423.2 19.8 %branch_backward.3 = (bf16[256,1024]{1,0:T(8,128)(2,1)}, bf16[2,4,256,512]{3,2,1,0:T(8,128)(2,1)}, f32[256,1024]{1,0:T(8,128)}, bf16[256,1024]{1,0:T(8,128)(2,1)...) custom-call(f32[256,192]{1,0:T(8,128)} %get-tuple-element.240.dpred_ref, ...), custom_call_target="tpu_custom_call" | custom-call | flops 6039797760 | bytes 23068672 | tf_op jit(solution)/shard_map/branch_backward/pallas_call | solution.py:566
  443.0 13.6 %exchange_swap.3 = (bf16[2048,128]{1,0:T(8,128)(2,1)}, bf16[2,4,256,512]{3,2,1,0:T(8,128)(2,1)}, bf16[2,4,256,512]{3,2,1,0:T(8,128)(2,1)}, bf16[2,4,256,128]{3,2...) custom-call(bf16[256,1024]{1,0:T(8,128)(2,1)} %get-tuple-element.173.refs_0_, ...), custom_call_target="tpu_custom_call" | custom-call | tf_op jit(solution)/shard_map/exchange_swap/pallas_call | solution.py:678
  456.7 144.2 %finish_program.1 = (bf16[256,3072]{1,0:T(8,128)(2,1)}, f32[256,384]{1,0:T(8,128)}, f32[512,256]{1,0:T(8,128)}, f32[640,256]{1,0:T(8,128)}) custom-call(bf16[2,4,256,512]{3,2,1,0:T(8,128)(2,1)} %get-tuple-element.163.refs_0_, bf16[2,4,256,512]{3,2,1,0:T(8,128)(2,1)} %get-tuple-element.164.refs_1_, bf16[2,4,256,128]{3,2,1,0:T(8,128)(2,1)} %get-tuple-element.165.refs_2_, ...), custom_call_target="tpu_custom_call" | custom-call | tf_op jit(solution)/shard_map/finish_program/pallas_call | solution.py:1040
  606.2 25.1 %entry_backward.3 = (f32[256,256]{1,0:T(8,128)}, f32[2,1024]{1,0:T(2,128)}, f32[1,1024]{1,0:T(1,128)}, f32[1024,256]{1,0:T(8,128)}, f32[1024,256]{1,0:T(8,128)}, /*index=5*/f32[16,256]{1,0:T(8,128)}, f32[16,256]{1,0:T(8,128)}) custom-call(bf16[256,3072]{1,0:T(8,128)(2,1)} %get-tuple-element.190.grad_ref, bf16[3072,1024]{1,0:T(8,128)(2,1)} %bitcast.69, ...), custom_call_target="tpu_custom_call" | custom-call | flops 4026531840 | bytes 10485760 | tf_op jit(solution)/shard_map/entry_backward/pallas_call | solution.py:1412
  633.9 7.2 table_grads.1.x_ref
  641.1 85.8 %exchange_sum.1 = (f32[512,1024]{1,0:T(8,128)}, f32[8,128]{1,0:T(8,128)}) custom-call(f32[512,1024]{1,0:T(8,128)} %table_grads.1.x_ref, f32[1,1]{1,0:T(1,128)} %bitcast.19.loss_ref, f32[256,384]{1,0:T(8,128)} %copy.78.qkv_ref.refs_4_, f32[640,256]{1,0:T(8,128)} %get-tuple-element.208.up_out_ref.refs_5_, f32[512,256]{1,0:T(8,128)} %get-tuple-element.209.down_ref.refs_6_), custom_call_target="tpu_custom_call" | custom-call | tf_op jit(solution)/shard_map/exchange_sum/pallas_call | solution.py:1197
  726.9 12.2 %update_all.1 = (f32[1,1]{1,0:T(1,128)}, f32[1,1]{1,0:T(1,128)}, f32[440,1024]{1,0:T(8,128)}, f32[440,1024]{1,0:T(8,128)}, f32[440,1024]{1,0:T(8,128)}, /*index=...) custom-call(s32[1]{0:T(128)} %bitcast.refs_0_, ...), custom_call_target="tpu_custom_call" | custom-call | tf_op jit(solution)/shard_map/update_all/pallas_call | solution.py:1554
  (87 shorter events, 33.2 us)
Async XLA Ops:
  8.3 2.8 copy-start
  10.1 2.1 copy-start.1
  12.2 1.2 copy-start.11
  12.2 1.3 copy-start.16
  12.2 1.5 copy-start.18
  12.2 1.6 copy-start.4
  15.4 161.3 %copy-start.10 = (f32[1,2,256,192]{2,3,1,0:T(8,128)S(1)}, f32[1,2,256,192]{2,3,1,0:T(8,128)}, u32[]{:S(2)}) copy-start(f32[1,2,256,192]{2,3,1,0:T(8,128)} %param.25) | copy-start | bytes 1179652
  176.9 125.7 %collective-permute-start = (f32[2,256,192]{2,1,0:T(8,128)S(1)}, f32[2,256,192]{2,1,0:T(8,128)S(1)}, u32[]{:S(2)}, u32[]{:S(2)}) collective-permute-start(f32[2,256,192]{2,1,0:T(8,128)S(1)} %bitcast.67), channel_id=1, source_target_pairs={{0,0},{1,1},{2,8},{3,9},{4,16},{5,17},{6,24},{7,25},{8,2},{9,3},{1... | collective-permute-start | bytes 1179656 | tf_op jit(solution)/shard_map/ppermute | solution.py:85
  180.6 19.1 %copy-start.12 = (f32[256,256]{1,0:T(8,128)S(1)}, f32[256,256]{1,0:T(8,128)}, u32[]{:S(2)}) copy-start(f32[256,256]{1,0:T(8,128)} %get-tuple-element.138.u_ref) | copy-start | bytes 786436
  363.4 2.4 copy-start.9
  365.8 25.3 %copy-start.2 = (bf16[2048,1024]{1,0:T(8,128)(2,1)S(1)}, bf16[2048,1024]{1,0:T(8,128)(2,1)}, u32[]{:S(2)}) copy-start(bf16[2048,1024]{1,0:T(8,128)(2,1)} %gather_rows.1) | copy-start | bytes 12582916
  365.9 1.1 copy-start.3
  396.0 24.9 %copy-start.5 = (f32[256,192]{1,0:T(8,128)S(1)}, f32[256,192]{1,0:T(8,128)}, u32[]{:S(2)}) copy-start(f32[256,192]{1,0:T(8,128)} %get-tuple-element.137) | copy-start | bytes 589828
  396.0 24.9 %copy-start.6 = (f32[256,192]{1,0:T(8,128)S(1)}, f32[256,192]{1,0:T(8,128)}, u32[]{:S(2)}) copy-start(f32[256,192]{1,0:T(8,128)} %get-tuple-element.143) | copy-start | bytes 589828
  600.9 3.6 copy-start.13
  600.9 3.6 copy-start.14
  600.9 4.2 copy-start.7
  600.9 4.2 copy-start.8
  606.2 25.1 %copy-start.15 = (f32[2,1024]{1,0:T(2,128)S(1)}, f32[2,1024]{1,0:T(2,128)}, u32[]{:S(2)}) copy-start(f32[2,1024]{1,0:T(2,128)} %get-tuple-element.201) | copy-start | bytes 24580
  606.2 26.4 %copy-start.17 = (f32[1,1024]{1,0:T(1,128)S(1)}, f32[1,1024]{1,0:T(1,128)}, u32[]{:S(2)}) copy-start(f32[1,1024]{1,0:T(1,128)} %get-tuple-element.200) | copy-start | bytes 12292

commit v6 on v5

--- a/solution.py
+++ b/solution.py
@@ -692,28 +692,158 @@
     )(value, act, dg, attended, dx2, h2, dx1)
 
 
-wait_one, wait_two, pieces_at = 2, 4, 9
-turns = 14
+class Scatter:
+    order = (0, 3, 1, 2)
+
+    def __init__(self, refs, sems):
+        self.send_ref, self.keep_ref, self.one_ref, self.two_ref, self.own_ref, self.deep_ref = refs
+        self.one, self.two, self.deep = sems
+        self.dp, self.level, self.core = mesh_place()
+        self.x, self.y = lax.rem(self.dp, 2), self.dp // 2
+        self.side = device_of(self.dp + 1 - 2 * self.x, self.level, self.core)
+        self.down = device_of(lax.rem(self.dp + 2, 4), self.level, self.core)
+
+    def copy(self, source, target_ref, sems, slot, place, target):
+        return pltpu.make_async_remote_copy(
+            src_ref=source,
+            dst_ref=target_ref,
+            send_sem=sems.at[0, slot],
+            recv_sem=sems.at[1, place],
+            device_id=target,
+            device_id_type=MESH,
+        )
+
+    def first(self, depth):
+        target = self.side if depth < 2 else self.down
+        return self.copy(
+            self.send_ref.at[depth], self.one_ref.at[depth], self.one, depth, depth, target
+        )
+
+    def second(self, depth):
+        target = self.down if depth < 2 else self.side
+        which = 1 - self.y if depth < 2 else 1 - self.x
+        return self.copy(
+            self.keep_ref.at[depth, which], self.two_ref.at[depth], self.two, depth, depth, target
+        )
+
+    def mine(self, depth):
+        return self.y if depth < 2 else self.x
+
+    def third(self, depth):
+        place = lax.rem(self.level + 7 - depth, 4)
+        return self.copy(
+            self.keep_ref.at[depth, self.mine(depth)], self.deep_ref.at[place], self.deep, depth,
+            place, device_of(self.dp, depth, self.core),
+        )
+
+    def begin(self, depth, products, held_ref):
+        height = self.keep_ref.shape[2]
+        top = 0
+        for product in products:
+            rows, size = product.shape[0], product.shape[1] // 4
+            for split in range(4):
+                held_ref[split, top : top + rows, :] = product[
+                    :, split * size : (split + 1) * size
+                ].astype(bf16)
+            top += rows
+        for which in range(2):
+            if depth < 2:
+                moved, stays = which * 2 + 1 - self.x, which * 2 + self.x
+            else:
+                moved, stays = (1 - self.y) * 2 + which, self.y * 2 + which
+            self.send_ref[depth, which] = held_ref[moved, :height, :]
+            self.keep_ref[depth, which] = held_ref[stays, :height, :]
+        self.first(depth).start()
+
+    def middle(self, depth):
+        self.first(depth).wait_recv()
+        for which in range(2):
+            self.keep_ref[depth, which] = (
+                self.keep_ref[depth, which].astype(f32) + self.one_ref[depth, which].astype(f32)
+            ).astype(bf16)
+        self.second(depth).start()
+
+    def end(self, depth):
+        self.second(depth).wait_recv()
+        total = self.keep_ref[depth, self.mine(depth)].astype(f32) + self.two_ref[depth].astype(f32)
+
+        @pl.when(self.level == depth)
+        def _():
+            self.own_ref[...] = total
+
+        @pl.when(self.level != depth)
+        def _():
+            self.keep_ref[depth, self.mine(depth)] = total.astype(bf16)
+            self.third(depth).start()
+
+    def finish(self, result_ref):
+        for place in range(3):
+            self.copy(
+                self.keep_ref.at[0, 0], self.deep_ref.at[place], self.deep, 0, place, self.side
+            ).wait_recv()
+        result_ref[...] = self.own_ref[...] + (
+            self.deep_ref[0].astype(f32) + self.deep_ref[1].astype(f32) + self.deep_ref[2].astype(f32)
+        )
+        for depth in range(4):
+            self.first(depth).wait_send()
+            self.second(depth).wait_send()
+
+            @pl.when(self.level != depth)
+            def _(depth=depth):
+                self.third(depth).wait_send()
+
+
+def scatter_scratch(height, share):
+    return [
+        pltpu.VMEM((4, 2, height, share), bf16),
+        pltpu.VMEM((4, 2, height, share), bf16),
+        pltpu.VMEM((4, 2, height, share), bf16),
+        pltpu.VMEM((4, height, share), bf16),
+        pltpu.VMEM((height, share), f32),
+        pltpu.VMEM((3, height, share), bf16),
+        pltpu.VMEM((4, height, share), bf16),
+        pltpu.SemaphoreType.DMA((2, 4)),
+        pltpu.SemaphoreType.DMA((2, 4)),
+        pltpu.SemaphoreType.DMA((2, 4)),
+    ]
+
+
+def summed(lefts, rights):
+    total = None
+    for left, right in zip(lefts, rights):
+        part = lax.dot_general(left, right, TN, preferred_element_type=f32)
+        total = part if total is None else total + part
+    return total
+
+
+def chunk_spec(shape):
+    def where(i):
+        index = jnp.minimum(i, 3)
+        first, last = (3 - index) // 3, index // 3
+        middle = 1 - first - last
+        return 0, middle * (5 - 2 * index) + 2 * last, 0, 0
+
+    return pl.BlockSpec((2, 1) + shape, where)
+
+
+def once(shape):
+    return pl.BlockSpec(shape, lambda i: (0,) * len(shape), pipeline_mode=pl.Buffered(1))
+
+
+pieces_at, turns, entry_turns = 9, 14, 11
 
 
 def finish_kernel(*refs):
-    steps = (refs[0:9], refs[9:18])
-    qkv_ref, do_ref, full_ref, lse_ref, rows_ref, prev_ref = refs[18:24]
-    token_out, share_ref, down_ref, up_out_ref = refs[24:28]
-    (dqkv_ref, kt_ref, dk_sum, dv_sum, held_ref, send_a, keep_a, one_a, two_a, own_a, deep_a,
-     send_b, keep_b, one_b, two_b, own_b, deep_b, piece_send, piece_recv, piece_own, landing_ref,
-     one_send, one_recv, two_send, two_recv, deep_send, deep_recv, part_send, part_recv,
-     piece_send_sem, piece_recv_sem, cross_sem, own_sem) = refs[28:]
-    groups = (
-        (send_a, keep_a, one_a, two_a, own_a, deep_a, down_ref),
-        (send_b, keep_b, one_b, two_b, own_b, deep_b, up_out_ref),
-    )
+    steps = (refs[0:3], refs[3:6])
+    qkv_ref, do_ref, full_ref, lse_ref, rows_ref, prev_ref = refs[6:12]
+    token_out, share_ref, down_ref = refs[12:15]
+    dqkv_ref, kt_ref, dk_sum, dv_sum, piece_send, piece_recv, piece_own = refs[15:22]
+    part_sem, piece_sem, own_sem = refs[22:25]
+    scatter = Scatter(refs[25:31], refs[32:35])
+    held_ref = refs[31]
     turn = pl.program_id(0)
     dp, level, core = mesh_place()
     me = dp * 2 + core
-    x, y = lax.rem(dp, 2), dp // 2
-    side, down = dp + 1 - 2 * x, lax.rem(dp + 2, 4)
-    across = device_of(level, dp, core)
     width = do_ref.shape[1]
     heads = width // HEAD_DIM
     rows = do_ref.shape[0] // 8
@@ -731,69 +861,24 @@
             device_id_type=MESH,
         )
 
-    def place_of(index):
-        depth = lax.rem(index, 2) * 2 + index // 2
-        early = 1 - depth // 2
-        return depth, early
-
-    def first_copy(group, index):
-        send_ref, _, one_ref = groups[group][:3]
-        depth, early = place_of(index)
-        slot = index * 2 + group
-        target = device_of(early * side + (1 - early) * down, level, core)
-        return remote(
-            send_ref.at[depth], one_ref.at[depth], one_send.at[slot], one_recv.at[slot], target
-        )
-
-    def second_copy(group, index):
-        _, keep_ref, _, two_ref = groups[group][:4]
-        depth, early = place_of(index)
-        slot = index * 2 + group
-        which = early * (1 - y) + (1 - early) * (1 - x)
-        target = device_of(early * down + (1 - early) * side, level, core)
-        return remote(
-            keep_ref.at[depth, which], two_ref.at[depth], two_send.at[slot], two_recv.at[slot], target
-        )
-
-    def deep_copy(group, index):
-        _, keep_ref, _, _, _, deep_ref = groups[group][:6]
-        depth, early = place_of(index)
-        slot = index * 2 + group
-        which = early * y + (1 - early) * x
-        place = lax.rem(level + 7 - depth, 4)
-        return remote(
-            keep_ref.at[depth, which],
-            deep_ref.at[place],
-            deep_send.at[slot],
-            deep_recv.at[group * 4 + place],
-            device_of(dp, depth, core),
-        )
+    def own_rows(part):
+        return dqkv_ref.at[pl.ds(pl.multiple_of(part * rows, rows), rows), :]
+
+    own_columns = token_out.at[:, pl.ds(pl.multiple_of(me * 3 * width, 3 * width), 3 * width)]
 
     def part_copy(move, part, target):
         return remote(
-            dqkv_ref.at[pl.ds(pl.multiple_of(part * rows, rows), rows), :],
-            token_out.at[:, pl.ds(pl.multiple_of(me * 3 * width, 3 * width), 3 * width)],
-            part_send.at[move],
-            part_recv.at[move],
-            target,
+            own_rows(part), own_columns, part_sem.at[0, move], part_sem.at[1, move], target
         )
 
     def piece_copy(index):
         place = lax.rem(level + 7 - index, 4)
         return remote(
-            piece_send.at[index],
-            piece_recv.at[place],
-            piece_send_sem.at[index],
-            piece_recv_sem.at[place],
-            device_of(dp, index, core),
-        )
-
-    own_part = pltpu.make_async_copy(
-        dqkv_ref.at[pl.ds(pl.multiple_of(me * rows, rows), rows), :],
-        token_out.at[:, pl.ds(pl.multiple_of(me * 3 * width, 3 * width), 3 * width)],
-        own_sem,
-    )
-    crossing = remote(piece_own, landing_ref, cross_sem.at[0], cross_sem.at[1], across)
+            piece_send.at[index], piece_recv.at[place], piece_sem.at[0, index],
+            piece_sem.at[1, place], device_of(dp, index, core),
+        )
+
+    own_part = pltpu.make_async_copy(own_rows(me), own_columns, own_sem)
 
     @pl.when(turn == 0)
     def _():
@@ -801,101 +886,35 @@
         deep = [device_of(dp, lax.rem(level + move, 4), core) for move in (1, 2, 3)]
         for target in [target for _, _, target in others] + deep:
             pl.semaphore_signal(barrier, inc=1, device_id=target, device_id_type=MESH)
-
-        @pl.when(dp != level)
-        def _():
-            pl.semaphore_signal(barrier, inc=1, device_id=across, device_id_type=MESH)
-            pl.semaphore_wait(barrier, 11)
-
-        @pl.when(dp == level)
-        def _():
-            pl.semaphore_wait(barrier, 10)
-
+        pl.semaphore_wait(barrier, 10)
         kt_ref[...] = qkv_ref[:, width : 2 * width].T
         dk_sum[...] = jnp.zeros_like(dk_sum)
         dv_sum[...] = jnp.zeros_like(dv_sum)
 
-    def summed(lefts, rights):
-        total = None
-        for left, right in zip(lefts, rights):
-            part = lax.dot_general(left, right, TN, preferred_element_type=f32)
-            total = part if total is None else total + part
-        return total
-
-    for group in range(2):
-        send_ref, keep_ref, one_ref, two_ref, own_ref, deep_ref, _ = groups[group]
-        height = keep_ref.shape[2]
-
-        @pl.when((lax.rem(turn + group, 2) == 0) & (turn < 8))
-        def _(group=group, send_ref=send_ref, keep_ref=keep_ref, height=height):
-            index = turn // 2
-            depth, early = place_of(index)
-            lefts, rights, smalls, wides = [], [], [], []
-            for act, dg, o, dx2, dx2_near, h2, h2_near, dx1, dx1_near in steps:
-                for source in range(2):
-                    if group == 0:
-                        lefts.append(act[source, 0])
-                        rights.append((dx2, dx2_near)[source][...])
-                    else:
-                        lefts.append(dg[source, 0])
-                        rights.append((h2, h2_near)[source][...])
-                        smalls.append(o[source, 0])
-                        wides.append((dx1, dx1_near)[source][...])
-            size = rights[0].shape[1] // 4
-            tops = summed(lefts, rights)
-            for split in range(4):
-                held_ref[split, : tops.shape[0], :] = tops[:, split * size : (split + 1) * size].astype(bf16)
-            if group == 1:
-                ends = summed(smalls, wides)
-                for split in range(4):
-                    held_ref[split, tops.shape[0] : height, :] = ends[
-                        :, split * size : (split + 1) * size
-                    ].astype(bf16)
-            for which in range(2):
-                moved = early * (which * 2 + 1 - x) + (1 - early) * ((1 - y) * 2 + which)
-                stays = early * (which * 2 + x) + (1 - early) * (y * 2 + which)
-                send_ref[depth, which] = held_ref[moved, :height, :]
-                keep_ref[depth, which] = held_ref[stays, :height, :]
-            first_copy(group, index).start()
-
-        after = turn - wait_one
-
-        @pl.when((lax.rem(after + 8 + group, 2) == 0) & (after >= 0) & (after < 8))
-        def _(group=group, keep_ref=keep_ref, one_ref=one_ref):
-            index = after // 2
-            depth, _ = place_of(index)
-            first_copy(group, index).wait_recv()
-            for which in range(2):
-                keep_ref[depth, which] = (
-                    keep_ref[depth, which].astype(f32) + one_ref[depth, which].astype(f32)
-                ).astype(bf16)
-            second_copy(group, index).start()
-
-        later = turn - wait_two
-
-        @pl.when((lax.rem(later + 8 + group, 2) == 0) & (later >= 0) & (later < 8))
-        def _(group=group, keep_ref=keep_ref, two_ref=two_ref, own_ref=own_ref):
-            index = later // 2
-            depth, early = place_of(index)
-            second_copy(group, index).wait_recv()
-            which = early * y + (1 - early) * x
-            total = keep_ref[depth, which].astype(f32) + two_ref[depth].astype(f32)
-
-            @pl.when(depth == level)
-            def _():
-                own_ref[...] = total
-
-            @pl.when(depth != level)
-            def _():
-                keep_ref[depth, which] = total.astype(bf16)
-                deep_copy(group, index).start()
+    for index, depth in enumerate(scatter.order):
+
+        @pl.when(turn == index)
+        def _(depth=depth):
+            lefts, rights = [], []
+            for act, dx2, dx2_near in steps:
+                lefts += [act[0, 0], act[1, 0]]
+                rights += [dx2[...], dx2_near[...]]
+            scatter.begin(depth, [summed(lefts, rights)], held_ref)
+
+        @pl.when(turn == index + 3)
+        def _(depth=depth):
+            scatter.middle(depth)
+
+        @pl.when(turn == index + 5)
+        def _(depth=depth):
+            scatter.end(depth)
 
     @pl.when(turn < 8)
     def _():
         where = pl.ds(pl.multiple_of(turn * rows, rows), rows)
         sums = [lse_ref[head : head + 1, where] for head in range(heads)]
         dqkv_ref[where, :width] = attend_back_rows(
-            heads, 512, qkv_ref[where, :width], do_ref[where, :], full_ref[where, :], sums,
+            heads, 1024, qkv_ref[where, :width], do_ref[where, :], full_ref[where, :], sums,
             qkv_ref.at[:, width : 2 * width], qkv_ref.at[:, 2 * width :], kt_ref, dk_sum, dv_sum,
         )
 
@@ -926,74 +945,31 @@
 
     @pl.when(turn == turns - 1)
     def _():
+        scatter.finish(down_ref)
         for place in range(3):
             remote(
-                piece_send.at[0], piece_recv.at[place], piece_send_sem.at[0],
-                piece_recv_sem.at[place], across,
+                piece_send.at[0], piece_recv.at[place], piece_sem.at[0, 0],
+                piece_sem.at[1, place], scatter.side,
             ).wait_recv()
-        piece_own[...] += (
+        share_ref[...] = piece_own[...] + (
             piece_recv[0].astype(f32) + piece_recv[1].astype(f32) + piece_recv[2].astype(f32)
         )
-
-        @pl.when(dp != level)
-        def _():
-            crossing.start()
-
-        for group in range(2):
-            _, keep_ref, _, _, own_ref, deep_ref, result_ref = groups[group]
-            for place in range(3):
-                remote(
-                    keep_ref.at[0, 0], deep_ref.at[place], deep_send.at[0],
-                    deep_recv.at[group * 4 + place], across,
-                ).wait_recv()
-            result_ref[...] = own_ref[...] + (
-                deep_ref[0].astype(f32) + deep_ref[1].astype(f32) + deep_ref[2].astype(f32)
-            )
         for other in others:
             part_copy(*other).wait()
         own_part.wait()
         for index in range(4):
-            depth = (index % 2) * 2 + index // 2
-            for group in range(2):
-                first_copy(group, index).wait_send()
-                second_copy(group, index).wait_send()
-
-                @pl.when(depth != level)
-                def _(group=group, index=index):
-                    deep_copy(group, index).wait_send()
 
             @pl.when(level != index)
             def _(index=index):
                 piece_copy(index).wait_send()
 
-        @pl.when(dp != level)
-        def _():
-            crossing.wait()
-            share_ref[...] = landing_ref[...]
-
-        @pl.when(dp == level)
-        def _():
-            share_ref[...] = piece_own[...]
-
 
 def finish_program(kept, packed, own_grad, full, logsum, rows_one, earlier):
     rows, width = own_grad.shape[0] // 8, own_grad.shape[1]
-    once = lambda shape: pl.BlockSpec(
-        shape, lambda i: (0,) * len(shape), pipeline_mode=pl.Buffered(1)
-    )
-
-    def chunk(shape):
-        def where(i):
-            index = jnp.minimum(i // 2, 3)
-            return 0, lax.rem(index, 2) * 2 + index // 2, 0, 0
-
-        return pl.BlockSpec((2, 1) + shape, where)
-
     in_specs, operands = [], []
-    for act, dg, o, dx2, dx2_near, h2, h2_near, dx1, dx1_near in kept:
-        operands += [act, dg, o, dx2, dx2_near, h2, h2_near, dx1, dx1_near]
-        in_specs += [chunk(act.shape[2:]), chunk(dg.shape[2:]), chunk(o.shape[2:])]
-        in_specs += [once(dx2.shape)] * 6
+    for act, dx2, dx2_near in kept:
+        operands += [act, dx2, dx2_near]
+        in_specs += [chunk_spec(act.shape[2:]), once(dx2.shape), once(dx2.shape)]
     piece = lambda i: jnp.clip(i - pieces_at, 0, 3)
     in_specs += [
         once(packed.shape),
@@ -1006,56 +982,36 @@
     operands += [packed, own_grad, full, logsum, rows_one, earlier]
     fixed = lambda shape: pl.BlockSpec(shape, lambda i: (0, 0))
     units = kept[0][0].shape[3]
-    heights = (units, units + width)
     share = D // 4
-    scratch = [
-        pltpu.VMEM((8 * rows, 3 * width), bf16),
-        pltpu.VMEM((width, 8 * rows), bf16),
-        pltpu.VMEM((8 * rows, width), f32),
-        pltpu.VMEM((8 * rows, width), f32),
-        pltpu.VMEM((4, heights[1], share), bf16),
-    ]
-    for height in heights:
-        scratch += [
-            pltpu.VMEM((4, 2, height, share), bf16),
-            pltpu.VMEM((4, 2, height, share), bf16),
-            pltpu.VMEM((4, 2, height, share), bf16),
-            pltpu.VMEM((4, height, share), bf16),
-            pltpu.VMEM((height, share), f32),
-            pltpu.VMEM((3, height, share), bf16),
-        ]
-    scratch += [
-        pltpu.VMEM((4, share, 3 * width), bf16),
-        pltpu.VMEM((3, share, 3 * width), bf16),
-        pltpu.VMEM((share, 3 * width), f32),
-        pltpu.VMEM((share, 3 * width), f32),
-    ]
-    scratch += [pltpu.SemaphoreType.DMA((8,))] * 8
-    scratch += [
-        pltpu.SemaphoreType.DMA((4,)),
-        pltpu.SemaphoreType.DMA((4,)),
-        pltpu.SemaphoreType.DMA((2,)),
-        pltpu.SemaphoreType.DMA,
-    ]
     return pl.pallas_call(
         finish_kernel,
         grid=(turns,),
         out_shape=[
             jax.ShapeDtypeStruct((rows, 24 * width), bf16),
             jax.ShapeDtypeStruct((share, 3 * width), f32),
-            jax.ShapeDtypeStruct((heights[0], share), f32),
-            jax.ShapeDtypeStruct((heights[1], share), f32),
+            jax.ShapeDtypeStruct((units, share), f32),
         ],
         in_specs=in_specs,
         out_specs=[
             pl.BlockSpec(memory_space=pl.ANY),
             fixed((share, 3 * width)),
-            fixed((heights[0], share)),
-            fixed((heights[1], share)),
+            fixed((units, share)),
         ],
-        scratch_shapes=scratch,
+        scratch_shapes=[
+            pltpu.VMEM((8 * rows, 3 * width), bf16),
+            pltpu.VMEM((width, 8 * rows), bf16),
+            pltpu.VMEM((8 * rows, width), f32),
+            pltpu.VMEM((8 * rows, width), f32),
+            pltpu.VMEM((4, share, 3 * width), bf16),
+            pltpu.VMEM((3, share, 3 * width), bf16),
+            pltpu.VMEM((share, 3 * width), f32),
+            pltpu.SemaphoreType.DMA((2, 8)),
+            pltpu.SemaphoreType.DMA((2, 4)),
+            pltpu.SemaphoreType.DMA,
+        ]
+        + scatter_scratch(units, share),
         compiler_params=pltpu.CompilerParams(
-            collective_id=4, has_side_effects=True, vmem_limit_bytes=60 * 2**20
+            collective_id=4, has_side_effects=True, vmem_limit_bytes=BIG
         ),
         name="finish_program",
     )(*operands)
@@ -1351,26 +1307,25 @@
     )(cells, keyed, bias, patch, variable, lead_row, norm_gains)
 
 
-def entry_back_kernel(
-    grad_ref, qkv_ref, x0_ref, mid_ref, gains_ref, u_ref, keyed_ref, bias_ref, patch_ref, var_ref,
-    du_ref, gain_ref, lead_ref, dpatch_ref, dvar_ref, dkeyed_ref, dbias_ref,
-    dx_ref, flip_ref,
+def entry_rows(
+    grad_ref, qkv_ref, x0_ref, mid_ref, gains_ref, du_ref, gain_ref, lead_ref, dx_ref, flip_ref
 ):
-    pair = pl.program_id(0)
-
-    @pl.when(pair == 0)
-    def _():
-        row_grad = jnp.dot(grad_ref[...], qkv_ref[...], preferred_element_type=f32)
-        unit, inverse = normed_parts(x0_ref[...])
-        part, gain_grad, bias_grad = norm_grad(unit, inverse, gains_ref[0:1, :], row_grad)
-        total = mid_ref[...] + part
-        dx_ref[...] = total
-        flip_ref[...] = total.T
-        lead_ref[...] = jnp.sum(total, axis=0, keepdims=True)
-        gain_ref[0:1, :] = gain_grad
-        gain_ref[1:2, :] = bias_grad
-        du_ref[...] = jnp.zeros_like(du_ref)
-
+    row_grad = jnp.dot(grad_ref[...], qkv_ref[...], preferred_element_type=f32)
+    unit, inverse = normed_parts(x0_ref[...])
+    part, gain_grad, bias_grad = norm_grad(unit, inverse, gains_ref[0:1, :], row_grad)
+    total = mid_ref[...] + part
+    dx_ref[...] = total
+    flip_ref[...] = total.T
+    lead_ref[...] = jnp.sum(total, axis=0, keepdims=True)
+    gain_ref[0:1, :] = gain_grad
+    gain_ref[1:2, :] = bias_grad
+    du_ref[...] = jnp.zeros_like(du_ref)
+
+
+def entry_pair(
+    pair, u_ref, keyed_ref, bias_ref, patch_ref, var_ref,
+    du_ref, dpatch_ref, dvar_ref, dkeyed_ref, dbias_ref, dx_ref, flip_ref,
+):
     cells = u_ref[...]
     size = 2 * HEAD_DIM
     columns = pl.ds(pl.multiple_of(pair * size, size), size)
@@ -1400,6 +1355,158 @@
         dpatch_ref[mine, :] = three_products(flipped, split_low(shares * cells))
         dvar_ref[mine, :] = three_products(flipped, split_low(shares))
     du_ref[...] += cells_grad
+
+
+def entry_back_kernel(
+    grad_ref, qkv_ref, x0_ref, mid_ref, gains_ref, u_ref, keyed_ref, bias_ref, patch_ref, var_ref,
+    du_ref, gain_ref, lead_ref, dpatch_ref, dvar_ref, dkeyed_ref, dbias_ref,
+    dx_ref, flip_ref,
+):
+    pair = pl.program_id(0)
+
+    @pl.when(pair == 0)
+    def _():
+        entry_rows(
+            grad_ref, qkv_ref, x0_ref, mid_ref, gains_ref, du_ref, gain_ref, lead_ref, dx_ref,
+            flip_ref,
+        )
+
+    entry_pair(
+        pair, u_ref, keyed_ref, bias_ref, patch_ref, var_ref,
+        du_ref, dpatch_ref, dvar_ref, dkeyed_ref, dbias_ref, dx_ref, flip_ref,
+    )
+
+
+def entry_last_kernel(*refs):
+    steps = (refs[0:6], refs[6:12])
+    share_ref = refs[12]
+    (grad_ref, qkv_ref, x0_ref, mid_ref, gains_ref, u_ref, keyed_ref, bias_ref, patch_ref,
+     var_ref) = refs[13:23]
+    (du_ref, gain_ref, lead_ref, dpatch_ref, dvar_ref, dkeyed_ref, dbias_ref, up_out_ref,
+     qkv_share_ref) = refs[23:32]
+    dx_ref, flip_ref, low_ref, landing_ref, cross_sem = refs[32:37]
+    scatter = Scatter(refs[37:43], refs[44:47])
+    held_ref = refs[43]
+    turn = pl.program_id(0)
+    dp, level, core = mesh_place()
+    across = device_of(level, dp, core)
+    crossing = scatter.copy(low_ref, landing_ref, cross_sem, 0, 0, across)
+
+    @pl.when(turn == 0)
+    def _():
+        barrier = pltpu.get_barrier_semaphore()
+        deep = [device_of(dp, lax.rem(level + move, 4), core) for move in (1, 2, 3)]
+        for target in (scatter.side, scatter.down, *deep):
+            pl.semaphore_signal(barrier, inc=1, device_id=target, device_id_type=MESH)
+        low_ref[...] = share_ref[...].astype(bf16)
+
+        @pl.when(dp != level)
+        def _():
+            pl.semaphore_signal(barrier, inc=1, device_id=across, device_id_type=MESH)
+            pl.semaphore_wait(barrier, 6)
+
+        @pl.when(dp == level)
+        def _():
+            pl.semaphore_wait(barrier, 5)
+
+    for index, depth in enumerate(scatter.order):
+
+        @pl.when(turn == index)
+        def _(depth=depth):
+            lefts, rights, smalls, wides = [], [], [], []
+            for dg, o, h2, h2_near, dx1, dx1_near in steps:
+                lefts += [dg[0, 0], dg[1, 0]]
+                rights += [h2[...], h2_near[...]]
+                smalls += [o[0, 0], o[1, 0]]
+                wides += [dx1[...], dx1_near[...]]
+            scatter.begin(depth, [summed(lefts, rights), summed(smalls, wides)], held_ref)
+
+        @pl.when(turn == index + 3)
+        def _(depth=depth):
+            scatter.middle(depth)
+
+        @pl.when(turn == index + 6)
+        def _(depth=depth):
+            scatter.end(depth)
+
+    @pl.when((turn == 2) & (dp != level))
+    def _():
+        crossing.start()
+
+    @pl.when(turn == 0)
+    def _():
+        entry_rows(
+            grad_ref, qkv_ref, x0_ref, mid_ref, gains_ref, du_ref, gain_ref, lead_ref, dx_ref,
+            flip_ref,
+        )
+
+    @pl.when((turn >= 1) & (turn <= HEADS // 2))
+    def _():
+        entry_pair(
+            turn - 1, u_ref, keyed_ref, bias_ref, patch_ref, var_ref,
+            du_ref, dpatch_ref, dvar_ref, dkeyed_ref, dbias_ref, dx_ref, flip_ref,
+        )
+
+    @pl.when(turn == entry_turns - 1)
+    def _():
+        @pl.when(dp != level)
+        def _():
+            crossing.wait()
+            qkv_share_ref[...] = landing_ref[...].astype(f32)
+
+        @pl.when(dp == level)
+        def _():
+            qkv_share_ref[...] = share_ref[...]
+
+        scatter.finish(up_out_ref)
+
+
+def entry_last(kept, share, token_grad, qkv_t, x_first, mid_grad, norm_gains, cells, prepared):
+    patch, variable, keyed, bias = prepared
+    rows, width = x_first.shape
+    padded = cells.shape[1]
+    in_specs, operands = [], []
+    for dg, o, h2, h2_near, dx1, dx1_near in kept:
+        operands += [dg, o, h2, h2_near, dx1, dx1_near]
+        in_specs += [chunk_spec(dg.shape[2:]), chunk_spec(o.shape[2:])]
+        in_specs += [once(h2.shape)] * 4
+    pair = lambda i: jnp.clip(i - 1, 0, HEADS // 2 - 1)
+    by_pair = pl.BlockSpec((padded, 2 * HEAD_DIM), lambda i: (0, pair(i)))
+    flipped = pl.BlockSpec((2 * HEAD_DIM, padded), lambda i: (pair(i), 0))
+    fixed = lambda shape: pl.BlockSpec(shape, lambda i: (0, 0))
+    values = [share, token_grad, qkv_t, x_first, mid_grad, norm_gains, cells, keyed, bias]
+    in_specs += [once(value.shape) for value in values] + [by_pair, by_pair]
+    height, columns = kept[0][0].shape[3] + kept[0][1].shape[3], width // 4
+    outs = [
+        ((rows, padded), None),
+        ((2, width), None),
+        ((1, width), None),
+        ((width, padded), flipped),
+        ((width, padded), flipped),
+        (keyed.shape, None),
+        (bias.shape, None),
+        ((height, columns), None),
+        (share.shape, None),
+    ]
+    return pl.pallas_call(
+        entry_last_kernel,
+        grid=(entry_turns,),
+        out_shape=[jax.ShapeDtypeStruct(shape, f32) for shape, _ in outs],
+        in_specs=in_specs,
+        out_specs=[fixed(shape) if spec is None else spec for shape, spec in outs],
+        scratch_shapes=[
+            pltpu.VMEM((rows, width), f32),
+            pltpu.VMEM((width, rows), f32),
+            pltpu.VMEM(share.shape, bf16),
+            pltpu.VMEM(share.shape, bf16),
+            pltpu.SemaphoreType.DMA((2, 1)),
+        ]
+        + scatter_scratch(height, columns),
+        compiler_params=pltpu.CompilerParams(
+            collective_id=6, has_side_effects=True, vmem_limit_bytes=BIG
+        ),
+        name="entry_last",
+    )(*operands, *values, patch, variable)
 
 
 def entry_backward(token_grad, qkv_t, x_first, mid_grad, norm_gains, cells, prepared):
@@ -2104,8 +2211,9 @@
             kept.append((attended, rows_two, flat(active), mid_low, flat(hidden_grad), last_low))
             own_grad = exchange(crossed, out_grad, False, 3)
         if crossed and rollout == 0:
-            token_grad, qkv_share, down_sum, up_out_sum = finish_program(
-                kept, packed, own_grad, full, logsum, rows_one, qkv_grad
+            token_grad, level_share, down_sum = finish_program(
+                [(step[0], step[3], step[4]) for step in kept],
+                packed, own_grad, full, logsum, rows_one, qkv_grad,
             )
         else:
             packed_grad = attend_back(own_grad, packed, full, logsum)
@@ -2113,9 +2221,13 @@
             qkv_grad = qkv_grad + lax.dot_general(
                 rows_one, packed_grad, TN, preferred_element_type=f32
             )
-        cells_grad, gain_one, lead_sum, *table_part = entry_backward(
-            token_grad, gathered[3], x_first, mid_grad, norm_gains, cells, prepared
-        )
+        entry = (token_grad, gathered[3], x_first, mid_grad, norm_gains, cells, prepared)
+        if crossed and rollout == 0:
+            cells_grad, gain_one, lead_sum, *table_part, up_out_sum, qkv_share = entry_last(
+                [step[1:3] + step[5:] for step in kept], level_share, *entry
+            )
+        else:
+            cells_grad, gain_one, lead_sum, *table_part = entry_backward(*entry)
         carried = cells_grad[:, : 4 * V]
         gain_low = gain_low + gain_one
         table_parts.append(table_part)

time: 744 us -> 696 us (0.935)
  Pallas kernels: 689 us -> 642 us
    pallas_call x0 -> x1, Pallas kernels: none -> 79.6 us  [entry_last(): pl.pallas_call(entry_last_kernel, grid=(entry_turns,), out_shape=[jax.Sha...]
    pallas_call x1, Pallas kernels: 144 us -> 73.3 us  [finish_program(): pl.pallas_call(finish_kernel, grid=(turns,), out_shape=[jax.ShapeDtypeStr...]
    pallas_call x1, Pallas kernels: 85.8 us -> 54.5 us  [exchange_sum(): pl.pallas_call(exchange_sum_kernel, out_shape=(jax.ShapeDtypeStruct(value...]
    pallas_call x2 -> x1, Pallas kernels: 49.9 us -> 24.9 us  [entry_backward(): pl.pallas_call(entry_back_kernel, grid=(HEADS // 2,), out_shape=(jax.Shap...]
  transfers between devices with their start and end apart: 1 -> 1, of which waited for: 0 -> 0; matrix products, arithmetic and copies ran while one was open for 2% -> 2% of each run, Pallas kernels for 14% -> 15%
where the time goes in v6:
time: 696 us; the launch traced here: 691 us
  Pallas kernels  642 us (92%)
  local copies, waits for them, and re-layouts  19.5 us (3%)
  other arithmetic  13.7 us (2%)
  matrix products  9.87 us (1%)
    pallas_call x1, Pallas kernels, start_program(): pl.pallas_call(partial(start_kernel, halves), grid=(groups * 3 + lag_two,...  150 us
    pallas_call x1, Pallas kernels, entry_last(): pl.pallas_call(entry_last_kernel, grid=(entry_turns,), out_shape=[jax.Sha...  79.6 us
    pallas_call x1, Pallas kernels, finish_program(): pl.pallas_call(finish_kernel, grid=(turns,), out_shape=[jax.ShapeDtypeStr...  73.3 us
    pallas_call x1, Pallas kernels, exchange_sum(): pl.pallas_call(exchange_sum_kernel, out_shape=(jax.ShapeDtypeStruct(value...  54.5 us
    pallas_call x3, Pallas kernels, exchange(): pl.pallas_call(partial(exchange_kernel, to_columns, rows, width), out_sha...  47.3 us
    pallas_call x2, Pallas kernels, branch_backward(): pl.pallas_call(branch_back_kernel, grid=(parts,), out_shape=(jax.ShapeDty...  39.6 us
    pallas_call x2, Pallas kernels, branch_forward(): pl.pallas_call(branch_kernel, grid=(parts,), out_shape=(jax.ShapeDtypeStr...  35.1 us
    pallas_call x1, Pallas kernels, spread_rows(): pl.pallas_call(gather_kernel, out_shape=jax.ShapeDtypeStruct((8 * rows, w...  27.8 us
  transfers between devices with their start and end apart: 1, of which 0 were waited for; matrix products, arithmetic and copies ran while one was open for 2% of the time, Pallas kernels for 15%

profile of v6, /device:TPU:0, one launch (start us, length us, event | category | flops | bytes accessed | tf_op | source)
XLA Modules:
  0.0 690.8 jit_solution(9894053235914698025)
XLA Ops:
  3.4 4.9 prepare_tables.1
  15.4 150.1 %start_program.1 = (f32[256,1024]{1,0:T(8,128)}, f32[256,256]{1,0:T(8,128)}, bf16[2048,384]{1,0:T(8,128)(2,1)}, bf16[2048,128]{1,0:T(8,128)(2,1)}, f32[2048,128]...) custom-call(f32[256,256]{1,0:T(8,128)} %maximum_maximum_fusion.refs_, ...), custom_call_target="tpu_custom_call" | custom-call | tf_op jit(solution)/shard_map/start_program/pallas_call | solution.py:2046
  165.5 11.5 %exchange_parts.3.o_ref.refs_3_ = bf16[256,1024]{1,0:T(8,128)(2,1)} custom-call(bf16[2048,128]{1,0:T(8,128)(2,1)} %get-tuple-element.132.x_ref), custom_call_target="tpu_custom_call" | custom-call | tf_op jit(solution)/shard_map/exchange_parts/pallas_call | solution.py:215
  180.8 17.4 %branch_forward.2 = (f32[256,1024]{1,0:T(8,128)}, bf16[256,1024]{1,0:T(8,128)(2,1)}, f32[256,4096]{1,0:T(8,128)}, bf16[2,4,256,512]{3,2,1,0:T(8,128)(2,1)}, f32[256,1024]{1,0:T(8,128)}, /*index=5*/f32[256,192]{1,0:T(8,128)}) custom-call(bf16[256,1024]{1,0:T(8,128)(2,1)} %exchange_parts.3.o_ref.refs_3_, f32[256,1024]{1,0:T(8,128)} %get-tuple-element.134.x0_ref.refs_15_, ...), custom_call_target="tpu_custom_call" | custom-call | flops 5435817984 | bytes 23068672 | tf_op jit(solution)/shard_map/branch_forward/pallas_call | solution.py:473
  203.3 15.7 %embed_forward.1 = (f32[256,1024]{1,0:T(8,128)}, bf16[256,1024]{1,0:T(8,128)(2,1)}) custom-call(f32[256,256]{1,0:T(8,128)} %pad.14.u_ref, f32[16,256]{1,0:T(8,128)} %get-tuple-element.128.refs_1_.keyed_ref.refs_19_, f32[16,256]{1,0:T(8,128)} %get-tuple-element.129.refs_2_.bias_ref.refs_20_, f32[256,1024]{1,0:T(8,128)} %get-tuple-element.130.refs_3_.patch_ref.refs_21_, ...), custom_call_target="tpu_custom_call" | custom-call | flops 1610612736 | bytes 3670016 | tf_op jit(solution)/shard_map/embed_forward/pallas_call | solution.py:1285
  219.0 27.8 %gather_rows.1 = bf16[2048,1024]{1,0:T(8,128)(2,1)} custom-call(bf16[256,1024]{1,0:T(8,128)(2,1)} %get-tuple-element.140.x_ref), custom_call_target="tpu_custom_call" | custom-call | tf_op jit(solution)/shard_map/gather_rows/pallas_call | solution.py:153
  246.8 4.8 convolution_convert_fusion
  252.8 16.2 %attend.1 = (bf16[2048,128]{1,0:T(8,128)(2,1)}, f32[2048,128]{1,0:T(8,128)}, f32[2,2048]{1,0:T(2,128)}) custom-call(bf16[2048,128]{1,0:T(8,128)(2,1)} %get-tuple-element.241.q_ref, bf16[2048,128]{1,0:T(8,128)(2,1)} %get-tuple-element.240.k_ref, bf16[2048,128]{1,0:T(8,128)(2,1)} %get-tuple-element.239.v_ref), custom_call_target="tpu_custom_call" | custom-call | flops 8589934592 | bytes 2621440 | tf_op jit(solution)/shard_map/attend/pallas_call | solution.py:271
  269.1 11.9 %exchange_parts.4.o_ref.refs_3_ = bf16[256,1024]{1,0:T(8,128)(2,1)} custom-call(bf16[2048,128]{1,0:T(8,128)(2,1)} %get-tuple-element.142.x_ref), custom_call_target="tpu_custom_call" | custom-call | tf_op jit(solution)/shard_map/exchange_parts/pallas_call | solution.py:215
  285.1 17.6 %branch_forward.3 = (f32[256,1024]{1,0:T(8,128)}, bf16[256,1024]{1,0:T(8,128)(2,1)}, f32[256,4096]{1,0:T(8,128)}, bf16[2,4,256,512]{3,2,1,0:T(8,128)(2,1)}, f32[256,1024]{1,0:T(8,128)}, /*index=5*/f32[256,192]{1,0:T(8,128)}) custom-call(bf16[256,1024]{1,0:T(8,128)(2,1)} %exchange_parts.4.o_ref.refs_3_, f32[256,1024]{1,0:T(8,128)} %get-tuple-element.143.x0_ref, ...), custom_call_target="tpu_custom_call" | custom-call | flops 5435817984 | bytes 23068672 | tf_op jit(solution)/shard_map/branch_forward/pallas_call | solution.py:473
  304.4 19.8 %branch_backward.2 = (bf16[256,1024]{1,0:T(8,128)(2,1)}, bf16[2,4,256,512]{3,2,1,0:T(8,128)(2,1)}, f32[256,1024]{1,0:T(8,128)}, bf16[256,1024]{1,0:T(8,128)(2,1)...) custom-call(f32[256,192]{1,0:T(8,128)} %multiply_divide_fusion.dpred_ref, ...), custom_call_target="tpu_custom_call" | custom-call | flops 6039797760 | bytes 23068672 | tf_op jit(solution)/shard_map/branch_backward/pallas_call | solution.py:566
  324.3 13.6 %exchange_swap.2 = (bf16[2048,128]{1,0:T(8,128)(2,1)}, bf16[2,4,256,512]{3,2,1,0:T(8,128)(2,1)}, bf16[2,4,256,512]{3,2,1,0:T(8,128)(2,1)}, bf16[2,4,256,128]{3,2...) custom-call(bf16[256,1024]{1,0:T(8,128)(2,1)} %get-tuple-element.150.refs_0_, ...), custom_call_target="tpu_custom_call" | custom-call | tf_op jit(solution)/shard_map/exchange_swap/pallas_call | solution.py:678
  337.9 25.8 %attend_back.1 = (bf16[2048,128]{1,0:T(8,128)(2,1)}, bf16[2048,128]{1,0:T(8,128)(2,1)}, bf16[2048,128]{1,0:T(8,128)(2,1)}) custom-call(bf16[2048,128]{1,0:T(8,128)(2,1)} %get-tuple-element.241.q_ref, bf16[2048,128]{1,0:T(8,128)(2,1)} %get-tuple-element.156.do_ref, f32[2048,128]{1,0:T(8,128)} %get-tuple-element.157.full_ref, ...), custom_call_target="tpu_custom_call" | custom-call | flops 21474836480 | bytes 4194304 | tf_op jit(solution)/shard_map/attend_back/pallas_call | solution.py:369
  367.3 24.0 %exchange_parts.5.grad_ref = bf16[256,3072]{1,0:T(8,128)(2,1)} custom-call(bf16[2048,384]{1,0:T(8,128)(2,1)} %copy-done.3), custom_call_target="tpu_custom_call" | custom-call | tf_op jit(solution)/shard_map/exchange_parts/pallas_call | solution.py:215
  391.3 4.9 fusion.32.refs_11_
  396.2 24.9 %entry_backward.1 = (f32[256,256]{1,0:T(8,128)}, f32[2,1024]{1,0:T(2,128)}, f32[1,1024]{1,0:T(1,128)}, f32[1024,256]{1,0:T(8,128)}, f32[1024,256]{1,0:T(8,128)}, /*index=5*/f32[16,256]{1,0:T(8,128)}, f32[16,256]{1,0:T(8,128)}) custom-call(bf16[256,3072]{1,0:T(8,128)(2,1)} %exchange_parts.5.grad_ref, bf16[3072,1024]{1,0:T(8,128)(2,1)} %bitcast.62, ...), custom_call_target="tpu_custom_call" | custom-call | flops 4026531840 | bytes 10485760 | tf_op jit(solution)/shard_map/entry_backward/pallas_call | solution.py:1519
  421.1 2.4 fusion.3
  423.5 19.8 %branch_backward.3 = (bf16[256,1024]{1,0:T(8,128)(2,1)}, bf16[2,4,256,512]{3,2,1,0:T(8,128)(2,1)}, f32[256,1024]{1,0:T(8,128)}, bf16[256,1024]{1,0:T(8,128)(2,1)...) custom-call(f32[256,192]{1,0:T(8,128)} %get-tuple-element.242.dpred_ref, ...), custom_call_target="tpu_custom_call" | custom-call | flops 6039797760 | bytes 23068672 | tf_op jit(solution)/shard_map/branch_backward/pallas_call | solution.py:566
  443.3 13.7 %exchange_swap.3 = (bf16[2048,128]{1,0:T(8,128)(2,1)}, bf16[2,4,256,512]{3,2,1,0:T(8,128)(2,1)}, bf16[2,4,256,512]{3,2,1,0:T(8,128)(2,1)}, bf16[2,4,256,128]{3,2...) custom-call(bf16[256,1024]{1,0:T(8,128)(2,1)} %get-tuple-element.172.refs_0_, ...), custom_call_target="tpu_custom_call" | custom-call | tf_op jit(solution)/shard_map/exchange_swap/pallas_call | solution.py:678
  457.0 73.3 %finish_program.1 = (bf16[256,3072]{1,0:T(8,128)(2,1)}, f32[256,384]{1,0:T(8,128)}, f32[512,256]{1,0:T(8,128)}) custom-call(bf16[2,4,256,512]{3,2,1,0:T(8,128)(2,1)} %get-tuple-element.182.refs_0_, bf16[256,1024]{1,0:T(8,128)(2,1)} %get-tuple-element.153.refs_4_.refs_1_, bf16[256,1024]{1,0:T(8,128)(2,1)} %get-tuple-element.183.refs_2_, ...), custom_call_target="tpu_custom_call" | custom-call | tf_op jit(solution)/shard_map/finish_program/pallas_call | solution.py:986
  530.3 79.6 %entry_last.1 = (f32[256,256]{1,0:T(8,128)}, f32[2,1024]{1,0:T(2,128)}, f32[1,1024]{1,0:T(1,128)}, f32[1024,256]{1,0:T(8,128)}, f32[1024,256]{1,0:T(8,128)}, /*i...) custom-call(bf16[2,4,256,512]{3,2,1,0:T(8,128)(2,1)} %get-tuple-element.164.refs_0_, ...), custom_call_target="tpu_custom_call" | custom-call | tf_op jit(solution)/shard_map/entry_last/pallas_call | solution.py:1491
  616.4 7.2 %table_grads.1.x_ref = f32[512,1024]{1,0:T(8,128)} custom-call(f32[1024,256]{1,0:T(8,128)} %get-tuple-element.163.pa_ref, f32[1024,256]{1,0:T(8,128)} %get-tuple-element.194.pb_ref, f32[1024,256]{1,0:T(8,128)} %get-tuple-element.195.va_ref, f32[1024,256]{1,0:T(8,128)} %get-tuple-element.196.vb_ref, f32[16,256]{1,0:T(8,128)} %get-tuple-element.197.ka_ref, ...), custom_call_target="tpu_custom_call" | custom-call | tf_op jit(solution)/shard_map/table_grads/pallas_call | solution.py:1592
  623.6 54.5 %exchange_sum.1 = (f32[512,1024]{1,0:T(8,128)}, f32[8,128]{1,0:T(8,128)}) custom-call(f32[512,1024]{1,0:T(8,128)} %table_grads.1.x_ref, f32[1,1]{1,0:T(1,128)} %bitcast.19.loss_ref, f32[256,384]{1,0:T(8,128)} %copy.78.qkv_ref.refs_4_, f32[640,256]{1,0:T(8,128)} %get-tuple-element.210.up_out_ref.refs_5_, f32[512,256]{1,0:T(8,128)} %get-tuple-element.211.down_ref.refs_6_), custom_call_target="tpu_custom_call" | custom-call | tf_op jit(solution)/shard_map/exchange_sum/pallas_call | solution.py:1153
  678.1 12.3 %update_all.1 = (f32[1,1]{1,0:T(1,128)}, f32[1,1]{1,0:T(1,128)}, f32[440,1024]{1,0:T(8,128)}, f32[440,1024]{1,0:T(8,128)}, f32[440,1024]{1,0:T(8,128)}, /*index=...) custom-call(s32[1]{0:T(128)} %bitcast.refs_0_, ...), custom_call_target="tpu_custom_call" | custom-call | tf_op jit(solution)/shard_map/update_all/pallas_call | solution.py:1661
  (91 shorter events, 31.7 us)
Async XLA Ops:
  8.3 2.8 copy-start
  10.1 2.1 copy-start.1
  12.2 1.2 copy-start.12
  12.2 1.3 copy-start.17
  12.2 1.5 copy-start.20
  12.2 1.6 copy-start.4
  15.4 161.6 %copy-start.11 = (f32[1,2,256,192]{2,3,1,0:T(8,128)S(1)}, f32[1,2,256,192]{2,3,1,0:T(8,128)}, u32[]{:S(2)}) copy-start(f32[1,2,256,192]{2,3,1,0:T(8,128)} %param.25) | copy-start | bytes 1179652
  177.2 125.5 %collective-permute-start = (f32[2,256,192]{2,1,0:T(8,128)S(1)}, f32[2,256,192]{2,1,0:T(8,128)S(1)}, u32[]{:S(2)}, u32[]{:S(2)}) collective-permute-start(f32[2,256,192]{2,1,0:T(8,128)S(1)} %bitcast.69), channel_id=1, source_target_pairs={{0,0},{1,1},{2,8},{3,9},{4,16},{5,17},{6,24},{7,25},{8,2},{9,3},{1... | collective-permute-start | bytes 1179656 | tf_op jit(solution)/shard_map/ppermute | solution.py:85
  180.8 19.1 %copy-start.9 = (f32[256,256]{1,0:T(8,128)S(1)}, f32[256,256]{1,0:T(8,128)}, u32[]{:S(2)}) copy-start(f32[256,256]{1,0:T(8,128)} %get-tuple-element.139.refs_18_) | copy-start | bytes 786436
  363.7 2.4 copy-start.10
  366.0 25.3 %copy-start.2 = (bf16[2048,1024]{1,0:T(8,128)(2,1)S(1)}, bf16[2048,1024]{1,0:T(8,128)(2,1)}, u32[]{:S(2)}) copy-start(bf16[2048,1024]{1,0:T(8,128)(2,1)} %gather_rows.1) | copy-start | bytes 12582916
  366.2 1.1 copy-start.3
  396.2 24.9 %copy-start.5 = (f32[256,192]{1,0:T(8,128)S(1)}, f32[256,192]{1,0:T(8,128)}, u32[]{:S(2)}) copy-start(f32[256,192]{1,0:T(8,128)} %get-tuple-element.138) | copy-start | bytes 589828
  396.2 24.9 %copy-start.6 = (f32[256,192]{1,0:T(8,128)S(1)}, f32[256,192]{1,0:T(8,128)}, u32[]{:S(2)}) copy-start(f32[256,192]{1,0:T(8,128)} %get-tuple-element.144) | copy-start | bytes 589828
  609.9 3.6 copy-start.13
  609.9 3.6 copy-start.14
  610.0 4.2 copy-start.7
  610.0 4.2 copy-start.8
  611.3 3.9 copy-start.15
  611.3 3.9 copy-start.16
  611.3 4.5 copy-start.18
  611.3 4.5 copy-start.19

commit v7 on v6

--- a/solution.py
+++ b/solution.py
@@ -437,11 +437,17 @@
         h2_ref[...] = (unit * gains_ref[2:3, :] + gains_ref[3:4, :]).astype(bf16)
         x2_ref[...] = x1_ref[...]
 
-    hidden = jnp.dot(h2_ref[...], up_ref[0], preferred_element_type=f32)
-    g_ref[...] = hidden
-    active = (hidden * gauss_share(hidden)).astype(bf16)
-    act_ref[0, 0] = active
-    x2_ref[...] += jnp.dot(active, down_ref[...], preferred_element_type=f32)
+    units = g_ref.shape[1]
+    total = None
+    for start in range(0, units, units // 2):
+        some = slice(start, start + units // 2)
+        hidden = jnp.dot(h2_ref[...], up_ref[0, :, some], preferred_element_type=f32)
+        g_ref[:, some] = hidden
+        active = (hidden * gauss_share(hidden)).astype(bf16)
+        act_ref[0, 0, :, some] = active
+        part = jnp.dot(active, down_ref[some, :], preferred_element_type=f32)
+        total = part if total is None else total + part
+    x2_ref[...] += total
 
     @pl.when(step == pl.num_programs(0) - 1)
     def _():
@@ -531,14 +537,22 @@
         dx2_ref[...] = wide.astype(bf16)
         sum_ref[...] = jnp.zeros_like(sum_ref)
 
-    active_grad = lax.dot_general(dx2_ref[...], down_ref[...], NT, preferred_element_type=f32)
-    hidden = g_ref[...]
-    slope = gauss_share(hidden) + hidden * (
-        jnp.exp(-0.5 * hidden * hidden) * (2.0 * math.pi) ** -0.5
-    )
-    hidden_grad = (active_grad * slope).astype(bf16)
-    dg_ref[0, 0] = hidden_grad
-    sum_ref[...] += lax.dot_general(hidden_grad, up_ref[0], NT, preferred_element_type=f32)
+    units = g_ref.shape[1]
+    total = None
+    for start in range(0, units, units // 2):
+        some = slice(start, start + units // 2)
+        active_grad = lax.dot_general(
+            dx2_ref[...], down_ref[some, :], NT, preferred_element_type=f32
+        )
+        hidden = g_ref[:, some]
+        slope = gauss_share(hidden) + hidden * (
+            jnp.exp(-0.5 * hidden * hidden) * (2.0 * math.pi) ** -0.5
+        )
+        hidden_grad = (active_grad * slope).astype(bf16)
+        dg_ref[0, 0, :, some] = hidden_grad
+        part = lax.dot_general(hidden_grad, up_ref[0, :, some], NT, preferred_element_type=f32)
+        total = part if total is None else total + part
+    sum_ref[...] += total
 
     @pl.when(step == pl.num_programs(0) - 1)
     def _():
@@ -830,6 +844,150 @@
     return pl.BlockSpec(shape, lambda i: (0,) * len(shape), pipeline_mode=pl.Buffered(1))
 
 
+class Returns:
+    def __init__(self, grads_ref, token_out, width, sems, own_sem):
+        self.grads_ref, self.token_out, self.width = grads_ref, token_out, width
+        self.sems, self.own_sem = sems, own_sem
+        dp, self.level, core = mesh_place()
+        self.me = dp * 2 + core
+        self.rows = grads_ref.shape[0] // 8
+
+    def part(self, move):
+        return lax.rem(self.me + move, 8)
+
+    def refs(self, part, start, size):
+        rows = pl.ds(pl.multiple_of(part * self.rows, self.rows), self.rows)
+        first = self.me * 3 * self.width + start
+        columns = pl.ds(pl.multiple_of(first, self.width), size)
+        return self.grads_ref.at[rows, start : start + size], self.token_out.at[:, columns]
+
+    def copy(self, move, late):
+        start, size = (self.width, 2 * self.width) if late else (0, self.width)
+        part = self.part(move)
+        source, target_ref = self.refs(part, start, size)
+        return pltpu.make_async_remote_copy(
+            src_ref=source,
+            dst_ref=target_ref,
+            send_sem=self.sems.at[2 * late, move],
+            recv_sem=self.sems.at[2 * late + 1, move],
+            device_id=device_of(part // 2, self.level, lax.rem(part, 2)),
+            device_id_type=MESH,
+        )
+
+    def own(self):
+        source, target_ref = self.refs(self.me, 0, 3 * self.width)
+        return pltpu.make_async_copy(source, target_ref, self.own_sem)
+
+    def peers(self):
+        parts = [self.part(move) for move in range(1, 8)]
+        return [device_of(part // 2, self.level, lax.rem(part, 2)) for part in parts]
+
+    def finish(self):
+        for move in range(1, 8):
+            self.copy(move, 0).wait()
+            self.copy(move, 1).wait()
+        self.own().wait()
+
+
+def attend_turns(turn, returns, qkv_ref, do_ref, full_ref, lse_ref, dqkv_ref, kt_ref, dk_sum, dv_sum):
+    width = do_ref.shape[1]
+    heads = width // HEAD_DIM
+    rows = returns.rows
+
+    @pl.when(turn == 0)
+    def _():
+        kt_ref[...] = qkv_ref[:, width : 2 * width].T
+        dk_sum[...] = jnp.zeros_like(dk_sum)
+        dv_sum[...] = jnp.zeros_like(dv_sum)
+
+    @pl.when(turn < 8)
+    def _():
+        part = returns.part(turn + 1)
+        where = pl.ds(pl.multiple_of(part * rows, rows), rows)
+        sums = [lse_ref[head : head + 1, where] for head in range(heads)]
+        dqkv_ref[where, :width] = attend_back_rows(
+            heads, 1024, qkv_ref[where, :width], do_ref[where, :], full_ref[where, :], sums,
+            qkv_ref.at[:, width : 2 * width], qkv_ref.at[:, 2 * width :], kt_ref, dk_sum, dv_sum,
+        )
+
+    @pl.when(turn < 7)
+    def _():
+        returns.copy(turn + 1, 0).start()
+
+    @pl.when(turn == 8)
+    def _():
+        dqkv_ref[:, width : 2 * width] = dk_sum[...].astype(bf16)
+        dqkv_ref[:, 2 * width :] = dv_sum[...].astype(bf16)
+        for move in (7, 6, 5, 4, 3, 2, 1):
+            returns.copy(move, 1).start()
+        returns.own().start()
+
+
+def attend_exchange_kernel(
+    qkv_ref, do_ref, full_ref, lse_ref, rows_ref, token_out, grad_ref,
+    dqkv_ref, kt_ref, dk_sum, dv_sum, sems, own_sem,
+):
+    turn = pl.program_id(0)
+    returns = Returns(dqkv_ref, token_out, do_ref.shape[1], sems, own_sem)
+
+    @pl.when(turn == 0)
+    def _():
+        barrier = pltpu.get_barrier_semaphore()
+        for target in returns.peers():
+            pl.semaphore_signal(barrier, inc=1, device_id=target, device_id_type=MESH)
+        pl.semaphore_wait(barrier, 7)
+
+    attend_turns(
+        turn, returns, qkv_ref, do_ref, full_ref, lse_ref, dqkv_ref, kt_ref, dk_sum, dv_sum
+    )
+
+    @pl.when(turn >= pieces_at)
+    def _():
+        grad_ref[...] = lax.dot_general(
+            rows_ref[...], dqkv_ref[...], TN, preferred_element_type=f32
+        )
+
+    @pl.when(turn == pieces_at + 3)
+    def _():
+        returns.finish()
+
+
+def attend_exchange(packed, own_grad, full, logsum, rows_one):
+    rows, width = own_grad.shape[0] // 8, own_grad.shape[1]
+    piece = lambda i: jnp.clip(i - pieces_at, 0, 3)
+    return pl.pallas_call(
+        attend_exchange_kernel,
+        grid=(pieces_at + 4,),
+        out_shape=[
+            jax.ShapeDtypeStruct((rows, 24 * width), bf16),
+            jax.ShapeDtypeStruct((D, 3 * width), f32),
+        ],
+        in_specs=[
+            once(packed.shape),
+            once(own_grad.shape),
+            once(full.shape),
+            once(logsum.shape),
+            pl.BlockSpec((8 * rows, D // 4), lambda i: (0, piece(i))),
+        ],
+        out_specs=[
+            pl.BlockSpec(memory_space=pl.ANY),
+            pl.BlockSpec((D // 4, 3 * width), lambda i: (piece(i), 0)),
+        ],
+        scratch_shapes=[
+            pltpu.VMEM((8 * rows, 3 * width), bf16),
+            pltpu.VMEM((width, 8 * rows), bf16),
+            pltpu.VMEM((8 * rows, width), f32),
+            pltpu.VMEM((8 * rows, width), f32),
+            pltpu.SemaphoreType.DMA((4, 8)),
+            pltpu.SemaphoreType.DMA,
+        ],
+        compiler_params=pltpu.CompilerParams(
+            collective_id=8, has_side_effects=True, vmem_limit_bytes=BIG
+        ),
+        name="attend_exchange",
+    )(packed, own_grad, full, logsum, rows_one)
+
+
 pieces_at, turns, entry_turns = 9, 14, 11
 
 
@@ -843,13 +1001,8 @@
     held_ref = refs[31]
     turn = pl.program_id(0)
     dp, level, core = mesh_place()
-    me = dp * 2 + core
     width = do_ref.shape[1]
-    heads = width // HEAD_DIM
-    rows = do_ref.shape[0] // 8
-    others = [
-        (move, part, device_of(part // 2, level, lax.rem(part, 2))) for move, part in plane_parts(me)
-    ]
+    returns = Returns(dqkv_ref, token_out, width, part_sem, own_sem)
 
     def remote(source, target_ref, send_sem, recv_sem, target):
         return pltpu.make_async_remote_copy(
@@ -861,16 +1014,6 @@
             device_id_type=MESH,
         )
 
-    def own_rows(part):
-        return dqkv_ref.at[pl.ds(pl.multiple_of(part * rows, rows), rows), :]
-
-    own_columns = token_out.at[:, pl.ds(pl.multiple_of(me * 3 * width, 3 * width), 3 * width)]
-
-    def part_copy(move, part, target):
-        return remote(
-            own_rows(part), own_columns, part_sem.at[0, move], part_sem.at[1, move], target
-        )
-
     def piece_copy(index):
         place = lax.rem(level + 7 - index, 4)
         return remote(
@@ -878,18 +1021,13 @@
             piece_sem.at[1, place], device_of(dp, index, core),
         )
 
-    own_part = pltpu.make_async_copy(own_rows(me), own_columns, own_sem)
-
     @pl.when(turn == 0)
     def _():
         barrier = pltpu.get_barrier_semaphore()
         deep = [device_of(dp, lax.rem(level + move, 4), core) for move in (1, 2, 3)]
-        for target in [target for _, _, target in others] + deep:
+        for target in returns.peers() + deep:
             pl.semaphore_signal(barrier, inc=1, device_id=target, device_id_type=MESH)
         pl.semaphore_wait(barrier, 10)
-        kt_ref[...] = qkv_ref[:, width : 2 * width].T
-        dk_sum[...] = jnp.zeros_like(dk_sum)
-        dv_sum[...] = jnp.zeros_like(dv_sum)
 
     for index, depth in enumerate(scatter.order):
 
@@ -909,22 +1047,9 @@
         def _(depth=depth):
             scatter.end(depth)
 
-    @pl.when(turn < 8)
-    def _():
-        where = pl.ds(pl.multiple_of(turn * rows, rows), rows)
-        sums = [lse_ref[head : head + 1, where] for head in range(heads)]
-        dqkv_ref[where, :width] = attend_back_rows(
-            heads, 1024, qkv_ref[where, :width], do_ref[where, :], full_ref[where, :], sums,
-            qkv_ref.at[:, width : 2 * width], qkv_ref.at[:, 2 * width :], kt_ref, dk_sum, dv_sum,
-        )
-
-    @pl.when(turn == 8)
-    def _():
-        dqkv_ref[:, width : 2 * width] = dk_sum[...].astype(bf16)
-        dqkv_ref[:, 2 * width :] = dv_sum[...].astype(bf16)
-        for other in others:
-            part_copy(*other).start()
-        own_part.start()
+    attend_turns(
+        turn, returns, qkv_ref, do_ref, full_ref, lse_ref, dqkv_ref, kt_ref, dk_sum, dv_sum
+    )
 
     for index in range(4):
 
@@ -954,9 +1079,7 @@
         share_ref[...] = piece_own[...] + (
             piece_recv[0].astype(f32) + piece_recv[1].astype(f32) + piece_recv[2].astype(f32)
         )
-        for other in others:
-            part_copy(*other).wait()
-        own_part.wait()
+        returns.finish()
         for index in range(4):
 
             @pl.when(level != index)
@@ -1005,7 +1128,7 @@
             pltpu.VMEM((4, share, 3 * width), bf16),
             pltpu.VMEM((3, share, 3 * width), bf16),
             pltpu.VMEM((share, 3 * width), f32),
-            pltpu.SemaphoreType.DMA((2, 8)),
+            pltpu.SemaphoreType.DMA((4, 8)),
             pltpu.SemaphoreType.DMA((2, 4)),
             pltpu.SemaphoreType.DMA,
         ]
@@ -1380,13 +1503,14 @@
 def entry_last_kernel(*refs):
     steps = (refs[0:6], refs[6:12])
     share_ref = refs[12]
-    (grad_ref, qkv_ref, x0_ref, mid_ref, gains_ref, u_ref, keyed_ref, bias_ref, patch_ref,
-     var_ref) = refs[13:23]
-    (du_ref, gain_ref, lead_ref, dpatch_ref, dvar_ref, dkeyed_ref, dbias_ref, up_out_ref,
-     qkv_share_ref) = refs[23:32]
-    dx_ref, flip_ref, low_ref, landing_ref, cross_sem = refs[32:37]
-    scatter = Scatter(refs[37:43], refs[44:47])
-    held_ref = refs[43]
+    grad_ref, qkv_ref, x0_ref, mid_ref, gains_ref, u_ref, keyed_ref, bias_ref = refs[13:21]
+    patch_ref, var_ref, query_ref, hot_ref, lead_hot_ref, head_a, head_b, high_a, high_b = refs[21:30]
+    patch_a, var_a, keyed_a, bias_a, lead_a, gain_a = refs[30:36]
+    rows_out, up_out_ref, qkv_share_ref = refs[36:39]
+    (dx_ref, flip_ref, low_ref, landing_ref, cross_sem, du_ref, gain_ref, lead_ref, dpatch_ref,
+     dvar_ref, dkeyed_ref, dbias_ref) = refs[39:51]
+    scatter = Scatter(refs[51:57], refs[58:61])
+    held_ref = refs[57]
     turn = pl.program_id(0)
     dp, level, core = mesh_place()
     across = device_of(level, dp, core)
@@ -1398,12 +1522,13 @@
         deep = [device_of(dp, lax.rem(level + move, 4), core) for move in (1, 2, 3)]
         for target in (scatter.side, scatter.down, *deep):
             pl.semaphore_signal(barrier, inc=1, device_id=target, device_id_type=MESH)
-        low_ref[...] = share_ref[...].astype(bf16)
+        low_ref[...] = share_ref[...]
 
         @pl.when(dp != level)
         def _():
             pl.semaphore_signal(barrier, inc=1, device_id=across, device_id_type=MESH)
             pl.semaphore_wait(barrier, 6)
+            crossing.start()
 
         @pl.when(dp == level)
         def _():
@@ -1429,22 +1554,33 @@
         def _(depth=depth):
             scatter.end(depth)
 
-    @pl.when((turn == 2) & (dp != level))
-    def _():
-        crossing.start()
-
     @pl.when(turn == 0)
     def _():
         entry_rows(
-            grad_ref, qkv_ref, x0_ref, mid_ref, gains_ref, du_ref, gain_ref, lead_ref, dx_ref,
-            flip_ref,
+            grad_ref, qkv_ref, x0_ref, mid_ref, gains_ref, du_ref, gain_ref,
+            lead_ref.at[0:1, :], dx_ref, flip_ref,
         )
 
     @pl.when((turn >= 1) & (turn <= HEADS // 2))
     def _():
+        size = 2 * HEAD_DIM
+        pair = turn - 1
+        some = pl.ds(pl.multiple_of(pair * size, size), size)
         entry_pair(
-            turn - 1, u_ref, keyed_ref, bias_ref, patch_ref, var_ref,
-            du_ref, dpatch_ref, dvar_ref, dkeyed_ref, dbias_ref, dx_ref, flip_ref,
+            pair, u_ref, keyed_ref, bias_ref, patch_ref.at[:, some], var_ref.at[:, some],
+            du_ref, dpatch_ref.at[some, :], dvar_ref.at[some, :], dkeyed_ref, dbias_ref,
+            dx_ref, flip_ref,
+        )
+
+    @pl.when(turn == entry_turns - 2)
+    def _():
+        gain_ref[...] += gain_a[...]
+        lead_ref[1:2, :] = lead_a[...]
+        lead_ref[2:8, :] = jnp.zeros((6, lead_ref.shape[1]), f32)
+        table_rows(
+            patch_a, dpatch_ref, var_a, dvar_ref, keyed_a, dkeyed_ref, bias_a, dbias_ref,
+            patch_ref, var_ref, query_ref, hot_ref, lead_hot_ref, lead_ref, gain_ref,
+            (head_a[...], head_b[...]), (high_a[2:6, :], high_b[2:6, :]), rows_out,
         )
 
     @pl.when(turn == entry_turns - 1)
@@ -1452,7 +1588,7 @@
         @pl.when(dp != level)
         def _():
             crossing.wait()
-            qkv_share_ref[...] = landing_ref[...].astype(f32)
+            qkv_share_ref[...] = landing_ref[...]
 
         @pl.when(dp == level)
         def _():
@@ -1461,7 +1597,10 @@
         scatter.finish(up_out_ref)
 
 
-def entry_last(kept, share, token_grad, qkv_t, x_first, mid_grad, norm_gains, cells, prepared):
+def entry_last(
+    kept, share, token_grad, qkv_t, x_first, mid_grad, norm_gains, cells, prepared,
+    query, var_hot, lead_hots, heads, highs, earlier,
+):
     patch, variable, keyed, bias = prepared
     rows, width = x_first.shape
     padded = cells.shape[1]
@@ -1470,43 +1609,39 @@
         operands += [dg, o, h2, h2_near, dx1, dx1_near]
         in_specs += [chunk_spec(dg.shape[2:]), chunk_spec(o.shape[2:])]
         in_specs += [once(h2.shape)] * 4
-    pair = lambda i: jnp.clip(i - 1, 0, HEADS // 2 - 1)
-    by_pair = pl.BlockSpec((padded, 2 * HEAD_DIM), lambda i: (0, pair(i)))
-    flipped = pl.BlockSpec((2 * HEAD_DIM, padded), lambda i: (pair(i), 0))
-    fixed = lambda shape: pl.BlockSpec(shape, lambda i: (0, 0))
-    values = [share, token_grad, qkv_t, x_first, mid_grad, norm_gains, cells, keyed, bias]
-    in_specs += [once(value.shape) for value in values] + [by_pair, by_pair]
+    values = [
+        share, token_grad, qkv_t, x_first, mid_grad, norm_gains, cells, keyed, bias,
+        patch, variable, query, var_hot, lead_hots, *heads, *highs, *earlier,
+    ]
+    in_specs += [once(value.shape) for value in values]
     height, columns = kept[0][0].shape[3] + kept[0][1].shape[3], width // 4
-    outs = [
-        ((rows, padded), None),
-        ((2, width), None),
-        ((1, width), None),
-        ((width, padded), flipped),
-        ((width, padded), flipped),
-        (keyed.shape, None),
-        (bias.shape, None),
-        ((height, columns), None),
-        (share.shape, None),
-    ]
+    outs = [(2 * padded, width), (height, columns), share.shape]
     return pl.pallas_call(
         entry_last_kernel,
         grid=(entry_turns,),
-        out_shape=[jax.ShapeDtypeStruct(shape, f32) for shape, _ in outs],
+        out_shape=[jax.ShapeDtypeStruct(shape, f32) for shape in outs],
         in_specs=in_specs,
-        out_specs=[fixed(shape) if spec is None else spec for shape, spec in outs],
+        out_specs=[pl.BlockSpec(shape, lambda i: (0, 0)) for shape in outs],
         scratch_shapes=[
             pltpu.VMEM((rows, width), f32),
             pltpu.VMEM((width, rows), f32),
-            pltpu.VMEM(share.shape, bf16),
-            pltpu.VMEM(share.shape, bf16),
+            pltpu.VMEM(share.shape, f32),
+            pltpu.VMEM(share.shape, f32),
             pltpu.SemaphoreType.DMA((2, 1)),
+            pltpu.VMEM((rows, padded), f32),
+            pltpu.VMEM((2, width), f32),
+            pltpu.VMEM((8, width), f32),
+            pltpu.VMEM((width, padded), f32),
+            pltpu.VMEM((width, padded), f32),
+            pltpu.VMEM(keyed.shape, f32),
+            pltpu.VMEM(bias.shape, f32),
         ]
         + scatter_scratch(height, columns),
         compiler_params=pltpu.CompilerParams(
             collective_id=6, has_side_effects=True, vmem_limit_bytes=BIG
         ),
         name="entry_last",
-    )(*operands, *values, patch, variable)
+    )(*operands, *values)
 
 
 def entry_backward(token_grad, qkv_t, x_first, mid_grad, norm_gains, cells, prepared):
@@ -1558,9 +1693,9 @@
     )(token_grad, qkv_t, x_first, mid_grad, norm_gains, cells, keyed, bias, patch, variable)
 
 
-def table_grads_kernel(
+def table_rows(
     pa_ref, pb_ref, va_ref, vb_ref, ka_ref, kb_ref, ba_ref, bb_ref,
-    patch_ref, var_ref, query_ref, hot_ref, lead_hot_ref, lead_ref, gain_ref, head_ref, high_ref, o_ref,
+    patch_ref, var_ref, query_ref, hot_ref, lead_hot_ref, lead_ref, gain_ref, heads, highs, o_ref,
 ):
     padded, width = patch_ref.shape
     marks = head_marks(width)
@@ -1580,11 +1715,17 @@
     )
     o_ref[5 * V + LEADS : 5 * V + LEADS + 1, :] = query_grad
     o_ref[5 * V + LEADS + 1 : 5 * V + LEADS + 3, :] = gain_ref[...]
-    o_ref[padded : padded + 4 * V, :] = head_ref[...]
-    o_ref[padded + 4 * V : padded + 4 * V + 4, :] = high_ref[...]
-
-
-def table_grads(first, second, prepared, query, var_hot, lead_hots, leads, gain_rows, head, high):
+    o_ref[padded : padded + 4 * V, :] = heads[0] + heads[1]
+    o_ref[padded + 4 * V : padded + 4 * V + 4, :] = highs[0] + highs[1]
+
+
+def table_grads_kernel(*refs):
+    head_a, head_b, high_a, high_b = refs[15:19]
+    heads, highs = (head_a[...], head_b[...]), (high_a[2:6, :], high_b[2:6, :])
+    table_rows(*refs[:15], heads, highs, refs[19])
+
+
+def table_grads(first, second, prepared, query, var_hot, lead_hots, leads, gain_rows, heads, highs):
     patch, variable, _, _ = prepared
     operands = []
     for one, two in zip(first, second):
@@ -1594,7 +1735,7 @@
         out_shape=jax.ShapeDtypeStruct((2 * patch.shape[0], D), f32),
         compiler_params=pltpu.CompilerParams(vmem_limit_bytes=BIG),
         name="table_grads",
-    )(*operands, patch, variable, query, var_hot, lead_hots, leads, gain_rows, head, high)
+    )(*operands, patch, variable, query, var_hot, lead_hots, leads, gain_rows, *heads, *highs)
 
 
 def adam_step(master, grad, first, second, rate):
@@ -2182,8 +2323,10 @@
              hidden, active, x_last, 2.0 * weighted * miss / denom)
         )
     carried = jnp.zeros_like(guess)
-    head_total = jnp.zeros_like(head)
-    gain_high = jnp.zeros((4, D), f32)
+    heads, highs = [], []
+    lead_hots = (leads[:, None] == jnp.arange(8, dtype=jnp.int32)[None, :]).astype(f32)
+    lead_hots = jnp.pad(lead_hots, ((0, 6), (0, 0)))
+    query = tables[5 * V + LEADS : 5 * V + LEADS + 1]
     gain_low = jnp.zeros((2, D), f32)
     table_parts, lead_sums = [], []
     qkv_grad = jnp.zeros((D, qkv_local.shape[0]), f32)
@@ -2195,8 +2338,8 @@
         last_low, hidden_grad, mid_grad, mid_low, out_grad, gain_part, head_grad = branch_backward(
             loss_grad + carried, x_last, x_mid, norm_gains, hidden, gathered, head
         )
-        head_total = head_total + head_grad
-        gain_high = gain_high + gain_part[2:]
+        heads.append(head_grad)
+        highs.append(gain_part)
         if crossed:
             (
                 own_grad, act_both, dg_both, o_both, dx2_near, h2_near, dx1_near
@@ -2215,6 +2358,8 @@
                 [(step[0], step[3], step[4]) for step in kept],
                 packed, own_grad, full, logsum, rows_one, qkv_grad,
             )
+        elif crossed:
+            token_grad, qkv_grad = attend_exchange(packed, own_grad, full, logsum, rows_one)
         else:
             packed_grad = attend_back(own_grad, packed, full, logsum)
             token_grad = exchange(crossed, packed_grad, True, 4 + 4)
@@ -2223,11 +2368,13 @@
             )
         entry = (token_grad, gathered[3], x_first, mid_grad, norm_gains, cells, prepared)
         if crossed and rollout == 0:
-            cells_grad, gain_one, lead_sum, *table_part, up_out_sum, qkv_share = entry_last(
-                [step[1:3] + step[5:] for step in kept], level_share, *entry
+            last_rows, up_out_sum, qkv_share = entry_last(
+                [step[1:3] + step[5:] for step in kept], level_share, *entry,
+                query, var_hot, lead_hots, heads, highs,
+                (*table_parts[0], lead_sums[0], gain_low),
             )
-        else:
-            cells_grad, gain_one, lead_sum, *table_part = entry_backward(*entry)
+            break
+        cells_grad, gain_one, lead_sum, *table_part = entry_backward(*entry)
         carried = cells_grad[:, : 4 * V]
         gain_low = gain_low + gain_one
         table_parts.append(table_part)
@@ -2236,13 +2383,11 @@
     def pair(index):
         return (kept[0][index], kept[1][index])
 
-    lead_hots = (leads[:, None] == jnp.arange(8, dtype=jnp.int32)[None, :]).astype(f32)
-    lead_hots = jnp.pad(lead_hots, ((0, 6), (0, 0)))
-    lead_rows = jnp.pad(jnp.concatenate((lead_sums[1], lead_sums[0])), ((0, 6), (0, 0)))
-    query = tables[5 * V + LEADS : 5 * V + LEADS + 1]
-    last_rows = table_grads(
-        *table_parts, prepared, query, var_hot, lead_hots, lead_rows, gain_low, head_total, gain_high
-    )
+    if not crossed:
+        lead_rows = jnp.pad(jnp.concatenate((lead_sums[1], lead_sums[0])), ((0, 6), (0, 0)))
+        last_rows = table_grads(
+            *table_parts, prepared, query, var_hot, lead_hots, lead_rows, gain_low, heads, highs
+        )
     if not crossed:
         qkv_share = lax.psum_scatter(qkv_grad, "dp", scatter_dimension=0, tiled=True)
     qkv_share = by_head(qkv_share)

time: 696 us -> 684 us (0.983)
    pallas_call x3 -> x2, Pallas kernels: 47.3 us -> 23.4 us  [exchange(): pl.pallas_call(partial(exchange_kernel, to_columns, rows, width), out_sha...]
    pallas_call x2 -> x1, Pallas kernels: 33 us -> 42.5 us  [attend_exchange(): pl.pallas_call(attend_exchange_kernel, grid=(pieces_at + 4,), out_shape=[...]
  transfers between devices with their start and end apart: 1 -> 1, of which waited for: 0 -> 0; matrix products, arithmetic and copies ran while one was open for 2% -> 2% of each run, Pallas kernels for 15% -> 16%
where the time goes in v7:
time: 684 us; the launch traced here: 679 us
  Pallas kernels  641 us (94%)
  local copies, waits for them, and re-layouts  16 us (2%)
  other arithmetic  10.9 us (2%)
    pallas_call x1, Pallas kernels, start_program(): pl.pallas_call(partial(start_kernel, halves), grid=(groups * 3 + lag_two,...  150 us
    pallas_call x1, Pallas kernels, entry_last(): pl.pallas_call(entry_last_kernel, grid=(entry_turns,), out_shape=[jax.Sha...  83.6 us
    pallas_call x1, Pallas kernels, finish_program(): pl.pallas_call(finish_kernel, grid=(turns,), out_shape=[jax.ShapeDtypeStr...  79.2 us
    pallas_call x1, Pallas kernels, exchange_sum(): pl.pallas_call(exchange_sum_kernel, out_shape=(jax.ShapeDtypeStruct(value...  58.7 us
    pallas_call x1, Pallas kernels, attend_exchange(): pl.pallas_call(attend_exchange_kernel, grid=(pieces_at + 4,), out_shape=[...  42.5 us
    pallas_call x2, Pallas kernels, branch_backward(): pl.pallas_call(branch_back_kernel, grid=(parts,), out_shape=(jax.ShapeDty...  39.6 us
    pallas_call x2, Pallas kernels, branch_forward(): pl.pallas_call(branch_kernel, grid=(parts,), out_shape=(jax.ShapeDtypeStr...  35.2 us
    pallas_call x1, Pallas kernels, spread_rows(): pl.pallas_call(gather_kernel, out_shape=jax.ShapeDtypeStruct((8 * rows, w...  27.8 us
  transfers between devices with their start and end apart: 1, of which 0 were waited for; matrix products, arithmetic and copies ran while one was open for 2% of the time, Pallas kernels for 16%

profile of v7, /device:TPU:0, one launch (start us, length us, event | category | flops | bytes accessed | tf_op | source)
XLA Modules:
  0.0 678.7 jit_solution(17374751882084509693)
XLA Ops:
  3.4 4.9 prepare_tables.1
  8.3 1.8 copy.67
  15.4 149.7 %start_program.1 = (f32[256,1024]{1,0:T(8,128)}, f32[256,256]{1,0:T(8,128)}, bf16[2048,384]{1,0:T(8,128)(2,1)}, bf16[2048,128]{1,0:T(8,128)(2,1)}, f32[2048,128]...) custom-call(f32[256,256]{1,0:T(8,128)} %maximum_maximum_fusion.refs_, ...), custom_call_target="tpu_custom_call" | custom-call | tf_op jit(solution)/shard_map/start_program/pallas_call | solution.py:2187
  165.1 11.5 %exchange_parts.2.o_ref.refs_3_ = bf16[256,1024]{1,0:T(8,128)(2,1)} custom-call(bf16[2048,128]{1,0:T(8,128)(2,1)} %get-tuple-element.127.x_ref), custom_call_target="tpu_custom_call" | custom-call | tf_op jit(solution)/shard_map/exchange_parts/pallas_call | solution.py:215
  177.6 2.1 slice.42.head_ref
  180.5 17.4 %branch_forward.2 = (f32[256,1024]{1,0:T(8,128)}, bf16[256,1024]{1,0:T(8,128)(2,1)}, f32[256,4096]{1,0:T(8,128)}, bf16[2,4,256,512]{3,2,1,0:T(8,128)(2,1)}, f32[256,1024]{1,0:T(8,128)}, /*index=5*/f32[256,192]{1,0:T(8,128)}) custom-call(bf16[256,1024]{1,0:T(8,128)(2,1)} %exchange_parts.2.o_ref.refs_3_, f32[256,1024]{1,0:T(8,128)} %get-tuple-element.129.x0_ref.refs_15_, ...), custom_call_target="tpu_custom_call" | custom-call | flops 5435817984 | bytes 23068672 | tf_op jit(solution)/shard_map/branch_forward/pallas_call | solution.py:479
  203.0 15.7 %embed_forward.1 = (f32[256,1024]{1,0:T(8,128)}, bf16[256,1024]{1,0:T(8,128)(2,1)}) custom-call(f32[256,256]{1,0:T(8,128)} %pad.10.u_ref, f32[16,256]{1,0:T(8,128)} %get-tuple-element.122.refs_1_.keyed_ref.refs_19_, f32[16,256]{1,0:T(8,128)} %get-tuple-element.123.refs_2_.bias_ref.refs_20_, f32[256,1024]{1,0:T(8,128)} %get-tuple-element.124.refs_3_.patch_ref.refs_21_, ...), custom_call_target="tpu_custom_call" | custom-call | flops 1610612736 | bytes 3670016 | tf_op jit(solution)/shard_map/embed_forward/pallas_call | solution.py:1408
  218.6 27.8 %gather_rows.1.rows_ref = bf16[2048,1024]{1,0:T(8,128)(2,1)} custom-call(bf16[256,1024]{1,0:T(8,128)(2,1)} %get-tuple-element.134.x_ref), custom_call_target="tpu_custom_call" | custom-call | tf_op jit(solution)/shard_map/gather_rows/pallas_call | solution.py:153
  246.5 4.8 convolution_convert_fusion.qkv_ref
  252.7 16.2 %attend.1 = (bf16[2048,128]{1,0:T(8,128)(2,1)}, f32[2048,128]{1,0:T(8,128)}, f32[2,2048]{1,0:T(2,128)}) custom-call(bf16[2048,128]{1,0:T(8,128)(2,1)} %get-tuple-element.229.q_ref, bf16[2048,128]{1,0:T(8,128)(2,1)} %get-tuple-element.228.k_ref, bf16[2048,128]{1,0:T(8,128)(2,1)} %get-tuple-element.227.v_ref), custom_call_target="tpu_custom_call" | custom-call | flops 8589934592 | bytes 2621440 | tf_op jit(solution)/shard_map/attend/pallas_call | solution.py:271
  269.0 11.9 %exchange_parts.3.o_ref.refs_3_ = bf16[256,1024]{1,0:T(8,128)(2,1)} custom-call(bf16[2048,128]{1,0:T(8,128)(2,1)} %get-tuple-element.136.x_ref), custom_call_target="tpu_custom_call" | custom-call | tf_op jit(solution)/shard_map/exchange_parts/pallas_call | solution.py:215
  284.9 17.8 %branch_forward.3 = (f32[256,1024]{1,0:T(8,128)}, bf16[256,1024]{1,0:T(8,128)(2,1)}, f32[256,4096]{1,0:T(8,128)}, bf16[2,4,256,512]{3,2,1,0:T(8,128)(2,1)}, f32[256,1024]{1,0:T(8,128)}, /*index=5*/f32[256,192]{1,0:T(8,128)}) custom-call(bf16[256,1024]{1,0:T(8,128)(2,1)} %exchange_parts.3.o_ref.refs_3_, f32[256,1024]{1,0:T(8,128)} %get-tuple-element.137.x0_ref, ...), custom_call_target="tpu_custom_call" | custom-call | flops 5435817984 | bytes 23068672 | tf_op jit(solution)/shard_map/branch_forward/pallas_call | solution.py:479
  302.7 1.7 multiply_divide_fusion.dpred_ref
  304.4 19.8 %branch_backward.2 = (bf16[256,1024]{1,0:T(8,128)(2,1)}, bf16[2,4,256,512]{3,2,1,0:T(8,128)(2,1)}, f32[256,1024]{1,0:T(8,128)}, bf16[256,1024]{1,0:T(8,128)(2,1)...) custom-call(f32[256,192]{1,0:T(8,128)} %multiply_divide_fusion.dpred_ref, ...), custom_call_target="tpu_custom_call" | custom-call | flops 6039797760 | bytes 23068672 | tf_op jit(solution)/shard_map/branch_backward/pallas_call | solution.py:580
  324.3 13.7 %exchange_swap.2 = (bf16[2048,128]{1,0:T(8,128)(2,1)}, bf16[2,4,256,512]{3,2,1,0:T(8,128)(2,1)}, bf16[2,4,256,512]{3,2,1,0:T(8,128)(2,1)}, bf16[2,4,256,128]{3,2...) custom-call(bf16[256,1024]{1,0:T(8,128)(2,1)} %get-tuple-element.144.refs_0_, ...), custom_call_target="tpu_custom_call" | custom-call | tf_op jit(solution)/shard_map/exchange_swap/pallas_call | solution.py:692
  338.0 42.5 %attend_exchange.1 = (bf16[256,3072]{1,0:T(8,128)(2,1)}, f32[1024,384]{1,0:T(8,128)}) custom-call(bf16[2048,384]{1,0:T(8,128)(2,1)} %copy-done.2, bf16[2048,128]{1,0:T(8,128)(2,1)} %get-tuple-element.154.do_ref, f32[2048,128]{1,0:T(8,128)} %get-tuple-element.155.full_ref, f32[2,2048]{1,0:T(2,128)} %get-tuple-element.156.lse_ref, ...), custom_call_target="tpu_custom_call" | custom-call | tf_op jit(solution)/shard_map/attend_exchange/pallas_call | solution.py:958
  380.5 25.0 %entry_backward.1 = (f32[256,256]{1,0:T(8,128)}, f32[2,1024]{1,0:T(2,128)}, f32[1,1024]{1,0:T(1,128)}, f32[1024,256]{1,0:T(8,128)}, f32[1024,256]{1,0:T(8,128)}, /*index=5*/f32[16,256]{1,0:T(8,128)}, f32[16,256]{1,0:T(8,128)}) custom-call(bf16[256,3072]{1,0:T(8,128)(2,1)} %get-tuple-element.157.grad_ref, bf16[3072,1024]{1,0:T(8,128)(2,1)} %bitcast.60, ...), custom_call_target="tpu_custom_call" | custom-call | flops 4026531840 | bytes 10485760 | tf_op jit(solution)/shard_map/entry_backward/pallas_call | solution.py:1654
  405.6 2.4 fusion.3
  407.9 19.8 %branch_backward.3 = (bf16[256,1024]{1,0:T(8,128)(2,1)}, bf16[2,4,256,512]{3,2,1,0:T(8,128)(2,1)}, f32[256,1024]{1,0:T(8,128)}, bf16[256,1024]{1,0:T(8,128)(2,1)...) custom-call(f32[256,192]{1,0:T(8,128)} %get-tuple-element.230.dpred_ref, ...), custom_call_target="tpu_custom_call" | custom-call | flops 6039797760 | bytes 23068672 | tf_op jit(solution)/shard_map/branch_backward/pallas_call | solution.py:580
  427.7 13.6 %exchange_swap.3 = (bf16[2048,128]{1,0:T(8,128)(2,1)}, bf16[2,4,256,512]{3,2,1,0:T(8,128)(2,1)}, bf16[2,4,256,512]{3,2,1,0:T(8,128)(2,1)}, bf16[2,4,256,128]{3,2...) custom-call(bf16[256,1024]{1,0:T(8,128)(2,1)} %get-tuple-element.163.refs_0_, ...), custom_call_target="tpu_custom_call" | custom-call | tf_op jit(solution)/shard_map/exchange_swap/pallas_call | solution.py:692
  441.4 79.2 %finish_program.1 = (bf16[256,3072]{1,0:T(8,128)(2,1)}, f32[256,384]{1,0:T(8,128)}, f32[512,256]{1,0:T(8,128)}) custom-call(bf16[2,4,256,512]{3,2,1,0:T(8,128)(2,1)} %get-tuple-element.173.refs_0_, bf16[256,1024]{1,0:T(8,128)(2,1)} %get-tuple-element.147.refs_4_.refs_1_, bf16[256,1024]{1,0:T(8,128)(2,1)} %get-tuple-element.174.refs_2_, ...), custom_call_target="tpu_custom_call" | custom-call | tf_op jit(solution)/shard_map/finish_program/pallas_call | solution.py:1109
  520.6 83.6 %entry_last.1 = (f32[512,1024]{1,0:T(8,128)}, f32[640,256]{1,0:T(8,128)}, f32[256,384]{1,0:T(8,128)}) custom-call(bf16[2,4,256,512]{3,2,1,0:T(8,128)(2,1)} %get-tuple-element.150.refs_0_, bf16[2,4,256,128]{3,2,1,0:T(8,128)(2,1)} %get-tuple-element.151.refs_1_, bf16[256,1024]{1,0:T(8,128)(2,1)} %get-tuple-element.148.refs_5_.refs_2_, ...), custom_call_target="tpu_custom_call" | custom-call | tf_op jit(solution)/shard_map/entry_last/pallas_call | solution.py:1619
  607.6 58.7 %exchange_sum.1 = (f32[512,1024]{1,0:T(8,128)}, f32[8,128]{1,0:T(8,128)}) custom-call(f32[512,1024]{1,0:T(8,128)} %get-tuple-element.196.x_ref, f32[1,1]{1,0:T(1,128)} %bitcast.19.loss_ref, f32[256,384]{1,0:T(8,128)} %copy.78.qkv_ref.refs_4_, f32[640,256]{1,0:T(8,128)} %get-tuple-element.198.up_out_ref.refs_5_, f32[512,256]{1,0:T(8,128)} %get-tuple-element.199.down_ref.refs_6_), custom_call_target="tpu_custom_call" | custom-call | tf_op jit(solution)/shard_map/exchange_sum/pallas_call | solution.py:1276
  666.2 12.3 %update_all.1 = (f32[1,1]{1,0:T(1,128)}, f32[1,1]{1,0:T(1,128)}, f32[440,1024]{1,0:T(8,128)}, f32[440,1024]{1,0:T(8,128)}, f32[440,1024]{1,0:T(8,128)}, /*index=...) custom-call(s32[1]{0:T(128)} %bitcast.refs_0_, ...), custom_call_target="tpu_custom_call" | custom-call | tf_op jit(solution)/shard_map/update_all/pallas_call | solution.py:1802
  (61 shorter events, 19.7 us)
Async XLA Ops:
  8.3 2.8 copy-start
  10.1 2.1 copy-start.1
  12.2 1.2 copy-start.8
  12.2 1.3 copy-start.9
  12.2 1.5 copy-start.10
  12.2 1.6 copy-start.3
  15.4 161.2 %copy-start.7 = (f32[1,2,256,192]{2,3,1,0:T(8,128)S(1)}, f32[1,2,256,192]{2,3,1,0:T(8,128)}, u32[]{:S(2)}) copy-start(f32[1,2,256,192]{2,3,1,0:T(8,128)} %param.25) | copy-start | bytes 1179652
  176.9 125.9 %collective-permute-start = (f32[2,256,192]{2,1,0:T(8,128)S(1)}, f32[2,256,192]{2,1,0:T(8,128)S(1)}, u32[]{:S(2)}, u32[]{:S(2)}) collective-permute-start(f32[2,256,192]{2,1,0:T(8,128)S(1)} %bitcast.67), channel_id=1, source_target_pairs={{0,0},{1,1},{2,8},{3,9},{4,16},{5,17},{6,24},{7,25},{8,2},{9,3},{1... | collective-permute-start | bytes 1179656 | tf_op jit(solution)/shard_map/ppermute | solution.py:85
  180.5 19.1 %copy-start.6 = (f32[256,256]{1,0:T(8,128)S(1)}, f32[256,256]{1,0:T(8,128)}, u32[]{:S(2)}) copy-start(f32[256,256]{1,0:T(8,128)} %get-tuple-element.126.refs_18_) | copy-start | bytes 786436
  251.2 17.7 %copy-start.2 = (bf16[2048,384]{1,0:T(8,128)(2,1)}, bf16[2048,384]{1,0:T(8,128)(2,1)S(1)}, u32[]{:S(2)}) copy-start(bf16[2048,384]{1,0:T(8,128)(2,1)S(1)} %convolution_convert_fusion.qkv_ref) | copy-start | bytes 4718596
  380.5 25.1 %copy-start.4 = (f32[256,192]{1,0:T(8,128)S(1)}, f32[256,192]{1,0:T(8,128)}, u32[]{:S(2)}) copy-start(f32[256,192]{1,0:T(8,128)} %get-tuple-element.133) | copy-start | bytes 589828
  380.5 25.1 %copy-start.5 = (f32[256,192]{1,0:T(8,128)S(1)}, f32[256,192]{1,0:T(8,128)}, u32[]{:S(2)}) copy-start(f32[256,192]{1,0:T(8,128)} %get-tuple-element.138) | copy-start | bytes 589828

commit v8 on v7

--- a/solution.py
+++ b/solution.py
@@ -85,144 +85,9 @@
     return lax.ppermute(value, ("dp", "mp"), cross_pairs())
 
 
-def gather_kernel(x_ref, o_ref, send_sem, recv_sem):
-    rows = x_ref.shape[0]
-    half = rows // 2
-    dp, level, core = mesh_place()
-    side = dp + 1 - 2 * lax.rem(dp, 2)
-    down = lax.rem(dp + 2, 4)
-    far = 3 - dp
-    to_side = device_of(side, level, core)
-    to_down = device_of(down, level, core)
-    to_core = device_of(dp, level, 1 - core)
-
-    def rows_of(owner, who, first, size):
-        return pl.ds(pl.multiple_of((owner * 2 + who) * rows + first, half), size)
-
-    barrier = pltpu.get_barrier_semaphore()
-    for target in (to_side, to_down, to_core):
-        pl.semaphore_signal(barrier, inc=1, device_id=target, device_id_type=MESH)
-    pl.semaphore_wait(barrier, 3)
-
-    def send(slot, source, where, target):
-        copy = pltpu.make_async_remote_copy(
-            src_ref=source,
-            dst_ref=o_ref.at[where],
-            send_sem=send_sem.at[slot],
-            recv_sem=recv_sem.at[slot],
-            device_id=target,
-            device_id_type=MESH,
-        )
-        copy.start()
-        return copy
-
-    first = x_ref.at[pl.ds(0, half)]
-    second = x_ref.at[pl.ds(half, half)]
-    side_a = send(0, first, rows_of(dp, core, 0, half), to_side)
-    down_b = send(1, second, rows_of(dp, core, half, half), to_down)
-    side_b = send(2, second, rows_of(dp, core, half, half), to_side)
-    down_a = send(3, first, rows_of(dp, core, 0, half), to_down)
-    near = send(4, x_ref, rows_of(dp, core, 0, rows), to_core)
-    o_ref[rows_of(dp, core, 0, rows)] = x_ref[...]
-    side_a.wait_recv()
-    place = rows_of(side, core, 0, half)
-    far_a = send(5, o_ref.at[place], place, to_down)
-    down_b.wait_recv()
-    place = rows_of(down, core, half, half)
-    far_b = send(6, o_ref.at[place], place, to_side)
-    side_b.wait_recv()
-    place = rows_of(side, core, 0, rows)
-    near_side = send(7, o_ref.at[place], place, to_core)
-    down_a.wait_recv()
-    place = rows_of(down, core, 0, rows)
-    near_down = send(8, o_ref.at[place], place, to_core)
-    far_a.wait_recv()
-    far_b.wait_recv()
-    place = rows_of(far, core, 0, rows)
-    near_far = send(9, o_ref.at[place], place, to_core)
-    for copy in (near, near_side, near_down, near_far):
-        copy.wait_recv()
-    for copy in (side_a, down_b, side_b, down_a, near, far_a, far_b, near_side, near_down, near_far):
-        copy.wait_send()
-
-
-def spread_rows(crossed, normed):
-    if not crossed:
-        return lax.all_gather(normed, "mp", axis=0, tiled=True)
-    rows, width = normed.shape
-    return pl.pallas_call(
-        gather_kernel,
-        out_shape=jax.ShapeDtypeStruct((8 * rows, width), normed.dtype),
-        in_specs=[VMEM],
-        out_specs=VMEM,
-        scratch_shapes=[pltpu.SemaphoreType.DMA((10,)), pltpu.SemaphoreType.DMA((10,))],
-        compiler_params=pltpu.CompilerParams(
-            collective_id=1, has_side_effects=True, vmem_limit_bytes=BIG
-        ),
-        name="gather_rows",
-    )(normed)
-
-
-def exchange_kernel(to_columns, rows, width, x_ref, o_ref, send_sem, recv_sem):
-    dp, level, core = mesh_place()
-    me = dp * 2 + core
-    barrier = pltpu.get_barrier_semaphore()
-    others = []
-    for step in (7, 6, 5, 4, 3, 2, 1):
-        part = lax.rem(me + step, 8)
-        others.append((step, part, device_of(part // 2, level, lax.rem(part, 2))))
-    for step, part, target in others:
-        pl.semaphore_signal(barrier, inc=1, device_id=target, device_id_type=MESH)
-    pl.semaphore_wait(barrier, 7)
-
-    def row_block(ref, part):
-        return ref.at[pl.ds(pl.multiple_of(part * rows, rows), rows), :]
-
-    def column_block(ref, part):
-        return ref.at[:, pl.ds(pl.multiple_of(part * width, width), width)]
-
-    source_block, target_block = (
-        (row_block, column_block) if to_columns else (column_block, row_block)
-    )
-    copies = []
-    for step, part, target in others:
-        copy = pltpu.make_async_remote_copy(
-            src_ref=source_block(x_ref, part),
-            dst_ref=target_block(o_ref, me),
-            send_sem=send_sem.at[step],
-            recv_sem=recv_sem.at[step],
-            device_id=target,
-            device_id_type=MESH,
-        )
-        copy.start()
-        copies.append(copy)
-    target_block(o_ref, me)[...] = source_block(x_ref, me)[...]
-    for copy in copies:
-        copy.wait()
-
-
-def exchange(crossed, value, to_columns, number):
-    parts = lax.axis_size("mp")
-    if to_columns:
-        rows, width = value.shape[0] // parts, value.shape[1]
-        shape = (rows, width * parts)
-    else:
-        rows, width = value.shape[0], value.shape[1] // parts
-        shape = (rows * parts, width)
-    if not crossed:
-        split, joined = (0, 1) if to_columns else (1, 0)
-        return lax.all_to_all(value, "mp", split_axis=split, concat_axis=joined, tiled=True)
-    return pl.pallas_call(
-        partial(exchange_kernel, to_columns, rows, width),
-        out_shape=jax.ShapeDtypeStruct(shape, value.dtype),
-        in_specs=[VMEM],
-        out_specs=VMEM,
-        scratch_shapes=[pltpu.SemaphoreType.DMA((8,)), pltpu.SemaphoreType.DMA((8,))],
-        compiler_params=pltpu.CompilerParams(
-            collective_id=number, has_side_effects=True, vmem_limit_bytes=BIG
-        ),
-        name="exchange_parts",
-    )(value)
+def exchange(value, to_columns):
+    split, joined = (0, 1) if to_columns else (1, 0)
+    return lax.all_to_all(value, "mp", split_axis=split, concat_axis=joined, tiled=True)
 
 
 def pick_head(value, head, heads):
@@ -1823,18 +1688,293 @@
     return shard.reshape(rows, 3, -1, HEAD_DIM).transpose(0, 2, 1, 3).reshape(rows, -1)
 
 
+class Rows:
+    count = 11
+
+    def __init__(self, refs, sems):
+        (self.h1, self.rows_ref, self.weight, self.qkv, self.vt, self.o_ref, self.full, self.lse,
+         self.attended) = refs
+        self.sems, self.o_sems, self.own_sem = sems
+        dp, level, core = mesh_place()
+        self.dp, self.core = dp, core
+        self.me = dp * 2 + core
+        self.height = self.h1.shape[0]
+        self.width = self.o_ref.shape[1]
+        half = self.height // 2
+        x = lax.rem(dp, 2)
+        beside, below, far = dp + 1 - 2 * x, lax.rem(dp + 2, 4), 3 - dp
+        self.owners = (beside, below, far)
+        self.peers = []
+        for move in range(1, 8):
+            part = lax.rem(self.me + move, 8)
+            self.peers.append(device_of(part // 2, level, lax.rem(part, 2)))
+        side = device_of(beside, level, core)
+        down = device_of(below, level, core)
+        near = device_of(dp, level, 1 - core)
+        self.level = level
+        slots = [0]
+
+        def remote(source, target_ref, target):
+            slot = slots[0]
+            slots[0] += 1
+            return pltpu.make_async_remote_copy(
+                src_ref=source,
+                dst_ref=target_ref,
+                send_sem=self.sems.at[0, slot],
+                recv_sem=self.sems.at[1, slot],
+                device_id=target,
+                device_id_type=MESH,
+            )
+
+        def place(owner, first, size):
+            start = pl.multiple_of((owner * 2 + core) * self.height + first, half)
+            return self.rows_ref.at[pl.ds(start, size)]
+
+        def relay(where, target):
+            return remote(where, where, target)
+
+        first, second = self.h1.at[pl.ds(0, half)], self.h1.at[pl.ds(half, half)]
+        self.side_a = remote(first, place(dp, 0, half), side)
+        self.down_b = remote(second, place(dp, half, half), down)
+        self.side_b = remote(second, place(dp, half, half), side)
+        self.down_a = remote(first, place(dp, 0, half), down)
+        self.near_own = remote(self.h1, place(dp, 0, self.height), near)
+        self.far_a = relay(place(beside, 0, half), down)
+        self.far_b = relay(place(below, half, half), side)
+        self.near_side = relay(place(beside, 0, self.height), near)
+        self.near_down = relay(place(below, 0, self.height), near)
+        self.near_far = relay(place(far, 0, self.height), near)
+
+    def part_rows(self, part):
+        return pl.ds(pl.multiple_of(part * self.height, self.height), self.height)
+
+    def project(self, owner, core):
+        where = self.part_rows(owner * 2 + core)
+        self.qkv[where, :] = lax.dot_general(
+            self.rows_ref[where, :], self.weight[...], NT, preferred_element_type=f32
+        ).astype(bf16)
+
+    def send_o(self, part, target):
+        columns = pl.ds(pl.multiple_of(self.me * self.width, self.width), self.width)
+        return pltpu.make_async_remote_copy(
+            src_ref=self.o_ref.at[self.part_rows(part), :],
+            dst_ref=self.attended.at[:, columns],
+            send_sem=self.o_sems.at[0, lax.rem(part + 8 - self.me, 8)],
+            recv_sem=self.o_sems.at[1, lax.rem(part + 8 - self.me, 8)],
+            device_id=target,
+            device_id_type=MESH,
+        )
+
+    def keep_o(self):
+        columns = pl.ds(pl.multiple_of(self.me * self.width, self.width), self.width)
+        return pltpu.make_async_copy(
+            self.o_ref.at[self.part_rows(self.me), :], self.attended.at[:, columns], self.own_sem
+        )
+
+    def phase(self, number):
+        beside, below, far = self.owners
+        if number == 0:
+            for copy in (self.side_a, self.down_b, self.side_b, self.down_a, self.near_own):
+                copy.start()
+            self.rows_ref[self.part_rows(self.me), :] = self.h1[...]
+        elif number == 1:
+            self.project(self.dp, self.core)
+            self.near_own.wait_recv()
+        elif number == 2:
+            self.side_a.wait_recv()
+            self.far_a.start()
+            self.down_b.wait_recv()
+            self.far_b.start()
+            self.project(self.dp, 1 - self.core)
+        elif number == 3:
+            self.side_b.wait_recv()
+            self.near_side.start()
+            self.down_a.wait_recv()
+            self.near_down.start()
+            self.project(beside, self.core)
+            self.project(below, self.core)
+        elif number == 4:
+            self.near_side.wait_recv()
+            self.near_down.wait_recv()
+            self.project(beside, 1 - self.core)
+            self.project(below, 1 - self.core)
+        elif number == 5:
+            self.far_a.wait_recv()
+            self.far_b.wait_recv()
+            self.near_far.start()
+            self.project(far, self.core)
+        elif number == 6:
+            self.near_far.wait_recv()
+            self.project(far, 1 - self.core)
+            self.vt[...] = self.qkv[:, 2 * self.width :].T
+
+    def attend(self, turn):
+        owner = lax.rem(self.dp + 1 + turn, 4)
+        size = 2 * self.height
+        where = pl.ds(pl.multiple_of(owner * size, size), size)
+        heads = self.width // HEAD_DIM
+        full, sums = attend_rows(
+            heads, self.qkv[where, : self.width],
+            self.qkv.at[:, self.width : 2 * self.width], self.vt,
+        )
+        for head in range(heads):
+            self.lse[head : head + 1, where] = sums[head]
+        self.full[where, :] = full
+        self.o_ref[where, :] = full.astype(bf16)
+
+        @pl.when(turn < 3)
+        def _():
+            for core in range(2):
+                self.send_o(owner * 2 + core, device_of(owner, self.level, core)).start()
+
+        @pl.when(turn == 3)
+        def _():
+            other = device_of(self.dp, self.level, 1 - self.core)
+            self.send_o(self.dp * 2 + 1 - self.core, other).start()
+            self.keep_o().start()
+
+    def finish(self):
+        for move in range(1, 8):
+            part = lax.rem(self.me + move, 8)
+            self.send_o(part, self.peers[move - 1]).wait()
+        self.keep_o().wait()
+        for copy in (
+            self.side_a, self.down_b, self.side_b, self.down_a, self.near_own, self.far_a,
+            self.far_b, self.near_side, self.near_down, self.near_far,
+        ):
+            copy.wait_send()
+
+
+def row_scratch(rows, width):
+    return [
+        pltpu.VMEM((rows, D), bf16),
+        pltpu.VMEM((8 * rows, D), bf16),
+        pltpu.VMEM((3 * width, D), bf16),
+        pltpu.VMEM((width, 8 * rows), bf16),
+        pltpu.VMEM((8 * rows, width), bf16),
+        pltpu.SemaphoreType.DMA((2, 10)),
+        pltpu.SemaphoreType.DMA((2, 8)),
+        pltpu.SemaphoreType.DMA((3,)),
+    ]
+
+
+def lead_rows_of(lead, lead_ref):
+    row = lax.broadcasted_iota(jnp.int32, (1, 8), 1).astype(f32)
+    lead_hot = jnp.where(row == lead, 1.0, 0.0).astype(f32)
+    return exact_product(lead_hot, lead_ref[...])
+
+
+def middle_kernel(
+    guess_ref, first_ref, keyed_ref, bias_ref, patch_ref, var_ref, lead_ref, gains_ref, weights_ref,
+    x0_ref, cells_ref, qkv_ref, full_ref, lse_ref, rows_out, attended_ref,
+    h1_ref, rows_ref, weight_ref, vt_ref, o_ref, sems, o_sems, own_sem,
+):
+    turn = pl.program_id(0)
+    dp, _, core = mesh_place()
+    rows = Rows(
+        (h1_ref, rows_ref, weight_ref, qkv_ref, vt_ref, o_ref, full_ref, lse_ref, attended_ref),
+        (sems, o_sems, own_sem.at[0]),
+    )
+    size = weight_ref.shape[0]
+    weight = pltpu.make_async_copy(
+        weights_ref.at[pl.ds(pl.multiple_of((dp * 2 + core) * size, size), size), :],
+        weight_ref, own_sem.at[1],
+    )
+    save = pltpu.make_async_copy(rows_ref, rows_out, own_sem.at[2])
+    pairs = HEADS // 2
+
+    @pl.when(turn == 0)
+    def _():
+        barrier = pltpu.get_barrier_semaphore()
+        for target in rows.peers:
+            pl.semaphore_signal(barrier, inc=1, device_id=target, device_id_type=MESH)
+        pl.semaphore_wait(barrier, 7)
+        weight.start()
+        cells_ref[:, : 4 * V] = guess_ref[...]
+        cells_ref[:, 4 * V :] = jnp.zeros_like(cells_ref[:, 4 * V :])
+
+    @pl.when(turn < pairs)
+    def _():
+        embed_pair(turn, cells_ref[...], keyed_ref, bias_ref, patch_ref, var_ref, x0_ref)
+
+    @pl.when(turn == pairs)
+    def _():
+        x0_ref[...] += lead_rows_of(first_ref[0:1, 4 * V + 5 : 4 * V + 6], lead_ref)
+        unit, _ = normed_parts(x0_ref[...])
+        h1_ref[...] = (unit * gains_ref[0:1, :] + gains_ref[1:2, :]).astype(bf16)
+        weight.wait()
+
+    for number in range(7):
+
+        @pl.when(turn == pairs + number)
+        def _(number=number):
+            rows.phase(number)
+            if number == 6:
+                save.start()
+
+    @pl.when(turn >= pairs + 7)
+    def _():
+        rows.attend(turn - pairs - 7)
+
+    @pl.when(turn == pairs + 10)
+    def _():
+        rows.finish()
+        save.wait()
+
+
+def middle_program(guess, first_cells, prepared, lead_table, norm_gains, qkv_t):
+    patch, variable, keyed, bias = prepared
+    rows = guess.shape[0]
+    padded = patch.shape[0]
+    width = D // 8
+    heads = width // HEAD_DIM
+    total = 8 * rows
+    anywhere = pl.BlockSpec(memory_space=pl.ANY)
+    fixed = lambda shape: pl.BlockSpec(shape, lambda i: (0, 0))
+    by_pair = pl.BlockSpec(
+        (padded, 2 * HEAD_DIM), lambda i: (0, jnp.clip(i, 0, HEADS // 2 - 1))
+    )
+    shapes = [
+        ((rows, D), f32),
+        ((rows, padded), f32),
+        ((total, 3 * width), bf16),
+        ((total, width), f32),
+        ((heads, total), f32),
+    ]
+    return pl.pallas_call(
+        middle_kernel,
+        grid=(HEADS // 2 + Rows.count,),
+        out_shape=[jax.ShapeDtypeStruct(shape, kind) for shape, kind in shapes]
+        + [jax.ShapeDtypeStruct((total, D), bf16), jax.ShapeDtypeStruct((rows, D), bf16)],
+        in_specs=[once(value.shape) for value in (guess, first_cells, keyed, bias)]
+        + [by_pair, by_pair, once(lead_table.shape), once(norm_gains.shape), anywhere],
+        out_specs=[fixed(shape) for shape, _ in shapes] + [anywhere, anywhere],
+        scratch_shapes=row_scratch(rows, width),
+        compiler_params=pltpu.CompilerParams(
+            collective_id=9, has_side_effects=True, vmem_limit_bytes=BIG
+        ),
+        name="middle_program",
+    )(guess, first_cells, keyed, bias, patch, variable, lead_table, norm_gains, qkv_t)
+
+
 lag_one, lag_two, ahead = 2, 4, 3
-embed_at, gather_at, project_at, attend_at = 3, 11, 14, 18
+embed_at, gather_at = 3, 11
 
 
 def start_kernel(halves, *refs):
     count = len(halves)
     packed_ref, keyed_ref, bias_ref, patch_ref, var_ref, lead_ref, gains_ref = refs[:7]
     shards = refs[7 : 7 + count]
-    x0_ref, cells_ref, qkv_ref, o_ref, full_ref, lse_ref, count_ref, rows_out = refs[7 + count : 15 + count]
+    x0_ref, cells_ref, qkv_ref, full_ref, lse_ref, count_ref, rows_out, attended_ref = refs[
+        7 + count : 15 + count
+    ]
     outs = refs[15 + count : 15 + 2 * count]
-    (held_ref, h1_ref, rows_ref, weight_ref, vt_ref, tile_ref, send_sem, recv_sem,
-     level_send, level_recv, own_sem) = refs[15 + 2 * count :]
+    (h1_ref, rows_ref, weight_ref, vt_ref, o_ref, row_sems, o_sems, row_own, held_ref, tile_ref,
+     send_sem, recv_sem, level_send, level_recv, own_sem) = refs[15 + 2 * count :]
+    rows = Rows(
+        (h1_ref, rows_ref, weight_ref, qkv_ref, vt_ref, o_ref, full_ref, lse_ref, attended_ref),
+        (row_sems, o_sems, row_own.at[0]),
+    )
     step = pl.program_id(0)
     dp, level, core = mesh_place()
     x = lax.rem(dp, 2)
@@ -1937,27 +2077,6 @@
         def _():
             openings[number][1].start()
 
-    rows = h1_ref.shape[0]
-    cut = rows // 2
-
-    def rows_of(owner, who, first, size):
-        return rows_ref.at[pl.ds(pl.multiple_of((owner * 2 + who) * rows + first, cut), size)]
-
-    def relay(place_ref, target):
-        return remote(place_ref, place_ref, target)
-
-    first_half, second_half = h1_ref.at[pl.ds(0, cut)], h1_ref.at[pl.ds(cut, cut)]
-    beside, below, far = columns["side"], columns["down"], columns["far"]
-    side_a = remote(first_half, rows_of(dp, core, 0, cut), side)
-    down_b = remote(second_half, rows_of(dp, core, cut, cut), down)
-    side_b = remote(second_half, rows_of(dp, core, cut, cut), side)
-    down_a = remote(first_half, rows_of(dp, core, 0, cut), down)
-    near_own = remote(h1_ref, rows_of(dp, core, 0, rows), near)
-    far_a = relay(rows_of(beside, core, 0, cut), down)
-    far_b = relay(rows_of(below, core, cut, cut), side)
-    near_side = relay(rows_of(beside, core, 0, rows), near)
-    near_down = relay(rows_of(below, core, 0, rows), near)
-    near_far = relay(rows_of(far, core, 0, rows), near)
     tiles = [
         remote(tile_ref.at[0], tile_ref.at[1], side),
         remote(tile_ref.at[2], tile_ref.at[3], down),
@@ -1965,24 +2084,24 @@
     ]
     deep = [device_of(dp, lax.rem(level + move, 4), core) for move in (1, 2, 3)]
     level_tiles = [remote(tile_ref.at[6], tile_ref.at[7 + move], deep[move]) for move in range(3)]
-    weight = pltpu.make_async_copy(outs[0].at[dp * 2 + core], weight_ref, own_sem.at[count + 1])
-    save = pltpu.make_async_copy(rows_ref, rows_out, own_sem.at[count + 2])
+    weight = pltpu.make_async_copy(outs[0].at[dp * 2 + core], weight_ref, row_own.at[1])
+    save = pltpu.make_async_copy(rows_ref, rows_out, row_own.at[2])
 
     @pl.when(step == 0)
     def _():
         barrier = pltpu.get_barrier_semaphore()
-        for target in (side, down, near, *deep):
+        for target in (*rows.peers, *deep):
             pl.semaphore_signal(barrier, inc=1, device_id=target, device_id_type=MESH)
 
         @pl.when(dp != level)
         def _():
             pl.semaphore_signal(barrier, inc=1, device_id=across, device_id_type=MESH)
-            pl.semaphore_wait(barrier, 7)
+            pl.semaphore_wait(barrier, 11)
             crossing.start()
 
         @pl.when(dp == level)
         def _():
-            pl.semaphore_wait(barrier, 6)
+            pl.semaphore_wait(barrier, 10)
             staying.start()
 
         for number in range(ahead):
@@ -2057,71 +2176,29 @@
     def _():
         embed_pair(step - embed_at, held_ref[...], keyed_ref, bias_ref, patch_ref, var_ref, x0_ref)
 
+    @pl.when(step == gather_at - 2)
+    def _():
+        kept[0].wait()
+        weight.start()
+
     @pl.when(step == gather_at)
     def _():
-        lead = held_ref[0:1, 4 * V + 4 : 4 * V + 5]
-        row = lax.broadcasted_iota(jnp.int32, (1, 8), 1).astype(f32)
-        lead_hot = jnp.where(row == lead, 1.0, 0.0).astype(f32)
-        x0_ref[...] += exact_product(lead_hot, lead_ref[...])
+        x0_ref[...] += lead_rows_of(held_ref[0:1, 4 * V + 4 : 4 * V + 5], lead_ref)
         unit, _ = normed_parts(x0_ref[...])
         h1_ref[...] = (unit * gains_ref[0:1, :] + gains_ref[1:2, :]).astype(bf16)
-        for copy in (side_a, down_b, side_b, down_a, near_own):
-            copy.start()
-        rows_of(dp, core, 0, rows)[...] = h1_ref[...]
-        kept[0].wait()
-        weight.start()
-
-    @pl.when(step == gather_at + 1)
-    def _():
-        side_a.wait_recv()
-        far_a.start()
-        down_b.wait_recv()
-        far_b.start()
-        side_b.wait_recv()
-        near_side.start()
-        down_a.wait_recv()
-        near_down.start()
-
-    @pl.when(step == gather_at + 2)
-    def _():
-        far_a.wait_recv()
-        far_b.wait_recv()
-        near_far.start()
-        for copy in (near_own, near_side, near_down):
-            copy.wait_recv()
-
-    block = rows_ref.shape[0] // 4
-
-    @pl.when(step == project_at)
-    def _():
-        near_far.wait_recv()
-        save.start()
         weight.wait()
 
-    @pl.when((step >= project_at) & (step < project_at + 4))
-    def _():
-        where = pl.ds(pl.multiple_of((step - project_at) * block, block), block)
-        qkv_ref[where, :] = lax.dot_general(
-            rows_ref[where, :], weight_ref[...], NT, preferred_element_type=f32
-        ).astype(bf16)
-
-    width = o_ref.shape[1]
-    heads = width // HEAD_DIM
-
-    @pl.when(step == attend_at)
-    def _():
-        vt_ref[...] = qkv_ref[:, 2 * width :].T
-
-    @pl.when((step >= attend_at) & (step < attend_at + 4))
-    def _():
-        where = pl.ds(pl.multiple_of((step - attend_at) * block, block), block)
-        full, sums = attend_rows(
-            heads, qkv_ref[where, :width], qkv_ref.at[:, width : 2 * width], vt_ref
-        )
-        for head in range(heads):
-            lse_ref[head : head + 1, where] = sums[head]
-        full_ref[where, :] = full
-        o_ref[where, :] = full.astype(bf16)
+    for number in range(7):
+
+        @pl.when(step == gather_at + number)
+        def _(number=number):
+            rows.phase(number)
+            if number == 6:
+                save.start()
+
+    @pl.when((step >= gather_at + 7) & (step < gather_at + 11))
+    def _():
+        rows.attend(step - gather_at - 7)
 
     @pl.when(step == total + lag_two - 1)
     def _():
@@ -2150,8 +2227,7 @@
             def _(chunk=chunk):
                 chunk["level"].wait_send()
 
-        for copy in (side_a, down_b, side_b, down_a, near_own, far_a, far_b, near_side, near_down, near_far):
-            copy.wait_send()
+        rows.finish()
         for copy in (*tiles, *level_tiles):
             copy.wait_send()
         save.wait()
@@ -2165,7 +2241,7 @@
     patch, variable, keyed, bias = prepared
     count = len(shards)
     groups = sum(halves)
-    copies = groups * 24 + count + 17
+    copies = groups * 24 + count + 7
     rows, padded = packed.shape
     total = 8 * rows
     width = shards[0].shape[0] // 3
@@ -2179,7 +2255,6 @@
         ((rows, D), f32),
         (packed.shape, f32),
         ((total, 3 * width), bf16),
-        ((total, width), bf16),
         ((total, width), f32),
         ((heads, total), f32),
         ((8, 128), f32),
@@ -2188,25 +2263,22 @@
         partial(start_kernel, halves),
         grid=(groups * 3 + lag_two,),
         out_shape=[jax.ShapeDtypeStruct(shape, kind) for shape, kind in shapes]
-        + [jax.ShapeDtypeStruct((total, D), bf16)]
+        + [jax.ShapeDtypeStruct((total, D), bf16), jax.ShapeDtypeStruct((rows, D), bf16)]
         + [jax.ShapeDtypeStruct((8,) + shard.shape, bf16) for shard in shards],
         in_specs=[anywhere]
         + [fixed(keyed.shape), fixed(bias.shape), by_pair, by_pair]
         + [fixed(lead_table.shape), fixed(norm_gains.shape)]
         + [fixed(shard.shape) for shard in shards],
-        out_specs=[fixed(shape) for shape, _ in shapes] + [anywhere] * (count + 1),
-        scratch_shapes=[
+        out_specs=[fixed(shape) for shape, _ in shapes] + [anywhere] * (count + 2),
+        scratch_shapes=row_scratch(rows, width)
+        + [
             pltpu.VMEM(packed.shape, f32),
-            pltpu.VMEM((rows, D), bf16),
-            pltpu.VMEM((total, D), bf16),
-            pltpu.VMEM(shards[0].shape, bf16),
-            pltpu.VMEM((width, total), bf16),
             pltpu.VMEM((10, 8, 128), f32),
             pltpu.SemaphoreType.DMA((copies,)),
             pltpu.SemaphoreType.DMA((copies,)),
             pltpu.SemaphoreType.DMA((groups * 5,)),
             pltpu.SemaphoreType.DMA((groups * 4,)),
-            pltpu.SemaphoreType.DMA((count + 3,)),
+            pltpu.SemaphoreType.DMA((count + 1,)),
         ],
         compiler_params=pltpu.CompilerParams(
             collective_id=7, has_side_effects=True, vmem_limit_bytes=BIG
@@ -2267,7 +2339,7 @@
     )
     if crossed:
         (
-            x_first, cells, packed, own_out, full, logsum, count, rows_one,
+            x_first, cells, packed, full, logsum, count, rows_one, attended,
             qkv_t, w_outs, w_ups, w_downs
         ) = start_program(
             packed, prepared, tables[5 * V : 5 * V + 8], norm_gains,
@@ -2283,7 +2355,9 @@
             for shard in (low(w_out), low(w_up), low(w_down), qkv_low.T)
         ]
     gathered = (w_outs.reshape(D, D), w_ups, w_downs.reshape(-1, D), qkv_t.reshape(3 * D, D))
-    qkv_local = choose(qkv_t, part)
+    if not crossed:
+        qkv_local = choose(qkv_t, part)
+    first_cells = cells
     leads = cells[0, 4 * V + 4 : 4 * V + 6].astype(jnp.int32)
     ocean = 1.0 - cells[:, 4 * V : 4 * V + 4]
     denom = 2.0 * V * jnp.maximum(count, 1.0)
@@ -2299,17 +2373,21 @@
     loss_part = f32(0.0)
     records = []
     for rollout in range(2):
-        if rollout == 1:
-            cells = jnp.pad(guess, ((0, 0), (0, 64)))
-        if rollout == 1 or not crossed:
+        if crossed and rollout == 1:
+            x_first, cells, packed, full, logsum, rows_one, attended = middle_program(
+                guess, first_cells, prepared, tables[5 * V : 5 * V + 8], norm_gains, gathered[3]
+            )
+        if not crossed:
+            if rollout == 1:
+                cells = jnp.pad(guess, ((0, 0), (0, 64)))
             lead_row = lax.dynamic_slice_in_dim(tables, 5 * V + leads[rollout], 1, 0)
             x_first, normed = embed_forward(cells, prepared, lead_row, norm_gains)
-            rows_one = spread_rows(crossed, normed)
+            rows_one = lax.all_gather(normed, "mp", axis=0, tiled=True)
             packed = lax.dot_general(
                 rows_one, qkv_local, NT, preferred_element_type=f32
             ).astype(bf16)
             own_out, full, logsum = attend(packed)
-        attended = exchange(crossed, own_out, True, 2)
+            attended = exchange(own_out, True)
         if crossed and rollout == 0:
             later_targets, attended = tie(targets[0], attended)
             answers = cross(crossed, later_targets)
@@ -2329,7 +2407,7 @@
     query = tables[5 * V + LEADS : 5 * V + LEADS + 1]
     gain_low = jnp.zeros((2, D), f32)
     table_parts, lead_sums = [], []
-    qkv_grad = jnp.zeros((D, qkv_local.shape[0]), f32)
+    qkv_grad = jnp.zeros((D, w_qkv.shape[1]), f32)
     kept = []
 
     for rollout in (1, 0):
@@ -2352,7 +2430,7 @@
         else:
             flat = lambda value: value.transpose(2, 1, 0, 3).reshape(shard_rows, -1)
             kept.append((attended, rows_two, flat(active), mid_low, flat(hidden_grad), last_low))
-            own_grad = exchange(crossed, out_grad, False, 3)
+            own_grad = exchange(out_grad, False)
         if crossed and rollout == 0:
             token_grad, level_share, down_sum = finish_program(
                 [(step[0], step[3], step[4]) for step in kept],
@@ -2362,7 +2440,7 @@
             token_grad, qkv_grad = attend_exchange(packed, own_grad, full, logsum, rows_one)
         else:
             packed_grad = attend_back(own_grad, packed, full, logsum)
-            token_grad = exchange(crossed, packed_grad, True, 4 + 4)
+            token_grad = exchange(packed_grad, True)
             qkv_grad = qkv_grad + lax.dot_general(
                 rows_one, packed_grad, TN, preferred_element_type=f32
             )

time: 684 us -> 655 us (0.958)
  Pallas kernels: 641 us -> 621 us
    pallas_call x5 -> x1, Pallas kernels: 83.1 us -> 61.5 us  [middle_program(): pl.pallas_call(middle_kernel, grid=(HEADS // 2 + Rows.count,), out_shape=...]
  transfers between devices with their start and end apart: 1 -> 1, of which waited for: 0 -> 0; matrix products, arithmetic and copies ran while one was open for 2% -> 1% of each run, Pallas kernels for 16% -> 15%
where the time goes in v8:
time: 655 us; the launch traced here: 650 us
  Pallas kernels  621 us (95%)
  other arithmetic  12.5 us (2%)
  local copies, waits for them, and re-layouts  12.1 us (2%)
    pallas_call x1, Pallas kernels, start_program(): pl.pallas_call(partial(start_kernel, halves), grid=(groups * 3 + lag_two,...  152 us
    pallas_call x1, Pallas kernels, entry_last(): pl.pallas_call(entry_last_kernel, grid=(entry_turns,), out_shape=[jax.Sha...  82.8 us
    pallas_call x1, Pallas kernels, finish_program(): pl.pallas_call(finish_kernel, grid=(turns,), out_shape=[jax.ShapeDtypeStr...  79.2 us
    pallas_call x1, Pallas kernels, middle_program(): pl.pallas_call(middle_kernel, grid=(HEADS // 2 + Rows.count,), out_shape=...  61.5 us
    pallas_call x1, Pallas kernels, exchange_sum(): pl.pallas_call(exchange_sum_kernel, out_shape=(jax.ShapeDtypeStruct(value...  58.1 us
    pallas_call x1, Pallas kernels, attend_exchange(): pl.pallas_call(attend_exchange_kernel, grid=(pieces_at + 4,), out_shape=[...  42.5 us
    pallas_call x2, Pallas kernels, branch_backward(): pl.pallas_call(branch_back_kernel, grid=(parts,), out_shape=(jax.ShapeDty...  39.7 us
    pallas_call x2, Pallas kernels, branch_forward(): pl.pallas_call(branch_kernel, grid=(parts,), out_shape=(jax.ShapeDtypeStr...  35.1 us
  transfers between devices with their start and end apart: 1, of which 0 were waited for; matrix products, arithmetic and copies ran while one was open for 1% of the time, Pallas kernels for 15%

profile of v8, /device:TPU:0, one launch (start us, length us, event | category | flops | bytes accessed | tf_op | source)
XLA Modules:
  0.0 650.0 jit_solution(18085492079613827918)
XLA Ops:
  0.7 1.3 fusion.6.hot_ref.refs_24_
  2.0 1.4 slice.28.refs_5_.lead_ref
  3.4 4.9 prepare_tables.1
  8.3 1.8 copy.67
  15.6 152.2 %start_program.1 = (f32[256,1024]{1,0:T(8,128)}, f32[256,256]{1,0:T(8,128)}, bf16[2048,384]{1,0:T(8,128)(2,1)}, f32[2048,128]{1,0:T(8,128)}, f32[2,2048]{1,0:T(2...) custom-call(f32[256,256]{1,0:T(8,128)} %maximum_maximum_fusion.refs_, ...), custom_call_target="tpu_custom_call" | custom-call | tf_op jit(solution)/shard_map/start_program/pallas_call | solution.py:2262
  168.5 2.1 slice.30.head_ref
  171.4 1.3 slice.35.refs_23_
  175.9 1.2 slice.32.refs_3_
  177.8 17.3 %branch_forward.2 = (f32[256,1024]{1,0:T(8,128)}, bf16[256,1024]{1,0:T(8,128)(2,1)}, f32[256,4096]{1,0:T(8,128)}, bf16[2,4,256,512]{3,2,1,0:T(8,128)(2,1)}, f32[256,1024]{1,0:T(8,128)}, /*index=5*/f32[256,192]{1,0:T(8,128)}) custom-call(bf16[256,1024]{1,0:T(8,128)(2,1)} %get-tuple-element.130.o_ref.refs_3_, f32[256,1024]{1,0:T(8,128)} %get-tuple-element.131.x0_ref.refs_15_, ...), custom_call_target="tpu_custom_call" | custom-call | flops 5435817984 | bytes 23068672 | tf_op jit(solution)/shard_map/branch_forward/pallas_call | solution.py:344
  195.2 61.5 %middle_program.1 = (f32[256,1024]{1,0:T(8,128)}, f32[256,256]{1,0:T(8,128)}, bf16[2048,384]{1,0:T(8,128)(2,1)}, f32[2048,128]{1,0:T(8,128)}, f32[2,2048]{1,0:T(...) custom-call(f32[256,192]{1,0:T(8,128)} %get-tuple-element.135.guess_ref, ...), custom_call_target="tpu_custom_call" | custom-call | tf_op jit(solution)/shard_map/middle_program/pallas_call | solution.py:1944
  257.3 17.8 %branch_forward.3 = (f32[256,1024]{1,0:T(8,128)}, bf16[256,1024]{1,0:T(8,128)(2,1)}, f32[256,4096]{1,0:T(8,128)}, bf16[2,4,256,512]{3,2,1,0:T(8,128)(2,1)}, f32[256,1024]{1,0:T(8,128)}, /*index=5*/f32[256,192]{1,0:T(8,128)}) custom-call(bf16[256,1024]{1,0:T(8,128)(2,1)} %get-tuple-element.137.o_ref.refs_3_, f32[256,1024]{1,0:T(8,128)} %get-tuple-element.138.x0_ref, ...), custom_call_target="tpu_custom_call" | custom-call | flops 5435817984 | bytes 23068672 | tf_op jit(solution)/shard_map/branch_forward/pallas_call | solution.py:344
  275.1 1.7 multiply_divide_fusion.dpred_ref
  276.8 19.9 %branch_backward.2 = (bf16[256,1024]{1,0:T(8,128)(2,1)}, bf16[2,4,256,512]{3,2,1,0:T(8,128)(2,1)}, f32[256,1024]{1,0:T(8,128)}, bf16[256,1024]{1,0:T(8,128)(2,1)...) custom-call(f32[256,192]{1,0:T(8,128)} %multiply_divide_fusion.dpred_ref, ...), custom_call_target="tpu_custom_call" | custom-call | flops 6039797760 | bytes 23068672 | tf_op jit(solution)/shard_map/branch_backward/pallas_call | solution.py:445
  296.7 13.8 %exchange_swap.2 = (bf16[2048,128]{1,0:T(8,128)(2,1)}, bf16[2,4,256,512]{3,2,1,0:T(8,128)(2,1)}, bf16[2,4,256,512]{3,2,1,0:T(8,128)(2,1)}, bf16[2,4,256,128]{3,2...) custom-call(bf16[256,1024]{1,0:T(8,128)(2,1)} %get-tuple-element.145.refs_0_, ...), custom_call_target="tpu_custom_call" | custom-call | tf_op jit(solution)/shard_map/exchange_swap/pallas_call | solution.py:557
  310.5 42.5 %attend_exchange.1 = (bf16[256,3072]{1,0:T(8,128)(2,1)}, f32[1024,384]{1,0:T(8,128)}) custom-call(bf16[2048,384]{1,0:T(8,128)(2,1)} %get-tuple-element.155.qkv_ref, bf16[2048,128]{1,0:T(8,128)(2,1)} %get-tuple-element.156.do_ref, f32[2048,128]{1,0:T(8,128)} %get-tuple-element.157.full_ref, f32[2,2048]{1,0:T(2,128)} %get-tuple-element.158.lse_ref, ...), custom_call_target="tpu_custom_call" | custom-call | tf_op jit(solution)/shard_map/attend_exchange/pallas_call | solution.py:823
  353.0 25.0 %entry_backward.1 = (f32[256,256]{1,0:T(8,128)}, f32[2,1024]{1,0:T(2,128)}, f32[1,1024]{1,0:T(1,128)}, f32[1024,256]{1,0:T(8,128)}, f32[1024,256]{1,0:T(8,128)}, /*index=5*/f32[16,256]{1,0:T(8,128)}, f32[16,256]{1,0:T(8,128)}) custom-call(bf16[256,3072]{1,0:T(8,128)(2,1)} %get-tuple-element.160.grad_ref, bf16[3072,1024]{1,0:T(8,128)(2,1)} %bitcast.55, ...), custom_call_target="tpu_custom_call" | custom-call | flops 4026531840 | bytes 10485760 | tf_op jit(solution)/shard_map/entry_backward/pallas_call | solution.py:1519
  378.1 2.4 fusion.1
  380.4 19.8 %branch_backward.3 = (bf16[256,1024]{1,0:T(8,128)(2,1)}, bf16[2,4,256,512]{3,2,1,0:T(8,128)(2,1)}, f32[256,1024]{1,0:T(8,128)}, bf16[256,1024]{1,0:T(8,128)(2,1)...) custom-call(f32[256,192]{1,0:T(8,128)} %get-tuple-element.229.dpred_ref, ...), custom_call_target="tpu_custom_call" | custom-call | flops 6039797760 | bytes 23068672 | tf_op jit(solution)/shard_map/branch_backward/pallas_call | solution.py:445
  400.2 13.6 %exchange_swap.3 = (bf16[2048,128]{1,0:T(8,128)(2,1)}, bf16[2,4,256,512]{3,2,1,0:T(8,128)(2,1)}, bf16[2,4,256,512]{3,2,1,0:T(8,128)(2,1)}, bf16[2,4,256,128]{3,2...) custom-call(bf16[256,1024]{1,0:T(8,128)(2,1)} %get-tuple-element.167.refs_0_, ...), custom_call_target="tpu_custom_call" | custom-call | tf_op jit(solution)/shard_map/exchange_swap/pallas_call | solution.py:557
  413.9 79.2 %finish_program.1 = (bf16[256,3072]{1,0:T(8,128)(2,1)}, f32[256,384]{1,0:T(8,128)}, f32[512,256]{1,0:T(8,128)}) custom-call(bf16[2,4,256,512]{3,2,1,0:T(8,128)(2,1)} %get-tuple-element.177.refs_0_, bf16[256,1024]{1,0:T(8,128)(2,1)} %get-tuple-element.148.refs_4_.refs_1_, bf16[256,1024]{1,0:T(8,128)(2,1)} %get-tuple-element.178.refs_2_, ...), custom_call_target="tpu_custom_call" | custom-call | tf_op jit(solution)/shard_map/finish_program/pallas_call | solution.py:974
  493.1 82.8 %entry_last.1 = (f32[512,1024]{1,0:T(8,128)}, f32[640,256]{1,0:T(8,128)}, f32[256,384]{1,0:T(8,128)}) custom-call(bf16[2,4,256,512]{3,2,1,0:T(8,128)(2,1)} %get-tuple-element.151.refs_0_, bf16[2,4,256,128]{3,2,1,0:T(8,128)(2,1)} %get-tuple-element.152.refs_1_, bf16[256,1024]{1,0:T(8,128)(2,1)} %get-tuple-element.149.refs_5_.refs_2_, ...), custom_call_target="tpu_custom_call" | custom-call | tf_op jit(solution)/shard_map/entry_last/pallas_call | solution.py:1484
  576.0 1.2 copy.76
  579.4 58.1 %exchange_sum.1 = (f32[512,1024]{1,0:T(8,128)}, f32[8,128]{1,0:T(8,128)}) custom-call(f32[512,1024]{1,0:T(8,128)} %get-tuple-element.200.x_ref, f32[1,1]{1,0:T(1,128)} %bitcast.16.loss_ref, f32[256,384]{1,0:T(8,128)} %copy.78.qkv_ref.refs_4_, f32[640,256]{1,0:T(8,128)} %get-tuple-element.202.up_out_ref.refs_5_, f32[512,256]{1,0:T(8,128)} %get-tuple-element.203.down_ref.refs_6_), custom_call_target="tpu_custom_call" | custom-call | tf_op jit(solution)/shard_map/exchange_sum/pallas_call | solution.py:1141
  637.5 12.3 %update_all.1 = (f32[1,1]{1,0:T(1,128)}, f32[1,1]{1,0:T(1,128)}, f32[440,1024]{1,0:T(8,128)}, f32[440,1024]{1,0:T(8,128)}, f32[440,1024]{1,0:T(8,128)}, /*index=...) custom-call(s32[1]{0:T(128)} %bitcast.refs_0_, ...), custom_call_target="tpu_custom_call" | custom-call | tf_op jit(solution)/shard_map/update_all/pallas_call | solution.py:1667
  (49 shorter events, 11.0 us)
Async XLA Ops:
  8.3 2.8 copy-start
  10.1 2.0 copy-start.1
  12.2 1.2 copy-start.6
  12.2 1.3 copy-start.7
  12.2 1.5 copy-start.8
  12.2 1.6 copy-start.2
  12.2 2.4 copy-start.5
  167.8 107.3 %collective-permute-start = (f32[2,256,192]{2,1,0:T(8,128)S(1)}, f32[2,256,192]{2,1,0:T(8,128)S(1)}, u32[]{:S(2)}, u32[]{:S(2)}) collective-permute-start(f32[2,256,192]{2,1,0:T(8,128)S(1)} %bitcast.62), channel_id=1, source_target_pairs={{0,0},{1,1},{2,8},{3,9},{4,16},{5,17},{6,24},{7,25},{8,2},{9,3},{1... | collective-permute-start | bytes 1179656 | tf_op jit(solution)/shard_map/ppermute | solution.py:85
  353.0 25.0 %copy-start.3 = (f32[256,192]{1,0:T(8,128)S(1)}, f32[256,192]{1,0:T(8,128)}, u32[]{:S(2)}) copy-start(f32[256,192]{1,0:T(8,128)} %get-tuple-element.135.guess_ref) | copy-start | bytes 589828
  353.0 25.0 %copy-start.4 = (f32[256,192]{1,0:T(8,128)S(1)}, f32[256,192]{1,0:T(8,128)}, u32[]{:S(2)}) copy-start(f32[256,192]{1,0:T(8,128)} %get-tuple-element.139) | copy-start | bytes 589828

commit v9 on v8

--- a/solution.py
+++ b/solution.py
@@ -319,7 +319,7 @@
         unit, _ = normed_parts(x2_ref[...])
         last = unit * gains_ref[4:5, :] + gains_ref[5:6, :]
         pred_ref[...] = lax.dot_general(
-            last, head_ref[...], NT, precision=highest, preferred_element_type=f32
+            last, head_ref[5 * V + LEADS + 1 :, :], NT, precision=highest, preferred_element_type=f32
         )
 
 
@@ -339,7 +339,7 @@
     fixed = lambda shape: pl.BlockSpec(shape, lambda i: (0, 0))
     by_units = pl.BlockSpec((rows, units), lambda i: (0, i))
     by_core = pl.BlockSpec((1, 1, rows, units), lambda i: (i % 2, i // 2, 0, 0))
-    columns = head.shape[0]
+    columns = 4 * V
     flops = 2 * rows * (width * width + 2 * width * parts * units + 6 * width * columns)
     return pl.pallas_call(
         branch_kernel,
@@ -393,7 +393,7 @@
         dhead_ref[...] = lax.dot_general(
             grad, last, TN, precision=highest, preferred_element_type=f32
         )
-        row_grad = jnp.dot(grad, head_ref[...], precision=highest, preferred_element_type=f32)
+        row_grad = jnp.dot(grad, head_ref[5 * V + LEADS + 1 :, :], precision=highest, preferred_element_type=f32)
         wide, gain_grad, bias_grad = norm_grad(unit, inverse, gain, row_grad)
         gain_ref[...] = jnp.zeros_like(gain_ref)
         gain_ref[4:5, :] = gain_grad
@@ -439,7 +439,7 @@
     fixed = lambda shape: pl.BlockSpec(shape, lambda i: (0, 0))
     by_units = pl.BlockSpec((rows, units), lambda i: (0, i))
     by_core = pl.BlockSpec((1, 1, rows, units), lambda i: (i % 2, i // 2, 0, 0))
-    columns = head.shape[0]
+    columns = 4 * V
     wide = (rows, width)
     flops = 2 * rows * (width * width + 2 * width * parts * units + 12 * width * columns)
     return pl.pallas_call(
@@ -765,7 +765,7 @@
         dk_sum[...] = jnp.zeros_like(dk_sum)
         dv_sum[...] = jnp.zeros_like(dv_sum)
 
-    @pl.when(turn < 8)
+    @pl.when((turn >= 0) & (turn < 8))
     def _():
         part = returns.part(turn + 1)
         where = pl.ds(pl.multiple_of(part * rows, rows), rows)
@@ -775,7 +775,7 @@
             qkv_ref.at[:, width : 2 * width], qkv_ref.at[:, 2 * width :], kt_ref, dk_sum, dv_sum,
         )
 
-    @pl.when(turn < 7)
+    @pl.when((turn >= 0) & (turn < 7))
     def _():
         returns.copy(turn + 1, 0).start()
 
@@ -853,7 +853,9 @@
     )(packed, own_grad, full, logsum, rows_one)
 
 
-pieces_at, turns, entry_turns = 9, 14, 11
+pieces_at, entry_turns, attend_from = 9, 15, 4
+middle_at, end_at = (5, 6, 8, 9), (7, 8, 10, 11)
+entry_middle_at, entry_end_at = (5, 6, 9, 10), (10, 11, 12, 13)
 
 
 def finish_kernel(*refs):
@@ -904,21 +906,21 @@
                 rights += [dx2[...], dx2_near[...]]
             scatter.begin(depth, [summed(lefts, rights)], held_ref)
 
-        @pl.when(turn == index + 3)
+        @pl.when(turn == middle_at[index])
         def _(depth=depth):
             scatter.middle(depth)
 
-        @pl.when(turn == index + 5)
+        @pl.when(turn == end_at[index])
         def _(depth=depth):
             scatter.end(depth)
 
     attend_turns(
-        turn, returns, qkv_ref, do_ref, full_ref, lse_ref, dqkv_ref, kt_ref, dk_sum, dv_sum
+        turn - attend_from, returns, qkv_ref, do_ref, full_ref, lse_ref, dqkv_ref, kt_ref, dk_sum, dv_sum
     )
 
     for index in range(4):
 
-        @pl.when(turn == pieces_at + index)
+        @pl.when(turn == attend_from + pieces_at + index)
         def _(index=index):
             piece = prev_ref[...] + lax.dot_general(
                 rows_ref[...], dqkv_ref[...], TN, preferred_element_type=f32
@@ -933,7 +935,7 @@
                 piece_send[index] = piece.astype(bf16)
                 piece_copy(index).start()
 
-    @pl.when(turn == turns - 1)
+    @pl.when(turn == attend_from + pieces_at + 4)
     def _():
         scatter.finish(down_ref)
         for place in range(3):
@@ -958,7 +960,7 @@
     for act, dx2, dx2_near in kept:
         operands += [act, dx2, dx2_near]
         in_specs += [chunk_spec(act.shape[2:]), once(dx2.shape), once(dx2.shape)]
-    piece = lambda i: jnp.clip(i - pieces_at, 0, 3)
+    piece = lambda i: jnp.clip(i - attend_from - pieces_at, 0, 3)
     in_specs += [
         once(packed.shape),
         once(own_grad.shape),
@@ -973,7 +975,7 @@
     share = D // 4
     return pl.pallas_call(
         finish_kernel,
-        grid=(turns,),
+        grid=(attend_from + pieces_at + 5,),
         out_shape=[
             jax.ShapeDtypeStruct((rows, 24 * width), bf16),
             jax.ShapeDtypeStruct((share, 3 * width), f32),
@@ -1393,7 +1395,6 @@
         def _():
             pl.semaphore_signal(barrier, inc=1, device_id=across, device_id_type=MESH)
             pl.semaphore_wait(barrier, 6)
-            crossing.start()
 
         @pl.when(dp == level)
         def _():
@@ -1411,25 +1412,29 @@
                 wides += [dx1[...], dx1_near[...]]
             scatter.begin(depth, [summed(lefts, rights), summed(smalls, wides)], held_ref)
 
-        @pl.when(turn == index + 3)
+        @pl.when(turn == entry_middle_at[index])
         def _(depth=depth):
             scatter.middle(depth)
 
-        @pl.when(turn == index + 6)
+        @pl.when(turn == entry_end_at[index])
         def _(depth=depth):
             scatter.end(depth)
 
-    @pl.when(turn == 0)
+    @pl.when((turn == 11) & (dp != level))
+    def _():
+        crossing.start()
+
+    @pl.when(turn == 4)
     def _():
         entry_rows(
             grad_ref, qkv_ref, x0_ref, mid_ref, gains_ref, du_ref, gain_ref,
             lead_ref.at[0:1, :], dx_ref, flip_ref,
         )
 
-    @pl.when((turn >= 1) & (turn <= HEADS // 2))
+    @pl.when((turn >= 5) & (turn < 5 + HEADS // 2))
     def _():
         size = 2 * HEAD_DIM
-        pair = turn - 1
+        pair = turn - 5
         some = pl.ds(pl.multiple_of(pair * size, size), size)
         entry_pair(
             pair, u_ref, keyed_ref, bias_ref, patch_ref.at[:, some], var_ref.at[:, some],
@@ -2369,7 +2374,7 @@
     )
     lat_pixels = jnp.broadcast_to(lat_rows[:, :, None], (shard_rows, 2, 2)).reshape(shard_rows, 4)
     weighted = jnp.tile(ocean * lat_pixels, (1, V))
-    head = tables[5 * V + LEADS + 1 :]
+    head = tables
     loss_part = f32(0.0)
     records = []
     for rollout in range(2):

time: 655 us -> 660 us (level)
  Pallas kernels: 621 us -> 629 us
where the time goes in v9:
time: 660 us; the launch traced here: 656 us
  Pallas kernels  629 us (95%)
  other arithmetic  12.5 us (2%)
  local copies, waits for them, and re-layouts  9.94 us (2%)
    pallas_call x1, Pallas kernels, start_program(): pl.pallas_call(partial(start_kernel, halves), grid=(groups * 3 + lag_two,...  152 us
    pallas_call x1, Pallas kernels, entry_last(): pl.pallas_call(entry_last_kernel, grid=(entry_turns,), out_shape=[jax.Sha...  86.7 us
    pallas_call x1, Pallas kernels, finish_program(): pl.pallas_call(finish_kernel, grid=(attend_from + pieces_at + 5,), out_sh...  78.2 us
    pallas_call x1, Pallas kernels, exchange_sum(): pl.pallas_call(exchange_sum_kernel, out_shape=(jax.ShapeDtypeStruct(value...  62.1 us
    pallas_call x1, Pallas kernels, middle_program(): pl.pallas_call(middle_kernel, grid=(HEADS // 2 + Rows.count,), out_shape=...  61.6 us
    pallas_call x1, Pallas kernels, attend_exchange(): pl.pallas_call(attend_exchange_kernel, grid=(pieces_at + 4,), out_shape=[...  42.5 us
    pallas_call x2, Pallas kernels, branch_backward(): pl.pallas_call(branch_back_kernel, grid=(parts,), out_shape=(jax.ShapeDty...  40.2 us
    pallas_call x2, Pallas kernels, branch_forward(): pl.pallas_call(branch_kernel, grid=(parts,), out_shape=(jax.ShapeDtypeStr...  35.9 us
  transfers between devices with their start and end apart: 1, of which 0 were waited for; matrix products, arithmetic and copies ran while one was open for 1% of the time, Pallas kernels for 15%

profile of v9, /device:TPU:0, one launch (start us, length us, event | category | flops | bytes accessed | tf_op | source)
XLA Modules:
  0.0 655.9 jit_solution(11066074292296950699)
XLA Ops:
  0.7 1.3 fusion.6.hot_ref.refs_24_
  2.0 1.4 slice.25.refs_5_.lead_ref
  3.4 4.9 prepare_tables.1
  8.3 1.8 copy.67
  12.2 1.1 convert_element_type.45.refs_10_
  15.6 152.1 %start_program.1 = (f32[256,1024]{1,0:T(8,128)}, f32[256,256]{1,0:T(8,128)}, bf16[2048,384]{1,0:T(8,128)(2,1)}, f32[2048,128]{1,0:T(8,128)}, f32[2,2048]{1,0:T(2...) custom-call(f32[256,256]{1,0:T(8,128)} %maximum_maximum_fusion.refs_, ...), custom_call_target="tpu_custom_call" | custom-call | tf_op jit(solution)/shard_map/start_program/pallas_call | solution.py:2267
  169.3 1.4 slice.31.refs_23_
  173.9 1.2 slice.28.refs_3_
  175.7 17.7 %branch_forward.2 = (f32[256,1024]{1,0:T(8,128)}, bf16[256,1024]{1,0:T(8,128)(2,1)}, f32[256,4096]{1,0:T(8,128)}, bf16[2,4,256,512]{3,2,1,0:T(8,128)(2,1)}, f32[256,1024]{1,0:T(8,128)}, /*index=5*/f32[256,192]{1,0:T(8,128)}) custom-call(bf16[256,1024]{1,0:T(8,128)(2,1)} %get-tuple-element.130.o_ref.refs_3_, f32[256,1024]{1,0:T(8,128)} %get-tuple-element.131.x0_ref.refs_15_, ...), custom_call_target="tpu_custom_call" | custom-call | flops 5435817984 | bytes 23068672 | tf_op jit(solution)/shard_map/branch_forward/pallas_call | solution.py:344
  193.4 61.6 %middle_program.1 = (f32[256,1024]{1,0:T(8,128)}, f32[256,256]{1,0:T(8,128)}, bf16[2048,384]{1,0:T(8,128)(2,1)}, f32[2048,128]{1,0:T(8,128)}, f32[2,2048]{1,0:T(...) custom-call(f32[256,192]{1,0:T(8,128)} %get-tuple-element.135.guess_ref, ...), custom_call_target="tpu_custom_call" | custom-call | tf_op jit(solution)/shard_map/middle_program/pallas_call | solution.py:1949
  255.5 18.2 %branch_forward.3 = (f32[256,1024]{1,0:T(8,128)}, bf16[256,1024]{1,0:T(8,128)(2,1)}, f32[256,4096]{1,0:T(8,128)}, bf16[2,4,256,512]{3,2,1,0:T(8,128)(2,1)}, f32[256,1024]{1,0:T(8,128)}, /*index=5*/f32[256,192]{1,0:T(8,128)}) custom-call(bf16[256,1024]{1,0:T(8,128)(2,1)} %get-tuple-element.137.o_ref.refs_3_, f32[256,1024]{1,0:T(8,128)} %get-tuple-element.138.x0_ref, ...), custom_call_target="tpu_custom_call" | custom-call | flops 5435817984 | bytes 23068672 | tf_op jit(solution)/shard_map/branch_forward/pallas_call | solution.py:344
  273.7 1.7 multiply_divide_fusion.dpred_ref
  275.4 20.1 %branch_backward.2 = (bf16[256,1024]{1,0:T(8,128)(2,1)}, bf16[2,4,256,512]{3,2,1,0:T(8,128)(2,1)}, f32[256,1024]{1,0:T(8,128)}, bf16[256,1024]{1,0:T(8,128)(2,1)...) custom-call(f32[256,192]{1,0:T(8,128)} %multiply_divide_fusion.dpred_ref, ...), custom_call_target="tpu_custom_call" | custom-call | flops 6039797760 | bytes 23068672 | tf_op jit(solution)/shard_map/branch_backward/pallas_call | solution.py:445
  295.6 13.7 %exchange_swap.2 = (bf16[2048,128]{1,0:T(8,128)(2,1)}, bf16[2,4,256,512]{3,2,1,0:T(8,128)(2,1)}, bf16[2,4,256,512]{3,2,1,0:T(8,128)(2,1)}, bf16[2,4,256,128]{3,2...) custom-call(bf16[256,1024]{1,0:T(8,128)(2,1)} %get-tuple-element.145.refs_0_, ...), custom_call_target="tpu_custom_call" | custom-call | tf_op jit(solution)/shard_map/exchange_swap/pallas_call | solution.py:557
  309.3 42.5 %attend_exchange.1 = (bf16[256,3072]{1,0:T(8,128)(2,1)}, f32[1024,384]{1,0:T(8,128)}) custom-call(bf16[2048,384]{1,0:T(8,128)(2,1)} %get-tuple-element.155.qkv_ref, bf16[2048,128]{1,0:T(8,128)(2,1)} %get-tuple-element.156.do_ref, f32[2048,128]{1,0:T(8,128)} %get-tuple-element.157.full_ref, f32[2,2048]{1,0:T(2,128)} %get-tuple-element.158.lse_ref, ...), custom_call_target="tpu_custom_call" | custom-call | tf_op jit(solution)/shard_map/attend_exchange/pallas_call | solution.py:823
  351.9 25.0 %entry_backward.1 = (f32[256,256]{1,0:T(8,128)}, f32[2,1024]{1,0:T(2,128)}, f32[1,1024]{1,0:T(1,128)}, f32[1024,256]{1,0:T(8,128)}, f32[1024,256]{1,0:T(8,128)}, /*index=5*/f32[16,256]{1,0:T(8,128)}, f32[16,256]{1,0:T(8,128)}) custom-call(bf16[256,3072]{1,0:T(8,128)(2,1)} %get-tuple-element.160.grad_ref, bf16[3072,1024]{1,0:T(8,128)(2,1)} %bitcast.55, ...), custom_call_target="tpu_custom_call" | custom-call | flops 4026531840 | bytes 10485760 | tf_op jit(solution)/shard_map/entry_backward/pallas_call | solution.py:1524
  376.9 2.4 fusion.1
  379.3 20.1 %branch_backward.3 = (bf16[256,1024]{1,0:T(8,128)(2,1)}, bf16[2,4,256,512]{3,2,1,0:T(8,128)(2,1)}, f32[256,1024]{1,0:T(8,128)}, bf16[256,1024]{1,0:T(8,128)(2,1)...) custom-call(f32[256,192]{1,0:T(8,128)} %get-tuple-element.229.dpred_ref, ...), custom_call_target="tpu_custom_call" | custom-call | flops 6039797760 | bytes 23068672 | tf_op jit(solution)/shard_map/branch_backward/pallas_call | solution.py:445
  399.4 13.6 %exchange_swap.3 = (bf16[2048,128]{1,0:T(8,128)(2,1)}, bf16[2,4,256,512]{3,2,1,0:T(8,128)(2,1)}, bf16[2,4,256,512]{3,2,1,0:T(8,128)(2,1)}, bf16[2,4,256,128]{3,2...) custom-call(bf16[256,1024]{1,0:T(8,128)(2,1)} %get-tuple-element.167.refs_0_, ...), custom_call_target="tpu_custom_call" | custom-call | tf_op jit(solution)/shard_map/exchange_swap/pallas_call | solution.py:557
  413.0 78.2 %finish_program.1 = (bf16[256,3072]{1,0:T(8,128)(2,1)}, f32[256,384]{1,0:T(8,128)}, f32[512,256]{1,0:T(8,128)}) custom-call(bf16[2,4,256,512]{3,2,1,0:T(8,128)(2,1)} %get-tuple-element.177.refs_0_, bf16[256,1024]{1,0:T(8,128)(2,1)} %get-tuple-element.148.refs_4_.refs_1_, bf16[256,1024]{1,0:T(8,128)(2,1)} %get-tuple-element.178.refs_2_, ...), custom_call_target="tpu_custom_call" | custom-call | tf_op jit(solution)/shard_map/finish_program/pallas_call | solution.py:976
  491.2 86.7 %entry_last.1 = (f32[512,1024]{1,0:T(8,128)}, f32[640,256]{1,0:T(8,128)}, f32[256,384]{1,0:T(8,128)}) custom-call(bf16[2,4,256,512]{3,2,1,0:T(8,128)(2,1)} %get-tuple-element.151.refs_0_, bf16[2,4,256,128]{3,2,1,0:T(8,128)(2,1)} %get-tuple-element.152.refs_1_, bf16[256,1024]{1,0:T(8,128)(2,1)} %get-tuple-element.149.refs_5_.refs_2_, ...), custom_call_target="tpu_custom_call" | custom-call | tf_op jit(solution)/shard_map/entry_last/pallas_call | solution.py:1489
  578.0 1.2 copy.76
  581.4 62.1 %exchange_sum.1 = (f32[512,1024]{1,0:T(8,128)}, f32[8,128]{1,0:T(8,128)}) custom-call(f32[512,1024]{1,0:T(8,128)} %get-tuple-element.200.x_ref, f32[1,1]{1,0:T(1,128)} %bitcast.16.loss_ref, f32[256,384]{1,0:T(8,128)} %copy.78.qkv_ref.refs_4_, f32[640,256]{1,0:T(8,128)} %get-tuple-element.202.up_out_ref.refs_5_, f32[512,256]{1,0:T(8,128)} %get-tuple-element.203.down_ref.refs_6_), custom_call_target="tpu_custom_call" | custom-call | tf_op jit(solution)/shard_map/exchange_sum/pallas_call | solution.py:1143
  643.5 12.2 %update_all.1 = (f32[1,1]{1,0:T(1,128)}, f32[1,1]{1,0:T(1,128)}, f32[440,1024]{1,0:T(8,128)}, f32[440,1024]{1,0:T(8,128)}, f32[440,1024]{1,0:T(8,128)}, /*index=...) custom-call(s32[1]{0:T(128)} %bitcast.refs_0_, ...), custom_call_target="tpu_custom_call" | custom-call | tf_op jit(solution)/shard_map/update_all/pallas_call | solution.py:1672
  (48 shorter events, 9.9 us)
Async XLA Ops:
  8.3 2.8 copy-start
  10.1 2.0 copy-start.1
  12.2 1.2 copy-start.6
  12.2 1.3 copy-start.7
  12.2 1.5 copy-start.8
  12.2 1.6 copy-start.2
  12.2 2.4 copy-start.5
  167.7 106.0 %collective-permute-start = (f32[2,256,192]{2,1,0:T(8,128)S(1)}, f32[2,256,192]{2,1,0:T(8,128)S(1)}, u32[]{:S(2)}, u32[]{:S(2)}) collective-permute-start(f32[2,256,192]{2,1,0:T(8,128)S(1)} %bitcast.62), channel_id=1, source_target_pairs={{0,0},{1,1},{2,8},{3,9},{4,16},{5,17},{6,24},{7,25},{8,2},{9,3},{1... | collective-permute-start | bytes 1179656 | tf_op jit(solution)/shard_map/ppermute | solution.py:85
  351.8 25.1 %copy-start.3 = (f32[256,192]{1,0:T(8,128)S(1)}, f32[256,192]{1,0:T(8,128)}, u32[]{:S(2)}) copy-start(f32[256,192]{1,0:T(8,128)} %get-tuple-element.135.guess_ref) | copy-start | bytes 589828
  351.8 25.1 %copy-start.4 = (f32[256,192]{1,0:T(8,128)S(1)}, f32[256,192]{1,0:T(8,128)}, u32[]{:S(2)}) copy-start(f32[256,192]{1,0:T(8,128)} %get-tuple-element.139) | copy-start | bytes 589828

commit v10 on v9

--- a/solution.py
+++ b/solution.py
@@ -302,14 +302,14 @@
         h2_ref[...] = (unit * gains_ref[2:3, :] + gains_ref[3:4, :]).astype(bf16)
         x2_ref[...] = x1_ref[...]
 
-    units = g_ref.shape[1]
+    units = g_ref.shape[1] // 2
     total = None
-    for start in range(0, units, units // 2):
-        some = slice(start, start + units // 2)
-        hidden = jnp.dot(h2_ref[...], up_ref[0, :, some], preferred_element_type=f32)
+    for which in range(2):
+        some = slice(which * units, (which + 1) * units)
+        hidden = jnp.dot(h2_ref[...], up_ref[which], preferred_element_type=f32)
         g_ref[:, some] = hidden
         active = (hidden * gauss_share(hidden)).astype(bf16)
-        act_ref[0, 0, :, some] = active
+        act_ref[which, 0] = active
         part = jnp.dot(active, down_ref[some, :], preferred_element_type=f32)
         total = part if total is None else total + part
     x2_ref[...] += total
@@ -327,8 +327,8 @@
     _, width, units = w_up.shape
     return (
         pl.BlockSpec(w_out.shape, lambda i: (0, 0)),
-        pl.BlockSpec((1, width, units), lambda i: (i, 0, 0)),
-        pl.BlockSpec((units, width), lambda i: (i, 0)),
+        pl.BlockSpec((2, width, units), lambda i: (i, 0, 0)),
+        pl.BlockSpec((2 * units, width), lambda i: (i, 0)),
     )
 
 
@@ -337,13 +337,13 @@
     rows, width = x_first.shape
     parts, units = w_up.shape[0], w_up.shape[2]
     fixed = lambda shape: pl.BlockSpec(shape, lambda i: (0, 0))
-    by_units = pl.BlockSpec((rows, units), lambda i: (0, i))
-    by_core = pl.BlockSpec((1, 1, rows, units), lambda i: (i % 2, i // 2, 0, 0))
+    by_units = pl.BlockSpec((rows, 2 * units), lambda i: (0, i))
+    by_core = pl.BlockSpec((2, 1, rows, units), lambda i: (0, i, 0, 0))
     columns = 4 * V
     flops = 2 * rows * (width * width + 2 * width * parts * units + 6 * width * columns)
     return pl.pallas_call(
         branch_kernel,
-        grid=(parts,),
+        grid=(parts // 2,),
         out_shape=(
             jax.ShapeDtypeStruct((rows, width), f32),
             jax.ShapeDtypeStruct((rows, width), bf16),
@@ -402,10 +402,10 @@
         dx2_ref[...] = wide.astype(bf16)
         sum_ref[...] = jnp.zeros_like(sum_ref)
 
-    units = g_ref.shape[1]
+    units = g_ref.shape[1] // 2
     total = None
-    for start in range(0, units, units // 2):
-        some = slice(start, start + units // 2)
+    for which in range(2):
+        some = slice(which * units, (which + 1) * units)
         active_grad = lax.dot_general(
             dx2_ref[...], down_ref[some, :], NT, preferred_element_type=f32
         )
@@ -414,8 +414,8 @@
             jnp.exp(-0.5 * hidden * hidden) * (2.0 * math.pi) ** -0.5
         )
         hidden_grad = (active_grad * slope).astype(bf16)
-        dg_ref[0, 0, :, some] = hidden_grad
-        part = lax.dot_general(hidden_grad, up_ref[0, :, some], NT, preferred_element_type=f32)
+        dg_ref[which, 0] = hidden_grad
+        part = lax.dot_general(hidden_grad, up_ref[which], NT, preferred_element_type=f32)
         total = part if total is None else total + part
     sum_ref[...] += total
 
@@ -437,14 +437,14 @@
     rows, width = x_last.shape
     parts, units = w_up.shape[0], w_up.shape[2]
     fixed = lambda shape: pl.BlockSpec(shape, lambda i: (0, 0))
-    by_units = pl.BlockSpec((rows, units), lambda i: (0, i))
-    by_core = pl.BlockSpec((1, 1, rows, units), lambda i: (i % 2, i // 2, 0, 0))
+    by_units = pl.BlockSpec((rows, 2 * units), lambda i: (0, i))
+    by_core = pl.BlockSpec((2, 1, rows, units), lambda i: (0, i, 0, 0))
     columns = 4 * V
     wide = (rows, width)
     flops = 2 * rows * (width * width + 2 * width * parts * units + 12 * width * columns)
     return pl.pallas_call(
         branch_back_kernel,
-        grid=(parts,),
+        grid=(parts // 2,),
         out_shape=(
             jax.ShapeDtypeStruct(wide, bf16),
             jax.ShapeDtypeStruct((2, parts // 2, rows, units), bf16),
@@ -853,9 +853,8 @@
     )(packed, own_grad, full, logsum, rows_one)
 
 
-pieces_at, entry_turns, attend_from = 9, 15, 4
+pieces_at, entry_turns, attend_from = 9, 11, 4
 middle_at, end_at = (5, 6, 8, 9), (7, 8, 10, 11)
-entry_middle_at, entry_end_at = (5, 6, 9, 10), (10, 11, 12, 13)
 
 
 def finish_kernel(*refs):
@@ -1361,10 +1360,14 @@
             flip_ref,
         )
 
-    entry_pair(
-        pair, u_ref, keyed_ref, bias_ref, patch_ref, var_ref,
-        du_ref, dpatch_ref, dvar_ref, dkeyed_ref, dbias_ref, dx_ref, flip_ref,
-    )
+    size = 2 * HEAD_DIM
+    for which in range(2):
+        some = slice(which * size, (which + 1) * size)
+        entry_pair(
+            pair * 2 + which, u_ref, keyed_ref, bias_ref, patch_ref.at[:, some],
+            var_ref.at[:, some], du_ref, dpatch_ref.at[some, :], dvar_ref.at[some, :],
+            dkeyed_ref, dbias_ref, dx_ref, flip_ref,
+        )
 
 
 def entry_last_kernel(*refs):
@@ -1395,6 +1398,7 @@
         def _():
             pl.semaphore_signal(barrier, inc=1, device_id=across, device_id_type=MESH)
             pl.semaphore_wait(barrier, 6)
+            crossing.start()
 
         @pl.when(dp == level)
         def _():
@@ -1412,29 +1416,25 @@
                 wides += [dx1[...], dx1_near[...]]
             scatter.begin(depth, [summed(lefts, rights), summed(smalls, wides)], held_ref)
 
-        @pl.when(turn == entry_middle_at[index])
+        @pl.when(turn == index + 3)
         def _(depth=depth):
             scatter.middle(depth)
 
-        @pl.when(turn == entry_end_at[index])
+        @pl.when(turn == index + 6)
         def _(depth=depth):
             scatter.end(depth)
 
-    @pl.when((turn == 11) & (dp != level))
-    def _():
-        crossing.start()
-
-    @pl.when(turn == 4)
+    @pl.when(turn == 0)
     def _():
         entry_rows(
             grad_ref, qkv_ref, x0_ref, mid_ref, gains_ref, du_ref, gain_ref,
             lead_ref.at[0:1, :], dx_ref, flip_ref,
         )
 
-    @pl.when((turn >= 5) & (turn < 5 + HEADS // 2))
+    @pl.when((turn >= 1) & (turn <= HEADS // 2))
     def _():
         size = 2 * HEAD_DIM
-        pair = turn - 5
+        pair = turn - 1
         some = pl.ds(pl.multiple_of(pair * size, size), size)
         entry_pair(
             pair, u_ref, keyed_ref, bias_ref, patch_ref.at[:, some], var_ref.at[:, some],
@@ -1519,11 +1519,11 @@
     rows, width = x_first.shape
     padded = cells.shape[1]
     fixed = lambda shape: pl.BlockSpec(shape, lambda i: (0, 0))
-    by_pair = pl.BlockSpec((padded, 2 * HEAD_DIM), lambda i: (0, i))
-    flipped = pl.BlockSpec((2 * HEAD_DIM, padded), lambda i: (i, 0))
+    by_pair = pl.BlockSpec((padded, 4 * HEAD_DIM), lambda i: (0, i))
+    flipped = pl.BlockSpec((4 * HEAD_DIM, padded), lambda i: (i, 0))
     return pl.pallas_call(
         entry_back_kernel,
-        grid=(HEADS // 2,),
+        grid=(HEADS // 4,),
         out_shape=(
             jax.ShapeDtypeStruct((rows, padded), f32),
             jax.ShapeDtypeStruct((2, width), f32),
@@ -1569,7 +1569,7 @@
 ):
     padded, width = patch_ref.shape
     marks = head_marks(width)
-    query = query_ref[...]
+    query = query_ref[5 * V + LEADS : 5 * V + LEADS + 1, :]
     keyed_grad = exact_product(ka_ref[...] + kb_ref[...], marks, TN)
     bias_grad = exact_product(ba_ref[...] + bb_ref[...], marks, TN)
     o_ref[...] = jnp.zeros_like(o_ref)
@@ -1866,7 +1866,7 @@
 def lead_rows_of(lead, lead_ref):
     row = lax.broadcasted_iota(jnp.int32, (1, 8), 1).astype(f32)
     lead_hot = jnp.where(row == lead, 1.0, 0.0).astype(f32)
-    return exact_product(lead_hot, lead_ref[...])
+    return exact_product(lead_hot, lead_ref[5 * V : 5 * V + 8, :])
 
 
 def middle_kernel(
@@ -2347,7 +2347,7 @@
             x_first, cells, packed, full, logsum, count, rows_one, attended,
             qkv_t, w_outs, w_ups, w_downs
         ) = start_program(
-            packed, prepared, tables[5 * V : 5 * V + 8], norm_gains,
+            packed, prepared, tables, norm_gains,
             (qkv_low.T, low(w_out), low(w_up), low(w_down)), (1, 1, 2, 2),
         )
         count = count[0, 0]
@@ -2380,7 +2380,7 @@
     for rollout in range(2):
         if crossed and rollout == 1:
             x_first, cells, packed, full, logsum, rows_one, attended = middle_program(
-                guess, first_cells, prepared, tables[5 * V : 5 * V + 8], norm_gains, gathered[3]
+                guess, first_cells, prepared, tables, norm_gains, gathered[3]
             )
         if not crossed:
             if rollout == 1:
@@ -2409,7 +2409,7 @@
     heads, highs = [], []
     lead_hots = (leads[:, None] == jnp.arange(8, dtype=jnp.int32)[None, :]).astype(f32)
     lead_hots = jnp.pad(lead_hots, ((0, 6), (0, 0)))
-    query = tables[5 * V + LEADS : 5 * V + LEADS + 1]
+    query = tables
     gain_low = jnp.zeros((2, D), f32)
     table_parts, lead_sums = [], []
     qkv_grad = jnp.zeros((D, w_qkv.shape[1]), f32)

time: 660 us -> 645 us (0.977)
  Pallas kernels: 629 us -> 617 us
    pallas_call x5, Pallas kernels: 101 us -> 94 us  [the longest x2 37.1 us: branch_backward(): pl.pallas_call(branch_back_kernel, grid=(parts // 2,), out_shape=(jax.Sha...]
where the time goes in v10:
time: 645 us; the launch traced here: 641 us
  Pallas kernels  617 us (96%)
  other arithmetic  12.7 us (2%)
  local copies, waits for them, and re-layouts  7.08 us (1%)
    pallas_call x1, Pallas kernels, start_program(): pl.pallas_call(partial(start_kernel, halves), grid=(groups * 3 + lag_two,...  153 us
    pallas_call x1, Pallas kernels, entry_last(): pl.pallas_call(entry_last_kernel, grid=(entry_turns,), out_shape=[jax.Sha...  83.6 us
    pallas_call x1, Pallas kernels, finish_program(): pl.pallas_call(finish_kernel, grid=(attend_from + pieces_at + 5,), out_sh...  78.4 us
    pallas_call x1, Pallas kernels, middle_program(): pl.pallas_call(middle_kernel, grid=(HEADS // 2 + Rows.count,), out_shape=...  62.2 us
    pallas_call x1, Pallas kernels, exchange_sum(): pl.pallas_call(exchange_sum_kernel, out_shape=(jax.ShapeDtypeStruct(value...  58.4 us
    pallas_call x1, Pallas kernels, attend_exchange(): pl.pallas_call(attend_exchange_kernel, grid=(pieces_at + 4,), out_shape=[...  42.7 us
    pallas_call x2, Pallas kernels, branch_backward(): pl.pallas_call(branch_back_kernel, grid=(parts // 2,), out_shape=(jax.Sha...  37.1 us
    pallas_call x2, Pallas kernels, branch_forward(): pl.pallas_call(branch_kernel, grid=(parts // 2,), out_shape=(jax.ShapeDty...  32.3 us
  transfers between devices with their start and end apart: 1, of which 0 were waited for; matrix products, arithmetic and copies ran while one was open for 1% of the time, Pallas kernels for 15%

profile of v10, /device:TPU:0, one launch (start us, length us, event | category | flops | bytes accessed | tf_op | source)
XLA Modules:
  0.0 641.0 jit_solution(10434190995244886969)
XLA Ops:
  0.7 1.5 fusion.6.hot_ref.refs_24_
  2.2 1.7 copy.67
  4.8 1.1 convert_element_type.44.refs_9_
  5.9 1.1 convert_element_type.45.refs_10_
  8.5 4.9 prepare_tables.1
  14.2 152.7 %start_program.1 = (f32[256,1024]{1,0:T(8,128)}, f32[256,256]{1,0:T(8,128)}, bf16[2048,384]{1,0:T(8,128)(2,1)}, f32[2048,128]{1,0:T(8,128)}, f32[2,2048]{1,0:T(2...) custom-call(f32[256,256]{1,0:T(8,128)} %maximum_maximum_fusion.refs_, ...), custom_call_target="tpu_custom_call" | custom-call | tf_op jit(solution)/shard_map/start_program/pallas_call | solution.py:2267
  170.3 1.0 subtract_multiply_fusion
  171.7 1.2 slice.20.refs_3_
  173.5 16.0 %branch_forward.2 = (f32[256,1024]{1,0:T(8,128)}, bf16[256,1024]{1,0:T(8,128)(2,1)}, f32[256,4096]{1,0:T(8,128)}, bf16[2,4,256,512]{3,2,1,0:T(8,128)(2,1)}, f32[256,1024]{1,0:T(8,128)}, /*index=5*/f32[256,192]{1,0:T(8,128)}) custom-call(bf16[256,1024]{1,0:T(8,128)(2,1)} %get-tuple-element.130.o_ref.refs_3_, f32[256,1024]{1,0:T(8,128)} %get-tuple-element.131.x0_ref.refs_15_, ...), custom_call_target="tpu_custom_call" | custom-call | flops 5435817984 | bytes 23068672 | tf_op jit(solution)/shard_map/branch_forward/pallas_call | solution.py:344
  189.5 62.2 %middle_program.1 = (f32[256,1024]{1,0:T(8,128)}, f32[256,256]{1,0:T(8,128)}, bf16[2048,384]{1,0:T(8,128)(2,1)}, f32[2048,128]{1,0:T(8,128)}, f32[2,2048]{1,0:T(...) custom-call(f32[256,192]{1,0:T(8,128)} %get-tuple-element.135.guess_ref, ...), custom_call_target="tpu_custom_call" | custom-call | tf_op jit(solution)/shard_map/middle_program/pallas_call | solution.py:1949
  252.3 16.4 %branch_forward.3 = (f32[256,1024]{1,0:T(8,128)}, bf16[256,1024]{1,0:T(8,128)(2,1)}, f32[256,4096]{1,0:T(8,128)}, bf16[2,4,256,512]{3,2,1,0:T(8,128)(2,1)}, f32[256,1024]{1,0:T(8,128)}, /*index=5*/f32[256,192]{1,0:T(8,128)}) custom-call(bf16[256,1024]{1,0:T(8,128)(2,1)} %get-tuple-element.137.o_ref.refs_3_, f32[256,1024]{1,0:T(8,128)} %get-tuple-element.138.x0_ref, ...), custom_call_target="tpu_custom_call" | custom-call | flops 5435817984 | bytes 23068672 | tf_op jit(solution)/shard_map/branch_forward/pallas_call | solution.py:344
  268.7 1.7 multiply_divide_fusion.dpred_ref
  270.4 18.6 %branch_backward.2 = (bf16[256,1024]{1,0:T(8,128)(2,1)}, bf16[2,4,256,512]{3,2,1,0:T(8,128)(2,1)}, f32[256,1024]{1,0:T(8,128)}, bf16[256,1024]{1,0:T(8,128)(2,1)...) custom-call(f32[256,192]{1,0:T(8,128)} %multiply_divide_fusion.dpred_ref, ...), custom_call_target="tpu_custom_call" | custom-call | flops 6039797760 | bytes 23068672 | tf_op jit(solution)/shard_map/branch_backward/pallas_call | solution.py:445
  289.0 13.7 %exchange_swap.2 = (bf16[2048,128]{1,0:T(8,128)(2,1)}, bf16[2,4,256,512]{3,2,1,0:T(8,128)(2,1)}, bf16[2,4,256,512]{3,2,1,0:T(8,128)(2,1)}, bf16[2,4,256,128]{3,2...) custom-call(bf16[256,1024]{1,0:T(8,128)(2,1)} %get-tuple-element.145.refs_0_, ...), custom_call_target="tpu_custom_call" | custom-call | tf_op jit(solution)/shard_map/exchange_swap/pallas_call | solution.py:557
  302.7 42.7 %attend_exchange.1 = (bf16[256,3072]{1,0:T(8,128)(2,1)}, f32[1024,384]{1,0:T(8,128)}) custom-call(bf16[2048,384]{1,0:T(8,128)(2,1)} %get-tuple-element.155.qkv_ref, bf16[2048,128]{1,0:T(8,128)(2,1)} %get-tuple-element.156.do_ref, f32[2048,128]{1,0:T(8,128)} %get-tuple-element.157.full_ref, f32[2,2048]{1,0:T(2,128)} %get-tuple-element.158.lse_ref, ...), custom_call_target="tpu_custom_call" | custom-call | tf_op jit(solution)/shard_map/attend_exchange/pallas_call | solution.py:823
  345.5 24.6 %entry_backward.1 = (f32[256,256]{1,0:T(8,128)}, f32[2,1024]{1,0:T(2,128)}, f32[1,1024]{1,0:T(1,128)}, f32[1024,256]{1,0:T(8,128)}, f32[1024,256]{1,0:T(8,128)}, /*index=5*/f32[16,256]{1,0:T(8,128)}, f32[16,256]{1,0:T(8,128)}) custom-call(bf16[256,3072]{1,0:T(8,128)(2,1)} %get-tuple-element.160.grad_ref, bf16[3072,1024]{1,0:T(8,128)(2,1)} %bitcast.55, ...), custom_call_target="tpu_custom_call" | custom-call | flops 4026531840 | bytes 10485760 | tf_op jit(solution)/shard_map/entry_backward/pallas_call | solution.py:1524
  370.1 2.4 fusion.1
  372.5 18.5 %branch_backward.3 = (bf16[256,1024]{1,0:T(8,128)(2,1)}, bf16[2,4,256,512]{3,2,1,0:T(8,128)(2,1)}, f32[256,1024]{1,0:T(8,128)}, bf16[256,1024]{1,0:T(8,128)(2,1)...) custom-call(f32[256,192]{1,0:T(8,128)} %get-tuple-element.229.dpred_ref, ...), custom_call_target="tpu_custom_call" | custom-call | flops 6039797760 | bytes 23068672 | tf_op jit(solution)/shard_map/branch_backward/pallas_call | solution.py:445
  391.0 13.6 %exchange_swap.3 = (bf16[2048,128]{1,0:T(8,128)(2,1)}, bf16[2,4,256,512]{3,2,1,0:T(8,128)(2,1)}, bf16[2,4,256,512]{3,2,1,0:T(8,128)(2,1)}, bf16[2,4,256,128]{3,2...) custom-call(bf16[256,1024]{1,0:T(8,128)(2,1)} %get-tuple-element.167.refs_0_, ...), custom_call_target="tpu_custom_call" | custom-call | tf_op jit(solution)/shard_map/exchange_swap/pallas_call | solution.py:557
  404.6 78.4 %finish_program.1 = (bf16[256,3072]{1,0:T(8,128)(2,1)}, f32[256,384]{1,0:T(8,128)}, f32[512,256]{1,0:T(8,128)}) custom-call(bf16[2,4,256,512]{3,2,1,0:T(8,128)(2,1)} %get-tuple-element.177.refs_0_, bf16[256,1024]{1,0:T(8,128)(2,1)} %get-tuple-element.148.refs_4_.refs_1_, bf16[256,1024]{1,0:T(8,128)(2,1)} %get-tuple-element.178.refs_2_, ...), custom_call_target="tpu_custom_call" | custom-call | tf_op jit(solution)/shard_map/finish_program/pallas_call | solution.py:975
  483.0 83.6 %entry_last.1 = (f32[512,1024]{1,0:T(8,128)}, f32[640,256]{1,0:T(8,128)}, f32[256,384]{1,0:T(8,128)}) custom-call(bf16[2,4,256,512]{3,2,1,0:T(8,128)(2,1)} %get-tuple-element.151.refs_0_, bf16[2,4,256,128]{3,2,1,0:T(8,128)(2,1)} %get-tuple-element.152.refs_1_, bf16[256,1024]{1,0:T(8,128)(2,1)} %get-tuple-element.149.refs_5_.refs_2_, ...), custom_call_target="tpu_custom_call" | custom-call | tf_op jit(solution)/shard_map/entry_last/pallas_call | solution.py:1489
  566.7 1.2 copy.76
  570.1 58.4 %exchange_sum.1 = (f32[512,1024]{1,0:T(8,128)}, f32[8,128]{1,0:T(8,128)}) custom-call(f32[512,1024]{1,0:T(8,128)} %get-tuple-element.200.x_ref, f32[1,1]{1,0:T(1,128)} %bitcast.16.loss_ref, f32[256,384]{1,0:T(8,128)} %copy.78.qkv_ref.refs_4_, f32[640,256]{1,0:T(8,128)} %get-tuple-element.202.up_out_ref.refs_5_, f32[512,256]{1,0:T(8,128)} %get-tuple-element.203.down_ref.refs_6_), custom_call_target="tpu_custom_call" | custom-call | tf_op jit(solution)/shard_map/exchange_sum/pallas_call | solution.py:1142
  628.4 12.3 %update_all.1 = (f32[1,1]{1,0:T(1,128)}, f32[1,1]{1,0:T(1,128)}, f32[440,1024]{1,0:T(8,128)}, f32[440,1024]{1,0:T(8,128)}, f32[440,1024]{1,0:T(8,128)}, /*index=...) custom-call(s32[1]{0:T(128)} %bitcast.refs_0_, ...), custom_call_target="tpu_custom_call" | custom-call | tf_op jit(solution)/shard_map/update_all/pallas_call | solution.py:1672
  (46 shorter events, 7.8 us)
Async XLA Ops:
  0.7 4.1 copy-start
  3.8 2.0 copy-start.1
  5.9 1.2 copy-start.6
  5.9 1.3 copy-start.7
  5.9 1.5 copy-start.8
  5.9 1.6 copy-start.2
  5.9 2.4 copy-start.5
  166.9 101.8 %collective-permute-start = (f32[2,256,192]{2,1,0:T(8,128)S(1)}, f32[2,256,192]{2,1,0:T(8,128)S(1)}, u32[]{:S(2)}, u32[]{:S(2)}) collective-permute-start(f32[2,256,192]{2,1,0:T(8,128)S(1)} %bitcast.62), channel_id=1, source_target_pairs={{0,0},{1,1},{2,8},{3,9},{4,16},{5,17},{6,24},{7,25},{8,2},{9,3},{1... | collective-permute-start | bytes 1179656 | tf_op jit(solution)/shard_map/ppermute | solution.py:85
  345.4 24.6 %copy-start.3 = (f32[256,192]{1,0:T(8,128)S(1)}, f32[256,192]{1,0:T(8,128)}, u32[]{:S(2)}) copy-start(f32[256,192]{1,0:T(8,128)} %get-tuple-element.139) | copy-start | bytes 589828
  345.5 24.6 %copy-start.4 = (f32[256,192]{1,0:T(8,128)S(1)}, f32[256,192]{1,0:T(8,128)}, u32[]{:S(2)}) copy-start(f32[256,192]{1,0:T(8,128)} %get-tuple-element.135.guess_ref) | copy-start | bytes 589828

commit v11 on v10

--- a/solution.py
+++ b/solution.py
@@ -1030,8 +1030,8 @@
 
 
 def exchange_sum_kernel(
-    x_ref, loss_ref, qkv_ref, up_out_ref, down_ref, o_ref, s_ref, work_ref, pair_ref, quad_ref, eight_ref, deep_ref, tile_ref,
-    send_sem, recv_sem,
+    x_ref, loss_ref, qkv_ref, up_out_ref, down_ref, o_ref, s_ref, share_ref, work_ref, pair_ref, quad_ref, eight_ref, deep_ref, tile_ref,
+    landing_ref, cross_sem, send_sem, recv_sem,
 ):
     dp, level, core = mesh_place()
     x, y = lax.rem(dp, 2), dp // 2
@@ -1042,7 +1042,26 @@
     barrier = pltpu.get_barrier_semaphore()
     for target in (side, down, near, *deep):
         pl.semaphore_signal(barrier, inc=1, device_id=target, device_id_type=MESH)
-    pl.semaphore_wait(barrier, 6)
+    across = device_of(level, dp, core)
+    crossing = pltpu.make_async_remote_copy(
+        src_ref=qkv_ref,
+        dst_ref=landing_ref,
+        send_sem=cross_sem.at[0],
+        recv_sem=cross_sem.at[1],
+        device_id=across,
+        device_id_type=MESH,
+    )
+
+    @pl.when(dp != level)
+    def _():
+        pl.semaphore_signal(barrier, inc=1, device_id=across, device_id_type=MESH)
+        pl.semaphore_wait(barrier, 7)
+        crossing.start()
+
+    @pl.when(dp == level)
+    def _():
+        pl.semaphore_wait(barrier, 6)
+
     started = []
 
     def send(source, target_ref, target):
@@ -1135,15 +1154,26 @@
     for copy in started:
         copy.wait_send()
 
+    @pl.when(dp != level)
+    def _():
+        crossing.wait()
+        share_ref[...] = landing_ref[...]
+
+    @pl.when(dp == level)
+    def _():
+        share_ref[...] = qkv_ref[...]
+
 
 def exchange_sum(value, loss, *shares):
     rows, width = value.shape
     tile = jax.ShapeDtypeStruct((8, 128), f32)
     return pl.pallas_call(
         exchange_sum_kernel,
-        out_shape=(jax.ShapeDtypeStruct(value.shape, f32), tile),
+        out_shape=(
+            jax.ShapeDtypeStruct(value.shape, f32), tile, jax.ShapeDtypeStruct(shares[0].shape, f32)
+        ),
         in_specs=[VMEM] * 5,
-        out_specs=[VMEM, VMEM],
+        out_specs=[VMEM] * 3,
         scratch_shapes=[
             pltpu.VMEM((rows // 2, width), f32),
             pltpu.VMEM((rows // 2, width), f32),
@@ -1151,6 +1181,8 @@
             pltpu.VMEM((2, rows // 16, width), f32),
             pltpu.VMEM((3, rows // 32, width), f32),
             pltpu.VMEM((10,) + tile.shape, f32),
+            pltpu.VMEM(shares[0].shape, f32),
+            pltpu.SemaphoreType.DMA((2,)),
             pltpu.SemaphoreType.DMA((24,)),
             pltpu.SemaphoreType.DMA((24,)),
         ],
@@ -1372,19 +1404,16 @@
 
 def entry_last_kernel(*refs):
     steps = (refs[0:6], refs[6:12])
-    share_ref = refs[12]
-    grad_ref, qkv_ref, x0_ref, mid_ref, gains_ref, u_ref, keyed_ref, bias_ref = refs[13:21]
-    patch_ref, var_ref, query_ref, hot_ref, lead_hot_ref, head_a, head_b, high_a, high_b = refs[21:30]
-    patch_a, var_a, keyed_a, bias_a, lead_a, gain_a = refs[30:36]
-    rows_out, up_out_ref, qkv_share_ref = refs[36:39]
-    (dx_ref, flip_ref, low_ref, landing_ref, cross_sem, du_ref, gain_ref, lead_ref, dpatch_ref,
-     dvar_ref, dkeyed_ref, dbias_ref) = refs[39:51]
-    scatter = Scatter(refs[51:57], refs[58:61])
-    held_ref = refs[57]
+    grad_ref, qkv_ref, x0_ref, mid_ref, gains_ref, u_ref, keyed_ref, bias_ref = refs[12:20]
+    patch_ref, var_ref, query_ref, hot_ref, lead_hot_ref, head_a, head_b, high_a, high_b = refs[20:29]
+    patch_a, var_a, keyed_a, bias_a, lead_a, gain_a = refs[29:35]
+    rows_out, up_out_ref = refs[35:37]
+    (dx_ref, flip_ref, du_ref, gain_ref, lead_ref, dpatch_ref, dvar_ref, dkeyed_ref,
+     dbias_ref) = refs[37:46]
+    scatter = Scatter(refs[46:52], refs[53:56])
+    held_ref = refs[52]
     turn = pl.program_id(0)
     dp, level, core = mesh_place()
-    across = device_of(level, dp, core)
-    crossing = scatter.copy(low_ref, landing_ref, cross_sem, 0, 0, across)
 
     @pl.when(turn == 0)
     def _():
@@ -1392,17 +1421,7 @@
         deep = [device_of(dp, lax.rem(level + move, 4), core) for move in (1, 2, 3)]
         for target in (scatter.side, scatter.down, *deep):
             pl.semaphore_signal(barrier, inc=1, device_id=target, device_id_type=MESH)
-        low_ref[...] = share_ref[...]
-
-        @pl.when(dp != level)
-        def _():
-            pl.semaphore_signal(barrier, inc=1, device_id=across, device_id_type=MESH)
-            pl.semaphore_wait(barrier, 6)
-            crossing.start()
-
-        @pl.when(dp == level)
-        def _():
-            pl.semaphore_wait(barrier, 5)
+        pl.semaphore_wait(barrier, 5)
 
     for index, depth in enumerate(scatter.order):
 
@@ -1455,20 +1474,11 @@
 
     @pl.when(turn == entry_turns - 1)
     def _():
-        @pl.when(dp != level)
-        def _():
-            crossing.wait()
-            qkv_share_ref[...] = landing_ref[...]
-
-        @pl.when(dp == level)
-        def _():
-            qkv_share_ref[...] = share_ref[...]
-
         scatter.finish(up_out_ref)
 
 
 def entry_last(
-    kept, share, token_grad, qkv_t, x_first, mid_grad, norm_gains, cells, prepared,
+    kept, token_grad, qkv_t, x_first, mid_grad, norm_gains, cells, prepared,
     query, var_hot, lead_hots, heads, highs, earlier,
 ):
     patch, variable, keyed, bias = prepared
@@ -1480,12 +1490,12 @@
         in_specs += [chunk_spec(dg.shape[2:]), chunk_spec(o.shape[2:])]
         in_specs += [once(h2.shape)] * 4
     values = [
-        share, token_grad, qkv_t, x_first, mid_grad, norm_gains, cells, keyed, bias,
+        token_grad, qkv_t, x_first, mid_grad, norm_gains, cells, keyed, bias,
         patch, variable, query, var_hot, lead_hots, *heads, *highs, *earlier,
     ]
     in_specs += [once(value.shape) for value in values]
     height, columns = kept[0][0].shape[3] + kept[0][1].shape[3], width // 4
-    outs = [(2 * padded, width), (height, columns), share.shape]
+    outs = [(2 * padded, width), (height, columns)]
     return pl.pallas_call(
         entry_last_kernel,
         grid=(entry_turns,),
@@ -1495,9 +1505,6 @@
         scratch_shapes=[
             pltpu.VMEM((rows, width), f32),
             pltpu.VMEM((width, rows), f32),
-            pltpu.VMEM(share.shape, f32),
-            pltpu.VMEM(share.shape, f32),
-            pltpu.SemaphoreType.DMA((2, 1)),
             pltpu.VMEM((rows, padded), f32),
             pltpu.VMEM((2, width), f32),
             pltpu.VMEM((8, width), f32),
@@ -2451,8 +2458,8 @@
             )
         entry = (token_grad, gathered[3], x_first, mid_grad, norm_gains, cells, prepared)
         if crossed and rollout == 0:
-            last_rows, up_out_sum, qkv_share = entry_last(
-                [step[1:3] + step[5:] for step in kept], level_share, *entry,
+            last_rows, up_out_sum = entry_last(
+                [step[1:3] + step[5:] for step in kept], *entry,
                 query, var_hot, lead_hots, heads, highs,
                 (*table_parts[0], lead_sums[0], gain_low),
             )
@@ -2472,12 +2479,13 @@
             *table_parts, prepared, query, var_hot, lead_hots, lead_rows, gain_low, heads, highs
         )
     if not crossed:
-        qkv_share = lax.psum_scatter(qkv_grad, "dp", scatter_dimension=0, tiled=True)
-    qkv_share = by_head(qkv_share)
+        qkv_share = by_head(lax.psum_scatter(qkv_grad, "dp", scatter_dimension=0, tiled=True))
     where = dp_index.astype(jnp.int32).reshape(1)
     if crossed:
-        shares = (qkv_share, up_out_sum, down_sum)
-        last_sum, tile = exchange_sum(last_rows, loss_part, *shares)
+        last_sum, tile, qkv_share = exchange_sum(
+            last_rows, loss_part, level_share, up_out_sum, down_sum
+        )
+        shares = (by_head(qkv_share), up_out_sum, down_sum)
         masters = (w_qkv, w_out, w_up, w_down)
     else:
         shares = (

time: 645 us -> 647 us (level)
  no operation moved by 1% of the time
where the time goes in v11:
time: 647 us; the launch traced here: 642 us
  Pallas kernels  618 us (96%)
  other arithmetic  12.7 us (2%)
  local copies, waits for them, and re-layouts  7.08 us (1%)
    pallas_call x1, Pallas kernels, start_program(): pl.pallas_call(partial(start_kernel, halves), grid=(groups * 3 + lag_two,...  153 us
    pallas_call x1, Pallas kernels, entry_last(): pl.pallas_call(entry_last_kernel, grid=(entry_turns,), out_shape=[jax.Sha...  80.9 us
    pallas_call x1, Pallas kernels, finish_program(): pl.pallas_call(finish_kernel, grid=(attend_from + pieces_at + 5,), out_sh...  78.4 us
    pallas_call x1, Pallas kernels, exchange_sum(): pl.pallas_call(exchange_sum_kernel, out_shape=(jax.ShapeDtypeStruct(value...  62.5 us
    pallas_call x1, Pallas kernels, middle_program(): pl.pallas_call(middle_kernel, grid=(HEADS // 2 + Rows.count,), out_shape=...  62.2 us
    pallas_call x1, Pallas kernels, attend_exchange(): pl.pallas_call(attend_exchange_kernel, grid=(pieces_at + 4,), out_shape=[...  42.7 us
    pallas_call x2, Pallas kernels, branch_backward(): pl.pallas_call(branch_back_kernel, grid=(parts // 2,), out_shape=(jax.Sha...  37.1 us
    pallas_call x2, Pallas kernels, branch_forward(): pl.pallas_call(branch_kernel, grid=(parts // 2,), out_shape=(jax.ShapeDty...  32.3 us
  transfers between devices with their start and end apart: 1, of which 0 were waited for; matrix products, arithmetic and copies ran while one was open for 1% of the time, Pallas kernels for 15%

profile of v11, /device:TPU:0, one launch (start us, length us, event | category | flops | bytes accessed | tf_op | source)
XLA Modules:
  0.0 642.4 jit_solution(7080996668555808170)
XLA Ops:
  0.7 1.5 fusion.6.hot_ref.refs_23_
  2.2 1.7 copy.66
  4.8 1.1 convert_element_type.44.refs_9_
  5.9 1.1 convert_element_type.45.refs_10_
  8.5 4.9 prepare_tables.1
  14.2 152.7 %start_program.1 = (f32[256,1024]{1,0:T(8,128)}, f32[256,256]{1,0:T(8,128)}, bf16[2048,384]{1,0:T(8,128)(2,1)}, f32[2048,128]{1,0:T(8,128)}, f32[2,2048]{1,0:T(2...) custom-call(f32[256,256]{1,0:T(8,128)} %maximum_maximum_fusion.refs_, ...), custom_call_target="tpu_custom_call" | custom-call | tf_op jit(solution)/shard_map/start_program/pallas_call | solution.py:2274
  170.3 1.0 subtract_multiply_fusion
  171.7 1.2 slice.20.refs_3_
  173.5 16.0 %branch_forward.2 = (f32[256,1024]{1,0:T(8,128)}, bf16[256,1024]{1,0:T(8,128)(2,1)}, f32[256,4096]{1,0:T(8,128)}, bf16[2,4,256,512]{3,2,1,0:T(8,128)(2,1)}, f32[256,1024]{1,0:T(8,128)}, /*index=5*/f32[256,192]{1,0:T(8,128)}) custom-call(bf16[256,1024]{1,0:T(8,128)(2,1)} %get-tuple-element.130.o_ref.refs_3_, f32[256,1024]{1,0:T(8,128)} %get-tuple-element.131.x0_ref.refs_14_, ...), custom_call_target="tpu_custom_call" | custom-call | flops 5435817984 | bytes 23068672 | tf_op jit(solution)/shard_map/branch_forward/pallas_call | solution.py:344
  189.5 62.2 %middle_program.1 = (f32[256,1024]{1,0:T(8,128)}, f32[256,256]{1,0:T(8,128)}, bf16[2048,384]{1,0:T(8,128)(2,1)}, f32[2048,128]{1,0:T(8,128)}, f32[2,2048]{1,0:T(...) custom-call(f32[256,192]{1,0:T(8,128)} %get-tuple-element.135.guess_ref, ...), custom_call_target="tpu_custom_call" | custom-call | tf_op jit(solution)/shard_map/middle_program/pallas_call | solution.py:1956
  252.3 16.4 %branch_forward.3 = (f32[256,1024]{1,0:T(8,128)}, bf16[256,1024]{1,0:T(8,128)(2,1)}, f32[256,4096]{1,0:T(8,128)}, bf16[2,4,256,512]{3,2,1,0:T(8,128)(2,1)}, f32[256,1024]{1,0:T(8,128)}, /*index=5*/f32[256,192]{1,0:T(8,128)}) custom-call(bf16[256,1024]{1,0:T(8,128)(2,1)} %get-tuple-element.137.o_ref.refs_3_, f32[256,1024]{1,0:T(8,128)} %get-tuple-element.138.x0_ref, ...), custom_call_target="tpu_custom_call" | custom-call | flops 5435817984 | bytes 23068672 | tf_op jit(solution)/shard_map/branch_forward/pallas_call | solution.py:344
  268.7 1.7 multiply_divide_fusion.dpred_ref
  270.4 18.6 %branch_backward.2 = (bf16[256,1024]{1,0:T(8,128)(2,1)}, bf16[2,4,256,512]{3,2,1,0:T(8,128)(2,1)}, f32[256,1024]{1,0:T(8,128)}, bf16[256,1024]{1,0:T(8,128)(2,1)...) custom-call(f32[256,192]{1,0:T(8,128)} %multiply_divide_fusion.dpred_ref, ...), custom_call_target="tpu_custom_call" | custom-call | flops 6039797760 | bytes 23068672 | tf_op jit(solution)/shard_map/branch_backward/pallas_call | solution.py:445
  289.0 13.7 %exchange_swap.2 = (bf16[2048,128]{1,0:T(8,128)(2,1)}, bf16[2,4,256,512]{3,2,1,0:T(8,128)(2,1)}, bf16[2,4,256,512]{3,2,1,0:T(8,128)(2,1)}, bf16[2,4,256,128]{3,2...) custom-call(bf16[256,1024]{1,0:T(8,128)(2,1)} %get-tuple-element.145.refs_0_, ...), custom_call_target="tpu_custom_call" | custom-call | tf_op jit(solution)/shard_map/exchange_swap/pallas_call | solution.py:557
  302.7 42.7 %attend_exchange.1 = (bf16[256,3072]{1,0:T(8,128)(2,1)}, f32[1024,384]{1,0:T(8,128)}) custom-call(bf16[2048,384]{1,0:T(8,128)(2,1)} %get-tuple-element.155.qkv_ref, bf16[2048,128]{1,0:T(8,128)(2,1)} %get-tuple-element.156.do_ref, f32[2048,128]{1,0:T(8,128)} %get-tuple-element.157.full_ref, f32[2,2048]{1,0:T(2,128)} %get-tuple-element.158.lse_ref, ...), custom_call_target="tpu_custom_call" | custom-call | tf_op jit(solution)/shard_map/attend_exchange/pallas_call | solution.py:823
  345.5 24.6 %entry_backward.1 = (f32[256,256]{1,0:T(8,128)}, f32[2,1024]{1,0:T(2,128)}, f32[1,1024]{1,0:T(1,128)}, f32[1024,256]{1,0:T(8,128)}, f32[1024,256]{1,0:T(8,128)}, /*index=5*/f32[16,256]{1,0:T(8,128)}, f32[16,256]{1,0:T(8,128)}) custom-call(bf16[256,3072]{1,0:T(8,128)(2,1)} %get-tuple-element.160.grad_ref, bf16[3072,1024]{1,0:T(8,128)(2,1)} %bitcast.55, ...), custom_call_target="tpu_custom_call" | custom-call | flops 4026531840 | bytes 10485760 | tf_op jit(solution)/shard_map/entry_backward/pallas_call | solution.py:1531
  370.1 2.4 fusion.1
  373.8 18.5 %branch_backward.3 = (bf16[256,1024]{1,0:T(8,128)(2,1)}, bf16[2,4,256,512]{3,2,1,0:T(8,128)(2,1)}, f32[256,1024]{1,0:T(8,128)}, bf16[256,1024]{1,0:T(8,128)(2,1)...) custom-call(f32[256,192]{1,0:T(8,128)} %get-tuple-element.229.dpred_ref, ...), custom_call_target="tpu_custom_call" | custom-call | flops 6039797760 | bytes 23068672 | tf_op jit(solution)/shard_map/branch_backward/pallas_call | solution.py:445
  392.3 13.6 %exchange_swap.3 = (bf16[2048,128]{1,0:T(8,128)(2,1)}, bf16[2,4,256,512]{3,2,1,0:T(8,128)(2,1)}, bf16[2,4,256,512]{3,2,1,0:T(8,128)(2,1)}, bf16[2,4,256,128]{3,2...) custom-call(bf16[256,1024]{1,0:T(8,128)(2,1)} %get-tuple-element.167.refs_0_, ...), custom_call_target="tpu_custom_call" | custom-call | tf_op jit(solution)/shard_map/exchange_swap/pallas_call | solution.py:557
  405.9 78.4 %finish_program.1 = (bf16[256,3072]{1,0:T(8,128)(2,1)}, f32[256,384]{1,0:T(8,128)}, f32[512,256]{1,0:T(8,128)}) custom-call(bf16[2,4,256,512]{3,2,1,0:T(8,128)(2,1)} %get-tuple-element.177.refs_0_, bf16[256,1024]{1,0:T(8,128)(2,1)} %get-tuple-element.148.refs_4_.refs_1_, bf16[256,1024]{1,0:T(8,128)(2,1)} %get-tuple-element.178.refs_2_, ...), custom_call_target="tpu_custom_call" | custom-call | tf_op jit(solution)/shard_map/finish_program/pallas_call | solution.py:975
  484.4 80.9 %entry_last.1 = (f32[512,1024]{1,0:T(8,128)}, f32[640,256]{1,0:T(8,128)}) custom-call(bf16[2,4,256,512]{3,2,1,0:T(8,128)(2,1)} %get-tuple-element.151.refs_0_, bf16[2,4,256,128]{3,2,1,0:T(8,128)(2,1)} %get-tuple-element.152.refs_1_, bf16[256,1024]{1,0:T(8,128)(2,1)} %get-tuple-element.149.refs_5_.refs_2_, bf16[256,1024]{1,0:T(8,128)(2,1)} %get-tuple-element.153.refs_3_, ...), custom_call_target="tpu_custom_call" | custom-call | tf_op jit(solution)/shard_map/entry_last/pallas_call | solution.py:1499
  565.3 62.5 %exchange_sum.1 = (f32[512,1024]{1,0:T(8,128)}, f32[8,128]{1,0:T(8,128)}, f32[256,384]{1,0:T(8,128)}) custom-call(f32[512,1024]{1,0:T(8,128)} %get-tuple-element.199.x_ref, f32[1,1]{1,0:T(1,128)} %bitcast.16.loss_ref, f32[256,384]{1,0:T(8,128)} %get-tuple-element.200.qkv_ref, f32[640,256]{1,0:T(8,128)} %get-tuple-element.201.up_out_ref.refs_5_, ...), custom_call_target="tpu_custom_call" | custom-call | tf_op jit(solution)/shard_map/exchange_sum/pallas_call | solution.py:1170
  627.8 1.2 copy.75
  629.9 12.3 %update_all.1 = (f32[1,1]{1,0:T(1,128)}, f32[1,1]{1,0:T(1,128)}, f32[440,1024]{1,0:T(8,128)}, f32[440,1024]{1,0:T(8,128)}, f32[440,1024]{1,0:T(8,128)}, /*index=...) custom-call(s32[1]{0:T(128)} %bitcast.refs_0_, ...), custom_call_target="tpu_custom_call" | custom-call | tf_op jit(solution)/shard_map/update_all/pallas_call | solution.py:1679
  (46 shorter events, 7.8 us)
Async XLA Ops:
  0.7 4.1 copy-start
  3.8 2.0 copy-start.1
  5.9 1.2 copy-start.6
  5.9 1.3 copy-start.7
  5.9 1.5 copy-start.8
  5.9 1.6 copy-start.2
  5.9 2.4 copy-start.5
  166.9 101.8 %collective-permute-start = (f32[2,256,192]{2,1,0:T(8,128)S(1)}, f32[2,256,192]{2,1,0:T(8,128)S(1)}, u32[]{:S(2)}, u32[]{:S(2)}) collective-permute-start(f32[2,256,192]{2,1,0:T(8,128)S(1)} %bitcast.62), channel_id=1, source_target_pairs={{0,0},{1,1},{2,8},{3,9},{4,16},{5,17},{6,24},{7,25},{8,2},{9,3},{1... | collective-permute-start | bytes 1179656 | tf_op jit(solution)/shard_map/ppermute | solution.py:85
  345.4 24.6 %copy-start.3 = (f32[256,192]{1,0:T(8,128)S(1)}, f32[256,192]{1,0:T(8,128)}, u32[]{:S(2)}) copy-start(f32[256,192]{1,0:T(8,128)} %get-tuple-element.139) | copy-start | bytes 589828
  345.5 24.6 %copy-start.4 = (f32[256,192]{1,0:T(8,128)S(1)}, f32[256,192]{1,0:T(8,128)}, u32[]{:S(2)}) copy-start(f32[256,192]{1,0:T(8,128)} %get-tuple-element.135.guess_ref) | copy-start | bytes 589828
